TPU v7x, 32 devices: a whole 2x2x4 slice. The times are simulated.
32 devices in a mesh: seq: 8 (over z, x), exp: 4 (over y, core).
Axes of the slice: x: 2, y: 2, z: 4, core: 2. Of those that a mesh axis runs over, the one named last changes fastest.
Arguments:
- block_input: float32 [4096, 768], P(('seq', 'exp')), may hold values from -6 to 6
- seq_lengths: int32 [10], replicated, may hold values from 1 to 2048, 4096 in all
- expert_ids: int32 [4096, 1], P(('seq', 'exp')), may hold values from 0 to 3
- output_grad: float32 [4096, 768], P(('seq', 'exp')), may hold values from -6 to 6
- mixer_gain: float32 [768], replicated, may hold values from 0.5 to 1.5
- in_proj: float32 [768, 3072], replicated, may hold values from -0.21875 to 0.21875
- conv_weight: float32 [4, 1536], replicated, may hold values from -3 to 3
- conv_bias: float32 [1536], replicated, may hold values from -1.75 to 1.75
- state_proj: float32 [1536, 80], replicated, may hold values from -0.15625 to 0.15625
- step_proj: float32 [48, 1536], replicated, may hold values from -0.875 to 0.875
- step_bias: float32 [1536], replicated, may hold values from -7 to -2.5
- decay_log: float32 [1536, 16], replicated, may hold values from 0 to 2.77
- skip_gain: float32 [1536], replicated, may hold values from 0.5 to 1.5
- out_proj: float32 [1536, 768], replicated, may hold values from -0.3125 to 0.3125
- router_gain: float32 [768], replicated, may hold values from 0.5 to 1.5
- router: float32 [768, 4], replicated, may hold values from -0.15625 to 0.15625
- expert_up: float32 [4, 768, 3072], P('exp', None, 'seq'), may hold values from -0.21875 to 0.21875
- expert_down: float32 [4, 3072, 768], P('exp', 'seq'), may hold values from -0.875 to 0.875
Outputs:
- block_output: float32 [4096, 768], P(('seq', 'exp'))
- input_grad: float32 [4096, 768], P(('seq', 'exp'))
- grad_mixer_gain: float32 [768], replicated
- grad_in_proj: float32 [768, 3072], replicated
- grad_conv_weight: float32 [4, 1536], replicated
- grad_conv_bias: float32 [1536], replicated
- grad_state_proj: float32 [1536, 80], replicated
- grad_step_proj: float32 [48, 1536], replicated
- grad_step_bias: float32 [1536], replicated
- grad_decay_log: float32 [1536, 16], replicated
- grad_skip_gain: float32 [1536], replicated
- grad_out_proj: float32 [1536, 768], replicated
- grad_router_gain: float32 [768], replicated
- grad_router: float32 [768, 4], replicated
- grad_expert_up: float32 [4, 768, 3072], P('exp', None, 'seq')
- grad_expert_down: float32 [4, 3072, 768], P('exp', 'seq')
- expert_load: int32 [4], replicated
- dropped_load: int32 [4], replicated
All inputs are finite; a program needn't handle non-finite values.
Results may differ from a plain program's by a relative error of at most 0.0003.
Values sent between devices are 32-bit elements; how exact they have to be, the bound alone decides.
No kernel may reach another device: no remote copies, remote signals or barrier semaphores. Data moves between devices by JAX's collectives and lax.ppermute only.
A program may use at most 448 MiB of HBM per device.

v0:
```python
import jax
import jax.numpy as jnp
from jax import lax
from jax.sharding import PartitionSpec as P

precise = lax.Precision.HIGHEST
epsilon = 1e-05


def passed_along(block, axis, distance):
    devices = range(lax.axis_size(axis))
    route = [(i - distance, i) for i in devices if i - distance in devices]
    return lax.ppermute(block, axis, route)


def entering(value, axis, join, neutral, backward):
    count, mine = (lax.axis_size(axis), lax.axis_index(axis))
    pieces = jax.tree.map(lambda part: lax.all_gather(part, axis), value)
    if backward:
        pieces = jax.tree.map(lambda part: part[::-1], pieces)
        mine = count - 1 - mine
    so_far = jax.tree.map(
        lambda part, zero: jnp.full_like(part, 0) + jnp.asarray(zero, part.dtype), value, neutral
    )

    def lap(position, so_far):
        longer = join(so_far, jax.tree.map(lambda part: part[position], pieces))
        return jax.tree.map(lambda new, old: jnp.where(position < mine, new, old), longer, so_far)

    return lax.fori_loop(0, count - 1, lap, so_far)


def matmul_high(left, right):
    return jnp.dot(left, right, precision=precise, preferred_element_type=jnp.float32)


def rms_scale(values_in, gain):
    return (
        values_in
        * lax.rsqrt(jnp.mean(values_in * values_in, axis=1, keepdims=True) + epsilon)
        * gain
    )


def chain_states(earlier, later):
    return (later[0] * earlier[0], later[0] * earlier[1] + later[1])


def per_device(
    block_input,
    seq_lengths,
    expert_ids,
    output_grad,
    mixer_gain,
    in_proj,
    conv_weight,
    conv_bias,
    state_proj,
    step_proj,
    step_bias,
    decay_log,
    skip_gain,
    out_proj,
    router_gain,
    router,
    expert_up,
    expert_down,
):
    tokens_n = block_input.shape[0]
    kernel_taps = conv_weight.shape[0]
    inner_width = in_proj.shape[1] // 2
    low_rank = step_proj.shape[0]
    state_size = decay_log.shape[1]
    experts_n = router.shape[1]
    capacity = (5 * tokens_n + 4 * experts_n - 1) // (4 * experts_n)
    span_index = lax.axis_index(("seq", "exp"))
    span_first = span_index * tokens_n
    position = span_first + jnp.arange(tokens_n, dtype=jnp.int32)
    seq_starts = jnp.cumsum(seq_lengths) - seq_lengths
    before = seq_starts[None, :] <= position[:, None]
    own_start = jnp.max(jnp.where(before, seq_starts[None, :], 0), axis=1)
    fresh = (own_start == position).astype(jnp.float32)
    alive = (own_start < span_first).astype(jnp.float32)
    tap_pos = (
        position[:, None] - (kernel_taps - 1) + jnp.arange(kernel_taps, dtype=jnp.int32)[None, :]
    )
    tap_valid = (tap_pos >= own_start[:, None]).astype(jnp.float32)

    def project_in(block_input, mixer_gain, in_proj):
        joined = matmul_high(rms_scale(block_input, mixer_gain), in_proj)
        return (joined[:, :inner_width], joined[:, inner_width:])

    def conv_features(extended, conv_weight, conv_bias, state_proj, step_proj, step_bias):
        summed = jnp.broadcast_to(conv_bias[None, :], (tokens_n, inner_width))
        for offset in range(kernel_taps):
            summed = (
                summed
                + extended[offset : offset + tokens_n]
                * tap_valid[:, offset : offset + 1]
                * conv_weight[offset][None, :]
            )
        activated = jax.nn.silu(summed)
        projected = matmul_high(activated, state_proj)
        step_sizes = jax.nn.softplus(matmul_high(projected[:, :low_rank], step_proj) + step_bias)
        return (
            activated,
            step_sizes,
            projected[:, low_rank : low_rank + state_size],
            projected[:, low_rank + state_size :],
        )

    def scan_part(activated, step_sizes, in_state, out_state, decay_log):
        decay_rate = -jnp.exp(decay_log)
        block_len = min(32, tokens_n)
        blocks = tokens_n // block_len

        def advance(carried, pieces):
            act_b, step_b, in_b, out_b, fresh_b = pieces
            outputs = []
            for index in range(block_len):
                decay_now = jnp.exp(step_b[index][:, None] * decay_rate) * (1.0 - fresh_b[index])
                carried = (
                    decay_now * carried
                    + (step_b[index] * act_b[index])[:, None] * in_b[index][None, :]
                )
                outputs.append(jnp.sum(carried * out_b[index][None, :], axis=1))
            return (carried, jnp.stack(outputs))

        pieces = tuple(
            (
                member.reshape((blocks, block_len) + member.shape[1:])
                for member in (activated, step_sizes, in_state, out_state, fresh)
            )
        )
        zero_end, local_out = lax.scan(advance, jnp.zeros(decay_log.shape, jnp.float32), pieces)
        running_end = jnp.sum(step_sizes, axis=0)
        end_decay = jnp.exp(running_end[:, None] * decay_rate) * alive[tokens_n - 1]
        return (local_out.reshape(tokens_n, -1), zero_end, end_decay)

    def carry_terms(out_state, step_sizes, decay_log, start_state):
        decay_rate = -jnp.exp(decay_log)
        running = jnp.cumsum(step_sizes, axis=0)
        block_len = min(64, tokens_n)
        blocks = tokens_n // block_len

        def one_block(pieces):
            run_b, out_b, alive_b = pieces
            factor = jnp.exp(run_b[:, :, None] * decay_rate[None]) * start_state[None]
            return jnp.sum(factor * out_b[:, None, :], axis=2) * alive_b[:, None]

        shaped = (
            running.reshape(blocks, block_len, -1),
            out_state.reshape(blocks, block_len, -1),
            alive.reshape(blocks, block_len),
        )
        return lax.map(one_block, shaped).reshape(tokens_n, -1)

    def mixer_out(scan_out, activated, gate_z, skip_gain, out_proj, block_input):
        return block_input + matmul_high(
            (scan_out + skip_gain * activated) * jax.nn.silu(gate_z), out_proj
        )

    chosen = (expert_ids == jnp.arange(experts_n, dtype=jnp.int32)[None, :]).astype(jnp.float32)

    def route(resid, router_gain, router):
        normed_moe = rms_scale(resid, router_gain)
        probs = jax.nn.softmax(matmul_high(normed_moe, router), axis=1)
        return (normed_moe, jnp.sum(probs * chosen, axis=1))

    (inner_x, gate_z), proj_back = jax.vjp(project_in, block_input, mixer_gain, in_proj)
    previous = passed_along(inner_x[tokens_n - kernel_taps + 1 :], ("seq", "exp"), 1)
    extended = jnp.concatenate([previous, inner_x], axis=0)
    (activated, step_sizes, in_state, out_state), conv_back = jax.vjp(
        conv_features, extended, conv_weight, conv_bias, state_proj, step_proj, step_bias
    )
    (local_out, zero_end, end_decay), scan_back = jax.vjp(
        scan_part, activated, step_sizes, in_state, out_state, decay_log
    )
    identity_pair = (jnp.ones_like(end_decay), jnp.zeros_like(zero_end))
    start_state = entering(
        (end_decay, zero_end), ("seq", "exp"), chain_states, identity_pair, False
    )[1]
    correction, carry_back = jax.vjp(carry_terms, out_state, step_sizes, decay_log, start_state)
    scan_out = local_out + correction
    resid, mixer_back = jax.vjp(
        mixer_out, scan_out, activated, gate_z, skip_gain, out_proj, block_input
    )
    (normed_moe, gate), route_back = jax.vjp(route, resid, router_gain, router)
    ahead_count = jnp.cumsum(chosen, axis=0) - chosen
    slot_rank = jnp.sum(ahead_count * chosen, axis=1).astype(jnp.int32)
    kept = (slot_rank < capacity).astype(jnp.float32)
    slot_ids = expert_ids[:, 0] * capacity + slot_rank
    dispatch = (
        jnp.arange(experts_n * capacity, dtype=jnp.int32)[:, None] == slot_ids[None, :]
    ).astype(jnp.float32) * kept[None, :]
    buffer = matmul_high(dispatch, normed_moe).reshape(experts_n, capacity, -1)
    full_up, full_down = (
        lax.all_gather(expert_up, "seq", axis=2, tiled=True),
        lax.all_gather(expert_down, "seq", axis=1, tiled=True),
    )
    received = lax.all_to_all(buffer, "exp", split_axis=0, concat_axis=0, tiled=True)
    local_n = full_up.shape[0]
    items = received.shape[1]
    grouped = received.reshape(-1, local_n, items, received.shape[2])
    hidden_pre = jnp.einsum("secd,edf->secf", grouped, full_up, precision=precise)
    result = jnp.einsum("secf,efd->secd", jax.nn.gelu(hidden_pre), full_down, precision=precise)
    returned = lax.all_to_all(
        result.reshape(received.shape), "exp", split_axis=0, concat_axis=0, tiled=True
    )
    returned, received, hidden_pre = (
        returned,
        received,
        hidden_pre.reshape(received.shape[0], items, -1),
    )
    combined = jnp.einsum(
        "st,sd->td", dispatch, returned.reshape(experts_n * capacity, -1), precision=precise
    )
    block_output = resid + gate[:, None] * combined
    grad_gate = jnp.sum(output_grad * combined, axis=1)
    grad_back = jnp.einsum(
        "st,td->sd", dispatch, output_grad * gate[:, None], precision=precise
    ).reshape(experts_n, capacity, -1)
    grad_result = lax.all_to_all(grad_back, "exp", split_axis=0, concat_axis=0, tiled=True)
    use_up, use_down = (
        lax.all_gather(expert_up, "seq", axis=2, tiled=True),
        lax.all_gather(expert_down, "seq", axis=1, tiled=True),
    )
    local_n = use_up.shape[0]
    sources = grad_result.shape[0] // local_n
    grad_group = grad_result.reshape(sources, local_n, capacity, -1)
    hidden_group = hidden_pre.reshape(sources, local_n, capacity, -1)
    input_group = received.reshape(sources, local_n, capacity, -1)
    gelu_hidden, gelu_back = jax.vjp(jax.nn.gelu, hidden_group)
    grad_down_full = jnp.einsum("secf,secd->efd", gelu_hidden, grad_group, precision=precise)
    grad_hidden = gelu_back(jnp.einsum("secd,efd->secf", grad_group, use_down, precision=precise))[
        0
    ]
    grad_up_full = jnp.einsum("secd,secf->edf", input_group, grad_hidden, precision=precise)
    grad_received = jnp.einsum("secf,edf->secd", grad_hidden, use_up, precision=precise).reshape(
        grad_result.shape
    )
    grad_buffer = lax.all_to_all(grad_received, "exp", split_axis=0, concat_axis=0, tiled=True)
    grad_expert_up, grad_expert_down = (
        lax.psum_scatter(grad_up_full, "seq", scatter_dimension=2, tiled=True),
        lax.psum_scatter(grad_down_full, "seq", scatter_dimension=1, tiled=True),
    )
    grad_normed_moe = jnp.einsum(
        "st,sd->td", dispatch, grad_buffer.reshape(experts_n * capacity, -1), precision=precise
    )
    grad_resid_route, grad_router_gain, grad_router = route_back((grad_normed_moe, grad_gate))
    grad_resid = output_grad + grad_resid_route
    grad_scan, grad_act_mix, grad_gate_z, grad_skip_gain, grad_out_proj, grad_input_mix = (
        mixer_back(grad_resid)
    )
    grad_out_carry, grad_step_carry, grad_decay_carry, grad_start = carry_back(grad_scan)
    grad_end = entering((end_decay, grad_start), ("seq", "exp"), chain_states, identity_pair, True)[
        1
    ]
    grad_act_scan, grad_step_scan, grad_in_state, grad_out_scan, grad_decay_scan = scan_back(
        (grad_scan, grad_end, grad_end * start_state)
    )
    (
        grad_extended,
        grad_conv_weight,
        grad_conv_bias,
        grad_state_proj,
        grad_step_proj,
        grad_step_bias,
    ) = conv_back(
        (
            grad_act_mix + grad_act_scan,
            grad_step_carry + grad_step_scan,
            grad_in_state,
            grad_out_carry + grad_out_scan,
        )
    )
    edge_grad = passed_along(grad_extended[: kernel_taps - 1], ("seq", "exp"), -1)
    grad_inner = grad_extended[kernel_taps - 1 :] + jnp.concatenate(
        [jnp.zeros((tokens_n - kernel_taps + 1, inner_width), jnp.float32), edge_grad], axis=0
    )
    grad_input_proj, grad_mixer_gain, grad_in_proj = proj_back((grad_inner, grad_gate_z))
    input_grad = grad_input_mix + grad_input_proj
    grad_decay_log = grad_decay_carry + grad_decay_scan
    load_local = jnp.sum(chosen, axis=0)
    drop_local = jnp.sum(chosen * (1.0 - kept)[:, None], axis=0)
    summed_grads = lax.psum(
        (
            grad_mixer_gain,
            grad_in_proj,
            grad_conv_weight,
            grad_conv_bias,
            grad_state_proj,
            grad_step_proj,
            grad_step_bias,
            grad_decay_log,
            grad_skip_gain,
            grad_out_proj,
            grad_router_gain,
            grad_router,
            load_local,
            drop_local,
        ),
        ("seq", "exp"),
    )
    expert_load = summed_grads[12].astype(jnp.int32)
    dropped_load = summed_grads[13].astype(jnp.int32)
    return (
        block_output,
        input_grad,
        summed_grads[0],
        summed_grads[1],
        summed_grads[2],
        summed_grads[3],
        summed_grads[4],
        summed_grads[5],
        summed_grads[6],
        summed_grads[7],
        summed_grads[8],
        summed_grads[9],
        summed_grads[10],
        summed_grads[11],
        grad_expert_up,
        grad_expert_down,
        expert_load,
        dropped_load,
    )


def solution(mesh):
    in_specs = (
        P(("seq", "exp"), None),
        P(),
        P(("seq", "exp"), None),
        P(("seq", "exp"), None),
        P(),
        P(),
        P(),
        P(),
        P(),
        P(),
        P(),
        P(),
        P(),
        P(),
        P(),
        P(),
        P("exp", None, "seq"),
        P("exp", "seq", None),
    )
    out_specs = (
        P(("seq", "exp"), None),
        P(("seq", "exp"), None),
        P(),
        P(),
        P(),
        P(),
        P(),
        P(),
        P(),
        P(),
        P(),
        P(),
        P(),
        P(),
        P("exp", None, "seq"),
        P("exp", "seq", None),
        P(),
        P(),
    )
    return jax.shard_map(
        per_device, mesh=mesh, in_specs=in_specs, out_specs=out_specs, check_vma=False
    )
```

profile of v0, /device:TPU:0, one launch (start us, length us, event | category | flops | bytes accessed | tf_op | source)
XLA Modules:
  0.0 3072.3 jit_solution(16956716026353753182)
XLA Ops:
  9.0 7.8 fusion.626
  36.6 739.1 %while.750 = (s32[]{:T(128)}, f32[1536,16]{0,1:T(8,128)S(1)}, f32[4,32,1536]{2,1,0:T(8,128)}, f32[4,1536,1]{1,2,0:T(1,128)}, f32[4,1536,16]{1,2,0:T(8,128)}, /*i...) while((s32[]{:T(128)}, f32[1536,16]{0,1:T(8,128)S(1)}, ...), condition=%wide.region_36.37_spmd.clone, body=%wide.region_3.36_spmd.clone.sunk | while | flops 11132994 | bytes 24794744 | solution.py:135
  785.5 52.7 %all-gather.15.cloned.1.call-done = f32[49152,16]{0,1:T(8,128)} async-done(((f32[1536,16]{0,1:T(8,128)}), f32[49152,16]{0,1:T(8,128)}) %all-gather.15.cloned.1.call-update) | async-done | bytes 3145744 | tf_op jit(solution)/shard_map/all_gather | solution.py:18
  838.2 5.4 copy.107
  843.6 56.0 %all-gather.13.cloned.1.call-done = f32[49152,16]{0,1:T(8,128)} async-done(((f32[1536,16]{0,1:T(8,128)}), f32[49152,16]{0,1:T(8,128)}) %all-gather.13.cloned.1.call-update) | async-done | bytes 3145744 | tf_op jit(solution)/shard_map/all_gather | solution.py:18
  903.4 68.8 %while.751 = (s32[]{:T(128)}, f32[1536,16]{0,1:T(8,128)S(1)}, s32[]{:T(128)}, f32[32,1536,16]{1,2,0:T(8,128)}, f32[32,1536,16]{1,0,2:T(8,128)}, /*index=5*/s32[]{:T(128)}, s32[]{:T(128)}) while((s32[]{:T(128)}, f32[1536,16]{0,1:T(8,128)S(1)}, s32[]{:T(128)}, f32[32,1536,16]{1,2,0:T(8,128)}, f32[32,1536,16]{1,0,2:T(8,128)}, ...), condition=%wide.region_40.41_spmd.clone, body=%wide.region_39.40_spmd.clone.sunk | while | flops 98308 | bytes 589929 | solution.py:30
  973.2 25.3 while.749
  977.8 6.1 multiply_dynamic-update-slice_fusion.38
  990.4 6.3 multiply_dynamic-update-slice_fusion.38
  1000.5 5.6 multiply_reduce_fusion.141
  1012.7 7.9 all-to-all-done
  1021.4 16.8 all-gather.9.cloned.1.call-done
  1038.3 8.4 fusion.586
  1046.7 129.9 %all-gather.11.cloned.1.call-done = f32[1,3072,768]{2,1,0:T(8,128)} async-done(((f32[1,384,768]{2,1,0:T(8,128)}), f32[1,3072,768]{2,1,0:T(8,128)}) %all-gather.11.cloned.1.call-update) | async-done | bytes 9437200 | tf_op jit(solution)/shard_map/all_gather | solution.py:199
  1176.5 9.3 fusion.580
  1192.6 5.9 all-to-all-done.1
  1204.1 11.0 all_to_all.20
  1215.2 13.0 fusion.598
  1229.5 13.1 fusion.582
  1247.2 7.5 all-to-all-done.3
  1257.9 9.3 multiply_reduce_fusion.131
  1268.8 23.9 while.752
  1271.2 7.2 multiply_reduce_fusion.199
  1283.2 7.2 multiply_reduce_fusion.199
  1299.3 15.4 reduce_window_sum.42
  1314.7 7.2 fusion.700
  1321.9 27.9 all-gather.17.cloned.1.call-done
  1349.8 5.4 copy.108
  1355.2 8.1 rev.7
  1363.4 68.2 %while.753 = (s32[]{:T(128)}, f32[1536,16]{0,1:T(8,128)S(1)}, s32[]{:T(128)}, f32[32,1536,16]{1,2,0:T(8,128)}, f32[32,1536,16]{1,0,2:T(8,128)}, /*index=5*/s32[]{:T(128)}, s32[]{:T(128)}) while((s32[]{:T(128)}, f32[1536,16]{0,1:T(8,128)S(1)}, s32[]{:T(128)}, f32[32,1536,16]{1,2,0:T(8,128)}, f32[32,1536,16]{1,0,2:T(8,128)}, ...), condition=%wide.region_60.61_spmd.clone, body=%wide.region_59.60_spmd.clone.sunk | while | flops 98308 | bytes 589929 | solution.py:30
  1434.8 710.7 %while.754 = (s32[]{:T(128)}, f32[1536,16]{0,1:T(8,128)}, f32[1536,16]{0,1:T(8,128)S(1)}, f32[4,32,1536]{2,1,0:T(8,128)}, f32[4,32,1536]{2,1,0:T(8,128)}, /*inde...) while((s32[]{:T(128)}, f32[1536,16]{0,1:T(8,128)}, ...), condition=%wide.region_190.191_spmd.clone, body=%wide.region_61.190_spmd.clone.sunk | while | flops 17356836 | bytes 57770112 | solution.py:135
  1464.1 13.3 multiply_reduce_fusion.200
  1506.5 15.2 multiply_reduce_fusion.201
  1641.6 13.3 multiply_reduce_fusion.200
  1683.9 15.2 multiply_reduce_fusion.201
  1819.2 13.3 multiply_reduce_fusion.200
  1861.6 15.2 multiply_reduce_fusion.201
  1996.3 13.3 multiply_reduce_fusion.200
  2038.7 15.2 multiply_reduce_fusion.201
  2160.2 10.1 fusion.603
  2172.0 10.4 convolution_bitcast_fusion
  2184.1 10.2 convolution_bitcast_fusion.1
  2196.0 12.1 multiply_reduce_fusion.137
  2208.2 44.7 %all-reduce.174 = (f32[768]{0:T(1024)}, f32[4,1536]{1,0:T(4,128)}, f32[1536]{0:T(1024)}, f32[1536]{0:T(1024)}, f32[1536]{0:T(1024)}, /*index=5*/f32[768]{0:T(102...) all-reduce(f32[768]{0:T(1024)S(1)} %get-tuple-element.12840, ...), channel_id=1, replica_groups=mesh['seq'=8,'exp'=4] {'seq','exp'}, use_global_device_ids=true, to_apply=%region_195.196 | all-reduce | flops 15368 | bytes 122944 | tf_op jit(solution)/shard_map/psum | solution.py:286
  2254.8 460.0 %all-reduce.178.cloned.1.call-done = (f32[768,3072]{1,0:T(8,128)}, f32[1536,80]{0,1:T(8,128)}, f32[48,1536]{1,0:T(8,128)}, f32[1536,16]{0,1:T(8,128)}, f32[1536,768]{1,0:T(8,128)}) async-done(((f32[768,3072]{1,0:T(8,128)}, f32[1536,80]{0,1:T(8,128)}, f32[48,1536]{1,0:T(8,128)}, f32[1536,16]{0,1:T(8,128)}, f32[1536,768]{1,0:T(8,128)}), (f32[768,3072]{1,0:T(8,128)}, f32[1536,80]{0,1:T(8,128)}, ...) | async-done | bytes 15040528 | tf_op jit(solution)/shard_map/psum | solution.py:286
  2714.8 170.9 %reduce-scatter.5.cloned.1.call-done = f32[1,384,768]{2,1,0:T(8,128)} async-done(((f32[1,3072,768]{2,1,0:T(8,128)}), f32[1,384,768]{2,1,0:T(8,128)}) %reduce-scatter.5.cloned.1.call-update) | async-done | bytes 1179664 | tf_op jit(solution)/shard_map/reduce_scatter | solution.py:245
  2885.7 166.6 %reduce-scatter.3.cloned.1.call-done = f32[1,768,384]{2,1,0:T(8,128)} async-done(((f32[1,768,3072]{2,1,0:T(8,128)}), f32[1,768,384]{2,1,0:T(8,128)}) %reduce-scatter.3.cloned.1.call-update) | async-done | bytes 1179664 | tf_op jit(solution)/shard_map/reduce_scatter | solution.py:244
  3052.2 8.8 copy.1512
  (3618 shorter events, 1503.3 us)
Async XLA Ops:
  7.2 831.0 %all-gather.15.cloned.1.call-start = ((), (), s32[]{:S(2)}) async-start(), calls=%async_computation.11 | async-start | bytes 3244032 | tf_op jit(solution)/shard_map/all_gather | solution.py:18
  16.8 9.4 collective-permute-start
  113.1 108.3 %copy-start.100 = (f32[4,32,16]{2,1,0:T(8,128)S(1)}, f32[4,32,16]{2,1,0:T(8,128)}, u32[]{:S(2)}) copy-start(f32[4,32,16]{2,1,0:T(8,128)} %copy-done.99) | copy-start | bytes 24580 | tf_op jit(solution)/shard_map/jvp()/while
  113.1 108.3 %copy-start.192 = (f32[4,1,16]{2,1,0:T(1,128)S(1)}, f32[4,1,16]{2,1,0:T(1,128)}, u32[]{:S(2)}) copy-start(f32[4,1,16]{2,1,0:T(1,128)} %copy-done.191) | copy-start | bytes 772 | tf_op jit(solution)/shard_map/jvp()/while
  116.7 104.5 %copy-start.205 = (f32[4]{0:T(128)}, f32[4]{0:T(128)S(1)}, u32[]{:S(2)}) copy-start(f32[4]{0:T(128)S(1)} %get-tuple-element.21621) | copy-start | bytes 52 | tf_op jit(solution)/shard_map/jvp()/while
  116.7 104.5 %copy-start.221 = (f32[4]{0:T(128)}, f32[4]{0:T(128)S(1)}, u32[]{:S(2)}) copy-start(f32[4]{0:T(128)S(1)} %get-tuple-element.21632) | copy-start | bytes 52 | tf_op jit(solution)/shard_map/jvp()/while
  116.8 104.4 %copy-start.225 = (f32[4]{0:T(128)}, f32[4]{0:T(128)S(1)}, u32[]{:S(2)}) copy-start(f32[4]{0:T(128)S(1)} %get-tuple-element.21642) | copy-start | bytes 52 | tf_op jit(solution)/shard_map/jvp()/while
  116.8 104.4 %copy-start.227 = (f32[4]{0:T(128)}, f32[4]{0:T(128)S(1)}, u32[]{:S(2)}) copy-start(f32[4]{0:T(128)S(1)} %get-tuple-element.21652) | copy-start | bytes 52 | tf_op jit(solution)/shard_map/jvp()/while
  116.9 104.4 %copy-start.229 = (f32[4]{0:T(128)}, f32[4]{0:T(128)S(1)}, u32[]{:S(2)}) copy-start(f32[4]{0:T(128)S(1)} %get-tuple-element.21662) | copy-start | bytes 52 | tf_op jit(solution)/shard_map/jvp()/while
  116.9 104.4 %copy-start.231 = (f32[4]{0:T(128)}, f32[4]{0:T(128)S(1)}, u32[]{:S(2)}) copy-start(f32[4]{0:T(128)S(1)} %get-tuple-element.21672) | copy-start | bytes 52 | tf_op jit(solution)/shard_map/jvp()/while
  297.8 108.3 %copy-start.100 = (f32[4,32,16]{2,1,0:T(8,128)S(1)}, f32[4,32,16]{2,1,0:T(8,128)}, u32[]{:S(2)}) copy-start(f32[4,32,16]{2,1,0:T(8,128)} %copy-done.99) | copy-start | bytes 24580 | tf_op jit(solution)/shard_map/jvp()/while
  297.8 108.3 %copy-start.192 = (f32[4,1,16]{2,1,0:T(1,128)S(1)}, f32[4,1,16]{2,1,0:T(1,128)}, u32[]{:S(2)}) copy-start(f32[4,1,16]{2,1,0:T(1,128)} %copy-done.191) | copy-start | bytes 772 | tf_op jit(solution)/shard_map/jvp()/while
  301.4 104.5 %copy-start.205 = (f32[4]{0:T(128)}, f32[4]{0:T(128)S(1)}, u32[]{:S(2)}) copy-start(f32[4]{0:T(128)S(1)} %get-tuple-element.21621) | copy-start | bytes 52 | tf_op jit(solution)/shard_map/jvp()/while
  301.4 104.5 %copy-start.221 = (f32[4]{0:T(128)}, f32[4]{0:T(128)S(1)}, u32[]{:S(2)}) copy-start(f32[4]{0:T(128)S(1)} %get-tuple-element.21632) | copy-start | bytes 52 | tf_op jit(solution)/shard_map/jvp()/while
  301.5 104.4 %copy-start.225 = (f32[4]{0:T(128)}, f32[4]{0:T(128)S(1)}, u32[]{:S(2)}) copy-start(f32[4]{0:T(128)S(1)} %get-tuple-element.21642) | copy-start | bytes 52 | tf_op jit(solution)/shard_map/jvp()/while
  301.5 104.4 %copy-start.227 = (f32[4]{0:T(128)}, f32[4]{0:T(128)S(1)}, u32[]{:S(2)}) copy-start(f32[4]{0:T(128)S(1)} %get-tuple-element.21652) | copy-start | bytes 52 | tf_op jit(solution)/shard_map/jvp()/while
  301.6 104.4 %copy-start.229 = (f32[4]{0:T(128)}, f32[4]{0:T(128)S(1)}, u32[]{:S(2)}) copy-start(f32[4]{0:T(128)S(1)} %get-tuple-element.21662) | copy-start | bytes 52 | tf_op jit(solution)/shard_map/jvp()/while
  301.6 104.4 %copy-start.231 = (f32[4]{0:T(128)}, f32[4]{0:T(128)S(1)}, u32[]{:S(2)}) copy-start(f32[4]{0:T(128)S(1)} %get-tuple-element.21672) | copy-start | bytes 52 | tf_op jit(solution)/shard_map/jvp()/while
  482.4 108.4 %copy-start.100 = (f32[4,32,16]{2,1,0:T(8,128)S(1)}, f32[4,32,16]{2,1,0:T(8,128)}, u32[]{:S(2)}) copy-start(f32[4,32,16]{2,1,0:T(8,128)} %copy-done.99) | copy-start | bytes 24580 | tf_op jit(solution)/shard_map/jvp()/while
  482.4 108.3 %copy-start.192 = (f32[4,1,16]{2,1,0:T(1,128)S(1)}, f32[4,1,16]{2,1,0:T(1,128)}, u32[]{:S(2)}) copy-start(f32[4,1,16]{2,1,0:T(1,128)} %copy-done.191) | copy-start | bytes 772 | tf_op jit(solution)/shard_map/jvp()/while
  486.0 104.6 %copy-start.205 = (f32[4]{0:T(128)}, f32[4]{0:T(128)S(1)}, u32[]{:S(2)}) copy-start(f32[4]{0:T(128)S(1)} %get-tuple-element.21621) | copy-start | bytes 52 | tf_op jit(solution)/shard_map/jvp()/while
  486.0 104.6 %copy-start.221 = (f32[4]{0:T(128)}, f32[4]{0:T(128)S(1)}, u32[]{:S(2)}) copy-start(f32[4]{0:T(128)S(1)} %get-tuple-element.21632) | copy-start | bytes 52 | tf_op jit(solution)/shard_map/jvp()/while
  486.1 104.5 %copy-start.225 = (f32[4]{0:T(128)}, f32[4]{0:T(128)S(1)}, u32[]{:S(2)}) copy-start(f32[4]{0:T(128)S(1)} %get-tuple-element.21642) | copy-start | bytes 52 | tf_op jit(solution)/shard_map/jvp()/while
  486.1 104.5 %copy-start.227 = (f32[4]{0:T(128)}, f32[4]{0:T(128)S(1)}, u32[]{:S(2)}) copy-start(f32[4]{0:T(128)S(1)} %get-tuple-element.21652) | copy-start | bytes 52 | tf_op jit(solution)/shard_map/jvp()/while
  486.2 104.4 %copy-start.229 = (f32[4]{0:T(128)}, f32[4]{0:T(128)S(1)}, u32[]{:S(2)}) copy-start(f32[4]{0:T(128)S(1)} %get-tuple-element.21662) | copy-start | bytes 52 | tf_op jit(solution)/shard_map/jvp()/while
  486.2 104.4 %copy-start.231 = (f32[4]{0:T(128)}, f32[4]{0:T(128)S(1)}, u32[]{:S(2)}) copy-start(f32[4]{0:T(128)S(1)} %get-tuple-element.21672) | copy-start | bytes 52 | tf_op jit(solution)/shard_map/jvp()/while
  486.3 104.3 %copy-start.233 = (f32[4]{0:T(128)}, f32[4]{0:T(128)S(1)}, u32[]{:S(2)}) copy-start(f32[4]{0:T(128)S(1)} %get-tuple-element.21682) | copy-start | bytes 52 | tf_op jit(solution)/shard_map/jvp()/while
  667.2 108.3 %copy-start.100 = (f32[4,32,16]{2,1,0:T(8,128)S(1)}, f32[4,32,16]{2,1,0:T(8,128)}, u32[]{:S(2)}) copy-start(f32[4,32,16]{2,1,0:T(8,128)} %copy-done.99) | copy-start | bytes 24580 | tf_op jit(solution)/shard_map/jvp()/while
  667.3 108.3 %copy-start.192 = (f32[4,1,16]{2,1,0:T(1,128)S(1)}, f32[4,1,16]{2,1,0:T(1,128)}, u32[]{:S(2)}) copy-start(f32[4,1,16]{2,1,0:T(1,128)} %copy-done.191) | copy-start | bytes 772 | tf_op jit(solution)/shard_map/jvp()/while
  670.8 104.5 %copy-start.205 = (f32[4]{0:T(128)}, f32[4]{0:T(128)S(1)}, u32[]{:S(2)}) copy-start(f32[4]{0:T(128)S(1)} %get-tuple-element.21621) | copy-start | bytes 52 | tf_op jit(solution)/shard_map/jvp()/while
  670.8 104.5 %copy-start.221 = (f32[4]{0:T(128)}, f32[4]{0:T(128)S(1)}, u32[]{:S(2)}) copy-start(f32[4]{0:T(128)S(1)} %get-tuple-element.21632) | copy-start | bytes 52 | tf_op jit(solution)/shard_map/jvp()/while
  670.9 104.4 %copy-start.225 = (f32[4]{0:T(128)}, f32[4]{0:T(128)S(1)}, u32[]{:S(2)}) copy-start(f32[4]{0:T(128)S(1)} %get-tuple-element.21642) | copy-start | bytes 52 | tf_op jit(solution)/shard_map/jvp()/while
  670.9 104.4 %copy-start.227 = (f32[4]{0:T(128)}, f32[4]{0:T(128)S(1)}, u32[]{:S(2)}) copy-start(f32[4]{0:T(128)S(1)} %get-tuple-element.21652) | copy-start | bytes 52 | tf_op jit(solution)/shard_map/jvp()/while
  671.0 104.4 %copy-start.229 = (f32[4]{0:T(128)}, f32[4]{0:T(128)S(1)}, u32[]{:S(2)}) copy-start(f32[4]{0:T(128)S(1)} %get-tuple-element.21662) | copy-start | bytes 52 | tf_op jit(solution)/shard_map/jvp()/while
  671.0 104.4 %copy-start.231 = (f32[4]{0:T(128)}, f32[4]{0:T(128)S(1)}, u32[]{:S(2)}) copy-start(f32[4]{0:T(128)S(1)} %get-tuple-element.21672) | copy-start | bytes 52 | tf_op jit(solution)/shard_map/jvp()/while
  776.4 123.1 %all-gather.13.cloned.1.call-start = ((), (), s32[]{:S(2)}) async-start(), calls=%async_computation.10 | async-start | bytes 3244032 | tf_op jit(solution)/shard_map/all_gather | solution.py:18
  777.2 261.1 %all-gather.9.cloned.1.call-start = ((), (), s32[]{:S(2)}) async-start(), calls=%async_computation.6 | async-start | bytes 10616832 | tf_op jit(solution)/shard_map/all_gather | solution.py:198
  777.9 398.6 %all-gather.11.cloned.1.call-start = ((), (), s32[]{:S(2)}) async-start(), calls=%async_computation.7 | async-start | bytes 10616832 | tf_op jit(solution)/shard_map/all_gather | solution.py:199
  1006.2 249.8 %copy-start.150 = (f32[128]{0:T(128)}, f32[128]{0:T(128)S(1)}, u32[]{:S(2)}) copy-start(f32[128]{0:T(128)S(1)} %fusion.679) | copy-start | bytes 1540
  1008.3 12.3 all-to-all-start
  1046.7 168.5 %copy-start.2 = (f32[4,1,40,3072]{3,2,0,1:T(8,128)}, f32[4,1,40,3072]{3,2,0,1:T(8,128)S(1)}, u32[]{:S(2)}) copy-start(f32[4,1,40,3072]{3,2,0,1:T(8,128)S(1)} %fusion.586) | copy-start | bytes 5898244
  1185.9 12.7 all-to-all-start.1
  1242.6 12.1 all-to-all-start.3
  1246.2 103.6 %all-gather.17.cloned.1.call-start = ((), (), s32[]{:S(2)}) async-start(), calls=%async_computation.12 | async-start | bytes 3244032 | tf_op jit(solution)/shard_map/all_gather | solution.py:18
  1293.3 1421.5 %all-reduce.178.cloned.1.call-start = ((), (), s32[]{:S(2)}) async-start(), calls=%async_computation.13 | async-start | bytes 30081024 | tf_op jit(solution)/shard_map/psum | solution.py:286
  2157.0 3.1 collective-permute-start.1
  2170.4 715.3 %reduce-scatter.5.cloned.1.call-start = ((), (), s32[]{:S(2)}) async-start(), calls=%async_computation.9 | async-start | bytes 10616832 | tf_op jit(solution)/shard_map/reduce_scatter | solution.py:245
  2182.4 869.8 %reduce-scatter.3.cloned.1.call-start = ((), (), s32[]{:S(2)}) async-start(), calls=%async_computation.8 | async-start | bytes 10616832 | tf_op jit(solution)/shard_map/reduce_scatter | solution.py:244
  (580 other events, 15908.5 us)
Sparse Core Ops, SparseCore 0:
  776.6 61.6 all-gather.14
  841.7 57.7 all-gather.12
  901.7 136.5 all-gather.8
  1040.3 136.1 all-gather.10
  1293.4 56.3 all-gather.16
  2170.5 544.2 all-reduce.177
  2720.9 164.7 reduce-scatter.4
  2889.8 162.3 reduce-scatter.2
where the time goes:
time: 3120 us; the launch traced here: 3070 us
  local copies, waits for them, and re-layouts  1110 us (36%)
  waiting for transfers between devices  1100 us (35%)
  other arithmetic  544 us (17%)
  matrix products  135 us (4%)
  loops' own time  92 us (3%)
  blocking collectives  55.7 us (2%)
    psum x1, waiting for transfers between devices, per_device(): lax.psum((grad_mixer_gain, grad_in_proj, grad_conv_weight, grad_conv_bias...  460 us
    dynamic_update_slice x388, local copies, waits for them, and re-layouts, scan_part(): lax.scan(advance, jnp.zeros(decay_log.shape, jnp.float32), pieces)  453 us
    dynamic_slice x324, local copies, waits for them, and re-layouts, scan_part(): lax.scan(advance, jnp.zeros(decay_log.shape, jnp.float32), pieces)  285 us
    reduce_scatter x1, waiting for transfers between devices, per_device(): lax.psum_scatter(grad_down_full, 'seq', scatter_dimension=1, tiled=True)  171 us
    reduce_scatter x1, waiting for transfers between devices, per_device(): lax.psum_scatter(grad_up_full, 'seq', scatter_dimension=2, tiled=True)  167 us
    all_gather x3, waiting for transfers between devices, entering(): pieces = jax.tree.map(lambda part: lax.all_gather(part, axis), value)  137 us
    all_gather x1, waiting for transfers between devices, per_device(): lax.all_gather(expert_down, 'seq', axis=1, tiled=True)  130 us
    mul x196, other arithmetic, advance(): step_b[index] * act_b[index]  128 us
  transfers between devices with their start and end apart: 13, of which 12 were waited for; matrix products, arithmetic and copies ran while one was open for 6% of the time, Pallas kernels for 0%

commit v1 on v0

v1 whole, which is shorter than its diff:
```python
import functools

import jax
import jax.numpy as jnp
from jax import lax
from jax.experimental import pallas as pl
from jax.experimental.pallas import tpu as pltpu
from jax.sharding import PartitionSpec as P

F32 = jnp.float32
BF16 = jnp.bfloat16
EPS = 1e-05
LOG2E = 1.4426950408889634
HALO = 16
RESET = 1e9
AXES = ("seq", "exp")
NN, NT, TN = ((1,), (0,)), ((1,), (1,)), ((0,), (0,))
VMEM_BYTES = 52 << 20


class Grid:
    def __init__(self):
        self.seq, self.exp = lax.axis_size("seq"), lax.axis_size("exp")
        self.outer = 4
        self.size = {
            "core": 2,
            "y": self.exp // 2,
            "inner": self.seq // self.outer,
            "outer": self.outer,
        }
        self.total = self.seq * self.exp
        index, step, self.step, self.at = lax.axis_index(AXES), 1, {}, {}
        for name in ("core", "y", "inner", "outer"):
            self.step[name] = step
            self.at[name] = (index // step) % self.size[name]
            step *= self.size[name]
        self.index = index

    def swap(self, block, name, mask):
        return self.swap_bits(block, mask * self.step[name])

    def swap_bits(self, block, bits):
        return lax.ppermute(block, AXES, [(i, i ^ bits) for i in range(self.total)])

    def along(self, block, distance):
        route = [(i - distance, i) for i in range(self.total) if 0 <= i - distance < self.total]
        return lax.ppermute(block, AXES, route)


def in_order(parts, place):
    bit = 1
    while bit < len(parts):
        turned = ((place // bit) % 2) == 1
        parts = [jnp.where(turned, parts[i ^ bit], parts[i]) for i in range(len(parts))]
        bit *= 2
    return parts


def scatter_rows(grid, block, name):
    count, place = grid.size[name], grid.at[name]
    if count == 1:
        return block
    rows = block.shape[0] // count
    piece = lambda s: lax.dynamic_slice_in_dim(block, (place ^ s) * rows, rows, 0)
    got = [grid.swap(piece(s), name, s) for s in range(1, count)]
    total = piece(0)
    for part in got:
        total = total + part
    return total


def gather_rows(grid, block, name):
    count = grid.size[name]
    if count == 1:
        return block
    parts = [block] + [grid.swap(block, name, s) for s in range(1, count)]
    return jnp.concatenate(in_order(parts, grid.at[name]), axis=0)


def sum_everywhere(grid, block):
    half = scatter_rows(grid, block, "core")
    rows, width = half.shape[0] // 2, half.shape[1]
    first = scatter_rows(grid, scatter_rows(grid, half[:rows], "inner"), "y")
    second = scatter_rows(grid, scatter_rows(grid, half[rows:], "y"), "inner")
    both = jnp.concatenate([first, second], axis=0)
    count, place = grid.size["outer"], grid.at["outer"]
    columns = width // count
    piece = lambda s: lax.dynamic_slice_in_dim(both, (place ^ s) * columns, columns, 1)
    got = [grid.swap(piece(s), "outer", s) for s in range(1, count)]
    total = piece(0)
    for part in got:
        total = total + part
    parts = [total] + [grid.swap(total, "outer", s) for s in range(1, count)]
    both = jnp.concatenate(in_order(parts, place), axis=1)
    own = both.shape[0] // 2
    first = gather_rows(grid, gather_rows(grid, both[:own], "y"), "inner")
    second = gather_rows(grid, gather_rows(grid, both[own:], "inner"), "y")
    return gather_rows(grid, jnp.concatenate([first, second], axis=0), "core")


def entering(grid, pair, rate, backward):
    states = pair.shape[0] - 1
    total, total_steps = pair[:states], pair[states:]
    ahead, ahead_steps = jnp.zeros_like(total), jnp.zeros_like(total_steps)
    bits = 1
    while bits < grid.total:
        got = grid.swap_bits(jnp.concatenate([total, total_steps], axis=0), bits)
        state, steps = got[:states], got[states:]
        later = ((grid.index // bits) % 2) == (0 if backward else 1)
        ahead = jnp.where(later, jnp.exp2(rate * ahead_steps) * state + ahead, ahead)
        ahead_steps = jnp.where(later, ahead_steps + steps, ahead_steps)
        early, late = jnp.where(later, state, total), jnp.where(later, total, state)
        total = jnp.exp2(rate * jnp.where(later, total_steps, steps)) * early + late
        total_steps = total_steps + steps
        bits *= 2
    return ahead


def pad_rows(block, rows):
    return jnp.pad(block, ((0, rows - block.shape[0]), (0, 0)))


def to_experts(grid, block, cap, tail):
    ny, width = grid.size["y"], 2 * cap
    slots = 2 * ny * cap
    held = [block[:width]]
    tails = [block[slots:]]
    for s in range(1, ny):
        part = block[s * width : (s + 1) * width]
        got = grid.swap(jnp.concatenate([part, block[slots:]], axis=0) if tail else part, "y", s)
        held.append(got[:width])
        tails.append(got[width:])
    mine = [h[:cap] for h in held]
    others = [h[cap:] for h in held]
    if tail:
        others.append(pad_rows(jnp.concatenate([t[2 * s + 1 : 2 * s + 2] for s, t in enumerate(tails)], axis=0), 8))
    got = grid.swap(jnp.concatenate(others, axis=0), "core", 1)
    out = mine + [got[: ny * cap]]
    if tail:
        ends = [t[2 * s : 2 * s + 1] for s, t in enumerate(tails)] + [got[ny * cap : ny * cap + ny]]
        out.append(pad_rows(jnp.concatenate(ends, axis=0), 8))
    return jnp.concatenate(out, axis=0)


def from_experts(grid, block, cap, tail):
    ny = grid.size["y"]
    half, slots = ny * cap, 2 * ny * cap
    send = block[half:slots]
    if tail:
        send = jnp.concatenate([send, pad_rows(block[slots + ny : slots + 2 * ny], 8)], axis=0)
    got = grid.swap(send, "core", 1)
    rows, ends = [], []
    for s in range(ny):
        pair = [block[s * cap : (s + 1) * cap], got[s * cap : (s + 1) * cap]]
        both = [block[slots + s : slots + s + 1], got[half + s : half + s + 1]] if tail else []
        if s:
            if tail:
                pair.append(pad_rows(jnp.concatenate(both, axis=0), 8))
            back = grid.swap(jnp.concatenate(pair, axis=0), "y", s)
            pair, both = [back[: 2 * cap]], [back[2 * cap : 2 * cap + 2]]
        rows += pair
        ends += both
    if tail:
        rows.append(pad_rows(jnp.concatenate(ends, axis=0), 8))
    return jnp.concatenate(rows, axis=0)


def split(value):
    high = value.astype(BF16)
    return high, (value - high.astype(F32)).astype(BF16)


def dot(left, right, dims):
    return lax.dot_general(left, right, (dims, ((), ())), preferred_element_type=F32)


def product(left, right, dims):
    return dot(left[0], right[0], dims) + (dot(left[0], right[1], dims) + dot(left[1], right[0], dims))


def pick(exact, value, dims):
    high, low = split(value)
    return dot(exact, high, dims) + dot(exact, low, dims)


def sigmoid(value):
    return 1.0 / (1.0 + jnp.exp(-value))


def softplus(value):
    small = jnp.exp(-jnp.abs(value))
    series = small * (1.0 - small * (0.5 - small * (1.0 / 3.0 - small * (0.25 - small * 0.2))))
    return jnp.maximum(value, 0.0) + jnp.where(small < 0.03, series, jnp.log(1.0 + small))


def iota(shape, dim):
    return lax.broadcasted_iota(jnp.int32, shape, dim)


def scale_of(value):
    return lax.rsqrt(jnp.mean(value * value, axis=1, keepdims=True) + EPS)


def over_lanes(ref, columns):
    rows = columns.shape[0]
    for t in range(columns.shape[1]):
        ref[t] = jnp.broadcast_to(columns[:, t : t + 1], (rows, 128))


def widen(value, width):
    return jnp.concatenate([value] * (width // 128), axis=1)


def call(kernel, outs, ins, grid=None, in_specs=None, out_specs=None, scratch=(), name=None):
    whole = pl.BlockSpec(memory_space=pltpu.VMEM)
    return pl.pallas_call(
        kernel,
        out_shape=outs,
        grid=grid or (),
        in_specs=in_specs or [whole] * len(ins),
        out_specs=out_specs or jax.tree.map(lambda _: whole, outs),
        scratch_shapes=scratch,
        name=name,
        compiler_params=pltpu.CompilerParams(vmem_limit_bytes=VMEM_BYTES),
    )(*ins)


def shape(*dims, dtype=F32):
    return jax.ShapeDtypeStruct(dims, dtype)


SMEM = pl.BlockSpec(memory_space=pltpu.SMEM)


def full(*dims):
    return pl.BlockSpec(dims, lambda c: (0,) * len(dims))


def route_kernel(experts, cap, me_ref, ids_ref, grad_ref, sent_ref, table_ref, rank_ref, load_ref):
    ids = ids_ref[...]
    tokens = ids.shape[0]
    chosen = (ids == iota((tokens, 128), 1)).astype(F32)
    before = (iota((tokens, tokens), 0) > iota((tokens, tokens), 1)).astype(BF16)
    rank = jnp.sum(dot(before, chosen.astype(BF16), NN) * chosen, axis=1, keepdims=True)
    kept = (rank < cap).astype(F32)
    place = jnp.where(rank < cap, ((ids ^ me_ref[0]) * cap).astype(F32) + rank, -1.0)
    row = jnp.broadcast_to(place, (tokens, tokens)).T
    slots = experts * cap
    table = (iota((slots, tokens), 0).astype(F32) == jnp.broadcast_to(row[0:1], (slots, tokens))).astype(F32)
    table = table.astype(BF16)
    table_ref[...] = table
    rank_ref[...] = rank
    sent_ref[...] = pick(table, grad_ref[...], NN)
    load_ref[...] = jnp.zeros_like(load_ref)
    load_ref[0:1, 0:128] = jnp.sum(chosen, axis=0, keepdims=True)
    load_ref[0:1, 128:256] = jnp.sum(chosen * (1.0 - kept), axis=0, keepdims=True)


def join_kernel(x_ref, halo_ref, gain_ref, weight_ref, joined_ref, high, low):
    @pl.when(pl.program_id(0) == 0)
    def _():
        x = jnp.concatenate([halo_ref[...], x_ref[...]], axis=0)
        high[...], low[...] = split(x * scale_of(x) * gain_ref[...])

    joined_ref[...] = product((high[...], low[...]), split(weight_ref[...]), NN)


def features_kernel(
    rank_n,
    states,
    inner_ref,
    since_ref,
    conv_w_ref,
    conv_b_ref,
    state_proj_ref,
    step_proj_ref,
    step_bias_ref,
    rate_ref,
    conv_ref,
    act_ref,
    pre_ref,
    steps_ref,
    masked_ref,
    drive_ref,
    proj_ref,
    pair_ref,
    in_lanes,
):
    tokens, width = act_ref.shape
    taps = conv_w_ref.shape[0]
    since = since_ref[...]
    conv = jnp.broadcast_to(conv_b_ref[...], (tokens, width))
    for k in range(taps):
        valid = (since >= taps - 1 - k).astype(F32)
        first = HALO - taps + 1 + k
        conv = conv + inner_ref[first : first + tokens, :] * valid * conv_w_ref[k : k + 1, :]
    act = conv * sigmoid(conv)
    conv_ref[...] = conv
    act_ref[...] = act
    proj = product(split(state_proj_ref[...]), split(act), NT)
    proj_ref[...] = proj
    pre = product(split(proj[:rank_n]), split(step_proj_ref[...]), TN) + step_bias_ref[...]
    pre_ref[...] = pre
    steps = softplus(pre)
    steps_ref[...] = steps
    masked = jnp.where(since == 0, RESET, steps)
    masked_ref[...] = masked
    drive_ref[...] = steps * act
    pair_ref[states : states + 1, :] = jnp.sum(masked, axis=0, keepdims=True)
    over_lanes(in_lanes, proj[rank_n : rank_n + states])
    chunk = 512
    for c in range(width // chunk):
        part = slice(c * chunk, (c + 1) * chunk)
        rate = rate_ref[:, part]

        def eight(group, state):
            for i in range(8):
                t = group * 8 + i
                decay = jnp.exp2(masked_ref[pl.ds(t, 1), part] * rate)
                state = decay * state + drive_ref[pl.ds(t, 1), part] * widen(in_lanes[t], chunk)
            return state

        pair_ref[0:states, part] = lax.fori_loop(0, tokens // 8, eight, jnp.zeros((states, chunk), F32))


def slot_tables(slots, cap, experts):
    slot = iota((slots, 8), 0)
    first = sum((slot >= cap * e).astype(jnp.int32) for e in range(1, experts))
    block = (first == iota((slots, 8), 1)).astype(F32)
    slot = iota((slots, 128), 0)
    first = sum(((slot >= cap * e).astype(jnp.int32) for e in range(1, experts)))
    within = (slot - first * cap == iota((slots, 128), 1)).astype(F32)
    return block, within


def scan_kernel(
    rank_n,
    states,
    experts,
    cap,
    me_ref,
    masked_ref,
    drive_ref,
    act_ref,
    gate_z_ref,
    start_ref,
    rate_ref,
    skip_ref,
    proj_ref,
    out_proj_ref,
    x_ref,
    gain_ref,
    router_ref,
    ids_ref,
    rank_ref,
    table_ref,
    scan_ref,
    history_ref,
    resid_ref,
    sent_ref,
    probs_ref,
    gate_ref,
    in_lanes,
    out_lanes,
    total,
):
    tokens, chunk = masked_ref.shape
    step = pl.program_id(0)

    @pl.when(step == 0)
    def _():
        over_lanes(in_lanes, proj_ref[rank_n : rank_n + states, :])
        over_lanes(out_lanes, proj_ref[rank_n + states : rank_n + 2 * states, :])
        total[...] = x_ref[...]

    rate = rate_ref[...]

    def eight(group, state):
        for i in range(8):
            t = group * 8 + i
            decay = jnp.exp2(masked_ref[pl.ds(t, 1), :] * rate)
            state = decay * state + drive_ref[pl.ds(t, 1), :] * widen(in_lanes[t], chunk)
            history_ref[t] = state
            scan_ref[pl.ds(t, 1), :] = jnp.sum(state * widen(out_lanes[t], chunk), axis=0, keepdims=True)
        return state

    lax.fori_loop(0, tokens // 8, eight, start_ref[...])
    gate_z = gate_z_ref[HALO:, :]
    mixed = (scan_ref[...] + skip_ref[...] * act_ref[...]) * (gate_z * sigmoid(gate_z))
    total[...] += product(split(mixed), split(out_proj_ref[...]), NN)

    @pl.when(step == pl.num_programs(0) - 1)
    def _():
        resid = total[...]
        resid_ref[...] = resid
        normed = resid * scale_of(resid) * gain_ref[...]
        logits = product(split(normed), split(router_ref[...]), NT)
        known = iota((tokens, 8), 1) < experts
        logits = jnp.where(known, logits, -1e30)
        raised = jnp.exp(logits - jnp.max(logits, axis=1, keepdims=True))
        raised = jnp.where(known, raised, 0.0)
        probs = raised / jnp.sum(raised, axis=1, keepdims=True)
        probs_ref[...] = probs
        ids = ids_ref[...]
        gate = jnp.sum(jnp.where(ids == iota((tokens, 8), 1), probs, 0.0), axis=1, keepdims=True)
        gate_ref[...] = gate
        slots = experts * cap
        sent_ref[0:slots, :] = pick(table_ref[...], normed, NN)
        sent_ref[slots:, :] = jnp.zeros((8, sent_ref.shape[1]), F32)
        rank = rank_ref[...].astype(jnp.int32)
        to_block = jnp.where(((ids ^ me_ref[0]) == iota((tokens, 8), 1)) & (rank < cap), gate, 0.0)
        at_rank = (rank == iota((tokens, 128), 1)).astype(BF16)
        high, low = split(to_block)
        rest = (to_block - high.astype(F32) - low.astype(F32)).astype(BF16)
        rows = dot(high, at_rank, TN) + (dot(low, at_rank, TN) + dot(rest, at_rank, TN))
        sent_ref[slots:, 0:128] = rows


def early_kernel(pieces, slices, *refs):
    grads, downs, out_ref = refs[:pieces], refs[pieces : pieces + slices], refs[-1]
    downs = [split(d[...]) for d in downs]
    for p in range(pieces):
        grad = split(grads[p][...])
        for i in range(slices):
            out_ref[p, i] = product(grad, downs[i], NT)


def gelu_parts(value):
    inner = 0.7978845608 * (value + 0.044715 * value * value * value)
    tanh = jnp.tanh(inner)
    slope = 0.5 * (1.0 + tanh) + 0.5 * value * (1.0 - tanh * tanh) * 0.7978845608 * (
        1.0 + 3.0 * 0.044715 * value * value
    )
    return 0.5 * value * (1.0 + tanh), slope


def expert_kernel(pieces, slices, experts, cap, *refs):
    tokens, ups, pulled = refs[:pieces], refs[pieces : pieces + slices], refs[pieces + slices]
    backs = refs[pieces + slices + 1 : 2 * pieces + slices + 1]
    hidden_ref, grad_ref = refs[-2:]
    slots = experts * cap
    ups = [split(u[...]) for u in ups]
    block, within = slot_tables(slots, cap, experts)
    within = within.astype(BF16)
    for p in range(pieces):
        rows = split(tokens[p][0:slots, :])
        back = jnp.zeros((slots, tokens[p].shape[1]), F32)
        to_gate = jnp.zeros((slots, 1), F32)
        for i in range(slices):
            hidden, slope = gelu_parts(product(rows, ups[i], NN))
            pull = pulled[p, i]
            grad = pull * slope
            hidden_ref[p, i] = hidden
            grad_ref[p, i] = grad
            to_gate += jnp.sum(hidden * pull, axis=1, keepdims=True)
            back += product(split(grad), ups[i], NT)
        backs[p][0:slots, :] = back
        backs[p][slots:, :] = jnp.zeros((8, tokens[p].shape[1]), F32)
        high, low = split(block * to_gate)
        rest = (block * to_gate - high.astype(F32) - low.astype(F32)).astype(BF16)
        backs[p][slots:, 0:128] = dot(high, within, TN) + (dot(low, within, TN) + dot(rest, within, TN))


def expert_grads_kernel(pieces, slices, experts, cap, *refs):
    tokens, grads = refs[:pieces], refs[pieces : 2 * pieces]
    downs = refs[2 * pieces : 2 * pieces + slices]
    hidden_ref, grad_ref = refs[2 * pieces + slices : 2 * pieces + slices + 2]
    outs = refs[2 * pieces + slices + 2 :]
    results, up_outs, down_outs = outs[:pieces], outs[pieces : pieces + slices], outs[pieces + slices :]
    slots = experts * cap
    downs = [split(d[...]) for d in downs]
    block, within = slot_tables(slots, cap, experts)
    within = within.astype(BF16)
    for p in range(pieces):
        ends = tokens[p][slots:, 0:128]
        high, low = split(ends)
        rest = (ends - high.astype(F32) - low.astype(F32)).astype(BF16)
        spread = dot(within, high, NT) + (dot(within, low, NT) + dot(within, rest, NT))
        gate = jnp.sum(spread * block, axis=1, keepdims=True)
        rows = split(tokens[p][0:slots, :] * gate)
        gated = split(grads[p][...] * gate)
        total = None
        for i in range(slices):
            hidden = split(hidden_ref[p, i])
            part = product(hidden, downs[i], NN)
            total = part if total is None else total + part
            up = product(rows, split(grad_ref[p, i]), TN)
            down = product(hidden, gated, TN)
            if p == 0:
                up_outs[i][...] = up
                down_outs[i][...] = down
            else:
                up_outs[i][...] += up
                down_outs[i][...] += down
        results[p][...] = total


def silu_parts(value):
    sig = sigmoid(value)
    return value * sig, sig * (1.0 + value * (1.0 - sig))


def mixer_back_kernel(
    rank_n,
    states,
    experts,
    cap,
    me_ref,
    back_ref,
    table_ref,
    gate_ref,
    probs_ref,
    ids_ref,
    rank_ref,
    resid_ref,
    grad_ref,
    gain_ref,
    router_ref,
    out_proj_ref,
    gate_z_ref,
    scan_ref,
    act_ref,
    skip_ref,
    masked_ref,
    rate_ref,
    proj_ref,
    steps_row_ref,
    grad_resid_ref,
    small_ref,
    grad_scan_ref,
    grad_gate_ref,
    grad_skip_ref,
    pair_ref,
    out_lanes,
    high,
    low,
):
    tokens, chunk = masked_ref.shape

    @pl.when(pl.program_id(0) == 0)
    def _():
        over_lanes(out_lanes, proj_ref[rank_n + states : rank_n + 2 * states, :])
        slots = experts * cap
        ids, rank = ids_ref[...], rank_ref[...].astype(jnp.int32)
        back = pick(table_ref[...], back_ref[0:slots, :], TN)
        at_rank = (rank == iota((tokens, 128), 1)).astype(BF16)
        ends = back_ref[slots:, 0:128]
        first, second = split(ends)
        third = (ends - first.astype(F32) - second.astype(F32)).astype(BF16)
        spread = dot(at_rank, first, NT) + (dot(at_rank, second, NT) + dot(at_rank, third, NT))
        mine = ((ids ^ me_ref[0]) == iota((tokens, 8), 1)) & (rank < cap)
        grad_gate = jnp.sum(jnp.where(mine, spread, 0.0), axis=1, keepdims=True)
        probs = probs_ref[...]
        grad_probs = jnp.where(ids == iota((tokens, 8), 1), grad_gate, 0.0)
        grad_logits = probs * (grad_probs - jnp.sum(probs * grad_probs, axis=1, keepdims=True))
        resid, gain = resid_ref[...], gain_ref[...]
        scale = scale_of(resid)
        normed = resid * scale * gain
        logits_two = split(grad_logits)
        grad_normed = gate_ref[...] * back + product(logits_two, split(router_ref[...]), NN)
        small_ref[...] = jnp.zeros_like(small_ref)
        small_ref[0:8, :] = product(logits_two, split(normed), TN)
        small_ref[8:9, :] = jnp.sum(grad_normed * resid * scale, axis=0, keepdims=True)
        pulled = gain * grad_normed
        grad_resid = (
            grad_ref[...]
            + scale * pulled
            - resid * (scale * scale * scale) * jnp.mean(pulled * resid, axis=1, keepdims=True)
        )
        grad_resid_ref[...] = grad_resid
        high[...], low[...] = split(grad_resid)

    grad_mixed = product((high[...], low[...]), split(out_proj_ref[...]), NT)
    silu, slope = silu_parts(gate_z_ref[HALO:, :])
    act = act_ref[...]
    grad_scan = grad_mixed * silu
    grad_scan_ref[...] = grad_scan
    grad_gate_ref[...] = grad_mixed * (scan_ref[...] + skip_ref[...] * act) * slope
    grad_skip_ref[...] = jnp.sum(grad_scan * act, axis=0, keepdims=True)
    rate = rate_ref[...]

    def eight(group, state):
        for i in range(8):
            t = tokens - 1 - (group * 8 + i)
            decay = jnp.exp2(masked_ref[pl.ds(t, 1), :] * rate)
            state = decay * (state + grad_scan_ref[pl.ds(t, 1), :] * widen(out_lanes[t], chunk))
        return state

    pair_ref[0:states, :] = lax.fori_loop(0, tokens // 8, eight, jnp.zeros((states, chunk), F32))
    pair_ref[states : states + 1, :] = steps_row_ref[...]


def out_grad_kernel(scan_ref, act_ref, skip_ref, gate_z_ref, grad_resid_ref, out_ref, high, low):
    @pl.when(pl.program_id(0) == 0)
    def _():
        high[...], low[...] = split(grad_resid_ref[...])

    gate_z = gate_z_ref[HALO:, :]
    mixed = (scan_ref[...] + skip_ref[...] * act_ref[...]) * (gate_z * sigmoid(gate_z))
    out_ref[...] = product(split(mixed), (high[...], low[...]), TN)


def gate_grad_kernel(x_ref, gain_ref, grad_gate_ref, weight_ref, out_ref, normed_ref, high, low):
    @pl.when(pl.program_id(0) == 0)
    def _():
        x = x_ref[...]
        high[...], low[...] = split(x * scale_of(x) * gain_ref[...])
        normed_ref[...] = jnp.zeros_like(normed_ref)

    grad = split(grad_gate_ref[...])
    out_ref[...] = product((high[...], low[...]), grad, TN)
    normed_ref[...] += product(grad, split(weight_ref[...]), NT)


def scan_back_kernel(
    rank_n,
    states,
    masked_ref,
    steps_ref,
    drive_ref,
    act_ref,
    pre_ref,
    grad_scan_ref,
    skip_ref,
    history_ref,
    start_ref,
    end_ref,
    rate_ref,
    proj_ref,
    step_proj_ref,
    grad_act_ref,
    grad_pre_ref,
    grad_decay_ref,
    grad_proj_ref,
    in_lanes,
    out_lanes,
    grad_drive,
    grad_steps,
):
    tokens, chunk = masked_ref.shape
    step = pl.program_id(0)

    @pl.when(step == 0)
    def _():
        over_lanes(in_lanes, proj_ref[rank_n : rank_n + states, :])
        over_lanes(out_lanes, proj_ref[rank_n + states : rank_n + 2 * states, :])
        grad_proj_ref[...] = jnp.zeros_like(grad_proj_ref)

    rate = rate_ref[...]
    lane = iota((states, tokens), 1)

    def one(t, before, carried):
        state, decays, grad_in, grad_out = carried
        masked = masked_ref[pl.ds(t, 1), :]
        grad = grad_scan_ref[pl.ds(t, 1), :]
        decay = jnp.exp2(masked * rate)
        state = state + grad * widen(out_lanes[t], chunk)
        at_out = jnp.sum(history_ref[t] * grad, axis=1, keepdims=True)
        at_in = jnp.sum(state * drive_ref[pl.ds(t, 1), :], axis=1, keepdims=True)
        grad_out = jnp.where(lane == t, at_out, grad_out)
        grad_in = jnp.where(lane == t, at_in, grad_in)
        grad_drive[pl.ds(t, 1), :] = jnp.sum(state * widen(in_lanes[t], chunk), axis=0, keepdims=True)
        state = decay * state
        pulled = state * before
        grad_steps[pl.ds(t, 1), :] = jnp.sum(pulled * rate, axis=0, keepdims=True)
        return state, decays + pulled * masked, grad_in, grad_out

    def four(group, carried):
        for i in range(4):
            t = tokens - 1 - (group * 4 + i)
            carried = one(t, history_ref[t - 1], carried)
        return carried

    nothing = jnp.zeros((states, tokens), F32)
    carried = lax.fori_loop(
        0, tokens // 4 - 1, four, (end_ref[...], jnp.zeros((states, chunk), F32), nothing, nothing)
    )
    for t in (3, 2, 1):
        carried = one(t, history_ref[t - 1], carried)
    _, decays, grad_in, grad_out = one(0, start_ref[...], carried)
    grad_decay_ref[...] = decays * (rate * (1.0 / LOG2E))
    steps, act = steps_ref[...], act_ref[...]
    grad_act_ref[...] = skip_ref[...] * grad_scan_ref[...] + grad_drive[...] * steps
    grad_pre = (grad_steps[...] * (1.0 / LOG2E) + grad_drive[...] * act) * sigmoid(pre_ref[...])
    grad_pre_ref[...] = grad_pre
    grad_proj_ref[0:rank_n, :] += product(split(step_proj_ref[...]), split(grad_pre), NT)
    grad_proj_ref[rank_n : rank_n + states, :] += grad_in
    grad_proj_ref[rank_n + states : rank_n + 2 * states, :] += grad_out


def input_back_kernel(
    rank_n,
    states,
    grad_proj_ref,
    proj_ref,
    state_proj_ref,
    act_ref,
    grad_act_ref,
    grad_pre_ref,
    conv_ref,
    inner_ref,
    conv_w_ref,
    since_ref,
    weight_ref,
    x_ref,
    halo_ref,
    gain_ref,
    grad_gate_normed_ref,
    grad_resid_ref,
    grad_decay_ref,
    grad_skip_ref,
    out_ref,
    input_ref,
    edge_ref,
    gain_row_ref,
    high,
    low,
    grad_inner,
    total,
):
    tokens, chunk = act_ref.shape
    depth = x_ref.shape[1]
    taps = conv_w_ref.shape[0]
    step = pl.program_id(0)

    @pl.when(step == 0)
    def _():
        x = jnp.concatenate([halo_ref[...], x_ref[...]], axis=0)
        high[...], low[...] = split(x * scale_of(x) * gain_ref[...])
        total[...] = jnp.zeros_like(total)

    act, grad_pre = split(act_ref[...]), grad_pre_ref[...]
    grad_pre_two = split(grad_pre)
    grad_proj = split(grad_proj_ref[...])
    grad_act = grad_act_ref[...] + product(grad_proj, split(state_proj_ref[...]), TN)
    _, slope = silu_parts(conv_ref[...])
    grad_conv = grad_act * slope
    since = since_ref[...]
    grad_inner[...] = jnp.zeros_like(grad_inner)
    base = depth
    out_ref[base : base + 2 * states + rank_n, :] = product(grad_proj, act, NN)
    base += 2 * states + rank_n
    out_ref[base : base + rank_n, :] = product(split(proj_ref[0:rank_n, :]), grad_pre_two, NN)
    base += rank_n
    out_ref[base : base + states, :] = grad_decay_ref[...]
    base += states
    rows = []
    for k in range(taps):
        valid = (since >= taps - 1 - k).astype(F32)
        first = HALO - taps + 1 + k
        held = grad_conv * valid
        rows.append(jnp.sum(held * inner_ref[first : first + tokens, :], axis=0, keepdims=True))
        grad_inner[first : first + tokens, :] += held * conv_w_ref[k : k + 1, :]
    rows.append(jnp.sum(grad_conv, axis=0, keepdims=True))
    rows.append(jnp.sum(grad_pre, axis=0, keepdims=True))
    rows.append(grad_skip_ref[...])
    out_ref[base:, :] = jnp.zeros((out_ref.shape[0] - base, chunk), F32)
    for i, row in enumerate(rows):
        out_ref[base + i : base + i + 1, :] = row
    grads = split(grad_inner[...])
    out_ref[0:depth, :] = product((high[...], low[...]), grads, TN)
    total[...] += product(grads, split(weight_ref[...]), NT)

    @pl.when(step == pl.num_programs(0) - 1)
    def _():
        gain = gain_ref[...]

        def rows_back(x, grad):
            scale = scale_of(x)
            pulled = gain * grad
            back = scale * pulled - x * (scale * scale * scale) * jnp.mean(pulled * x, axis=1, keepdims=True)
            return back, jnp.sum(grad * x * scale, axis=0, keepdims=True)

        edge, edge_gain = rows_back(halo_ref[...], total[0:HALO, :])
        own, own_gain = rows_back(x_ref[...], total[HALO:, :] + grad_gate_normed_ref[...])
        edge_ref[...] = edge
        input_ref[...] = grad_resid_ref[...] + own
        gain_row_ref[...] = edge_gain + own_gain


def per_device(
    block_input,
    seq_lengths,
    expert_ids,
    output_grad,
    mixer_gain,
    in_proj,
    conv_weight,
    conv_bias,
    state_proj,
    step_proj,
    step_bias,
    decay_log,
    skip_gain,
    out_proj,
    router_gain,
    router,
    expert_up,
    expert_down,
):
    grid = Grid()
    tokens, depth = block_input.shape
    taps, width = conv_weight.shape
    rank_n, states, experts = step_proj.shape[0], decay_log.shape[1], router.shape[1]
    cap = (5 * tokens + 4 * experts - 1) // (4 * experts)
    slots, hidden = experts * cap, expert_up.shape[2]
    chunk = 512
    chunks = width // chunk
    pieces, slices = grid.size["outer"], grid.size["inner"]
    me = lax.axis_index("exp").astype(jnp.int32).reshape(1)
    ext = HALO + tokens

    halo = grid.along(block_input[tokens - HALO :], 1)

    count = seq_lengths.shape[0]
    earlier = jnp.arange(count)[:, None] > jnp.arange(count)[None, :]
    starts = jnp.sum(jnp.where(earlier, seq_lengths[None, :], 0), axis=1)
    position = grid.index * tokens + jnp.arange(tokens, dtype=jnp.int32)
    own_start = jnp.max(jnp.where(starts[None, :] <= position[:, None], starts[None, :], 0), axis=1)
    since = (position - own_start)[:, None]
    rate = -jnp.exp(decay_log.T) * LOG2E
    state_proj_t = state_proj.T
    router_t = pad_rows(router.T, 8)
    row = lambda vector: vector.reshape(1, -1)

    sent_grads, table, rank, loads = call(
        functools.partial(route_kernel, experts, cap),
        [shape(slots, depth), shape(slots, tokens, dtype=BF16), shape(tokens, 1), shape(8, depth)],
        (me, expert_ids, output_grad),
        in_specs=[SMEM] + [pl.BlockSpec(memory_space=pltpu.VMEM)] * 2,
        name="route",
    )
    own_grads = to_experts(grid, sent_grads, cap, False)
    grad_pieces = [own_grads] + [grid.swap(own_grads, "outer", s) for s in range(1, pieces)]
    up, down = expert_up[0], expert_down[0]
    ups = [up] + [grid.swap(up, "inner", s) for s in range(1, slices)]
    downs = [down] + [grid.swap(down, "inner", s) for s in range(1, slices)]

    block = lambda c: (0, c)
    joined = call(
        join_kernel,
        shape(ext, 2 * width),
        (block_input, halo, row(mixer_gain), in_proj),
        grid=(2 * chunks,),
        in_specs=[full(tokens, depth), full(HALO, depth), full(1, depth), pl.BlockSpec((depth, chunk), block)],
        out_specs=pl.BlockSpec((ext, chunk), block),
        scratch=[pltpu.VMEM((ext, depth), BF16)] * 2,
        name="join",
    )
    conv, act, pre, steps, masked, drive, proj, pair = call(
        functools.partial(features_kernel, rank_n, states),
        [shape(tokens, width)] * 6 + [shape(rank_n + 2 * states, tokens), shape(states + 1, width)],
        (joined, since, conv_weight, row(conv_bias), state_proj_t, step_proj, row(step_bias), rate),
        grid=(1,),
        in_specs=[
            full(ext, width),
            full(tokens, 1),
            full(taps, width),
            full(1, width),
            full(rank_n + 2 * states, width),
            full(rank_n, width),
            full(1, width),
            full(states, width),
        ],
        out_specs=[full(tokens, width)] * 6 + [full(rank_n + 2 * states, tokens), full(states + 1, width)],
        scratch=[pltpu.VMEM((tokens, states, 128), F32)],
        name="features",
    )
    start = entering(grid, pair, rate, False)
    tok = pl.BlockSpec((tokens, chunk), block)
    gate_half = pl.BlockSpec((ext, chunk), lambda c: (0, chunks + c))
    one_row = pl.BlockSpec((1, chunk), block)
    state_rows = pl.BlockSpec((states, chunk), block)
    history_block = pl.BlockSpec((tokens, states, chunk), lambda c: (0, 0, c))
    out_rows = pl.BlockSpec((chunk, depth), lambda c: (c, 0))
    proj_full = full(rank_n + 2 * states, tokens)
    lanes = pltpu.VMEM((tokens, states, 128), F32)
    scan, history, resid, sent, probs, gate = call(
        functools.partial(scan_kernel, rank_n, states, experts, cap),
        [
            shape(tokens, width),
            shape(tokens, states, width),
            shape(tokens, depth),
            shape(slots + 8, depth),
            shape(tokens, 8),
            shape(tokens, 1),
        ],
        (
            me, masked, drive, act, joined, start, rate, row(skip_gain), proj, out_proj, block_input,
            row(router_gain), router_t, expert_ids, rank, table,
        ),
        grid=(chunks,),
        in_specs=[
            SMEM, tok, tok, tok, gate_half, state_rows, state_rows, one_row, proj_full, out_rows,
            full(tokens, depth), full(1, depth), full(8, depth), full(tokens, 1), full(tokens, 1),
            full(slots, tokens),
        ],
        out_specs=[
            tok, history_block, full(tokens, depth), full(slots + 8, depth), full(tokens, 8), full(tokens, 1),
        ],
        scratch=[lanes, lanes, pltpu.VMEM((tokens, depth), F32)],
        name="scan",
    )

    pulled = call(
        functools.partial(early_kernel, pieces, slices),
        shape(pieces, slices, slots, hidden),
        (*grad_pieces, *downs),
        name="early",
    )
    own_tokens = to_experts(grid, sent, cap, True)
    token_pieces = [own_tokens] + [grid.swap(own_tokens, "outer", s) for s in range(1, pieces)]
    *backs, hiddens, hidden_grads = call(
        functools.partial(expert_kernel, pieces, slices, experts, cap),
        [shape(slots + 8, depth)] * pieces + [shape(pieces, slices, slots, hidden)] * 2,
        (*token_pieces, *ups, pulled),
        name="expert",
    )
    back = backs[0]
    for s in range(1, pieces):
        back = back + grid.swap(backs[s], "outer", s)
    back = from_experts(grid, back, cap, True)
    outs = call(
        functools.partial(expert_grads_kernel, pieces, slices, experts, cap),
        [shape(slots, depth)] * pieces + [shape(depth, hidden)] * slices + [shape(hidden, depth)] * slices,
        (*token_pieces, *grad_pieces, *downs, hiddens, hidden_grads),
        name="expert_grads",
    )
    results, up_grads, down_grads = outs[:pieces], outs[pieces : pieces + slices], outs[pieces + slices :]
    grad_up, grad_down, result = up_grads[0], down_grads[0], results[0]
    for s in range(1, slices):
        grad_up = grad_up + grid.swap(up_grads[s], "inner", s)
        grad_down = grad_down + grid.swap(down_grads[s], "inner", s)
    for s in range(1, pieces):
        result = result + grid.swap(results[s], "outer", s)
    result = from_experts(grid, result, cap, False)

    grad_resid, small, grad_scan, grad_gate, grad_skip, back_pair = call(
        functools.partial(mixer_back_kernel, rank_n, states, experts, cap),
        [
            shape(tokens, depth),
            shape(16, depth),
            shape(tokens, width),
            shape(tokens, width),
            shape(1, width),
            shape(states + 1, width),
        ],
        (
            me, back, table, gate, probs, expert_ids, rank, resid, output_grad, row(router_gain), router_t,
            out_proj, joined, scan, act, row(skip_gain), masked, rate, proj, pair[states:],
        ),
        grid=(chunks,),
        in_specs=[
            SMEM, full(slots + 8, depth), full(slots, tokens), full(tokens, 1), full(tokens, 8),
            full(tokens, 1), full(tokens, 1), full(tokens, depth), full(tokens, depth), full(1, depth),
            full(8, depth), out_rows, gate_half, tok, tok, one_row, tok, state_rows, proj_full, one_row,
        ],
        out_specs=[
            full(tokens, depth), full(16, depth), tok, tok, one_row,
            pl.BlockSpec((states + 1, chunk), block),
        ],
        scratch=[lanes] + [pltpu.VMEM((tokens, depth), BF16)] * 2,
        name="mixer_back",
    )
    end = entering(grid, back_pair, rate, True)
    grad_out_proj = call(
        out_grad_kernel,
        shape(width, depth),
        (scan, act, row(skip_gain), joined, grad_resid),
        grid=(chunks,),
        in_specs=[tok, tok, one_row, gate_half, full(tokens, depth)],
        out_specs=out_rows,
        scratch=[pltpu.VMEM((tokens, depth), BF16)] * 2,
        name="out_grad",
    )
    grad_in_gate, grad_gate_normed = call(
        gate_grad_kernel,
        [shape(depth, width), shape(tokens, depth)],
        (block_input, row(mixer_gain), grad_gate, in_proj),
        grid=(chunks,),
        in_specs=[
            full(tokens, depth), full(1, depth), tok,
            pl.BlockSpec((depth, chunk), lambda c: (0, chunks + c)),
        ],
        out_specs=[pl.BlockSpec((depth, chunk), block), full(tokens, depth)],
        scratch=[pltpu.VMEM((tokens, depth), BF16)] * 2,
        name="gate_grad",
    )
    grad_out_proj = sum_everywhere(grid, grad_out_proj)
    grad_in_gate = sum_everywhere(grid, grad_in_gate)
    grad_act, grad_pre, grad_decay, grad_proj = call(
        functools.partial(scan_back_kernel, rank_n, states),
        [
            shape(tokens, width), shape(tokens, width), shape(states, width), shape(rank_n + 2 * states, tokens),
        ],
        (
            masked, steps, drive, act, pre, grad_scan, row(skip_gain), history, start, end, rate, proj, step_proj,
        ),
        grid=(chunks,),
        in_specs=[
            tok, tok, tok, tok, tok, tok, one_row, history_block, state_rows, state_rows, state_rows, proj_full,
            pl.BlockSpec((rank_n, chunk), block),
        ],
        out_specs=[tok, tok, state_rows, proj_full],
        scratch=[lanes, lanes] + [pltpu.VMEM((tokens, chunk), F32)] * 2,
        name="scan_back",
    )
    used = depth + 2 * states + 2 * rank_n + states + taps + 4
    unit = 16 * grid.size["inner"] * grid.size["y"]
    packed = -(-(used + 8) // unit) * unit
    grads, input_grad, edge, gain_row = call(
        functools.partial(input_back_kernel, rank_n, states),
        [shape(packed, width), shape(tokens, depth), shape(HALO, depth), shape(1, depth)],
        (
            grad_proj, proj, state_proj_t, act, grad_act, grad_pre, conv, joined, conv_weight, since, in_proj,
            block_input, halo, row(mixer_gain), grad_gate_normed, grad_resid, grad_decay, grad_skip,
        ),
        grid=(chunks,),
        in_specs=[
            proj_full, proj_full, pl.BlockSpec((rank_n + 2 * states, chunk), block), tok, tok, tok, tok,
            pl.BlockSpec((ext, chunk), block), pl.BlockSpec((taps, chunk), block), full(tokens, 1),
            pl.BlockSpec((depth, chunk), block), full(tokens, depth), full(HALO, depth), full(1, depth),
            full(tokens, depth), full(tokens, depth), state_rows, one_row,
        ],
        out_specs=[
            pl.BlockSpec((packed, chunk), block), full(tokens, depth), full(HALO, depth), full(1, depth),
        ],
        scratch=[pltpu.VMEM((ext, depth), BF16)] * 2
        + [pltpu.VMEM((ext, chunk), F32), pltpu.VMEM((ext, depth), F32)],
        name="input_back",
    )
    from_next = grid.along(edge, -1)
    input_grad = jnp.concatenate([input_grad[: tokens - HALO], input_grad[tokens - HALO :] + from_next], axis=0)
    small = jnp.concatenate([small[:9], gain_row, loads[0:1], small[11:]], axis=0).reshape(8, width)
    grads = lax.dynamic_update_slice(grads, small, (used, 0))
    grads = sum_everywhere(grid, grads)

    combined = jnp.dot(table.T, result.astype(F32), precision=lax.Precision.HIGHEST, preferred_element_type=F32)
    block_output = resid + gate * combined

    at = depth
    grad_state_proj = grads[at : at + 2 * states + rank_n].T
    at += 2 * states + rank_n
    grad_step_proj = grads[at : at + rank_n]
    at += rank_n
    grad_decay_log = grads[at : at + states].T
    at += states
    grad_conv_weight = grads[at : at + taps]
    at += taps
    grad_conv_bias, grad_step_bias, grad_skip_gain = grads[at], grads[at + 1], grads[at + 2]
    small = grads[used : used + 8].reshape(16, depth)
    return (
        block_output,
        input_grad,
        small[9],
        jnp.concatenate([grads[:depth], grad_in_gate], axis=1),
        grad_conv_weight,
        grad_conv_bias,
        grad_state_proj,
        grad_step_proj,
        grad_step_bias,
        grad_decay_log,
        grad_skip_gain,
        grad_out_proj,
        small[8],
        small[:experts].T,
        grad_up[None],
        grad_down[None],
        small[10, :experts].astype(jnp.int32),
        small[10, 128 : 128 + experts].astype(jnp.int32),
    )


def solution(mesh):
    rows, copied = P(("seq", "exp"), None), P()
    up, down = P("exp", None, "seq"), P("exp", "seq", None)
    in_specs = (rows, copied, rows, rows) + (copied,) * 12 + (up, down)
    out_specs = (rows, rows) + (copied,) * 12 + (up, down, copied, copied)
    return jax.shard_map(per_device, mesh=mesh, in_specs=in_specs, out_specs=out_specs, check_vma=False)
```

time: 3120 us -> 643 us (0.21); the launches traced: 3070 us -> 636 us
  local copies, waits for them, and re-layouts: 1110 us -> 29 us
  waiting for transfers between devices: 1100 us -> 294 us
  other arithmetic: 544 us -> 49.3 us
  matrix products: 135 us -> 2.15 us
  Pallas kernels: 0 us -> 125 us
  starting transfers between devices: 16.3 us -> 134 us
  loops' own time: 92 us -> 0 us
  blocking collectives: 55.7 us -> 0 us
    psum x1 -> x0, waiting for transfers between devices: 460 us -> none  [per_device(): lax.psum((grad_mixer_gain, grad_in_proj, grad_conv_weight, grad_conv_bias...]
    dynamic_update_slice x398 -> x1, local copies, waits for them, and re-layouts: 458 us -> 0.63 us  [per_device(): grads = lax.dynamic_update_slice(grads, small, (used, 0))]
    dynamic_slice x390 -> x15, local copies, waits for them, and re-layouts: 363 us -> 9.13 us  [scatter_rows(): lax.dynamic_slice_in_dim(block, (place ^ s) * rows, rows, 0)]
    reduce_scatter x2 -> x0, waiting for transfers between devices: 337 us -> none  [the longest x1 171 us: per_device(): lax.psum_scatter(grad_down_full, 'seq', scatter_dimension=1, tiled=True)]
    ppermute x2 -> x84, waiting for transfers between devices: 0.53 us -> 294 us  [the longest x82 294 us: swap_bits(): return lax.ppermute(block, AXES, [(i, i ^ bits) for i in range(self.total)])]
    all_gather x5 -> x0, waiting for transfers between devices: 283 us -> none  [the longest x3 137 us: entering(): pieces = jax.tree.map(lambda part: lax.all_gather(part, axis), value)]
    reduce_sum x241 -> x1, other arithmetic: 202 us -> 0.77 us  [per_device(): starts = jnp.sum(jnp.where(earlier, seq_lengths[None, :], 0), axis=1)]
    mul x269 -> x0, local copies, waits for them, and re-layouts: 167 us -> none  [the longest x128 81.3 us: advance(): (step_b[index] * act_b[index])[:, None] * in_b[index][None, :]]
  transfers between devices with their start and end apart: 13 -> 84, of which waited for: 12 -> 40; matrix products, arithmetic and copies ran while one was open for 6% -> 8% of each run, Pallas kernels for 0% -> 15%
where the time goes in v1:
time: 643 us; the launch traced here: 636 us
  waiting for transfers between devices  294 us (46%)
  starting transfers between devices  134 us (21%)
  Pallas kernels  125 us (19%)
  other arithmetic  49.3 us (8%)
  local copies, waits for them, and re-layouts  29 us (5%)
    ppermute x82, waiting for transfers between devices, swap_bits(): return lax.ppermute(block, AXES, [(i, i ^ bits) for i in range(self.total)])  294 us
    ppermute x82, starting transfers between devices, swap_bits(): return lax.ppermute(block, AXES, [(i, i ^ bits) for i in range(self.total)])  131 us
    pallas_call x12, Pallas kernels, call(): pl.pallas_call(kernel, out_shape=outs, grid=grid or (), in_specs=in_specs...  125 us
  transfers between devices with their start and end apart: 84, of which 40 were waited for; matrix products, arithmetic and copies ran while one was open for 8% of the time, Pallas kernels for 15%

profile of v1, /device:TPU:0, one launch (start us, length us, event | category | flops | bytes accessed | tf_op | source)
XLA Modules:
  0.0 636.4 jit_solution(10654123277299570843)
XLA Ops:
  8.9 7.9 %join.1.inner_ref.gate_z_ref = f32[144,3072]{1,0:T(8,128)} custom-call(f32[128,768]{1,0:T(8,128)S(1)} %copy-done.1, f32[16,768]{1,0:T(8,128)S(1)} %collective-permute-done.halo_ref, f32[1,768]{1,0:T(1,128)S(1)} %reshape.120.gain_ref, f32[768,3072]{1,0:T(8,128)} %weight_ref.5), custom_call_target="tpu_custom_call" | custom-call | tf_op jit(solution)/shard_map/join/pallas_call | solution.py:216
  16.9 8.3 %features.1 = (f32[128,1536]{1,0:T(8,128)S(1)}, f32[128,1536]{1,0:T(8,128)}, f32[128,1536]{1,0:T(8,128)}, f32[128,1536]{1,0:T(8,128)}, f32[128,1536]{1,0:T(8,128...) custom-call(f32[144,3072]{1,0:T(8,128)} %join.1.inner_ref.gate_z_ref, ...), custom_call_target="tpu_custom_call" | custom-call | tf_op jit(solution)/shard_map/features/pallas_call | solution.py:216
  33.5 3.7 collective-permute-done.2
  39.6 3.7 collective-permute-done.3
  51.8 4.6 collective-permute-done.5
  56.7 14.7 %scan.1 = (f32[128,1536]{1,0:T(8,128)}, f32[128,16,1536]{2,1,0:T(8,128)}, f32[128,768]{1,0:T(8,128)S(1)}, f32[168,768]{1,0:T(8,128)S(1)}, f32[128,8]{1,0:T(8,128)S(1)}, /*index=5*/f32[128,1]{1,0:T(8,128)S(1)}) custom-call(s32[1]{0:T(128)} %bitcast.me_ref, f32[128,1536]{1,0:T(8,128)} %get-tuple-element.66.masked_ref, ...), custom_call_target="tpu_custom_call" | custom-call | tf_op jit(solution)/shard_map/scan/pallas_call | solution.py:216
  73.0 5.0 collective-permute-done.6
  80.3 3.7 collective-permute-start.15
  84.9 11.5 %collective-permute-done.15.refs_3_.refs_7_ = f32[160,768]{1,0:T(8,128)S(1)} collective-permute-done((f32[160,768]{1,0:T(8,128)S(1)}, f32[160,768]{1,0:T(8,128)S(1)}, u32[]{:S(2)}, u32[]{:S(2)}) %collective-permute-start.15) | collective-permute-done | bytes 491552 | tf_op jit(solution)/shard_map/ppermute | solution.py:43
  96.4 3.6 collective-permute-start.10
  100.0 37.4 %collective-permute-done.14.refs_2_.refs_6_ = f32[160,768]{1,0:T(8,128)S(1)} collective-permute-done((f32[160,768]{1,0:T(8,128)S(1)}, f32[160,768]{1,0:T(8,128)S(1)}, u32[]{:S(2)}, u32[]{:S(2)}) %collective-permute-start.14) | collective-permute-done | bytes 491552 | tf_op jit(solution)/shard_map/ppermute | solution.py:43
  141.0 7.4 %early.1.refs_6_ = f32[4,2,160,384]{3,2,1,0:T(8,128)} custom-call(f32[160,768]{1,0:T(8,128)S(1)} %pad_maximum_fusion.16.refs_0_.refs_4_, f32[160,768]{1,0:T(8,128)S(1)} %collective-permute-done.13.refs_1_.refs_5_, f32[160,768]{1,0:T(8,128)S(1)} %collective-permute-done.14.refs_2_.refs_6_, f32[160,768]{1,0:T(8,128)S(1)} %collective-permute-done.15.refs_3_.refs_7_, ...), custom_call_target="tpu_custom_call" | custom-call | tf_op jit(solution)/shard_map/early/pallas_call | solution.py:216
  148.5 20.9 %collective-permute-done.9.refs_2_ = f32[168,768]{1,0:T(8,128)S(1)} collective-permute-done((f32[168,768]{1,0:T(8,128)S(1)}, f32[168,768]{1,0:T(8,128)S(1)}, u32[]{:S(2)}, u32[]{:S(2)}) %collective-permute-start.9) | collective-permute-done | bytes 516128 | tf_op jit(solution)/shard_map/ppermute | solution.py:43
  171.0 14.0 %expert.1 = (f32[168,768]{1,0:T(8,128)S(1)}, f32[168,768]{1,0:T(8,128)}, f32[168,768]{1,0:T(8,128)}, f32[168,768]{1,0:T(8,128)}, f32[4,2,160,384]{3,2,1,0:T(8,128)}, /*index=5*/f32[4,2,160,384]{3,2,1,0:T(8,128)}) custom-call(f32[168,768]{1,0:T(8,128)} %copy-done.60, f32[168,768]{1,0:T(8,128)} %copy-done.63, f32[168,768]{1,0:T(8,128)} %copy-done.62, ...), custom_call_target="tpu_custom_call" | custom-call | tf_op jit(solution)/shard_map/expert/pallas_call | solution.py:216
  190.3 17.6 %expert_grads.1 = (f32[160,768]{1,0:T(8,128)S(1)}, f32[160,768]{1,0:T(8,128)S(1)}, f32[160,768]{1,0:T(8,128)S(1)}, f32[160,768]{1,0:T(8,128)S(1)}, f32[768,384]{...) custom-call(f32[168,768]{1,0:T(8,128)} %copy-done.60, f32[168,768]{1,0:T(8,128)} %copy-done.63, ...), custom_call_target="tpu_custom_call" | custom-call | tf_op jit(solution)/shard_map/expert_grads/pallas_call | solution.py:216
  212.3 10.9 %collective-permute-done.24 = f32[168,768]{1,0:T(8,128)S(1)} collective-permute-done((f32[168,768]{1,0:T(8,128)}, f32[168,768]{1,0:T(8,128)S(1)}, u32[]{:S(2)}, u32[]{:S(2)}) %collective-permute-start.24) | collective-permute-done | bytes 516128 | tf_op jit(solution)/shard_map/ppermute | solution.py:43
  231.2 34.7 %collective-permute-done.19 = f32[160,768]{1,0:T(8,128)S(1)} collective-permute-done((f32[160,768]{1,0:T(8,128)S(1)}, f32[160,768]{1,0:T(8,128)S(1)}, u32[]{:S(2)}, u32[]{:S(2)}) %collective-permute-start.19) | collective-permute-done | bytes 491552 | tf_op jit(solution)/shard_map/ppermute | solution.py:43
  267.2 9.5 %mixer_back.1 = (f32[128,768]{1,0:T(8,128)S(1)}, f32[16,768]{1,0:T(8,128)S(1)}, f32[128,1536]{1,0:T(8,128)}, f32[128,1536]{1,0:T(8,128)}, f32[1,1536]{1,0:T(1,128)S(1)}, /*index=5*/f32[17,1536]{1,0:T(8,128)S(1)}) custom-call(s32[1]{0:T(128)} %bitcast.me_ref, f32[168,768]{1,0:T(8,128)} %pad_maximum_fusion.15.back_ref, bf16[160,128]{1,0:T(8,128)(2,1)S(1)} %copy-done.23, ...), custom_call_target="tpu_custom_call" | custom-call | tf_op jit(solution)/shard_map/mixer_back/pallas_call | solution.py:216
  279.8 5.2 out_grad.1
  289.5 6.8 %gate_grad.1 = (f32[768,1536]{1,0:T(8,128)}, f32[128,768]{1,0:T(8,128)S(1)}) custom-call(f32[128,768]{1,0:T(8,128)S(1)} %copy-done.2, f32[1,768]{1,0:T(1,128)S(1)} %reshape.120.gain_ref, f32[128,1536]{1,0:T(8,128)S(1)} %copy-done.17, f32[768,3072]{1,0:T(8,128)} %weight_ref.5), custom_call_target="tpu_custom_call" | custom-call | tf_op jit(solution)/shard_map/gate_grad/pallas_call | solution.py:216
  296.5 9.2 %collective-permute-start.31 = (f32[17,1536]{1,0:T(8,128)S(1)}, f32[17,1536]{1,0:T(8,128)S(1)}, u32[]{:S(2)}, u32[]{:S(2)}) collective-permute-start(f32[17,1536]{1,0:T(8,128)S(1)} %pad_maximum_fusion.28), channel_id=1, source_target_pairs={{0,8},{1,9},{2,10},{3,11},{4,12},{5,13},{6,14},{7,15},{8,0},{9,1},... | collective-permute-start | bytes 313352 | tf_op jit(solution)/shard_map/ppermute | solution.py:43
  313.8 6.3 collective-permute-done.32
  320.3 21.8 %scan_back.1 = (f32[128,1536]{1,0:T(8,128)S(1)}, f32[128,1536]{1,0:T(8,128)}, f32[16,1536]{1,0:T(8,128)S(1)}, f32[80,128]{1,0:T(8,128)S(1)}) custom-call(f32[128,1536]{1,0:T(8,128)} %get-tuple-element.66.masked_ref, f32[128,1536]{1,0:T(8,128)} %get-tuple-element.83.steps_ref, f32[128,1536]{1,0:T(8,128)} %get-tuple-element.67.drive_ref, ...), custom_call_target="tpu_custom_call" | custom-call | tf_op jit(solution)/shard_map/scan_back/pallas_call | solution.py:216
  342.9 10.9 %input_back.1 = (f32[960,1536]{1,0:T(8,128)}, f32[128,768]{1,0:T(8,128)S(1)}, f32[16,768]{1,0:T(8,128)S(1)}, f32[1,768]{1,0:T(1,128)S(1)}) custom-call(f32[80,128]{1,0:T(8,128)S(1)} %get-tuple-element.94.grad_proj_ref, f32[80,128]{1,0:T(8,128)S(1)} %copy-done.19, f32[80,1536]{1,0:T(8,128)} %bitcast.94, f32[128,1536]{1,0:T(8,128)} %get-tuple-element.68.act_ref, ...), custom_call_target="tpu_custom_call" | custom-call | tf_op jit(solution)/shard_map/input_back/pallas_call | solution.py:216
  365.3 10.7 %collective-permute-done.67 = f32[192,768]{1,0:T(8,128)S(1)} collective-permute-done((f32[192,768]{1,0:T(8,128)S(1)}, f32[192,768]{1,0:T(8,128)S(1)}, u32[]{:S(2)}, u32[]{:S(2)}) %collective-permute-start.67) | collective-permute-done | bytes 589856 | tf_op jit(solution)/shard_map/ppermute | solution.py:43
  378.3 9.9 %collective-permute-done.51 = f32[96,1536]{1,0:T(8,128)S(1)} collective-permute-done((f32[96,1536]{1,0:T(8,128)S(1)}, f32[96,1536]{1,0:T(8,128)S(1)}, u32[]{:S(2)}, u32[]{:S(2)}) %collective-permute-start.51) | collective-permute-done | bytes 589856 | tf_op jit(solution)/shard_map/ppermute | solution.py:43
  393.3 9.8 %collective-permute-done.52 = f32[48,1536]{1,0:T(8,128)S(1)} collective-permute-done((f32[48,1536]{1,0:T(8,128)S(1)}, f32[48,1536]{1,0:T(8,128)S(1)}, u32[]{:S(2)}, u32[]{:S(2)}) %collective-permute-start.52) | collective-permute-done | bytes 294944 | tf_op jit(solution)/shard_map/ppermute | solution.py:43
  403.9 6.3 collective-permute-done.54
  426.0 9.6 %collective-permute-start.60 = (f32[96,384]{1,0:T(8,128)S(1)}, f32[96,384]{1,0:T(8,128)S(1)}, u32[]{:S(2)}, u32[]{:S(2)}) collective-permute-start(f32[96,384]{1,0:T(8,128)S(1)} %fusion.25), channel_id=1, source_target_pairs={{0,8},{1,9},{2,10},{3,11},{4,12},{5,13},{6,14},{7,15},{8,0},{9,1},... | collective-permute-start | bytes 442376 | tf_op jit(solution)/shard_map/ppermute | solution.py:43
  439.1 5.2 collective-permute-start.58
  444.4 6.6 %collective-permute-start.76 = (f32[192,192]{1,0:T(8,128)S(1)}, f32[192,192]{1,0:T(8,128)S(1)}, u32[]{:S(2)}, u32[]{:S(2)}) collective-permute-start(f32[192,192]{1,0:T(8,128)S(1)} %fusion.11), channel_id=1, source_target_pairs={{0,8},{1,9},{2,10},{3,11},{4,12},{5,13},{6,14},{7,15},{8,0},{9,1},... | collective-permute-start | bytes 442376 | tf_op jit(solution)/shard_map/ppermute | solution.py:43
  454.6 4.4 collective-permute-start.74
  459.9 7.6 %collective-permute-done.75 = f32[192,192]{1,0:T(8,128)S(1)} collective-permute-done((f32[192,192]{1,0:T(8,128)S(1)}, f32[192,192]{1,0:T(8,128)S(1)}, u32[]{:S(2)}, u32[]{:S(2)}) %collective-permute-start.75) | collective-permute-done | bytes 147488 | tf_op jit(solution)/shard_map/ppermute | solution.py:43
  470.2 8.8 %collective-permute-done.61 = f32[48,1536]{1,0:T(8,128)S(1)} collective-permute-done((f32[48,1536]{1,0:T(8,128)S(1)}, f32[48,1536]{1,0:T(8,128)S(1)}, u32[]{:S(2)}, u32[]{:S(2)}) %collective-permute-start.61) | collective-permute-done | bytes 294944 | tf_op jit(solution)/shard_map/ppermute | solution.py:43
  482.5 5.5 collective-permute-done.77
  494.1 12.7 %collective-permute-done.36 = f32[60,1536]{1,0:T(8,128)S(1)} collective-permute-done((f32[60,1536]{1,0:T(8,128)S(1)}, f32[60,1536]{1,0:T(8,128)S(1)}, u32[]{:S(2)}, u32[]{:S(2)}) %collective-permute-start.36) | collective-permute-done | bytes 368672 | tf_op jit(solution)/shard_map/ppermute | solution.py:43
  514.7 3.7 collective-permute-done.40
  518.4 5.9 collective-permute-done.41
  524.4 5.6 collective-permute-start.44
  534.2 6.2 collective-permute-done.43
  543.3 10.9 %collective-permute-done.62 = f32[96,1536]{1,0:T(8,128)S(1)} collective-permute-done((f32[96,1536]{1,0:T(8,128)S(1)}, f32[96,1536]{1,0:T(8,128)S(1)}, u32[]{:S(2)}, u32[]{:S(2)}) %collective-permute-start.62) | collective-permute-done | bytes 589856 | tf_op jit(solution)/shard_map/ppermute | solution.py:43
  558.5 6.7 %collective-permute-done.47 = f32[60,1536]{1,0:T(8,128)S(1)} collective-permute-done((f32[60,1536]{1,0:T(8,128)S(1)}, f32[60,1536]{1,0:T(8,128)S(1)}, u32[]{:S(2)}, u32[]{:S(2)}) %collective-permute-start.47) | collective-permute-done | bytes 368672 | tf_op jit(solution)/shard_map/ppermute | solution.py:43
  566.7 5.7 collective-permute-done.80
  574.2 7.0 %collective-permute-done.78 = f32[192,768]{1,0:T(8,128)S(1)} collective-permute-done((f32[192,768]{1,0:T(8,128)S(1)}, f32[192,768]{1,0:T(8,128)S(1)}, u32[]{:S(2)}, u32[]{:S(2)}) %collective-permute-start.78) | collective-permute-done | bytes 589856 | tf_op jit(solution)/shard_map/ppermute | solution.py:43
  584.7 8.0 %collective-permute-done.46 = f32[120,1536]{1,0:T(8,128)S(1)} collective-permute-done((f32[120,1536]{1,0:T(8,128)S(1)}, f32[120,1536]{1,0:T(8,128)S(1)}, u32[]{:S(2)}, u32[]{:S(2)}) %collective-permute-start.46) | collective-permute-done | bytes 737312 | tf_op jit(solution)/shard_map/ppermute | solution.py:43
  610.5 4.5 broadcast_select_fusion.5
  615.0 3.9 broadcast_select_fusion
  627.3 8.5 %fusion = f32[768,3072]{1,0:T(8,128)} fusion(f32[480,1536]{1,0:T(8,128)} %copy-done.38, f32[480,1536]{1,0:T(8,128)} %get-tuple-element.131, f32[384,1536]{1,0:T(8,128)} %get-tuple-element.136, f32[384,1536]{1,0:T(8,128)} %get-tuple-element.135), kind=kLoop, calls=%fused_computation.1 | loop fusion | flops 7077888 | bytes 20054016 | tf_op jit(solution)/shard_map/concatenate | solution.py:1056
  (455 shorter events, 180.6 us)
Async XLA Ops:
  51.7 28.5 %collective-permute-start.12 = (f32[80,768]{1,0:T(8,128)S(1)}, f32[80,768]{1,0:T(8,128)S(1)}, u32[]{:S(2)}, u32[]{:S(2)}) collective-permute-start(f32[80,768]{1,0:T(8,128)S(1)} %pad_maximum_fusion.20), channel_id=1, source_target_pairs={{0,1},{1,0},{2,3},{3,2},{4,5},{5,4},{6,7},{7,6},{8,9},{9,8},{10,11... | collective-permute-start | bytes 737288 | tf_op jit(solution)/shard_map/ppermute | solution.py:43
  78.2 61.9 %collective-permute-start.16 = (f32[384,768]{1,0:T(8,128)S(1)}, f32[384,768]{1,0:T(8,128)S(1)}, u32[]{:S(2)}, u32[]{:S(2)}) collective-permute-start(f32[384,768]{1,0:T(8,128)S(1)} %bitcast.101), channel_id=1, source_target_pairs={{0,4},{1,5},{2,6},{3,7},{4,0},{5,1},{6,2},{7,3},{8,12},{9,13},{10,... | collective-permute-start | bytes 3538952 | tf_op jit(solution)/shard_map/ppermute | solution.py:43
  79.7 68.8 %collective-permute-start.17 = (f32[768,384]{1,0:T(8,128)S(1)}, f32[768,384]{1,0:T(8,128)S(1)}, u32[]{:S(2)}, u32[]{:S(2)}) collective-permute-start(f32[768,384]{1,0:T(8,128)S(1)} %bitcast.105), channel_id=1, source_target_pairs={{0,4},{1,5},{2,6},{3,7},{4,0},{5,1},{6,2},{7,3},{8,12},{9,13},{10,... | collective-permute-start | bytes 3538952 | tf_op jit(solution)/shard_map/ppermute | solution.py:43
  80.3 16.1 %collective-permute-start.15 = (f32[160,768]{1,0:T(8,128)S(1)}, f32[160,768]{1,0:T(8,128)S(1)}, u32[]{:S(2)}, u32[]{:S(2)}) collective-permute-start(f32[160,768]{1,0:T(8,128)S(1)} %pad_maximum_fusion.16.refs_0_.refs_4_), channel_id=1, source_target_pairs={{0,24},{1,25},{2,26},{3,27},{4,28},{5,29},{6,30},{7,31},{8,16},{9,... | collective-permute-start | bytes 1474568 | tf_op jit(solution)/shard_map/ppermute | solution.py:43
  84.0 53.4 %collective-permute-start.14 = (f32[160,768]{1,0:T(8,128)S(1)}, f32[160,768]{1,0:T(8,128)S(1)}, u32[]{:S(2)}, u32[]{:S(2)}) collective-permute-start(f32[160,768]{1,0:T(8,128)S(1)} %pad_maximum_fusion.16.refs_0_.refs_4_), channel_id=1, source_target_pairs={{0,16},{1,17},{2,18},{3,19},{4,20},{5,21},{6,22},{7,23},{8,24},{9,... | collective-permute-start | bytes 1474568 | tf_op jit(solution)/shard_map/ppermute | solution.py:43
  84.0 53.4 %collective-permute-start.13 = (f32[160,768]{1,0:T(8,128)S(1)}, f32[160,768]{1,0:T(8,128)S(1)}, u32[]{:S(2)}, u32[]{:S(2)}) collective-permute-start(f32[160,768]{1,0:T(8,128)S(1)} %pad_maximum_fusion.16.refs_0_.refs_4_), channel_id=1, source_target_pairs={{0,8},{1,9},{2,10},{3,11},{4,12},{5,13},{6,14},{7,15},{8,0},{9,1},... | collective-permute-start | bytes 1474568 | tf_op jit(solution)/shard_map/ppermute | solution.py:43
  96.4 52.1 %collective-permute-start.10 = (f32[168,768]{1,0:T(8,128)S(1)}, f32[168,768]{1,0:T(8,128)S(1)}, u32[]{:S(2)}, u32[]{:S(2)}) collective-permute-start(f32[168,768]{1,0:T(8,128)S(1)} %pad_maximum_fusion.14.refs_0_), channel_id=1, source_target_pairs={{0,24},{1,25},{2,26},{3,27},{4,28},{5,29},{6,30},{7,31},{8,16},{9,... | collective-permute-start | bytes 1548296 | tf_op jit(solution)/shard_map/ppermute | solution.py:43
  137.4 32.1 %collective-permute-start.9 = (f32[168,768]{1,0:T(8,128)S(1)}, f32[168,768]{1,0:T(8,128)S(1)}, u32[]{:S(2)}, u32[]{:S(2)}) collective-permute-start(f32[168,768]{1,0:T(8,128)S(1)} %pad_maximum_fusion.14.refs_0_), channel_id=1, source_target_pairs={{0,16},{1,17},{2,18},{3,19},{4,20},{5,21},{6,22},{7,23},{8,24},{9,... | collective-permute-start | bytes 1548296 | tf_op jit(solution)/shard_map/ppermute | solution.py:43
  137.4 32.1 %collective-permute-start.8 = (f32[168,768]{1,0:T(8,128)S(1)}, f32[168,768]{1,0:T(8,128)S(1)}, u32[]{:S(2)}, u32[]{:S(2)}) collective-permute-start(f32[168,768]{1,0:T(8,128)S(1)} %pad_maximum_fusion.14.refs_0_), channel_id=1, source_target_pairs={{0,8},{1,9},{2,10},{3,11},{4,12},{5,13},{6,14},{7,15},{8,0},{9,1},... | collective-permute-start | bytes 1548296 | tf_op jit(solution)/shard_map/ppermute | solution.py:43
  185.0 25.6 %collective-permute-start.23 = (f32[168,768]{1,0:T(8,128)}, f32[168,768]{1,0:T(8,128)S(1)}, u32[]{:S(2)}, u32[]{:S(2)}) collective-permute-start(f32[168,768]{1,0:T(8,128)} %get-tuple-element.86), channel_id=1, source_target_pairs={{0,8},{1,9},{2,10},{3,11},{4,12},{5,13},{6,14},{7,15},{8,0},{9,1},... | collective-permute-start | bytes 1548296 | tf_op jit(solution)/shard_map/ppermute | solution.py:43
  185.2 38.0 %collective-permute-start.24 = (f32[168,768]{1,0:T(8,128)}, f32[168,768]{1,0:T(8,128)S(1)}, u32[]{:S(2)}, u32[]{:S(2)}) collective-permute-start(f32[168,768]{1,0:T(8,128)} %get-tuple-element.87), channel_id=1, source_target_pairs={{0,16},{1,17},{2,18},{3,19},{4,20},{5,21},{6,22},{7,23},{8,24},{9,... | collective-permute-start | bytes 1548296 | tf_op jit(solution)/shard_map/ppermute | solution.py:43
  187.9 36.9 %collective-permute-start.25 = (f32[168,768]{1,0:T(8,128)}, f32[168,768]{1,0:T(8,128)}, u32[]{:S(2)}, u32[]{:S(2)}) collective-permute-start(f32[168,768]{1,0:T(8,128)} %get-tuple-element.88), channel_id=1, source_target_pairs={{0,24},{1,25},{2,26},{3,27},{4,28},{5,29},{6,30},{7,31},{8,16},{9,... | collective-permute-start | bytes 1548296 | tf_op jit(solution)/shard_map/ppermute | solution.py:43
  208.0 23.2 %collective-permute-start.18 = (f32[160,768]{1,0:T(8,128)S(1)}, f32[160,768]{1,0:T(8,128)S(1)}, u32[]{:S(2)}, u32[]{:S(2)}) collective-permute-start(f32[160,768]{1,0:T(8,128)S(1)} %get-tuple-element.80), channel_id=1, source_target_pairs={{0,8},{1,9},{2,10},{3,11},{4,12},{5,13},{6,14},{7,15},{8,0},{9,1},... | collective-permute-start | bytes 1474568 | tf_op jit(solution)/shard_map/ppermute | solution.py:43
  208.0 57.9 %collective-permute-start.19 = (f32[160,768]{1,0:T(8,128)S(1)}, f32[160,768]{1,0:T(8,128)S(1)}, u32[]{:S(2)}, u32[]{:S(2)}) collective-permute-start(f32[160,768]{1,0:T(8,128)S(1)} %get-tuple-element.81), channel_id=1, source_target_pairs={{0,16},{1,17},{2,18},{3,19},{4,20},{5,21},{6,22},{7,23},{8,24},{9,... | collective-permute-start | bytes 1474568 | tf_op jit(solution)/shard_map/ppermute | solution.py:43
  210.6 55.3 %collective-permute-start.20 = (f32[160,768]{1,0:T(8,128)S(1)}, f32[160,768]{1,0:T(8,128)S(1)}, u32[]{:S(2)}, u32[]{:S(2)}) collective-permute-start(f32[160,768]{1,0:T(8,128)S(1)} %get-tuple-element.82), channel_id=1, source_target_pairs={{0,24},{1,25},{2,26},{3,27},{4,28},{5,29},{6,30},{7,31},{8,16},{9,... | collective-permute-start | bytes 1474568 | tf_op jit(solution)/shard_map/ppermute | solution.py:43
  223.2 374.9 %collective-permute-start.82 = (f32[768,384]{1,0:T(8,128)}, f32[768,384]{1,0:T(8,128)}, u32[]{:S(2)}, u32[]{:S(2)}) collective-permute-start(f32[768,384]{1,0:T(8,128)} %get-tuple-element.111), channel_id=1, source_target_pairs={{0,4},{1,5},{2,6},{3,7},{4,0},{5,1},{6,2},{7,3},{8,12},{9,13},{10,... | collective-permute-start | bytes 3538952 | tf_op jit(solution)/shard_map/ppermute | solution.py:43
  227.8 38.5 %collective-permute-start.27 = (f32[88,768]{1,0:T(8,128)S(1)}, f32[88,768]{1,0:T(8,128)S(1)}, u32[]{:S(2)}, u32[]{:S(2)}) collective-permute-start(f32[88,768]{1,0:T(8,128)S(1)} %pad_maximum_fusion.19), channel_id=1, source_target_pairs={{0,2},{1,3},{2,0},{3,1},{4,6},{5,7},{6,4},{7,5},{8,10},{9,11},{10,... | collective-permute-start | bytes 811016 | tf_op jit(solution)/shard_map/ppermute | solution.py:43
  289.5 67.3 %collective-permute-start.66 = (f32[768,768]{1,0:T(8,128)}, f32[768,768]{1,0:T(8,128)}, u32[]{:S(2)}, u32[]{:S(2)}) collective-permute-start(f32[768,768]{1,0:T(8,128)} %constant_dynamic-slice_fusion.4), channel_id=1, source_target_pairs={{0,1},{1,0},{2,3},{3,2},{4,5},{5,4},{6,7},{7,6},{8,9},{9,8},{10,11... | collective-permute-start | bytes 7077896 | tf_op jit(solution)/shard_map/ppermute | solution.py:43
  308.9 52.6 %collective-permute-start.50 = (f32[384,1536]{1,0:T(8,128)}, f32[384,1536]{1,0:T(8,128)}, u32[]{:S(2)}, u32[]{:S(2)}) collective-permute-start(f32[384,1536]{1,0:T(8,128)} %constant_dynamic-slice_fusion.9), channel_id=1, source_target_pairs={{0,1},{1,0},{2,3},{3,2},{4,5},{5,4},{6,7},{7,6},{8,9},{9,8},{10,11... | collective-permute-start | bytes 7077896 | tf_op jit(solution)/shard_map/ppermute | solution.py:43
  356.7 87.6 %collective-permute-start.34 = (f32[480,1536]{1,0:T(8,128)S(1)}, f32[480,1536]{1,0:T(8,128)S(1)}, u32[]{:S(2)}, u32[]{:S(2)}) collective-permute-start(f32[480,1536]{1,0:T(8,128)S(1)} %constant_dynamic-slice_fusion.14), channel_id=1, source_target_pairs={{0,1},{1,0},{2,3},{3,2},{4,5},{5,4},{6,7},{7,6},{8,9},{9,8},{10,11... | collective-permute-start | bytes 8847368 | tf_op jit(solution)/shard_map/ppermute | solution.py:43
  359.8 16.2 %collective-permute-start.67 = (f32[192,768]{1,0:T(8,128)S(1)}, f32[192,768]{1,0:T(8,128)S(1)}, u32[]{:S(2)}, u32[]{:S(2)}) collective-permute-start(f32[192,768]{1,0:T(8,128)S(1)} %constant_dynamic-slice_fusion.3), channel_id=1, source_target_pairs={{0,4},{1,5},{2,6},{3,7},{4,0},{5,1},{6,2},{7,3},{8,12},{9,13},{10,... | collective-permute-start | bytes 1769480 | tf_op jit(solution)/shard_map/ppermute | solution.py:43
  360.7 16.2 %collective-permute-start.69 = (f32[192,768]{1,0:T(8,128)S(1)}, f32[192,768]{1,0:T(8,128)S(1)}, u32[]{:S(2)}, u32[]{:S(2)}) collective-permute-start(f32[192,768]{1,0:T(8,128)S(1)} %constant_dynamic-slice_fusion.1), channel_id=1, source_target_pairs={{0,2},{1,3},{2,0},{3,1},{4,6},{5,7},{6,4},{7,5},{8,10},{9,11},{10,... | collective-permute-start | bytes 1769480 | tf_op jit(solution)/shard_map/ppermute | solution.py:43
  363.8 24.4 %collective-permute-start.51 = (f32[96,1536]{1,0:T(8,128)S(1)}, f32[96,1536]{1,0:T(8,128)S(1)}, u32[]{:S(2)}, u32[]{:S(2)}) collective-permute-start(f32[96,1536]{1,0:T(8,128)S(1)} %constant_dynamic-slice_fusion.8), channel_id=1, source_target_pairs={{0,4},{1,5},{2,6},{3,7},{4,0},{5,1},{6,2},{7,3},{8,12},{9,13},{10,... | collective-permute-start | bytes 1769480 | tf_op jit(solution)/shard_map/ppermute | solution.py:43
  376.0 16.3 %collective-permute-start.53 = (f32[96,1536]{1,0:T(8,128)S(1)}, f32[96,1536]{1,0:T(8,128)S(1)}, u32[]{:S(2)}, u32[]{:S(2)}) collective-permute-start(f32[96,1536]{1,0:T(8,128)S(1)} %constant_dynamic-slice_fusion.6), channel_id=1, source_target_pairs={{0,2},{1,3},{2,0},{3,1},{4,6},{5,7},{6,4},{7,5},{8,10},{9,11},{10,... | collective-permute-start | bytes 1769480 | tf_op jit(solution)/shard_map/ppermute | solution.py:43
  377.0 33.4 %collective-permute-start.68 = (f32[96,768]{1,0:T(8,128)S(1)}, f32[96,768]{1,0:T(8,128)S(1)}, u32[]{:S(2)}, u32[]{:S(2)}) collective-permute-start(f32[96,768]{1,0:T(8,128)S(1)} %constant_dynamic-slice_fusion.2), channel_id=1, source_target_pairs={{0,2},{1,3},{2,0},{3,1},{4,6},{5,7},{6,4},{7,5},{8,10},{9,11},{10,... | collective-permute-start | bytes 884744 | tf_op jit(solution)/shard_map/ppermute | solution.py:43
  388.2 25.3 %collective-permute-start.70 = (f32[96,768]{1,0:T(8,128)S(1)}, f32[96,768]{1,0:T(8,128)S(1)}, u32[]{:S(2)}, u32[]{:S(2)}) collective-permute-start(f32[96,768]{1,0:T(8,128)S(1)} %constant_dynamic-slice_fusion), channel_id=1, source_target_pairs={{0,4},{1,5},{2,6},{3,7},{4,0},{5,1},{6,2},{7,3},{8,12},{9,13},{10,... | collective-permute-start | bytes 884744 | tf_op jit(solution)/shard_map/ppermute | solution.py:43
  422.1 16.9 %collective-permute-start.72 = (f32[192,192]{1,0:T(8,128)S(1)}, f32[192,192]{1,0:T(8,128)S(1)}, u32[]{:S(2)}, u32[]{:S(2)}) collective-permute-start(f32[192,192]{1,0:T(8,128)S(1)} %get-tuple-element.187), channel_id=1, source_target_pairs={{0,16},{1,17},{2,18},{3,19},{4,20},{5,21},{6,22},{7,23},{8,24},{9,... | collective-permute-start | bytes 442376 | tf_op jit(solution)/shard_map/ppermute | solution.py:43
  423.5 15.5 %collective-permute-start.73 = (f32[192,192]{1,0:T(8,128)S(1)}, f32[192,192]{1,0:T(8,128)S(1)}, u32[]{:S(2)}, u32[]{:S(2)}) collective-permute-start(f32[192,192]{1,0:T(8,128)S(1)} %get-tuple-element.188), channel_id=1, source_target_pairs={{0,24},{1,25},{2,26},{3,27},{4,28},{5,29},{6,30},{7,31},{8,16},{9,... | collective-permute-start | bytes 442376 | tf_op jit(solution)/shard_map/ppermute | solution.py:43
  426.0 25.8 %collective-permute-start.60 = (f32[96,384]{1,0:T(8,128)S(1)}, f32[96,384]{1,0:T(8,128)S(1)}, u32[]{:S(2)}, u32[]{:S(2)}) collective-permute-start(f32[96,384]{1,0:T(8,128)S(1)} %fusion.25), channel_id=1, source_target_pairs={{0,8},{1,9},{2,10},{3,11},{4,12},{5,13},{6,14},{7,15},{8,0},{9,1},... | collective-permute-start | bytes 442376 | tf_op jit(solution)/shard_map/ppermute | solution.py:43
  439.1 15.5 %collective-permute-start.59 = (f32[96,384]{1,0:T(8,128)S(1)}, f32[96,384]{1,0:T(8,128)S(1)}, u32[]{:S(2)}, u32[]{:S(2)}) collective-permute-start(f32[96,384]{1,0:T(8,128)S(1)} %fusion.25), channel_id=1, source_target_pairs={{0,16},{1,17},{2,18},{3,19},{4,20},{5,21},{6,22},{7,23},{8,24},{9,... | collective-permute-start | bytes 442376 | tf_op jit(solution)/shard_map/ppermute | solution.py:43
  439.1 19.9 %collective-permute-start.58 = (f32[96,384]{1,0:T(8,128)S(1)}, f32[96,384]{1,0:T(8,128)S(1)}, u32[]{:S(2)}, u32[]{:S(2)}) collective-permute-start(f32[96,384]{1,0:T(8,128)S(1)} %fusion.25), channel_id=1, source_target_pairs={{0,24},{1,25},{2,26},{3,27},{4,28},{5,29},{6,30},{7,31},{8,16},{9,... | collective-permute-start | bytes 442376 | tf_op jit(solution)/shard_map/ppermute | solution.py:43
  444.4 14.8 %collective-permute-start.76 = (f32[192,192]{1,0:T(8,128)S(1)}, f32[192,192]{1,0:T(8,128)S(1)}, u32[]{:S(2)}, u32[]{:S(2)}) collective-permute-start(f32[192,192]{1,0:T(8,128)S(1)} %fusion.11), channel_id=1, source_target_pairs={{0,8},{1,9},{2,10},{3,11},{4,12},{5,13},{6,14},{7,15},{8,0},{9,1},... | collective-permute-start | bytes 442376 | tf_op jit(solution)/shard_map/ppermute | solution.py:43
  451.8 15.7 %collective-permute-start.75 = (f32[192,192]{1,0:T(8,128)S(1)}, f32[192,192]{1,0:T(8,128)S(1)}, u32[]{:S(2)}, u32[]{:S(2)}) collective-permute-start(f32[192,192]{1,0:T(8,128)S(1)} %fusion.11), channel_id=1, source_target_pairs={{0,16},{1,17},{2,18},{3,19},{4,20},{5,21},{6,22},{7,23},{8,24},{9,... | collective-permute-start | bytes 442376 | tf_op jit(solution)/shard_map/ppermute | solution.py:43
  454.6 14.3 %collective-permute-start.74 = (f32[192,192]{1,0:T(8,128)S(1)}, f32[192,192]{1,0:T(8,128)S(1)}, u32[]{:S(2)}, u32[]{:S(2)}) collective-permute-start(f32[192,192]{1,0:T(8,128)S(1)} %fusion.11), channel_id=1, source_target_pairs={{0,24},{1,25},{2,26},{3,27},{4,28},{5,29},{6,30},{7,31},{8,16},{9,... | collective-permute-start | bytes 442376 | tf_op jit(solution)/shard_map/ppermute | solution.py:43
  459.0 30.5 %collective-permute-start.35 = (f32[120,1536]{1,0:T(8,128)S(1)}, f32[120,1536]{1,0:T(8,128)S(1)}, u32[]{:S(2)}, u32[]{:S(2)}) collective-permute-start(f32[120,1536]{1,0:T(8,128)S(1)} %constant_dynamic-slice_fusion.13), channel_id=1, source_target_pairs={{0,4},{1,5},{2,6},{3,7},{4,0},{5,1},{6,2},{7,3},{8,12},{9,13},{10,... | collective-permute-start | bytes 2211848 | tf_op jit(solution)/shard_map/ppermute | solution.py:43
  459.1 32.2 %collective-permute-start.37 = (f32[120,1536]{1,0:T(8,128)S(1)}, f32[120,1536]{1,0:T(8,128)S(1)}, u32[]{:S(2)}, u32[]{:S(2)}) collective-permute-start(f32[120,1536]{1,0:T(8,128)S(1)} %constant_dynamic-slice_fusion.11), channel_id=1, source_target_pairs={{0,2},{1,3},{2,0},{3,1},{4,6},{5,7},{6,4},{7,5},{8,10},{9,11},{10,... | collective-permute-start | bytes 2211848 | tf_op jit(solution)/shard_map/ppermute | solution.py:43
  488.0 43.1 %collective-permute-start.64 = (f32[96,1536]{1,0:T(8,128)S(1)}, f32[96,1536]{1,0:T(8,128)S(1)}, u32[]{:S(2)}, u32[]{:S(2)}) collective-permute-start(f32[96,1536]{1,0:T(8,128)S(1)} %pad_maximum_fusion.10), channel_id=1, source_target_pairs={{0,2},{1,3},{2,0},{3,1},{4,6},{5,7},{6,4},{7,5},{8,10},{9,11},{10,... | collective-permute-start | bytes 1769480 | tf_op jit(solution)/shard_map/ppermute | solution.py:43
  489.6 17.1 %collective-permute-start.36 = (f32[60,1536]{1,0:T(8,128)S(1)}, f32[60,1536]{1,0:T(8,128)S(1)}, u32[]{:S(2)}, u32[]{:S(2)}) collective-permute-start(f32[60,1536]{1,0:T(8,128)S(1)} %constant_dynamic-slice_fusion.12), channel_id=1, source_target_pairs={{0,2},{1,3},{2,0},{3,1},{4,6},{5,7},{6,4},{7,5},{8,10},{9,11},{10,... | collective-permute-start | bytes 1105928 | tf_op jit(solution)/shard_map/ppermute | solution.py:43
  491.5 15.3 %collective-permute-start.38 = (f32[60,1536]{1,0:T(8,128)S(1)}, f32[60,1536]{1,0:T(8,128)S(1)}, u32[]{:S(2)}, u32[]{:S(2)}) collective-permute-start(f32[60,1536]{1,0:T(8,128)S(1)} %constant_dynamic-slice_fusion.10), channel_id=1, source_target_pairs={{0,4},{1,5},{2,6},{3,7},{4,0},{5,1},{6,2},{7,3},{8,12},{9,13},{10,... | collective-permute-start | bytes 1105928 | tf_op jit(solution)/shard_map/ppermute | solution.py:43
  514.0 88.5 %collective-permute-start.83 = (f32[384,768]{1,0:T(8,128)}, f32[384,768]{1,0:T(8,128)}, u32[]{:S(2)}, u32[]{:S(2)}) collective-permute-start(f32[384,768]{1,0:T(8,128)} %get-tuple-element.113), channel_id=1, source_target_pairs={{0,4},{1,5},{2,6},{3,7},{4,0},{5,1},{6,2},{7,3},{8,12},{9,13},{10,... | collective-permute-start | bytes 3538952 | tf_op jit(solution)/shard_map/ppermute | solution.py:43
  533.4 61.2 %collective-permute-start.22 = (f32[80,768]{1,0:T(8,128)}, f32[80,768]{1,0:T(8,128)S(1)}, u32[]{:S(2)}, u32[]{:S(2)}) collective-permute-start(f32[80,768]{1,0:T(8,128)} %pad_maximum_fusion.21), channel_id=1, source_target_pairs={{0,2},{1,3},{2,0},{3,1},{4,6},{5,7},{6,4},{7,5},{8,10},{9,11},{10,... | collective-permute-start | bytes 737288 | tf_op jit(solution)/shard_map/ppermute | solution.py:43
  540.3 13.9 %collective-permute-start.62 = (f32[96,1536]{1,0:T(8,128)S(1)}, f32[96,1536]{1,0:T(8,128)S(1)}, u32[]{:S(2)}, u32[]{:S(2)}) collective-permute-start(f32[96,1536]{1,0:T(8,128)S(1)} %pad_maximum_fusion.9), channel_id=1, source_target_pairs={{0,4},{1,5},{2,6},{3,7},{4,0},{5,1},{6,2},{7,3},{8,12},{9,13},{10,... | collective-permute-start | bytes 1769480 | tf_op jit(solution)/shard_map/ppermute | solution.py:43
  540.9 15.9 %collective-permute-start.45 = (f32[60,1536]{1,0:T(8,128)S(1)}, f32[60,1536]{1,0:T(8,128)S(1)}, u32[]{:S(2)}, u32[]{:S(2)}) collective-permute-start(f32[60,1536]{1,0:T(8,128)S(1)} %get-tuple-element.176), channel_id=1, source_target_pairs={{0,2},{1,3},{2,0},{3,1},{4,6},{5,7},{6,4},{7,5},{8,10},{9,11},{10,... | collective-permute-start | bytes 1105928 | tf_op jit(solution)/shard_map/ppermute | solution.py:43
  556.7 15.6 %collective-permute-start.80 = (f32[192,768]{1,0:T(8,128)S(1)}, f32[192,768]{1,0:T(8,128)S(1)}, u32[]{:S(2)}, u32[]{:S(2)}) collective-permute-start(f32[192,768]{1,0:T(8,128)S(1)} %pad_maximum_fusion.13), channel_id=1, source_target_pairs={{0,2},{1,3},{2,0},{3,1},{4,6},{5,7},{6,4},{7,5},{8,10},{9,11},{10,... | collective-permute-start | bytes 1769480 | tf_op jit(solution)/shard_map/ppermute | solution.py:43
  565.2 16.0 %collective-permute-start.78 = (f32[192,768]{1,0:T(8,128)S(1)}, f32[192,768]{1,0:T(8,128)S(1)}, u32[]{:S(2)}, u32[]{:S(2)}) collective-permute-start(f32[192,768]{1,0:T(8,128)S(1)} %pad_maximum_fusion.12), channel_id=1, source_target_pairs={{0,4},{1,5},{2,6},{3,7},{4,0},{5,1},{6,2},{7,3},{8,12},{9,13},{10,... | collective-permute-start | bytes 1769480 | tf_op jit(solution)/shard_map/ppermute | solution.py:43
  584.5 21.4 %collective-permute-start.81 = (f32[768,768]{1,0:T(8,128)}, f32[768,768]{1,0:T(8,128)}, u32[]{:S(2)}, u32[]{:S(2)}) collective-permute-start(f32[768,768]{1,0:T(8,128)} %pad_maximum_fusion.4), channel_id=1, source_target_pairs={{0,1},{1,0},{2,3},{3,2},{4,5},{5,4},{6,7},{7,6},{8,9},{9,8},{10,11... | collective-permute-start | bytes 7077896 | tf_op jit(solution)/shard_map/ppermute | solution.py:43
  592.7 17.8 %collective-permute-start.65 = (f32[384,1536]{1,0:T(8,128)}, f32[384,1536]{1,0:T(8,128)}, u32[]{:S(2)}, u32[]{:S(2)}) collective-permute-start(f32[384,1536]{1,0:T(8,128)} %pad_maximum_fusion.3), channel_id=1, source_target_pairs={{0,1},{1,0},{2,3},{3,2},{4,5},{5,4},{6,7},{7,6},{8,9},{9,8},{10,11... | collective-permute-start | bytes 7077896 | tf_op jit(solution)/shard_map/ppermute | solution.py:43
  595.4 19.6 %collective-permute-start.49 = (f32[480,1536]{1,0:T(8,128)}, f32[480,1536]{1,0:T(8,128)}, u32[]{:S(2)}, u32[]{:S(2)}) collective-permute-start(f32[480,1536]{1,0:T(8,128)} %pad_maximum_fusion.2), channel_id=1, source_target_pairs={{0,1},{1,0},{2,3},{3,2},{4,5},{5,4},{6,7},{7,6},{8,9},{9,8},{10,11... | collective-permute-start | bytes 8847368 | tf_op jit(solution)/shard_map/ppermute | solution.py:43
  (112 other events, 1787.0 us)

commit v2 on v1

--- a/solution.py
+++ b/solution.py
@@ -47,6 +47,22 @@
         return lax.ppermute(block, AXES, route)
 
 
+def tie(*values):
+    return lax.optimization_barrier(values)
+
+
+def outer_reduce(grid, parts):
+    through = grid.swap(parts[3], "outer", 1)
+    return outer_reduce_rest(grid, parts, through)
+
+
+def outer_reduce_rest(grid, parts, through):
+    through, near = tie(through, parts[1])
+    near = grid.swap(near, "outer", 1)
+    far = grid.swap(parts[2] + through, "outer", 2)
+    return parts[0] + near + far
+
+
 def in_order(parts, place):
     bit = 1
     while bit < len(parts):
@@ -77,61 +93,104 @@
     return jnp.concatenate(in_order(parts, grid.at[name]), axis=0)
 
 
-def sum_everywhere(grid, block):
-    half = scatter_rows(grid, block, "core")
-    rows, width = half.shape[0] // 2, half.shape[1]
-    first = scatter_rows(grid, scatter_rows(grid, half[:rows], "inner"), "y")
-    second = scatter_rows(grid, scatter_rows(grid, half[rows:], "y"), "inner")
-    both = jnp.concatenate([first, second], axis=0)
+def sum_first(grid, half):
+    rows = half.shape[0] // 2
+    return scatter_rows(grid, half[:rows], "inner"), scatter_rows(grid, half[rows:], "y")
+
+
+def sum_second(grid, first, second):
+    return jnp.concatenate([scatter_rows(grid, first, "y"), scatter_rows(grid, second, "inner")], axis=0)
+
+
+def sum_outer(grid, both):
     count, place = grid.size["outer"], grid.at["outer"]
-    columns = width // count
+    columns = both.shape[1] // count
     piece = lambda s: lax.dynamic_slice_in_dim(both, (place ^ s) * columns, columns, 1)
     got = [grid.swap(piece(s), "outer", s) for s in range(1, count)]
     total = piece(0)
     for part in got:
         total = total + part
+    return total
+
+
+def spread_outer(grid, total):
+    count = grid.size["outer"]
     parts = [total] + [grid.swap(total, "outer", s) for s in range(1, count)]
-    both = jnp.concatenate(in_order(parts, place), axis=1)
+    return jnp.concatenate(in_order(parts, grid.at["outer"]), axis=1)
+
+
+def spread_second(grid, both):
     own = both.shape[0] // 2
-    first = gather_rows(grid, gather_rows(grid, both[:own], "y"), "inner")
-    second = gather_rows(grid, gather_rows(grid, both[own:], "inner"), "y")
-    return gather_rows(grid, jnp.concatenate([first, second], axis=0), "core")
-
-
-def entering(grid, pair, rate, backward):
-    states = pair.shape[0] - 1
-    total, total_steps = pair[:states], pair[states:]
-    ahead, ahead_steps = jnp.zeros_like(total), jnp.zeros_like(total_steps)
+    return gather_rows(grid, both[:own], "y"), gather_rows(grid, both[own:], "inner")
+
+
+def spread_first(grid, first, second):
+    return jnp.concatenate([gather_rows(grid, first, "inner"), gather_rows(grid, second, "y")], axis=0)
+
+
+def join_states_kernel(last, later_ref, total_ref, got_ref, ahead_ref, rate_ref, *outs):
+    states = rate_ref.shape[0]
+    rows, sums = slice(0, states), slice(states, states + 1)
+
+    def follow(early, late, out):
+        out[rows, :] = jnp.exp2(rate_ref[...] * late[sums, :]) * early[rows, :] + late[rows, :]
+        out[sums, :] = early[sums, :] + late[sums, :]
+
+    @pl.when(later_ref[0] == 1)
+    def _():
+        follow(got_ref, ahead_ref, outs[0])
+        if not last:
+            follow(got_ref, total_ref, outs[1])
+
+    @pl.when(later_ref[0] == 0)
+    def _():
+        outs[0][...] = ahead_ref[...]
+        if not last:
+            follow(total_ref, got_ref, outs[1])
+
+
+def entering(grid, pair, rate, backward, between=None):
+    states = rate.shape[0]
+    total, ahead, extra = pair, jnp.zeros_like(pair), None
     bits = 1
     while bits < grid.total:
-        got = grid.swap_bits(jnp.concatenate([total, total_steps], axis=0), bits)
-        state, steps = got[:states], got[states:]
-        later = ((grid.index // bits) % 2) == (0 if backward else 1)
-        ahead = jnp.where(later, jnp.exp2(rate * ahead_steps) * state + ahead, ahead)
-        ahead_steps = jnp.where(later, ahead_steps + steps, ahead_steps)
-        early, late = jnp.where(later, state, total), jnp.where(later, total, state)
-        total = jnp.exp2(rate * jnp.where(later, total_steps, steps)) * early + late
-        total_steps = total_steps + steps
+        got = grid.swap_bits(total, bits)
+        later = ((grid.index // bits) % 2).astype(jnp.int32)
+        later = (1 - later if backward else later).reshape(1)
+        last = 2 * bits >= grid.total
+        whole = pl.BlockSpec(memory_space=pltpu.VMEM)
+        ahead, *rest = call(
+            functools.partial(join_states_kernel, last),
+            [shape(*pair.shape)] * (1 if last else 2),
+            (later, total, got, ahead, rate),
+            in_specs=[SMEM] + [whole] * 4,
+            name="join_states",
+        )
+        total = rest[0] if rest else None
+        if bits == 4 and between:
+            total, *extra = between(total)
         bits *= 2
-    return ahead
+    return ahead[:states], extra
 
 
 def pad_rows(block, rows):
     return jnp.pad(block, ((0, rows - block.shape[0]), (0, 0)))
 
 
-def to_experts(grid, block, cap, tail):
-    ny, width = grid.size["y"], 2 * cap
-    slots = 2 * ny * cap
-    held = [block[:width]]
-    tails = [block[slots:]]
-    for s in range(1, ny):
+def send_y(grid, block, cap, tail):
+    width, slots = 2 * cap, grid.exp * cap
+    held, tails = [block[:width]], [block[slots:]]
+    for s in range(1, grid.size["y"]):
         part = block[s * width : (s + 1) * width]
         got = grid.swap(jnp.concatenate([part, block[slots:]], axis=0) if tail else part, "y", s)
         held.append(got[:width])
         tails.append(got[width:])
-    mine = [h[:cap] for h in held]
-    others = [h[cap:] for h in held]
+    return held, tails
+
+
+def send_core(grid, held, tails, cap, tail):
+    ny = grid.size["y"]
+    mine, others = [h[:cap] for h in held], [h[cap:] for h in held]
     if tail:
         others.append(pad_rows(jnp.concatenate([t[2 * s + 1 : 2 * s + 2] for s, t in enumerate(tails)], axis=0), 8))
     got = grid.swap(jnp.concatenate(others, axis=0), "core", 1)
@@ -221,6 +280,7 @@
         out_specs=out_specs or jax.tree.map(lambda _: whole, outs),
         scratch_shapes=scratch,
         name=name,
+        cost_estimate=pl.CostEstimate(flops=1000, transcendentals=0, bytes_accessed=1000),
         compiler_params=pltpu.CompilerParams(vmem_limit_bytes=VMEM_BYTES),
     )(*ins)
 
@@ -417,12 +477,12 @@
 
 
 def early_kernel(pieces, slices, *refs):
-    grads, downs, out_ref = refs[:pieces], refs[pieces : pieces + slices], refs[-1]
+    grads, downs, outs = refs[:pieces], refs[pieces : pieces + slices], refs[pieces + slices :]
     downs = [split(d[...]) for d in downs]
     for p in range(pieces):
         grad = split(grads[p][...])
         for i in range(slices):
-            out_ref[p, i] = product(grad, downs[i], NT)
+            outs[p][i] = product(grad, downs[i], NT)
 
 
 def gelu_parts(value):
@@ -434,38 +494,34 @@
     return 0.5 * value * (1.0 + tanh), slope
 
 
-def expert_kernel(pieces, slices, experts, cap, *refs):
-    tokens, ups, pulled = refs[:pieces], refs[pieces : pieces + slices], refs[pieces + slices]
-    backs = refs[pieces + slices + 1 : 2 * pieces + slices + 1]
-    hidden_ref, grad_ref = refs[-2:]
+def expert_kernel(slices, experts, cap, *refs):
+    tokens_ref, ups, pulled_ref = refs[0], refs[1 : slices + 1], refs[slices + 1]
+    back_ref, hidden_ref, grad_ref = refs[slices + 2 :]
     slots = experts * cap
-    ups = [split(u[...]) for u in ups]
     block, within = slot_tables(slots, cap, experts)
     within = within.astype(BF16)
-    for p in range(pieces):
-        rows = split(tokens[p][0:slots, :])
-        back = jnp.zeros((slots, tokens[p].shape[1]), F32)
-        to_gate = jnp.zeros((slots, 1), F32)
-        for i in range(slices):
-            hidden, slope = gelu_parts(product(rows, ups[i], NN))
-            pull = pulled[p, i]
-            grad = pull * slope
-            hidden_ref[p, i] = hidden
-            grad_ref[p, i] = grad
-            to_gate += jnp.sum(hidden * pull, axis=1, keepdims=True)
-            back += product(split(grad), ups[i], NT)
-        backs[p][0:slots, :] = back
-        backs[p][slots:, :] = jnp.zeros((8, tokens[p].shape[1]), F32)
-        high, low = split(block * to_gate)
-        rest = (block * to_gate - high.astype(F32) - low.astype(F32)).astype(BF16)
-        backs[p][slots:, 0:128] = dot(high, within, TN) + (dot(low, within, TN) + dot(rest, within, TN))
+    rows = split(tokens_ref[0:slots, :])
+    back = jnp.zeros((slots, tokens_ref.shape[1]), F32)
+    to_gate = jnp.zeros((slots, 1), F32)
+    for i in range(slices):
+        up = split(ups[i][...])
+        hidden, slope = gelu_parts(product(rows, up, NN))
+        pull = pulled_ref[i]
+        grad = pull * slope
+        hidden_ref[i] = hidden
+        grad_ref[i] = grad
+        to_gate += jnp.sum(hidden * pull, axis=1, keepdims=True)
+        back += product(split(grad), up, NT)
+    back_ref[0:slots, :] = back
+    back_ref[slots:, :] = jnp.zeros((8, tokens_ref.shape[1]), F32)
+    high, low = split(block * to_gate)
+    rest = (block * to_gate - high.astype(F32) - low.astype(F32)).astype(BF16)
+    back_ref[slots:, 0:128] = dot(high, within, TN) + (dot(low, within, TN) + dot(rest, within, TN))
 
 
 def expert_grads_kernel(pieces, slices, experts, cap, *refs):
-    tokens, grads = refs[:pieces], refs[pieces : 2 * pieces]
-    downs = refs[2 * pieces : 2 * pieces + slices]
-    hidden_ref, grad_ref = refs[2 * pieces + slices : 2 * pieces + slices + 2]
-    outs = refs[2 * pieces + slices + 2 :]
+    tokens, grads, hiddens, pulls = (refs[i * pieces : (i + 1) * pieces] for i in range(4))
+    downs, outs = refs[4 * pieces : 4 * pieces + slices], refs[4 * pieces + slices :]
     results, up_outs, down_outs = outs[:pieces], outs[pieces : pieces + slices], outs[pieces + slices :]
     slots = experts * cap
     downs = [split(d[...]) for d in downs]
@@ -481,10 +537,10 @@
         gated = split(grads[p][...] * gate)
         total = None
         for i in range(slices):
-            hidden = split(hidden_ref[p, i])
+            hidden = split(hiddens[p][i])
             part = product(hidden, downs[i], NN)
             total = part if total is None else total + part
-            up = product(rows, split(grad_ref[p, i]), TN)
+            up = product(rows, split(pulls[p][i]), TN)
             down = product(hidden, gated, TN)
             if p == 0:
                 up_outs[i][...] = up
@@ -590,26 +646,25 @@
     pair_ref[states : states + 1, :] = steps_row_ref[...]
 
 
-def out_grad_kernel(scan_ref, act_ref, skip_ref, gate_z_ref, grad_resid_ref, out_ref, high, low):
-    @pl.when(pl.program_id(0) == 0)
-    def _():
-        high[...], low[...] = split(grad_resid_ref[...])
-
-    gate_z = gate_z_ref[HALO:, :]
-    mixed = (scan_ref[...] + skip_ref[...] * act_ref[...]) * (gate_z * sigmoid(gate_z))
-    out_ref[...] = product(split(mixed), (high[...], low[...]), TN)
-
-
-def gate_grad_kernel(x_ref, gain_ref, grad_gate_ref, weight_ref, out_ref, normed_ref, high, low):
+def late_grads_kernel(
+    scan_ref, act_ref, skip_ref, gate_z_ref, grad_resid_ref, x_ref, gain_ref, grad_gate_ref, weight_ref,
+    out_ref, normed_ref, high, low, high_x, low_x,
+):
+    depth = x_ref.shape[1]
+
     @pl.when(pl.program_id(0) == 0)
     def _():
         x = x_ref[...]
-        high[...], low[...] = split(x * scale_of(x) * gain_ref[...])
+        high_x[...], low_x[...] = split(x * scale_of(x) * gain_ref[...])
+        high[...], low[...] = split(grad_resid_ref[...])
         normed_ref[...] = jnp.zeros_like(normed_ref)
 
     grad = split(grad_gate_ref[...])
-    out_ref[...] = product((high[...], low[...]), grad, TN)
+    out_ref[0:depth, :] = product((high_x[...], low_x[...]), grad, TN)
     normed_ref[...] += product(grad, split(weight_ref[...]), NT)
+    gate_z = gate_z_ref[HALO:, :]
+    mixed = (scan_ref[...] + skip_ref[...] * act_ref[...]) * (gate_z * sigmoid(gate_z))
+    out_ref[depth:, :] = product(split(mixed), (high[...], low[...]), TN)
 
 
 def scan_back_kernel(
@@ -830,8 +885,8 @@
         in_specs=[SMEM] + [pl.BlockSpec(memory_space=pltpu.VMEM)] * 2,
         name="route",
     )
-    own_grads = to_experts(grid, sent_grads, cap, False)
-    grad_pieces = [own_grads] + [grid.swap(own_grads, "outer", s) for s in range(1, pieces)]
+    halo, sent_grads = tie(halo, sent_grads)
+    held_grads, _ = send_y(grid, sent_grads, cap, False)
     up, down = expert_up[0], expert_down[0]
     ups = [up] + [grid.swap(up, "inner", s) for s in range(1, slices)]
     downs = [down] + [grid.swap(down, "inner", s) for s in range(1, slices)]
@@ -847,6 +902,7 @@
         scratch=[pltpu.VMEM((ext, depth), BF16)] * 2,
         name="join",
     )
+    joined, *held_grads = tie(joined, *held_grads)
     conv, act, pre, steps, masked, drive, proj, pair = call(
         functools.partial(features_kernel, rank_n, states),
         [shape(tokens, width)] * 6 + [shape(rank_n + 2 * states, tokens), shape(states + 1, width)],
@@ -866,7 +922,14 @@
         scratch=[pltpu.VMEM((tokens, states, 128), F32)],
         name="features",
     )
-    start = entering(grid, pair, rate, False)
+    own_grads = send_core(grid, held_grads, None, cap, False)
+    pair, own_grads, *downs = tie(pair, own_grads, *downs)
+    near_grads, far_grads = grid.swap(own_grads, "outer", 1), grid.swap(own_grads, "outer", 2)
+    start, (near_grads, far_grads) = entering(
+        grid, pair, rate, False, lambda total: tie(total, near_grads, far_grads)
+    )
+    last_grads = grid.swap(far_grads, "outer", 1)
+    start, last_grads = tie(start, last_grads)
     tok = pl.BlockSpec((tokens, chunk), block)
     gate_half = pl.BlockSpec((ext, chunk), lambda c: (0, chunks + c))
     one_row = pl.BlockSpec((1, chunk), block)
@@ -902,38 +965,45 @@
         name="scan",
     )
 
+    grad_pieces = [own_grads, near_grads, far_grads, last_grads]
     pulled = call(
         functools.partial(early_kernel, pieces, slices),
-        shape(pieces, slices, slots, hidden),
+        [shape(slices, slots, hidden)] * pieces,
         (*grad_pieces, *downs),
         name="early",
     )
-    own_tokens = to_experts(grid, sent, cap, True)
-    token_pieces = [own_tokens] + [grid.swap(own_tokens, "outer", s) for s in range(1, pieces)]
-    *backs, hiddens, hidden_grads = call(
-        functools.partial(expert_kernel, pieces, slices, experts, cap),
-        [shape(slots + 8, depth)] * pieces + [shape(pieces, slices, slots, hidden)] * 2,
-        (*token_pieces, *ups, pulled),
-        name="expert",
-    )
-    back = backs[0]
-    for s in range(1, pieces):
-        back = back + grid.swap(backs[s], "outer", s)
-    back = from_experts(grid, back, cap, True)
+    own_tokens = send_core(grid, *send_y(grid, sent, cap, True), cap, True)
+    own_tokens, *pulled = tie(own_tokens, *pulled)
+    near_tokens, far_tokens = grid.swap(own_tokens, "outer", 1), grid.swap(own_tokens, "outer", 2)
+
+    def expert(rows, pulled_rows):
+        return call(
+            functools.partial(expert_kernel, slices, experts, cap),
+            [shape(slots + 8, depth)] + [shape(slices, slots, hidden)] * 2,
+            (rows, *ups, pulled_rows),
+            name="expert",
+        )
+
+    own_outs = expert(own_tokens, pulled[0])
+    near_tokens, far_tokens, *own_outs = tie(near_tokens, far_tokens, *own_outs)
+    last_tokens = grid.swap(far_tokens, "outer", 1)
+    near_outs, far_outs = expert(near_tokens, pulled[1]), expert(far_tokens, pulled[2])
+    last_tokens, near_outs, far_outs = tie(last_tokens, near_outs, far_outs)
+    last_outs = expert(last_tokens, pulled[3])
+    token_pieces = [own_tokens, near_tokens, far_tokens, last_tokens]
+    backs, hiddens, pulls = zip(own_outs, near_outs, far_outs, last_outs)
+    back = from_experts(grid, outer_reduce(grid, backs), cap, True)
     outs = call(
         functools.partial(expert_grads_kernel, pieces, slices, experts, cap),
         [shape(slots, depth)] * pieces + [shape(depth, hidden)] * slices + [shape(hidden, depth)] * slices,
-        (*token_pieces, *grad_pieces, *downs, hiddens, hidden_grads),
+        (*token_pieces, *grad_pieces, *hiddens, *pulls, *downs),
         name="expert_grads",
     )
     results, up_grads, down_grads = outs[:pieces], outs[pieces : pieces + slices], outs[pieces + slices :]
-    grad_up, grad_down, result = up_grads[0], down_grads[0], results[0]
-    for s in range(1, slices):
-        grad_up = grad_up + grid.swap(up_grads[s], "inner", s)
-        grad_down = grad_down + grid.swap(down_grads[s], "inner", s)
-    for s in range(1, pieces):
-        result = result + grid.swap(results[s], "outer", s)
-    result = from_experts(grid, result, cap, False)
+    others_up = [grid.swap(up_grads[s], "inner", s) for s in range(1, slices)]
+    back, *others_up = tie(back, *others_up)
+    grad_up = functools.reduce(jnp.add, others_up, up_grads[0])
+    others_down = [grid.swap(down_grads[s], "inner", s) for s in range(1, slices)]
 
     grad_resid, small, grad_scan, grad_gate, grad_skip, back_pair = call(
         functools.partial(mixer_back_kernel, rank_n, states, experts, cap),
@@ -962,32 +1032,27 @@
         scratch=[lanes] + [pltpu.VMEM((tokens, depth), BF16)] * 2,
         name="mixer_back",
     )
-    end = entering(grid, back_pair, rate, True)
-    grad_out_proj = call(
-        out_grad_kernel,
-        shape(width, depth),
-        (scan, act, row(skip_gain), joined, grad_resid),
-        grid=(chunks,),
-        in_specs=[tok, tok, one_row, gate_half, full(tokens, depth)],
-        out_specs=out_rows,
-        scratch=[pltpu.VMEM((tokens, depth), BF16)] * 2,
-        name="out_grad",
-    )
-    grad_in_gate, grad_gate_normed = call(
-        gate_grad_kernel,
-        [shape(depth, width), shape(tokens, depth)],
-        (block_input, row(mixer_gain), grad_gate, in_proj),
-        grid=(chunks,),
+    back_pair, *results = tie(back_pair, *results)
+    wide = pl.BlockSpec((tokens, depth), block)
+    late, grad_gate_normed = call(
+        late_grads_kernel,
+        [shape(2 * depth, width), shape(tokens, depth)],
+        (scan, act, row(skip_gain), joined, grad_resid, block_input, row(mixer_gain), grad_gate, in_proj),
+        grid=(2,),
         in_specs=[
-            full(tokens, depth), full(1, depth), tok,
-            pl.BlockSpec((depth, chunk), lambda c: (0, chunks + c)),
+            wide, wide, pl.BlockSpec((1, depth), block), pl.BlockSpec((ext, depth), lambda c: (0, 2 + c)),
+            full(tokens, depth), full(tokens, depth), full(1, depth), wide,
+            pl.BlockSpec((depth, depth), lambda c: (0, 2 + c)),
         ],
-        out_specs=[pl.BlockSpec((depth, chunk), block), full(tokens, depth)],
-        scratch=[pltpu.VMEM((tokens, depth), BF16)] * 2,
-        name="gate_grad",
-    )
-    grad_out_proj = sum_everywhere(grid, grad_out_proj)
-    grad_in_gate = sum_everywhere(grid, grad_in_gate)
+        out_specs=[pl.BlockSpec((2 * depth, depth), block), full(tokens, depth)],
+        scratch=[pltpu.VMEM((tokens, depth), BF16)] * 4,
+        name="late_grads",
+    )
+    end, _ = entering(grid, back_pair, rate, True)
+    late = scatter_rows(grid, late, "core")
+    end, late = tie(end, late)
+    late = sum_first(grid, late)
+    through = grid.swap(results[3], "outer", 1)
     grad_act, grad_pre, grad_decay, grad_proj = call(
         functools.partial(scan_back_kernel, rank_n, states),
         [
@@ -1005,6 +1070,10 @@
         scratch=[lanes, lanes] + [pltpu.VMEM((tokens, chunk), F32)] * 2,
         name="scan_back",
     )
+    grad_proj, through, first, second, *others_down = tie(grad_proj, through, *late, *others_down)
+    grad_down = functools.reduce(jnp.add, others_down, down_grads[0])
+    late = sum_second(grid, first, second)
+    result = outer_reduce_rest(grid, results, through)
     used = depth + 2 * states + 2 * rank_n + states + taps + 4
     unit = 16 * grid.size["inner"] * grid.size["y"]
     packed = -(-(used + 8) // unit) * unit
@@ -1033,7 +1102,23 @@
     input_grad = jnp.concatenate([input_grad[: tokens - HALO], input_grad[tokens - HALO :] + from_next], axis=0)
     small = jnp.concatenate([small[:9], gain_row, loads[0:1], small[11:]], axis=0).reshape(8, width)
     grads = lax.dynamic_update_slice(grads, small, (used, 0))
-    grads = sum_everywhere(grid, grads)
+    grads, late, result = tie(grads, late, result)
+    result = from_experts(grid, result, cap, False)
+    late = sum_outer(grid, late)
+    grads = sum_second(grid, *sum_first(grid, scatter_rows(grid, grads, "core")))
+    late, grads, result = tie(late, grads, result)
+    late = spread_outer(grid, late)
+    late, grads = tie(late, grads)
+    first, second = spread_second(grid, late)
+    grads = sum_outer(grid, grads)
+    first, second, grads = tie(first, second, grads)
+    late = spread_first(grid, first, second)
+    grads = spread_outer(grid, grads)
+    late, grads = tie(late, grads)
+    late = gather_rows(grid, late, "core")
+    first, second = spread_second(grid, grads)
+    late, first, second = tie(late, first, second)
+    grads = gather_rows(grid, spread_first(grid, first, second), "core")
 
     combined = jnp.dot(table.T, result.astype(F32), precision=lax.Precision.HIGHEST, preferred_element_type=F32)
     block_output = resid + gate * combined
@@ -1053,7 +1138,7 @@
         block_output,
         input_grad,
         small[9],
-        jnp.concatenate([grads[:depth], grad_in_gate], axis=1),
+        jnp.concatenate([grads[:depth], late[:depth]], axis=1),
         grad_conv_weight,
         grad_conv_bias,
         grad_state_proj,
@@ -1061,7 +1146,7 @@
         grad_step_bias,
         grad_decay_log,
         grad_skip_gain,
-        grad_out_proj,
+        jnp.concatenate([late[depth:, :depth], late[depth:, depth:]], axis=0),
         small[8],
         small[:experts].T,
         grad_up[None],

time: 643 us -> 605 us (0.941)
  starting transfers between devices: 134 us -> 82.2 us
  waiting for transfers between devices: 294 us -> 259 us
  local copies, waits for them, and re-layouts: 29 us -> 52.6 us
  other arithmetic: 49.3 us -> 70.7 us
    ppermute x82 -> x66, starting transfers between devices: 131 us -> 78.1 us  [swap_bits(): return lax.ppermute(block, AXES, [(i, i ^ bits) for i in range(self.total)])]
    ppermute x82 -> x66, waiting for transfers between devices: 294 us -> 259 us  [swap_bits(): return lax.ppermute(block, AXES, [(i, i ^ bits) for i in range(self.total)])]
    unnamed x153 -> x147, local copies, waits for them, and re-layouts: 6.59 us -> 21.5 us
    add x15 -> x10, other arithmetic: 6.02 us -> 13.3 us  [scatter_rows(): total = total + part]
    pallas_call x12 -> x24, Pallas kernels: 125 us -> 129 us  [call(): pl.pallas_call(kernel, out_shape=outs, grid=grid or (), in_specs=in_specs...]
    select_n x15 -> x10, other arithmetic: 11.5 us -> 14.5 us  [in_order(): jnp.where(turned, parts[i ^ bit], parts[i])]
    concatenate x24 -> x14, other arithmetic: 15.5 us -> 15.4 us  [the longest x1 8.01 us: per_device(): jnp.concatenate([grads[:depth], late[:depth]], axis=1)]
  transfers between devices with their start and end apart: 84 -> 68, of which waited for: 40 -> 48; matrix products, arithmetic and copies ran while one was open for 8% -> 8% of each run, Pallas kernels for 15% -> 17%
where the time goes in v2:
time: 605 us; the launch traced here: 597 us
  waiting for transfers between devices  259 us (43%)
  Pallas kernels  129 us (21%)
  starting transfers between devices  82.2 us (14%)
  other arithmetic  70.7 us (12%)
  local copies, waits for them, and re-layouts  52.6 us (9%)
    ppermute x66, waiting for transfers between devices, swap_bits(): return lax.ppermute(block, AXES, [(i, i ^ bits) for i in range(self.total)])  259 us
    pallas_call x24, Pallas kernels, call(): pl.pallas_call(kernel, out_shape=outs, grid=grid or (), in_specs=in_specs...  129 us
    ppermute x66, starting transfers between devices, swap_bits(): return lax.ppermute(block, AXES, [(i, i ^ bits) for i in range(self.total)])  78.1 us
    unnamed x147, local copies, waits for them, and re-layouts  21.5 us
    select_n x10, other arithmetic, in_order(): jnp.where(turned, parts[i ^ bit], parts[i])  14.5 us
    add x10, other arithmetic, scatter_rows(): total = total + part  13.3 us
    dynamic_slice x10, local copies, waits for them, and re-layouts, scatter_rows(): lax.dynamic_slice_in_dim(block, (place ^ s) * rows, rows, 0)  12.2 us
  transfers between devices with their start and end apart: 68, of which 48 were waited for; matrix products, arithmetic and copies ran while one was open for 8% of the time, Pallas kernels for 17%

profile of v2, /device:TPU:0, one launch (start us, length us, event | category | flops | bytes accessed | tf_op | source)
XLA Modules:
  0.0 596.8 jit_solution(16994727988395512180)
XLA Ops:
  14.3 7.9 %join.1.inner_ref.gate_z_ref = f32[144,3072]{1,0:T(8,128)} custom-call(f32[128,768]{1,0:T(8,128)S(1)} %copy-done, f32[16,768]{1,0:T(8,128)S(1)} %collective-permute-done.halo_ref, f32[1,768]{1,0:T(1,128)S(1)} %reshape.118.gain_ref, f32[768,3072]{1,0:T(8,128)} %weight_ref.5), custom_call_target="tpu_custom_call" | custom-call | flops 1000 | bytes 1000 | tf_op jit(solution)/shard_map/join/pallas_call | solution.py:275
  23.8 8.2 %features.1 = (f32[128,1536]{1,0:T(8,128)S(1)}, f32[128,1536]{1,0:T(8,128)}, f32[128,1536]{1,0:T(8,128)}, f32[128,1536]{1,0:T(8,128)}, f32[128,1536]{1,0:T(8,128...) custom-call(f32[144,3072]{1,0:T(8,128)} %join.1.inner_ref.gate_z_ref, ...), custom_call_target="tpu_custom_call" | custom-call | flops 1000 | bytes 1000 | tf_op jit(solution)/shard_map/features/pallas_call | solution.py:275
  41.6 4.2 collective-permute-done.5.got_ref
  46.6 4.8 collective-permute-done.6.got_ref
  51.5 7.0 %collective-permute-done.8.refs_2_.refs_6_ = f32[160,768]{1,0:T(8,128)S(1)} collective-permute-done((f32[160,768]{1,0:T(8,128)S(1)}, f32[160,768]{1,0:T(8,128)S(1)}, u32[]{:S(2)}, u32[]{:S(2)}) %collective-permute-start.8) | collective-permute-done | bytes 491552 | tf_op jit(solution)/shard_map/ppermute | solution.py:43
  60.8 13.8 %collective-permute-done.9.got_ref = f32[17,1536]{1,0:T(8,128)S(1)} collective-permute-done((f32[17,1536]{1,0:T(8,128)S(1)}, f32[17,1536]{1,0:T(8,128)S(1)}, u32[]{:S(2)}, u32[]{:S(2)}) %collective-permute-start.9) | collective-permute-done | bytes 104480 | tf_op jit(solution)/shard_map/ppermute | solution.py:43
  78.8 5.2 collective-permute-done.10.got_ref
  84.0 14.1 %scan.1 = (f32[128,1536]{1,0:T(8,128)}, f32[128,16,1536]{2,1,0:T(8,128)}, f32[128,768]{1,0:T(8,128)S(1)}, f32[168,768]{1,0:T(8,128)S(1)}, f32[128,8]{1,0:T(8,128)S(1)}, /*index=5*/f32[128,1]{1,0:T(8,128)S(1)}) custom-call(s32[1]{0:T(128)} %bitcast.me_ref, f32[128,1536]{1,0:T(8,128)} %get-tuple-element.161.masked_ref, ...), custom_call_target="tpu_custom_call" | custom-call | flops 1000 | bytes 1000 | tf_op jit(solution)/shard_map/scan/pallas_call | solution.py:275
  100.4 5.7 collective-permute-done.12
  106.3 6.7 %early.1 = (f32[2,160,384]{2,1,0:T(8,128)S(1)}, f32[2,160,384]{2,1,0:T(8,128)S(1)}, f32[2,160,384]{2,1,0:T(8,128)S(1)}, f32[2,160,384]{2,1,0:T(8,128)S(1)}) custom-call(f32[160,768]{1,0:T(8,128)} %copy-done.61, f32[160,768]{1,0:T(8,128)} %collective-permute-done.7.refs_1_.refs_5_, f32[160,768]{1,0:T(8,128)} %copy-done.66, ...), custom_call_target="tpu_custom_call" | custom-call | flops 1000 | bytes 1000 | tf_op jit(solution)/shard_map/early/pallas_call | solution.py:275
  113.2 5.0 collective-permute-start.14
  118.2 4.4 expert.4
  124.2 15.2 %collective-permute-done.15.refs_0_.refs_2_ = f32[168,768]{1,0:T(8,128)S(1)} collective-permute-done((f32[168,768]{1,0:T(8,128)S(1)}, f32[168,768]{1,0:T(8,128)S(1)}, u32[]{:S(2)}, u32[]{:S(2)}) %collective-permute-start.15) | collective-permute-done | bytes 516128 | tf_op jit(solution)/shard_map/ppermute | solution.py:43
  140.2 4.4 expert.6
  145.4 4.6 expert.5
  153.6 4.8 expert.7
  158.8 12.1 %collective-permute-done.18 = f32[168,768]{1,0:T(8,128)S(1)} collective-permute-done((f32[168,768]{1,0:T(8,128)S(1)}, f32[168,768]{1,0:T(8,128)S(1)}, u32[]{:S(2)}, u32[]{:S(2)}) %collective-permute-start.18) | collective-permute-done | bytes 516128 | tf_op jit(solution)/shard_map/ppermute | solution.py:43
  175.2 17.4 %expert_grads.1 = (f32[160,768]{1,0:T(8,128)S(1)}, f32[160,768]{1,0:T(8,128)}, f32[160,768]{1,0:T(8,128)S(1)}, f32[160,768]{1,0:T(8,128)S(1)}, f32[768,384]{1,0:...) custom-call(f32[168,768]{1,0:T(8,128)} %copy-done.60, f32[168,768]{1,0:T(8,128)} %copy-done.63, ...), custom_call_target="tpu_custom_call" | custom-call | flops 1000 | bytes 1000 | tf_op jit(solution)/shard_map/expert_grads/pallas_call | solution.py:275
  201.4 7.2 %collective-permute-done.22 = f32[88,768]{1,0:T(8,128)} collective-permute-done((f32[88,768]{1,0:T(8,128)}, f32[88,768]{1,0:T(8,128)}, u32[]{:S(2)}, u32[]{:S(2)}) %collective-permute-start.22) | collective-permute-done | bytes 270368 | tf_op jit(solution)/shard_map/ppermute | solution.py:43
  212.7 5.4 collective-permute-done.23
  219.7 9.7 %mixer_back.1 = (f32[128,768]{1,0:T(8,128)S(1)}, f32[16,768]{1,0:T(8,128)S(1)}, f32[128,1536]{1,0:T(8,128)}, f32[128,1536]{1,0:T(8,128)}, f32[1,1536]{1,0:T(1,128)S(1)}, /*index=5*/f32[17,1536]{1,0:T(8,128)}) custom-call(s32[1]{0:T(128)} %bitcast.me_ref, f32[168,768]{1,0:T(8,128)} %pad_maximum_fusion.14.back_ref, ...), custom_call_target="tpu_custom_call" | custom-call | flops 1000 | bytes 1000 | tf_op jit(solution)/shard_map/mixer_back/pallas_call | solution.py:275
  229.4 10.7 %late_grads.1 = (f32[1536,1536]{1,0:T(8,128)}, f32[128,768]{1,0:T(8,128)S(1)}) custom-call(f32[128,1536]{1,0:T(8,128)S(1)} %copy-done.2, f32[128,1536]{1,0:T(8,128)} %get-tuple-element.163.act_ref, f32[1,1536]{1,0:T(1,128)S(1)} %reshape.126.skip_ref, f32[144,3072]{1,0:T(8,128)} %join.1.inner_ref.gate_z_ref, ...), custom_call_target="tpu_custom_call" | custom-call | flops 1000 | bytes 1000 | tf_op jit(solution)/shard_map/late_grads/pallas_call | solution.py:275
  240.1 5.0 constant_dynamic-slice_fusion.15
  245.6 6.0 %collective-permute-done.24.got_ref = f32[17,1536]{1,0:T(8,128)S(1)} collective-permute-done((f32[17,1536]{1,0:T(8,128)}, f32[17,1536]{1,0:T(8,128)S(1)}, u32[]{:S(2)}, u32[]{:S(2)}) %collective-permute-start.24) | collective-permute-done | bytes 104480 | tf_op jit(solution)/shard_map/ppermute | solution.py:43
  255.9 4.4 collective-permute-done.25.got_ref
  270.8 4.2 collective-permute-done.27.got_ref
  276.7 7.5 %collective-permute-done.28.got_ref = f32[17,1536]{1,0:T(8,128)S(1)} collective-permute-done((f32[17,1536]{1,0:T(8,128)}, f32[17,1536]{1,0:T(8,128)S(1)}, u32[]{:S(2)}, u32[]{:S(2)}) %collective-permute-start.28) | collective-permute-done | bytes 104480 | tf_op jit(solution)/shard_map/ppermute | solution.py:43
  286.0 4.8 dynamic-slice_add_fusion
  302.0 21.5 %scan_back.1 = (f32[128,1536]{1,0:T(8,128)S(1)}, f32[128,1536]{1,0:T(8,128)}, f32[16,1536]{1,0:T(8,128)S(1)}, f32[80,128]{1,0:T(8,128)S(1)}) custom-call(f32[128,1536]{1,0:T(8,128)} %get-tuple-element.161.masked_ref, f32[128,1536]{1,0:T(8,128)} %get-tuple-element.185.steps_ref, f32[128,1536]{1,0:T(8,128)} %get-tuple-element.162.drive_ref, ...), custom_call_target="tpu_custom_call" | custom-call | flops 1000 | bytes 1000 | tf_op jit(solution)/shard_map/scan_back/pallas_call | solution.py:275
  327.8 17.0 %collective-permute-done.33 = f32[384,768]{1,0:T(8,128)} collective-permute-done((f32[384,768]{1,0:T(8,128)}, f32[384,768]{1,0:T(8,128)}, u32[]{:S(2)}, u32[]{:S(2)}) %collective-permute-start.33) | collective-permute-done | bytes 1179680 | tf_op jit(solution)/shard_map/ppermute | solution.py:43
  350.0 10.8 %input_back.1 = (f32[960,1536]{1,0:T(8,128)}, f32[128,768]{1,0:T(8,128)S(1)}, f32[16,768]{1,0:T(8,128)S(1)}, f32[1,768]{1,0:T(1,128)S(1)}) custom-call(f32[80,128]{1,0:T(8,128)S(1)} %get-tuple-element.255.grad_proj_ref, f32[80,128]{1,0:T(8,128)S(1)} %get-tuple-element.180.proj_ref, f32[80,1536]{1,0:T(8,128)} %bitcast.34, ...), custom_call_target="tpu_custom_call" | custom-call | flops 1000 | bytes 1000 | tf_op jit(solution)/shard_map/input_back/pallas_call | solution.py:275
  385.7 6.5 %collective-permute-done.40 = f32[192,384]{1,0:T(8,128)S(1)} collective-permute-done((f32[192,384]{1,0:T(8,128)S(1)}, f32[192,384]{1,0:T(8,128)S(1)}, u32[]{:S(2)}, u32[]{:S(2)}) %collective-permute-start.40) | collective-permute-done | bytes 294944 | tf_op jit(solution)/shard_map/ppermute | solution.py:43
  392.2 12.0 %collective-permute-done.39 = f32[192,384]{1,0:T(8,128)S(1)} collective-permute-done((f32[192,384]{1,0:T(8,128)S(1)}, f32[192,384]{1,0:T(8,128)S(1)}, u32[]{:S(2)}, u32[]{:S(2)}) %collective-permute-start.39) | collective-permute-done | bytes 294944 | tf_op jit(solution)/shard_map/ppermute | solution.py:43
  409.3 16.2 %collective-permute-done.42 = f32[120,1536]{1,0:T(8,128)S(1)} collective-permute-done((f32[120,1536]{1,0:T(8,128)S(1)}, f32[120,1536]{1,0:T(8,128)S(1)}, u32[]{:S(2)}, u32[]{:S(2)}) %collective-permute-start.42) | collective-permute-done | bytes 737312 | tf_op jit(solution)/shard_map/ppermute | solution.py:43
  426.6 5.5 collective-permute-done.45
  438.0 8.6 %collective-permute-done.51 = f32[192,384]{1,0:T(8,128)S(1)} collective-permute-done((f32[192,384]{1,0:T(8,128)}, f32[192,384]{1,0:T(8,128)S(1)}, u32[]{:S(2)}, u32[]{:S(2)}) %collective-permute-start.51) | collective-permute-done | bytes 294944 | tf_op jit(solution)/shard_map/ppermute | solution.py:43
  446.6 9.5 %collective-permute-done.50 = f32[192,384]{1,0:T(8,128)S(1)} collective-permute-done((f32[192,384]{1,0:T(8,128)}, f32[192,384]{1,0:T(8,128)S(1)}, u32[]{:S(2)}, u32[]{:S(2)}) %collective-permute-start.50) | collective-permute-done | bytes 294944 | tf_op jit(solution)/shard_map/ppermute | solution.py:43
  461.8 4.1 collective-permute-start.54
  471.3 3.7 collective-permute-done.56
  474.9 5.8 collective-permute-done.55
  492.0 6.9 %collective-permute-done.60 = f32[120,384]{1,0:T(8,128)S(1)} collective-permute-done((f32[120,384]{1,0:T(8,128)S(1)}, f32[120,384]{1,0:T(8,128)S(1)}, u32[]{:S(2)}, u32[]{:S(2)}) %collective-permute-start.60) | collective-permute-done | bytes 184352 | tf_op jit(solution)/shard_map/ppermute | solution.py:43
  499.0 10.1 %collective-permute-done.57 = f32[192,1536]{1,0:T(8,128)S(1)} collective-permute-done((f32[192,1536]{1,0:T(8,128)S(1)}, f32[192,1536]{1,0:T(8,128)S(1)}, u32[]{:S(2)}, u32[]{:S(2)}) %collective-permute-start.57) | collective-permute-done | bytes 1179680 | tf_op jit(solution)/shard_map/ppermute | solution.py:43
  517.7 9.5 %collective-permute-done.64 = f32[60,1536]{1,0:T(8,128)S(1)} collective-permute-done((f32[60,1536]{1,0:T(8,128)S(1)}, f32[60,1536]{1,0:T(8,128)S(1)}, u32[]{:S(2)}, u32[]{:S(2)}) %collective-permute-start.64) | collective-permute-done | bytes 368672 | tf_op jit(solution)/shard_map/ppermute | solution.py:43
  528.8 7.0 %broadcast_select_fusion.1 = (f32[768,1536]{1,0:T(8,128)S(1)}, f32[768,1536]{1,0:T(8,128)}) fusion(f32[768,1536]{1,0:T(8,128)} %collective-permute-done.62, f32[768,1536]{1,0:T(8,128)} %pad_maximum_fusion.2, pred[]{:T(512)S(6)} %eq.53), kind=kLoop, calls=%fused_computation.9 | loop fusion | flops 2359296 | bytes 18874368 | tf_op jit(solution)/shard_map/jit(_where)/select_n | solution.py:70
  535.8 7.3 %pad_maximum_fusion.1 = f32[1536,1536]{1,0:T(8,128)} fusion(f32[768,1536]{1,0:T(8,128)} %get-tuple-element.304, f32[768,1536]{1,0:T(8,128)S(1)} %get-tuple-element.303), kind=kLoop, calls=%fused_computation.2 | loop fusion | flops 2359296 | bytes 18874368 | tf_op jit(solution)/shard_map/concatenate | solution.py:93
  544.6 16.4 %collective-permute-done.65 = f32[120,1536]{1,0:T(8,128)S(1)} collective-permute-done((f32[120,1536]{1,0:T(8,128)S(1)}, f32[120,1536]{1,0:T(8,128)S(1)}, u32[]{:S(2)}, u32[]{:S(2)}) %collective-permute-start.65) | collective-permute-done | bytes 737312 | tf_op jit(solution)/shard_map/ppermute | solution.py:43
  579.1 4.2 broadcast_select_fusion.2
  588.5 8.0 %fusion = f32[768,3072]{1,0:T(8,128)} fusion(f32[480,1536]{1,0:T(8,128)S(1)} %get-tuple-element.306, f32[480,1536]{1,0:T(8,128)} %get-tuple-element.305, f32[768,1536]{1,0:T(8,128)} %slice.273), kind=kLoop, calls=%fused_computation.1 | loop fusion | flops 4718592 | bytes 20054016 | tf_op jit(solution)/shard_map/concatenate | solution.py:1141
  (389 shorter events, 193.8 us)
Async XLA Ops:
  3.8 29.1 %collective-permute-start.3 = (f32[384,768]{1,0:T(8,128)}, f32[384,768]{1,0:T(8,128)}, u32[]{:S(2)}, u32[]{:S(2)}) collective-permute-start(f32[384,768]{1,0:T(8,128)} %bitcast.42), channel_id=1, source_target_pairs={{0,4},{1,5},{2,6},{3,7},{4,0},{5,1},{6,2},{7,3},{8,12},{9,13},{10,... | collective-permute-start | bytes 3538952 | tf_op jit(solution)/shard_map/ppermute | solution.py:43
  9.4 12.9 %collective-permute-start.1 = (f32[80,768]{1,0:T(8,128)S(1)}, f32[80,768]{1,0:T(8,128)S(1)}, u32[]{:S(2)}, u32[]{:S(2)}) collective-permute-start(f32[80,768]{1,0:T(8,128)S(1)} %get-tuple-element.359), channel_id=1, source_target_pairs={{0,2},{1,3},{2,0},{3,1},{4,6},{5,7},{6,4},{7,5},{8,10},{9,11},{10,... | collective-permute-start | bytes 737288 | tf_op jit(solution)/shard_map/ppermute | solution.py:43
  22.3 10.5 %collective-permute-start.2 = (f32[80,768]{1,0:T(8,128)S(1)}, f32[80,768]{1,0:T(8,128)S(1)}, u32[]{:S(2)}, u32[]{:S(2)}) collective-permute-start(f32[80,768]{1,0:T(8,128)S(1)} %pad_maximum_fusion.20), channel_id=1, source_target_pairs={{0,1},{1,0},{2,3},{3,2},{4,5},{5,4},{6,7},{7,6},{8,9},{9,8},{10,11... | collective-permute-start | bytes 737288 | tf_op jit(solution)/shard_map/ppermute | solution.py:43
  33.0 25.5 %collective-permute-start.8 = (f32[160,768]{1,0:T(8,128)S(1)}, f32[160,768]{1,0:T(8,128)S(1)}, u32[]{:S(2)}, u32[]{:S(2)}) collective-permute-start(f32[160,768]{1,0:T(8,128)S(1)} %pad_maximum_fusion.15.refs_0_.refs_4_), channel_id=1, source_target_pairs={{0,16},{1,17},{2,18},{3,19},{4,20},{5,21},{6,22},{7,23},{8,24},{9,... | collective-permute-start | bytes 1474568 | tf_op jit(solution)/shard_map/ppermute | solution.py:43
  36.0 22.7 %collective-permute-start.7 = (f32[160,768]{1,0:T(8,128)S(1)}, f32[160,768]{1,0:T(8,128)}, u32[]{:S(2)}, u32[]{:S(2)}) collective-permute-start(f32[160,768]{1,0:T(8,128)S(1)} %pad_maximum_fusion.15.refs_0_.refs_4_), channel_id=1, source_target_pairs={{0,8},{1,9},{2,10},{3,11},{4,12},{5,13},{6,14},{7,15},{8,0},{9,1},... | collective-permute-start | bytes 1474568 | tf_op jit(solution)/shard_map/ppermute | solution.py:43
  58.8 25.2 %collective-permute-start.11 = (f32[160,768]{1,0:T(8,128)S(1)}, f32[160,768]{1,0:T(8,128)}, u32[]{:S(2)}, u32[]{:S(2)}) collective-permute-start(f32[160,768]{1,0:T(8,128)S(1)} %collective-permute-done.8.refs_2_.refs_6_), channel_id=1, source_target_pairs={{0,8},{1,9},{2,10},{3,11},{4,12},{5,13},{6,14},{7,15},{8,0},{9,1},... | collective-permute-start | bytes 1474568 | tf_op jit(solution)/shard_map/ppermute | solution.py:43
  60.3 14.3 %collective-permute-start.9 = (f32[17,1536]{1,0:T(8,128)S(1)}, f32[17,1536]{1,0:T(8,128)S(1)}, u32[]{:S(2)}, u32[]{:S(2)}) collective-permute-start(f32[17,1536]{1,0:T(8,128)S(1)} %get-tuple-element.174.total_ref), channel_id=1, source_target_pairs={{0,8},{1,9},{2,10},{3,11},{4,12},{5,13},{6,14},{7,15},{8,0},{9,1},... | collective-permute-start | bytes 313352 | tf_op jit(solution)/shard_map/ppermute | solution.py:43
  77.2 41.0 %collective-permute-start.16 = (f32[768,384]{1,0:T(8,128)}, f32[768,384]{1,0:T(8,128)}, u32[]{:S(2)}, u32[]{:S(2)}) collective-permute-start(f32[768,384]{1,0:T(8,128)} %bitcast.37), channel_id=1, source_target_pairs={{0,4},{1,5},{2,6},{3,7},{4,0},{5,1},{6,2},{7,3},{8,12},{9,13},{10,... | collective-permute-start | bytes 3538952 | tf_op jit(solution)/shard_map/ppermute | solution.py:43
  113.1 26.3 %collective-permute-start.15 = (f32[168,768]{1,0:T(8,128)S(1)}, f32[168,768]{1,0:T(8,128)S(1)}, u32[]{:S(2)}, u32[]{:S(2)}) collective-permute-start(f32[168,768]{1,0:T(8,128)S(1)} %pad_maximum_fusion.13.refs_0_), channel_id=1, source_target_pairs={{0,16},{1,17},{2,18},{3,19},{4,20},{5,21},{6,22},{7,23},{8,24},{9,... | collective-permute-start | bytes 1548296 | tf_op jit(solution)/shard_map/ppermute | solution.py:43
  113.2 26.3 %collective-permute-start.14 = (f32[168,768]{1,0:T(8,128)S(1)}, f32[168,768]{1,0:T(8,128)S(1)}, u32[]{:S(2)}, u32[]{:S(2)}) collective-permute-start(f32[168,768]{1,0:T(8,128)S(1)} %pad_maximum_fusion.13.refs_0_), channel_id=1, source_target_pairs={{0,8},{1,9},{2,10},{3,11},{4,12},{5,13},{6,14},{7,15},{8,0},{9,1},... | collective-permute-start | bytes 1548296 | tf_op jit(solution)/shard_map/ppermute | solution.py:43
  139.5 13.3 %collective-permute-start.17 = (f32[168,768]{1,0:T(8,128)S(1)}, f32[168,768]{1,0:T(8,128)S(1)}, u32[]{:S(2)}, u32[]{:S(2)}) collective-permute-start(f32[168,768]{1,0:T(8,128)S(1)} %collective-permute-done.15.refs_0_.refs_2_), channel_id=1, source_target_pairs={{0,8},{1,9},{2,10},{3,11},{4,12},{5,13},{6,14},{7,15},{8,0},{9,1},... | collective-permute-start | bytes 1548296 | tf_op jit(solution)/shard_map/ppermute | solution.py:43
  158.4 12.5 %collective-permute-start.18 = (f32[168,768]{1,0:T(8,128)S(1)}, f32[168,768]{1,0:T(8,128)S(1)}, u32[]{:S(2)}, u32[]{:S(2)}) collective-permute-start(f32[168,768]{1,0:T(8,128)S(1)} %get-tuple-element.214), channel_id=1, source_target_pairs={{0,8},{1,9},{2,10},{3,11},{4,12},{5,13},{6,14},{7,15},{8,0},{9,1},... | collective-permute-start | bytes 1548296 | tf_op jit(solution)/shard_map/ppermute | solution.py:43
  171.0 24.1 %collective-permute-start.20 = (f32[168,768]{1,0:T(8,128)S(1)}, f32[168,768]{1,0:T(8,128)S(1)}, u32[]{:S(2)}, u32[]{:S(2)}) collective-permute-start(f32[168,768]{1,0:T(8,128)S(1)} %add.261), channel_id=1, source_target_pairs={{0,16},{1,17},{2,18},{3,19},{4,20},{5,21},{6,22},{7,23},{8,24},{9,... | collective-permute-start | bytes 1548296 | tf_op jit(solution)/shard_map/ppermute | solution.py:43
  173.8 22.0 %collective-permute-start.19 = (f32[168,768]{1,0:T(8,128)S(1)}, f32[168,768]{1,0:T(8,128)S(1)}, u32[]{:S(2)}, u32[]{:S(2)}) collective-permute-start(f32[168,768]{1,0:T(8,128)S(1)} %get-tuple-element.216), channel_id=1, source_target_pairs={{0,8},{1,9},{2,10},{3,11},{4,12},{5,13},{6,14},{7,15},{8,0},{9,1},... | collective-permute-start | bytes 1548296 | tf_op jit(solution)/shard_map/ppermute | solution.py:43
  192.5 25.6 %collective-permute-start.23 = (f32[768,384]{1,0:T(8,128)}, f32[768,384]{1,0:T(8,128)}, u32[]{:S(2)}, u32[]{:S(2)}) collective-permute-start(f32[768,384]{1,0:T(8,128)} %get-tuple-element.227), channel_id=1, source_target_pairs={{0,4},{1,5},{2,6},{3,7},{4,0},{5,1},{6,2},{7,3},{8,12},{9,13},{10,... | collective-permute-start | bytes 3538952 | tf_op jit(solution)/shard_map/ppermute | solution.py:43
  245.1 41.0 %collective-permute-start.29 = (f32[768,1536]{1,0:T(8,128)}, f32[768,1536]{1,0:T(8,128)}, u32[]{:S(2)}, u32[]{:S(2)}) collective-permute-start(f32[768,1536]{1,0:T(8,128)} %constant_dynamic-slice_fusion.15), channel_id=1, source_target_pairs={{0,1},{1,0},{2,3},{3,2},{4,5},{5,4},{6,7},{7,6},{8,9},{9,8},{10,11... | collective-permute-start | bytes 14155784 | tf_op jit(solution)/shard_map/ppermute | solution.py:43
  295.0 29.2 %collective-permute-start.31 = (f32[192,1536]{1,0:T(8,128)}, f32[192,1536]{1,0:T(8,128)}, u32[]{:S(2)}, u32[]{:S(2)}) collective-permute-start(f32[192,1536]{1,0:T(8,128)} %constant_dynamic-slice_fusion.14), channel_id=1, source_target_pairs={{0,4},{1,5},{2,6},{3,7},{4,0},{5,1},{6,2},{7,3},{8,12},{9,13},{10,... | collective-permute-start | bytes 3538952 | tf_op jit(solution)/shard_map/ppermute | solution.py:43
  298.5 27.4 %collective-permute-start.32 = (f32[192,1536]{1,0:T(8,128)}, f32[192,1536]{1,0:T(8,128)}, u32[]{:S(2)}, u32[]{:S(2)}) collective-permute-start(f32[192,1536]{1,0:T(8,128)} %constant_dynamic-slice_fusion.13), channel_id=1, source_target_pairs={{0,2},{1,3},{2,0},{3,1},{4,6},{5,7},{6,4},{7,5},{8,10},{9,11},{10,... | collective-permute-start | bytes 3538952 | tf_op jit(solution)/shard_map/ppermute | solution.py:43
  299.4 45.5 %collective-permute-start.33 = (f32[384,768]{1,0:T(8,128)}, f32[384,768]{1,0:T(8,128)}, u32[]{:S(2)}, u32[]{:S(2)}) collective-permute-start(f32[384,768]{1,0:T(8,128)} %get-tuple-element.254), channel_id=1, source_target_pairs={{0,4},{1,5},{2,6},{3,7},{4,0},{5,1},{6,2},{7,3},{8,12},{9,13},{10,... | collective-permute-start | bytes 3538952 | tf_op jit(solution)/shard_map/ppermute | solution.py:43
  301.9 43.0 %collective-permute-start.30 = (f32[160,768]{1,0:T(8,128)}, f32[160,768]{1,0:T(8,128)}, u32[]{:S(2)}, u32[]{:S(2)}) collective-permute-start(f32[160,768]{1,0:T(8,128)} %copy-done.42), channel_id=1, source_target_pairs={{0,8},{1,9},{2,10},{3,11},{4,12},{5,13},{6,14},{7,15},{8,0},{9,1},... | collective-permute-start | bytes 1474568 | tf_op jit(solution)/shard_map/ppermute | solution.py:43
  346.7 19.3 %collective-permute-start.37 = (f32[160,768]{1,0:T(8,128)}, f32[160,768]{1,0:T(8,128)}, u32[]{:S(2)}, u32[]{:S(2)}) collective-permute-start(f32[160,768]{1,0:T(8,128)} %add.279), channel_id=1, source_target_pairs={{0,16},{1,17},{2,18},{3,19},{4,20},{5,21},{6,22},{7,23},{8,24},{9,... | collective-permute-start | bytes 1474568 | tf_op jit(solution)/shard_map/ppermute | solution.py:43
  346.7 19.4 %collective-permute-start.36 = (f32[160,768]{1,0:T(8,128)}, f32[160,768]{1,0:T(8,128)}, u32[]{:S(2)}, u32[]{:S(2)}) collective-permute-start(f32[160,768]{1,0:T(8,128)} %get-tuple-element.271), channel_id=1, source_target_pairs={{0,8},{1,9},{2,10},{3,11},{4,12},{5,13},{6,14},{7,15},{8,0},{9,1},... | collective-permute-start | bytes 1474568 | tf_op jit(solution)/shard_map/ppermute | solution.py:43
  348.9 19.3 %collective-permute-start.35 = (f32[96,1536]{1,0:T(8,128)}, f32[96,1536]{1,0:T(8,128)}, u32[]{:S(2)}, u32[]{:S(2)}) collective-permute-start(f32[96,1536]{1,0:T(8,128)} %constant_dynamic-slice_fusion.11), channel_id=1, source_target_pairs={{0,4},{1,5},{2,6},{3,7},{4,0},{5,1},{6,2},{7,3},{8,12},{9,13},{10,... | collective-permute-start | bytes 1769480 | tf_op jit(solution)/shard_map/ppermute | solution.py:43
  361.8 10.2 %collective-permute-start.34 = (f32[96,1536]{1,0:T(8,128)}, f32[96,1536]{1,0:T(8,128)S(1)}, u32[]{:S(2)}, u32[]{:S(2)}) collective-permute-start(f32[96,1536]{1,0:T(8,128)} %constant_dynamic-slice_fusion.12), channel_id=1, source_target_pairs={{0,2},{1,3},{2,0},{3,1},{4,6},{5,7},{6,4},{7,5},{8,10},{9,11},{10,... | collective-permute-start | bytes 1769480 | tf_op jit(solution)/shard_map/ppermute | solution.py:43
  374.6 11.1 %collective-permute-start.38 = (f32[192,384]{1,0:T(8,128)S(1)}, f32[192,384]{1,0:T(8,128)S(1)}, u32[]{:S(2)}, u32[]{:S(2)}) collective-permute-start(f32[192,384]{1,0:T(8,128)S(1)} %get-tuple-element.331), channel_id=1, source_target_pairs={{0,8},{1,9},{2,10},{3,11},{4,12},{5,13},{6,14},{7,15},{8,0},{9,1},... | collective-permute-start | bytes 884744 | tf_op jit(solution)/shard_map/ppermute | solution.py:43
  375.6 16.6 %collective-permute-start.40 = (f32[192,384]{1,0:T(8,128)S(1)}, f32[192,384]{1,0:T(8,128)S(1)}, u32[]{:S(2)}, u32[]{:S(2)}) collective-permute-start(f32[192,384]{1,0:T(8,128)S(1)} %get-tuple-element.332), channel_id=1, source_target_pairs={{0,24},{1,25},{2,26},{3,27},{4,28},{5,29},{6,30},{7,31},{8,16},{9,... | collective-permute-start | bytes 884744 | tf_op jit(solution)/shard_map/ppermute | solution.py:43
  378.0 26.2 %collective-permute-start.39 = (f32[192,384]{1,0:T(8,128)S(1)}, f32[192,384]{1,0:T(8,128)S(1)}, u32[]{:S(2)}, u32[]{:S(2)}) collective-permute-start(f32[192,384]{1,0:T(8,128)S(1)} %get-tuple-element.333), channel_id=1, source_target_pairs={{0,16},{1,17},{2,18},{3,19},{4,20},{5,21},{6,22},{7,23},{8,24},{9,... | collective-permute-start | bytes 884744 | tf_op jit(solution)/shard_map/ppermute | solution.py:43
  383.5 24.7 %collective-permute-start.44 = (f32[120,1536]{1,0:T(8,128)S(1)}, f32[120,1536]{1,0:T(8,128)S(1)}, u32[]{:S(2)}, u32[]{:S(2)}) collective-permute-start(f32[120,1536]{1,0:T(8,128)S(1)} %constant_dynamic-slice_fusion.4), channel_id=1, source_target_pairs={{0,2},{1,3},{2,0},{3,1},{4,6},{5,7},{6,4},{7,5},{8,10},{9,11},{10,... | collective-permute-start | bytes 2211848 | tf_op jit(solution)/shard_map/ppermute | solution.py:43
  384.5 22.9 %collective-permute-start.47 = (f32[80,768]{1,0:T(8,128)S(1)}, f32[80,768]{1,0:T(8,128)S(1)}, u32[]{:S(2)}, u32[]{:S(2)}) collective-permute-start(f32[80,768]{1,0:T(8,128)S(1)} %pad_maximum_fusion.21), channel_id=1, source_target_pairs={{0,2},{1,3},{2,0},{3,1},{4,6},{5,7},{6,4},{7,5},{8,10},{9,11},{10,... | collective-permute-start | bytes 737288 | tf_op jit(solution)/shard_map/ppermute | solution.py:43
  406.0 19.5 %collective-permute-start.42 = (f32[120,1536]{1,0:T(8,128)S(1)}, f32[120,1536]{1,0:T(8,128)S(1)}, u32[]{:S(2)}, u32[]{:S(2)}) collective-permute-start(f32[120,1536]{1,0:T(8,128)S(1)} %constant_dynamic-slice_fusion.6), channel_id=1, source_target_pairs={{0,4},{1,5},{2,6},{3,7},{4,0},{5,1},{6,2},{7,3},{8,12},{9,13},{10,... | collective-permute-start | bytes 2211848 | tf_op jit(solution)/shard_map/ppermute | solution.py:43
  408.3 23.7 %collective-permute-start.45 = (f32[60,1536]{1,0:T(8,128)S(1)}, f32[60,1536]{1,0:T(8,128)S(1)}, u32[]{:S(2)}, u32[]{:S(2)}) collective-permute-start(f32[60,1536]{1,0:T(8,128)S(1)} %constant_dynamic-slice_fusion.3), channel_id=1, source_target_pairs={{0,4},{1,5},{2,6},{3,7},{4,0},{5,1},{6,2},{7,3},{8,12},{9,13},{10,... | collective-permute-start | bytes 1105928 | tf_op jit(solution)/shard_map/ppermute | solution.py:43
  433.6 13.1 %collective-permute-start.51 = (f32[192,384]{1,0:T(8,128)}, f32[192,384]{1,0:T(8,128)S(1)}, u32[]{:S(2)}, u32[]{:S(2)}) collective-permute-start(f32[192,384]{1,0:T(8,128)} %add_add_fusion.2), channel_id=1, source_target_pairs={{0,8},{1,9},{2,10},{3,11},{4,12},{5,13},{6,14},{7,15},{8,0},{9,1},... | collective-permute-start | bytes 884744 | tf_op jit(solution)/shard_map/ppermute | solution.py:43
  433.7 22.5 %collective-permute-start.50 = (f32[192,384]{1,0:T(8,128)}, f32[192,384]{1,0:T(8,128)S(1)}, u32[]{:S(2)}, u32[]{:S(2)}) collective-permute-start(f32[192,384]{1,0:T(8,128)} %add_add_fusion.2), channel_id=1, source_target_pairs={{0,16},{1,17},{2,18},{3,19},{4,20},{5,21},{6,22},{7,23},{8,24},{9,... | collective-permute-start | bytes 884744 | tf_op jit(solution)/shard_map/ppermute | solution.py:43
  436.9 19.3 %collective-permute-start.49 = (f32[192,384]{1,0:T(8,128)}, f32[192,384]{1,0:T(8,128)S(1)}, u32[]{:S(2)}, u32[]{:S(2)}) collective-permute-start(f32[192,384]{1,0:T(8,128)} %add_add_fusion.2), channel_id=1, source_target_pairs={{0,24},{1,25},{2,26},{3,27},{4,28},{5,29},{6,30},{7,31},{8,16},{9,... | collective-permute-start | bytes 884744 | tf_op jit(solution)/shard_map/ppermute | solution.py:43
  458.4 23.4 %collective-permute-start.53 = (f32[96,1536]{1,0:T(8,128)}, f32[96,1536]{1,0:T(8,128)}, u32[]{:S(2)}, u32[]{:S(2)}) collective-permute-start(f32[96,1536]{1,0:T(8,128)} %get-tuple-element.325), channel_id=1, source_target_pairs={{0,4},{1,5},{2,6},{3,7},{4,0},{5,1},{6,2},{7,3},{8,12},{9,13},{10,... | collective-permute-start | bytes 1769480 | tf_op jit(solution)/shard_map/ppermute | solution.py:43
  459.4 22.5 %collective-permute-start.52 = (f32[96,1536]{1,0:T(8,128)}, f32[96,1536]{1,0:T(8,128)}, u32[]{:S(2)}, u32[]{:S(2)}) collective-permute-start(f32[96,1536]{1,0:T(8,128)} %get-tuple-element.326), channel_id=1, source_target_pairs={{0,2},{1,3},{2,0},{3,1},{4,6},{5,7},{6,4},{7,5},{8,10},{9,11},{10,... | collective-permute-start | bytes 1769480 | tf_op jit(solution)/shard_map/ppermute | solution.py:43
  461.8 9.5 %collective-permute-start.54 = (f32[120,384]{1,0:T(8,128)}, f32[120,384]{1,0:T(8,128)}, u32[]{:S(2)}, u32[]{:S(2)}) collective-permute-start(f32[120,384]{1,0:T(8,128)} %get-tuple-element.346), channel_id=1, source_target_pairs={{0,8},{1,9},{2,10},{3,11},{4,12},{5,13},{6,14},{7,15},{8,0},{9,1},... | collective-permute-start | bytes 552968 | tf_op jit(solution)/shard_map/ppermute | solution.py:43
  467.9 12.8 %collective-permute-start.55 = (f32[120,384]{1,0:T(8,128)S(1)}, f32[120,384]{1,0:T(8,128)}, u32[]{:S(2)}, u32[]{:S(2)}) collective-permute-start(f32[120,384]{1,0:T(8,128)S(1)} %get-tuple-element.348), channel_id=1, source_target_pairs={{0,16},{1,17},{2,18},{3,19},{4,20},{5,21},{6,22},{7,23},{8,24},{9,... | collective-permute-start | bytes 552968 | tf_op jit(solution)/shard_map/ppermute | solution.py:43
  483.5 25.7 %collective-permute-start.57 = (f32[192,1536]{1,0:T(8,128)S(1)}, f32[192,1536]{1,0:T(8,128)S(1)}, u32[]{:S(2)}, u32[]{:S(2)}) collective-permute-start(f32[192,1536]{1,0:T(8,128)S(1)} %pad_maximum_fusion.7), channel_id=1, source_target_pairs={{0,4},{1,5},{2,6},{3,7},{4,0},{5,1},{6,2},{7,3},{8,12},{9,13},{10,... | collective-permute-start | bytes 3538952 | tf_op jit(solution)/shard_map/ppermute | solution.py:43
  483.9 15.0 %collective-permute-start.60 = (f32[120,384]{1,0:T(8,128)S(1)}, f32[120,384]{1,0:T(8,128)S(1)}, u32[]{:S(2)}, u32[]{:S(2)}) collective-permute-start(f32[120,384]{1,0:T(8,128)S(1)} %add_add_fusion.3), channel_id=1, source_target_pairs={{0,16},{1,17},{2,18},{3,19},{4,20},{5,21},{6,22},{7,23},{8,24},{9,... | collective-permute-start | bytes 552968 | tf_op jit(solution)/shard_map/ppermute | solution.py:43
  486.9 12.0 %collective-permute-start.59 = (f32[120,384]{1,0:T(8,128)S(1)}, f32[120,384]{1,0:T(8,128)S(1)}, u32[]{:S(2)}, u32[]{:S(2)}) collective-permute-start(f32[120,384]{1,0:T(8,128)S(1)} %add_add_fusion.3), channel_id=1, source_target_pairs={{0,24},{1,25},{2,26},{3,27},{4,28},{5,29},{6,30},{7,31},{8,16},{9,... | collective-permute-start | bytes 552968 | tf_op jit(solution)/shard_map/ppermute | solution.py:43
  488.2 24.6 %collective-permute-start.58 = (f32[192,1536]{1,0:T(8,128)S(1)}, f32[192,1536]{1,0:T(8,128)S(1)}, u32[]{:S(2)}, u32[]{:S(2)}) collective-permute-start(f32[192,1536]{1,0:T(8,128)S(1)} %pad_maximum_fusion.8), channel_id=1, source_target_pairs={{0,2},{1,3},{2,0},{3,1},{4,6},{5,7},{6,4},{7,5},{8,10},{9,11},{10,... | collective-permute-start | bytes 3538952 | tf_op jit(solution)/shard_map/ppermute | solution.py:43
  515.5 13.3 %collective-permute-start.62 = (f32[768,1536]{1,0:T(8,128)}, f32[768,1536]{1,0:T(8,128)}, u32[]{:S(2)}, u32[]{:S(2)}) collective-permute-start(f32[768,1536]{1,0:T(8,128)} %pad_maximum_fusion.2), channel_id=1, source_target_pairs={{0,1},{1,0},{2,3},{3,2},{4,5},{5,4},{6,7},{7,6},{8,9},{9,8},{10,11... | collective-permute-start | bytes 14155784 | tf_op jit(solution)/shard_map/ppermute | solution.py:43
  515.6 11.6 %collective-permute-start.64 = (f32[60,1536]{1,0:T(8,128)S(1)}, f32[60,1536]{1,0:T(8,128)S(1)}, u32[]{:S(2)}, u32[]{:S(2)}) collective-permute-start(f32[60,1536]{1,0:T(8,128)S(1)} %get-tuple-element.340), channel_id=1, source_target_pairs={{0,4},{1,5},{2,6},{3,7},{4,0},{5,1},{6,2},{7,3},{8,12},{9,13},{10,... | collective-permute-start | bytes 1105928 | tf_op jit(solution)/shard_map/ppermute | solution.py:43
  517.3 11.2 %collective-permute-start.63 = (f32[60,1536]{1,0:T(8,128)S(1)}, f32[60,1536]{1,0:T(8,128)S(1)}, u32[]{:S(2)}, u32[]{:S(2)}) collective-permute-start(f32[60,1536]{1,0:T(8,128)S(1)} %get-tuple-element.341), channel_id=1, source_target_pairs={{0,2},{1,3},{2,0},{3,1},{4,6},{5,7},{6,4},{7,5},{8,10},{9,11},{10,... | collective-permute-start | bytes 1105928 | tf_op jit(solution)/shard_map/ppermute | solution.py:43
  543.1 17.8 %collective-permute-start.65 = (f32[120,1536]{1,0:T(8,128)S(1)}, f32[120,1536]{1,0:T(8,128)S(1)}, u32[]{:S(2)}, u32[]{:S(2)}) collective-permute-start(f32[120,1536]{1,0:T(8,128)S(1)} %pad_maximum_fusion.11), channel_id=1, source_target_pairs={{0,4},{1,5},{2,6},{3,7},{4,0},{5,1},{6,2},{7,3},{8,12},{9,13},{10,... | collective-permute-start | bytes 2211848 | tf_op jit(solution)/shard_map/ppermute | solution.py:43
  543.5 17.8 %collective-permute-start.66 = (f32[120,1536]{1,0:T(8,128)S(1)}, f32[120,1536]{1,0:T(8,128)S(1)}, u32[]{:S(2)}, u32[]{:S(2)}) collective-permute-start(f32[120,1536]{1,0:T(8,128)S(1)} %pad_maximum_fusion.12), channel_id=1, source_target_pairs={{0,2},{1,3},{2,0},{3,1},{4,6},{5,7},{6,4},{7,5},{8,10},{9,11},{10,... | collective-permute-start | bytes 2211848 | tf_op jit(solution)/shard_map/ppermute | solution.py:43
  563.6 15.0 %collective-permute-start.67 = (f32[480,1536]{1,0:T(8,128)}, f32[480,1536]{1,0:T(8,128)}, u32[]{:S(2)}, u32[]{:S(2)}) collective-permute-start(f32[480,1536]{1,0:T(8,128)} %pad_maximum_fusion.4), channel_id=1, source_target_pairs={{0,1},{1,0},{2,3},{3,2},{4,5},{5,4},{6,7},{7,6},{8,9},{9,8},{10,11... | collective-permute-start | bytes 8847368 | tf_op jit(solution)/shard_map/ppermute | solution.py:43
  (93 other events, 912.9 us)

commit v3 on v2

--- a/solution.py
+++ b/solution.py
@@ -16,6 +16,10 @@
 AXES = ("seq", "exp")
 NN, NT, TN = ((1,), (0,)), ((1,), (1,)), ((0,), (0,))
 VMEM_BYTES = 52 << 20
+MICROSECONDS = {
+    "route": 1, "join": 8, "features": 8, "join_states": 1, "scan": 14, "early": 7, "expert": 4.4,
+    "expert_grads": 17, "mixer_back": 9.6, "late": 6, "scan_back": 10, "input_back": 11, "finish_late": 8, "finish": 6,
+}
 
 
 class Grid:
@@ -51,11 +55,6 @@
     return lax.optimization_barrier(values)
 
 
-def outer_reduce(grid, parts):
-    through = grid.swap(parts[3], "outer", 1)
-    return outer_reduce_rest(grid, parts, through)
-
-
 def outer_reduce_rest(grid, parts, through):
     through, near = tie(through, parts[1])
     near = grid.swap(near, "outer", 1)
@@ -119,6 +118,17 @@
     return jnp.concatenate(in_order(parts, grid.at["outer"]), axis=1)
 
 
+def cut_outer(grid, both):
+    columns = both.shape[1] // 4
+    return [
+        lax.dynamic_slice_in_dim(both, (grid.at["outer"] ^ s) * columns, columns, 1) for s in range(4)
+    ]
+
+
+def join_outer(grid, own, near, far, last):
+    return jnp.concatenate(in_order([own, near, far, last], grid.at["outer"]), axis=1)
+
+
 def spread_second(grid, both):
     own = both.shape[0] // 2
     return gather_rows(grid, both[:own], "y"), gather_rows(grid, both[own:], "inner")
@@ -149,9 +159,9 @@
             follow(total_ref, got_ref, outs[1])
 
 
-def entering(grid, pair, rate, backward, between=None):
+def entering(grid, pair, rate, backward, after):
     states = rate.shape[0]
-    total, ahead, extra = pair, jnp.zeros_like(pair), None
+    total, ahead, hop = pair, jnp.zeros_like(pair), 1
     bits = 1
     while bits < grid.total:
         got = grid.swap_bits(total, bits)
@@ -167,10 +177,10 @@
             name="join_states",
         )
         total = rest[0] if rest else None
-        if bits == 4 and between:
-            total, *extra = between(total)
-        bits *= 2
-    return ahead[:states], extra
+        if hop in after:
+            total = after[hop](total)
+        bits, hop = 2 * bits, hop + 1
+    return ahead[:states]
 
 
 def pad_rows(block, rows):
@@ -201,13 +211,18 @@
     return jnp.concatenate(out, axis=0)
 
 
-def from_experts(grid, block, cap, tail):
+def back_core(grid, block, cap, tail):
     ny = grid.size["y"]
     half, slots = ny * cap, 2 * ny * cap
     send = block[half:slots]
     if tail:
         send = jnp.concatenate([send, pad_rows(block[slots + ny : slots + 2 * ny], 8)], axis=0)
-    got = grid.swap(send, "core", 1)
+    return grid.swap(send, "core", 1)
+
+
+def back_y(grid, block, got, cap, tail):
+    ny = grid.size["y"]
+    half, slots = ny * cap, 2 * ny * cap
     rows, ends = [], []
     for s in range(ny):
         pair = [block[s * cap : (s + 1) * cap], got[s * cap : (s + 1) * cap]]
@@ -270,7 +285,7 @@
     return jnp.concatenate([value] * (width // 128), axis=1)
 
 
-def call(kernel, outs, ins, grid=None, in_specs=None, out_specs=None, scratch=(), name=None):
+def call(kernel, outs, ins, grid=None, in_specs=None, out_specs=None, scratch=(), name=None, aliases=None):
     whole = pl.BlockSpec(memory_space=pltpu.VMEM)
     return pl.pallas_call(
         kernel,
@@ -280,7 +295,10 @@
         out_specs=out_specs or jax.tree.map(lambda _: whole, outs),
         scratch_shapes=scratch,
         name=name,
-        cost_estimate=pl.CostEstimate(flops=1000, transcendentals=0, bytes_accessed=1000),
+        cost_estimate=pl.CostEstimate(
+            flops=int(MICROSECONDS[name] * 1.1e9), transcendentals=0, bytes_accessed=int(MICROSECONDS[name] * 1e6)
+        ),
+        input_output_aliases=aliases or {},
         compiler_params=pltpu.CompilerParams(vmem_limit_bytes=VMEM_BYTES),
     )(*ins)
 
@@ -646,25 +664,41 @@
     pair_ref[states : states + 1, :] = steps_row_ref[...]
 
 
-def late_grads_kernel(
-    scan_ref, act_ref, skip_ref, gate_z_ref, grad_resid_ref, x_ref, gain_ref, grad_gate_ref, weight_ref,
-    out_ref, normed_ref, high, low, high_x, low_x,
+def late_kernel(
+    which_ref, scan_ref, act_ref, skip_ref, gate_z_ref, grad_resid_ref, x_ref, gain_ref, grad_gate_ref, *refs
 ):
-    depth = x_ref.shape[1]
+    high, low = refs[-2:]
+    if len(refs) == 5:
+        weight_ref, out_ref, normed_ref = refs[:3]
+    else:
+        weight_ref, out_ref, normed_ref = None, refs[0], None
 
     @pl.when(pl.program_id(0) == 0)
     def _():
-        x = x_ref[...]
-        high_x[...], low_x[...] = split(x * scale_of(x) * gain_ref[...])
-        high[...], low[...] = split(grad_resid_ref[...])
-        normed_ref[...] = jnp.zeros_like(normed_ref)
-
-    grad = split(grad_gate_ref[...])
-    out_ref[0:depth, :] = product((high_x[...], low_x[...]), grad, TN)
-    normed_ref[...] += product(grad, split(weight_ref[...]), NT)
-    gate_z = gate_z_ref[HALO:, :]
-    mixed = (scan_ref[...] + skip_ref[...] * act_ref[...]) * (gate_z * sigmoid(gate_z))
-    out_ref[depth:, :] = product(split(mixed), (high[...], low[...]), TN)
+        @pl.when(which_ref[0] == 0)
+        def _():
+            high[...], low[...] = split(grad_resid_ref[...])
+
+        @pl.when(which_ref[0] == 1)
+        def _():
+            x = x_ref[...]
+            high[...], low[...] = split(x * scale_of(x) * gain_ref[...])
+
+        if normed_ref is not None:
+            normed_ref[...] = jnp.zeros_like(normed_ref)
+
+    @pl.when(which_ref[0] == 0)
+    def _():
+        gate_z = gate_z_ref[HALO:, :]
+        mixed = (scan_ref[...] + skip_ref[...] * act_ref[...]) * (gate_z * sigmoid(gate_z))
+        out_ref[...] = product(split(mixed), (high[...], low[...]), TN)
+
+    @pl.when(which_ref[0] == 1)
+    def _():
+        out_ref[...] = product((high[...], low[...]), split(grad_gate_ref[...]), TN)
+
+    if normed_ref is not None:
+        normed_ref[...] += product(split(grad_gate_ref[...]), split(weight_ref[...]), NT)
 
 
 def scan_back_kernel(
@@ -683,23 +717,12 @@
     rate_ref,
     proj_ref,
     step_proj_ref,
-    grad_act_ref,
-    grad_pre_ref,
-    grad_decay_ref,
-    grad_proj_ref,
-    in_lanes,
-    out_lanes,
-    grad_drive,
-    grad_steps,
+    *refs,
 ):
+    grad_act_ref, grad_pre_ref, grad_decay_ref, grad_proj_ref, in_lanes, out_lanes, grad_drive, grad_steps = refs[-8:]
     tokens, chunk = masked_ref.shape
-    step = pl.program_id(0)
-
-    @pl.when(step == 0)
-    def _():
-        over_lanes(in_lanes, proj_ref[rank_n : rank_n + states, :])
-        over_lanes(out_lanes, proj_ref[rank_n + states : rank_n + 2 * states, :])
-        grad_proj_ref[...] = jnp.zeros_like(grad_proj_ref)
+    over_lanes(in_lanes, proj_ref[rank_n : rank_n + states, :])
+    over_lanes(out_lanes, proj_ref[rank_n + states : rank_n + 2 * states, :])
 
     rate = rate_ref[...]
     lane = iota((states, tokens), 1)
@@ -738,15 +761,18 @@
     grad_act_ref[...] = skip_ref[...] * grad_scan_ref[...] + grad_drive[...] * steps
     grad_pre = (grad_steps[...] * (1.0 / LOG2E) + grad_drive[...] * act) * sigmoid(pre_ref[...])
     grad_pre_ref[...] = grad_pre
-    grad_proj_ref[0:rank_n, :] += product(split(step_proj_ref[...]), split(grad_pre), NT)
-    grad_proj_ref[rank_n : rank_n + states, :] += grad_in
-    grad_proj_ref[rank_n + states : rank_n + 2 * states, :] += grad_out
+    grad_proj_ref[0:rank_n, :] = product(split(step_proj_ref[...]), split(grad_pre), NT)
+    grad_proj_ref[rank_n : rank_n + states, :] = grad_in
+    grad_proj_ref[rank_n + states : rank_n + 2 * states, :] = grad_out
 
 
 def input_back_kernel(
     rank_n,
     states,
-    grad_proj_ref,
+    core_ref,
+    proj_a_ref,
+    proj_b_ref,
+    proj_c_ref,
     proj_ref,
     state_proj_ref,
     act_ref,
@@ -764,10 +790,11 @@
     grad_resid_ref,
     grad_decay_ref,
     grad_skip_ref,
-    out_ref,
+    small_ref,
+    keep_ref,
+    send_ref,
     input_ref,
     edge_ref,
-    gain_row_ref,
     high,
     low,
     grad_inner,
@@ -775,6 +802,7 @@
 ):
     tokens, chunk = act_ref.shape
     depth = x_ref.shape[1]
+    half = depth // 2
     taps = conv_w_ref.shape[0]
     step = pl.program_id(0)
 
@@ -785,20 +813,12 @@
         total[...] = jnp.zeros_like(total)
 
     act, grad_pre = split(act_ref[...]), grad_pre_ref[...]
-    grad_pre_two = split(grad_pre)
-    grad_proj = split(grad_proj_ref[...])
+    grad_proj = split(proj_a_ref[...] + proj_b_ref[...] + proj_c_ref[...])
     grad_act = grad_act_ref[...] + product(grad_proj, split(state_proj_ref[...]), TN)
     _, slope = silu_parts(conv_ref[...])
     grad_conv = grad_act * slope
     since = since_ref[...]
     grad_inner[...] = jnp.zeros_like(grad_inner)
-    base = depth
-    out_ref[base : base + 2 * states + rank_n, :] = product(grad_proj, act, NN)
-    base += 2 * states + rank_n
-    out_ref[base : base + rank_n, :] = product(split(proj_ref[0:rank_n, :]), grad_pre_two, NN)
-    base += rank_n
-    out_ref[base : base + states, :] = grad_decay_ref[...]
-    base += states
     rows = []
     for k in range(taps):
         valid = (since >= taps - 1 - k).astype(F32)
@@ -809,12 +829,36 @@
     rows.append(jnp.sum(grad_conv, axis=0, keepdims=True))
     rows.append(jnp.sum(grad_pre, axis=0, keepdims=True))
     rows.append(grad_skip_ref[...])
-    out_ref[base:, :] = jnp.zeros((out_ref.shape[0] - base, chunk), F32)
-    for i, row in enumerate(rows):
-        out_ref[base + i : base + i + 1, :] = row
     grads = split(grad_inner[...])
-    out_ref[0:depth, :] = product((high[...], low[...]), grads, TN)
     total[...] += product(grads, split(weight_ref[...]), NT)
+    of_state_proj = product(grad_proj, act, NN)
+    of_step_proj = product(split(proj_ref[0:rank_n, :]), split(grad_pre), NN)
+
+    def first_half(out_ref):
+        out_ref[0:half, :] = product((high[:, 0:half], low[:, 0:half]), grads, TN)
+        at = half + 2 * states + rank_n
+        out_ref[half:at, :] = of_state_proj
+        out_ref[at : at + states, :] = grad_decay_ref[...]
+        if at + states < out_ref.shape[0]:
+            out_ref[at + states :, :] = jnp.zeros((out_ref.shape[0] - at - states, chunk), F32)
+
+    def second_half(out_ref):
+        out_ref[0:half, :] = product((high[:, half:], low[:, half:]), grads, TN)
+        out_ref[half : half + rank_n, :] = of_step_proj
+        at = half + rank_n
+        out_ref[at:, :] = jnp.zeros((out_ref.shape[0] - at, chunk), F32)
+        for i, row in enumerate(rows):
+            out_ref[at + i : at + i + 1, :] = row
+
+    @pl.when(core_ref[0] == 0)
+    def _():
+        first_half(keep_ref)
+        second_half(send_ref)
+
+    @pl.when(core_ref[0] == 1)
+    def _():
+        second_half(keep_ref)
+        first_half(send_ref)
 
     @pl.when(step == pl.num_programs(0) - 1)
     def _():
@@ -830,7 +874,75 @@
         own, own_gain = rows_back(x_ref[...], total[HALO:, :] + grad_gate_normed_ref[...])
         edge_ref[...] = edge
         input_ref[...] = grad_resid_ref[...] + own
-        gain_row_ref[...] = edge_gain + own_gain
+        small = jnp.concatenate([small_ref[0:10, :], edge_gain + own_gain], axis=0)
+
+        def place_small(out_ref):
+            at = half + rank_n + 8
+            out_ref[at : at + 11, :] = small[:, 0:chunk]
+            out_ref[at + 16 : at + 27, 0 : depth - chunk] = small[:, chunk:]
+
+        @pl.when(core_ref[0] == 0)
+        def _():
+            place_small(send_ref)
+
+        @pl.when(core_ref[0] == 1)
+        def _():
+            place_small(keep_ref)
+
+
+def finish_late_kernel(core_ref, first_ref, second_ref, got_first_ref, got_second_ref, in_ref, out_ref):
+    depth = out_ref.shape[2]
+    step = pl.program_id(0)
+
+    def write(gate, out):
+        in_ref[...] = gate
+        out_ref[0] = out[:, 0:depth]
+        out_ref[1] = out[:, depth:]
+
+    for i, (own, got) in enumerate(((first_ref, got_first_ref), (second_ref, got_second_ref))):
+
+        @pl.when((core_ref[0] == 0) & (step == i))
+        def _():
+            write(own[...], got[...])
+
+        @pl.when((core_ref[0] == 1) & (step == i))
+        def _():
+            write(got[...], own[...])
+
+
+def finish_kernel(
+    rank_n, states, taps, core_ref, first_ref, second_ref, got_first_ref, got_second_ref, _,
+    in_ref, state_proj_ref, step_proj_ref, decay_ref, conv_w_ref, rows_ref, small_ref,
+):
+    depth = in_ref.shape[0]
+    half, quarter = depth // 2, first_ref.shape[0]
+    rest = half - quarter
+
+    def first_half(one, two):
+        in_ref[0:quarter, :] = one[...]
+        in_ref[quarter:half, :] = two[0:rest, :]
+        at = rest + 2 * states + rank_n
+        state_proj_ref[...] = two[rest:at, :].T
+        decay_ref[...] = two[at : at + states, :].T
+
+    def second_half(one, two):
+        in_ref[half : half + quarter, :] = one[...]
+        in_ref[half + quarter :, :] = two[0:rest, :]
+        step_proj_ref[...] = two[rest : rest + rank_n, :]
+        at = rest + rank_n
+        conv_w_ref[...] = two[at : at + taps, :]
+        rows_ref[...] = two[at : at + 8, :]
+        small_ref[...] = two[at + 8 : at + 40, :]
+
+    @pl.when(core_ref[0] == 0)
+    def _():
+        first_half(first_ref, second_ref)
+        second_half(got_first_ref, got_second_ref)
+
+    @pl.when(core_ref[0] == 1)
+    def _():
+        first_half(got_first_ref, got_second_ref)
+        second_half(first_ref, second_ref)
 
 
 def per_device(
@@ -925,11 +1037,16 @@
     own_grads = send_core(grid, held_grads, None, cap, False)
     pair, own_grads, *downs = tie(pair, own_grads, *downs)
     near_grads, far_grads = grid.swap(own_grads, "outer", 1), grid.swap(own_grads, "outer", 2)
-    start, (near_grads, far_grads) = entering(
-        grid, pair, rate, False, lambda total: tie(total, near_grads, far_grads)
-    )
+    held = {}
+
+    def third(total):
+        total, held["near"], held["far"] = tie(total, near_grads, far_grads)
+        return total
+
+    start = entering(grid, pair, rate, False, {3: third})
+    near_grads = held["near"]
+    start, far_grads = tie(start, held["far"])
     last_grads = grid.swap(far_grads, "outer", 1)
-    start, last_grads = tie(start, last_grads)
     tok = pl.BlockSpec((tokens, chunk), block)
     gate_half = pl.BlockSpec((ext, chunk), lambda c: (0, chunks + c))
     one_row = pl.BlockSpec((1, chunk), block)
@@ -965,6 +1082,7 @@
         name="scan",
     )
 
+    sent, last_grads = tie(sent, last_grads)
     grad_pieces = [own_grads, near_grads, far_grads, last_grads]
     pulled = call(
         functools.partial(early_kernel, pieces, slices),
@@ -992,18 +1110,26 @@
     last_outs = expert(last_tokens, pulled[3])
     token_pieces = [own_tokens, near_tokens, far_tokens, last_tokens]
     backs, hiddens, pulls = zip(own_outs, near_outs, far_outs, last_outs)
-    back = from_experts(grid, outer_reduce(grid, backs), cap, True)
+    back_through = grid.swap(backs[3], "outer", 1)
     outs = call(
         functools.partial(expert_grads_kernel, pieces, slices, experts, cap),
         [shape(slots, depth)] * pieces + [shape(depth, hidden)] * slices + [shape(hidden, depth)] * slices,
         (*token_pieces, *grad_pieces, *hiddens, *pulls, *downs),
         name="expert_grads",
     )
+    back, *outs = tie(outer_reduce_rest(grid, backs, back_through), *outs)
+    back = back_y(grid, back, back_core(grid, back, cap, True), cap, True)
     results, up_grads, down_grads = outs[:pieces], outs[pieces : pieces + slices], outs[pieces + slices :]
-    others_up = [grid.swap(up_grads[s], "inner", s) for s in range(1, slices)]
-    back, *others_up = tie(back, *others_up)
-    grad_up = functools.reduce(jnp.add, others_up, up_grads[0])
-    others_down = [grid.swap(down_grads[s], "inner", s) for s in range(1, slices)]
+    halves = lambda array: [array[: array.shape[0] // 2], array[array.shape[0] // 2 :]]
+    ups_sent, downs_sent = ([halves(g) for g in grads[1:]] for grads in (up_grads, down_grads))
+
+    def inner_swaps(sent, half):
+        return [grid.swap(pair[half], "inner", s) for s, pair in enumerate(sent, 1)]
+
+    up_first = inner_swaps(ups_sent, 0)
+    back, last_result, ups_sent, *up_first = tie(back, results[3], ups_sent, *up_first)
+    through = grid.swap(last_result, "outer", 1)
+    up_second = inner_swaps(ups_sent, 1)
 
     grad_resid, small, grad_scan, grad_gate, grad_skip, back_pair = call(
         functools.partial(mixer_back_kernel, rank_n, states, experts, cap),
@@ -1032,127 +1158,208 @@
         scratch=[lanes] + [pltpu.VMEM((tokens, depth), BF16)] * 2,
         name="mixer_back",
     )
-    back_pair, *results = tie(back_pair, *results)
+    back_pair, through, downs_sent, *up_second = tie(back_pair, through, downs_sent, *up_second)
+    core = grid.at["core"].astype(jnp.int32).reshape(1)
     wide = pl.BlockSpec((tokens, depth), block)
-    late, grad_gate_normed = call(
-        late_grads_kernel,
-        [shape(2 * depth, width), shape(tokens, depth)],
-        (scan, act, row(skip_gain), joined, grad_resid, block_input, row(mixer_gain), grad_gate, in_proj),
-        grid=(2,),
-        in_specs=[
-            wide, wide, pl.BlockSpec((1, depth), block), pl.BlockSpec((ext, depth), lambda c: (0, 2 + c)),
-            full(tokens, depth), full(tokens, depth), full(1, depth), wide,
-            pl.BlockSpec((depth, depth), lambda c: (0, 2 + c)),
-        ],
-        out_specs=[pl.BlockSpec((2 * depth, depth), block), full(tokens, depth)],
-        scratch=[pltpu.VMEM((tokens, depth), BF16)] * 4,
-        name="late_grads",
-    )
-    end, _ = entering(grid, back_pair, rate, True)
-    late = scatter_rows(grid, late, "core")
-    end, late = tie(end, late)
-    late = sum_first(grid, late)
-    through = grid.swap(results[3], "outer", 1)
-    grad_act, grad_pre, grad_decay, grad_proj = call(
-        functools.partial(scan_back_kernel, rank_n, states),
-        [
-            shape(tokens, width), shape(tokens, width), shape(states, width), shape(rank_n + 2 * states, tokens),
-        ],
+
+    def late(which, weight):
+        return call(
+            late_kernel,
+            [shape(depth, width)] + [shape(tokens, depth)] * len(weight),
+            (
+                which, scan, act, row(skip_gain), joined, grad_resid, block_input, row(mixer_gain), grad_gate,
+                *weight,
+            ),
+            grid=(2,),
+            in_specs=[
+                SMEM, wide, wide, pl.BlockSpec((1, depth), block), pl.BlockSpec((ext, depth), lambda c: (0, 2 + c)),
+                full(tokens, depth), full(tokens, depth), full(1, depth), wide,
+            ]
+            + [pl.BlockSpec((depth, depth), lambda c: (0, 2 + c))] * len(weight),
+            out_specs=[pl.BlockSpec((depth, depth), block)] + [full(tokens, depth)] * len(weight),
+            scratch=[pltpu.VMEM((tokens, depth), BF16)] * 2,
+            name="late",
+        )
+
+    (late_sent,) = late(core, ())
+    late_kept, grad_gate_normed = late(1 - core, (in_proj,))
+    late_got = grid.swap(late_sent, "core", 1)
+    near = grid.swap(results[1], "outer", 1)
+    far = grid.swap(results[2] + through, "outer", 2)
+    down_first = inner_swaps(downs_sent, 0)
+
+    def second(total):
+        total, held["second"], *held["down_first"] = tie(total, downs_sent, *down_first)
+        held["down_second"] = inner_swaps(held["second"], 1)
+        return total
+
+    def third(total):
+        total, held["late_got"], held["late_kept"], held["normed"], held["near"], held["far"] = tie(
+            total, late_got, late_kept, grad_gate_normed, near, far
+        )
+        held["late"] = sum_first(grid, held["late_kept"] + held["late_got"])
+        return total
+
+    def fourth(total):
+        total, *held["down_second"] = tie(total, *held["down_second"])
+        return total
+
+    end = entering(grid, back_pair, rate, True, {2: second, 3: third, 4: fourth})
+    grad_gate_normed = held["normed"]
+    late_first, late_second = held["late"]
+
+    def with_others(own, firsts, seconds):
+        for pair in zip(firsts, seconds):
+            own = own + jnp.concatenate(pair, axis=0)
+        return own
+
+    grad_up = with_others(up_grads[0], up_first, up_second)
+    grad_down = with_others(down_grads[0], held["down_first"], held["down_second"])
+    result = results[0] + held["near"] + held["far"]
+    result_got = back_core(grid, result, cap, False)
+
+    def scan_back(c, before):
+        at = lambda _: (0, c)
+        tok, one_row = pl.BlockSpec((tokens, chunk), at), pl.BlockSpec((1, chunk), at)
+        state_rows = pl.BlockSpec((states, chunk), at)
+        return call(
+            functools.partial(scan_back_kernel, rank_n, states),
+            [
+                shape(tokens, width), shape(tokens, width), shape(states, width),
+                shape(rank_n + 2 * states, tokens),
+            ],
+            (
+                masked, steps, drive, act, pre, grad_scan, row(skip_gain), history, start, end, rate, proj,
+                step_proj, *before,
+            ),
+            grid=(1,),
+            in_specs=[
+                tok, tok, tok, tok, tok, tok, one_row,
+                pl.BlockSpec((tokens, states, chunk), lambda _: (0, 0, c)), state_rows, state_rows, state_rows,
+                proj_full, pl.BlockSpec((rank_n, chunk), at),
+            ]
+            + [pl.BlockSpec(memory_space=pl.ANY)] * len(before),
+            out_specs=[tok, tok, state_rows, proj_full],
+            scratch=[lanes, lanes] + [pltpu.VMEM((tokens, chunk), F32)] * 2,
+            name="scan_back",
+            aliases={13 + i: i for i in range(len(before))},
+        )
+
+    *filled, grad_proj_a = scan_back(0, ())
+    *filled, late_first, late_second, result_got = tie(*filled, late_first, late_second, result_got)
+    late_both = sum_second(grid, late_first, late_second)
+    result = back_y(grid, result, result_got, cap, False)
+    *filled, grad_proj_b = scan_back(1, filled)
+    *filled, late_both = tie(*filled, late_both)
+    late_cut = cut_outer(grid, late_both)
+    late_through = grid.swap(late_cut[3], "outer", 1)
+    grad_act, grad_pre, grad_decay, grad_proj_c = scan_back(2, filled)
+    grad_act, late_through, result = tie(grad_act, late_through, result)
+    late_total = outer_reduce_rest(grid, late_cut, late_through)
+    unit = 2 * grid.size["inner"] * grid.size["y"]
+    half = -(-max(depth // 2 + 3 * states + rank_n, depth // 2 + rank_n + 40) // unit) * unit
+    small = jnp.concatenate([small[:9], loads[0:1]], axis=0)
+    kept, sent_half, input_grad, edge = call(
+        functools.partial(input_back_kernel, rank_n, states),
+        [shape(half, width), shape(half, width), shape(tokens, depth), shape(HALO, depth)],
         (
-            masked, steps, drive, act, pre, grad_scan, row(skip_gain), history, start, end, rate, proj, step_proj,
+            core, grad_proj_a, grad_proj_b, grad_proj_c, proj, state_proj_t, act, grad_act, grad_pre, conv, joined,
+            conv_weight, since, in_proj, block_input, halo, row(mixer_gain), grad_gate_normed, grad_resid,
+            grad_decay, grad_skip, small,
         ),
         grid=(chunks,),
         in_specs=[
-            tok, tok, tok, tok, tok, tok, one_row, history_block, state_rows, state_rows, state_rows, proj_full,
-            pl.BlockSpec((rank_n, chunk), block),
-        ],
-        out_specs=[tok, tok, state_rows, proj_full],
-        scratch=[lanes, lanes] + [pltpu.VMEM((tokens, chunk), F32)] * 2,
-        name="scan_back",
-    )
-    grad_proj, through, first, second, *others_down = tie(grad_proj, through, *late, *others_down)
-    grad_down = functools.reduce(jnp.add, others_down, down_grads[0])
-    late = sum_second(grid, first, second)
-    result = outer_reduce_rest(grid, results, through)
-    used = depth + 2 * states + 2 * rank_n + states + taps + 4
-    unit = 16 * grid.size["inner"] * grid.size["y"]
-    packed = -(-(used + 8) // unit) * unit
-    grads, input_grad, edge, gain_row = call(
-        functools.partial(input_back_kernel, rank_n, states),
-        [shape(packed, width), shape(tokens, depth), shape(HALO, depth), shape(1, depth)],
-        (
-            grad_proj, proj, state_proj_t, act, grad_act, grad_pre, conv, joined, conv_weight, since, in_proj,
-            block_input, halo, row(mixer_gain), grad_gate_normed, grad_resid, grad_decay, grad_skip,
-        ),
-        grid=(chunks,),
-        in_specs=[
-            proj_full, proj_full, pl.BlockSpec((rank_n + 2 * states, chunk), block), tok, tok, tok, tok,
-            pl.BlockSpec((ext, chunk), block), pl.BlockSpec((taps, chunk), block), full(tokens, 1),
-            pl.BlockSpec((depth, chunk), block), full(tokens, depth), full(HALO, depth), full(1, depth),
-            full(tokens, depth), full(tokens, depth), state_rows, one_row,
+            SMEM, proj_full, proj_full, proj_full, proj_full, pl.BlockSpec((rank_n + 2 * states, chunk), block),
+            tok, tok, tok, tok, pl.BlockSpec((ext, chunk), block), pl.BlockSpec((taps, chunk), block),
+            full(tokens, 1), pl.BlockSpec((depth, chunk), block), full(tokens, depth), full(HALO, depth),
+            full(1, depth), full(tokens, depth), full(tokens, depth), state_rows, one_row, full(10, depth),
         ],
         out_specs=[
-            pl.BlockSpec((packed, chunk), block), full(tokens, depth), full(HALO, depth), full(1, depth),
+            pl.BlockSpec((half, chunk), block), pl.BlockSpec((half, chunk), block), full(tokens, depth),
+            full(HALO, depth),
         ],
         scratch=[pltpu.VMEM((ext, depth), BF16)] * 2
         + [pltpu.VMEM((ext, chunk), F32), pltpu.VMEM((ext, depth), F32)],
         name="input_back",
     )
+    kept, sent_half, late_total = tie(kept, sent_half, late_total)
+    late_near, late_far = grid.swap(late_total, "outer", 1), grid.swap(late_total, "outer", 2)
     from_next = grid.along(edge, -1)
     input_grad = jnp.concatenate([input_grad[: tokens - HALO], input_grad[tokens - HALO :] + from_next], axis=0)
-    small = jnp.concatenate([small[:9], gain_row, loads[0:1], small[11:]], axis=0).reshape(8, width)
-    grads = lax.dynamic_update_slice(grads, small, (used, 0))
-    grads, late, result = tie(grads, late, result)
-    result = from_experts(grid, result, cap, False)
-    late = sum_outer(grid, late)
-    grads = sum_second(grid, *sum_first(grid, scatter_rows(grid, grads, "core")))
-    late, grads, result = tie(late, grads, result)
-    late = spread_outer(grid, late)
-    late, grads = tie(late, grads)
-    first, second = spread_second(grid, late)
-    grads = sum_outer(grid, grads)
-    first, second, grads = tie(first, second, grads)
-    late = spread_first(grid, first, second)
-    grads = spread_outer(grid, grads)
-    late, grads = tie(late, grads)
-    late = gather_rows(grid, late, "core")
-    first, second = spread_second(grid, grads)
-    late, first, second = tie(late, first, second)
-    grads = gather_rows(grid, spread_first(grid, first, second), "core")
-
     combined = jnp.dot(table.T, result.astype(F32), precision=lax.Precision.HIGHEST, preferred_element_type=F32)
     block_output = resid + gate * combined
-
-    at = depth
-    grad_state_proj = grads[at : at + 2 * states + rank_n].T
-    at += 2 * states + rank_n
-    grad_step_proj = grads[at : at + rank_n]
-    at += rank_n
-    grad_decay_log = grads[at : at + states].T
-    at += states
-    grad_conv_weight = grads[at : at + taps]
-    at += taps
-    grad_conv_bias, grad_step_bias, grad_skip_gain = grads[at], grads[at + 1], grads[at + 2]
-    small = grads[used : used + 8].reshape(16, depth)
+    grads_first, grads_second = sum_first(grid, kept + grid.swap(sent_half, "core", 1))
+    late_near, late_far, grads_first, grads_second, input_grad, block_output, grad_up, grad_down = tie(
+        late_near, late_far, grads_first, grads_second, input_grad, block_output, grad_up, grad_down
+    )
+    late_last = grid.swap(late_far, "outer", 1)
+    grads = sum_second(grid, grads_first, grads_second)
+    late_last, grads = tie(late_last, grads)
+    late_first, late_second = spread_second(grid, join_outer(grid, late_total, late_near, late_far, late_last))
+    grads = sum_outer(grid, grads)
+    late_first, late_second, grads = tie(late_first, late_second, grads)
+    late_first, late_second = gather_rows(grid, late_first, "inner"), gather_rows(grid, late_second, "y")
+    grads = spread_outer(grid, grads)
+    late_first, late_second, grads = tie(late_first, late_second, grads)
+    late_other = [grid.swap(late_first, "core", 1), grid.swap(late_second, "core", 1)]
+    grads_first, grads_second = spread_second(grid, grads)
+    grads_first, grads_second, *late_other = tie(grads_first, grads_second, *late_other)
+    grads_first, grads_second = gather_rows(grid, grads_first, "inner"), gather_rows(grid, grads_second, "y")
+    quarter = pl.BlockSpec((half // 2, chunk), block)
+    late_rows = full(depth // 2, width)
+    grad_in_proj, grad_out_proj = call(
+        finish_late_kernel,
+        [shape(depth, 2 * width), shape(2, depth, depth)],
+        (core, late_first, late_second, *late_other),
+        grid=(2,),
+        in_specs=[SMEM] + [late_rows] * 4,
+        out_specs=[
+            pl.BlockSpec((depth // 2, width), lambda r: (r, 1)),
+            pl.BlockSpec((2, depth // 2, depth), lambda r: (0, r, 0)),
+        ],
+        name="finish_late",
+    )
+    grads_first, grads_second, grad_in_proj = tie(grads_first, grads_second, grad_in_proj)
+    grads_other = [grid.swap(grads_first, "core", 1), grid.swap(grads_second, "core", 1)]
+    tall = lambda columns: pl.BlockSpec((chunk, columns), lambda c: (c, 0))
+    (
+        grad_in_proj, grad_state_proj, grad_step_proj, grad_decay_log, grad_conv_weight, rows, small,
+    ) = call(
+        functools.partial(finish_kernel, rank_n, states, taps),
+        [
+            shape(depth, 2 * width), shape(width, rank_n + 2 * states), shape(rank_n, width),
+            shape(width, states), shape(taps, width), shape(8, width), shape(32, chunk),
+        ],
+        (core, grads_first, grads_second, *grads_other, grad_in_proj),
+        grid=(chunks,),
+        in_specs=[SMEM] + [quarter] * 4 + [pl.BlockSpec(memory_space=pl.ANY)],
+        out_specs=[
+            pl.BlockSpec((depth, chunk), block), tall(rank_n + 2 * states), pl.BlockSpec((rank_n, chunk), block),
+            tall(states), pl.BlockSpec((taps, chunk), block), pl.BlockSpec((8, chunk), block), full(32, chunk),
+        ],
+        name="finish",
+        aliases={5: 0},
+    )
+    small = jnp.concatenate([small[:16], small[16:, : depth - chunk]], axis=1)
     return (
         block_output,
         input_grad,
-        small[9],
-        jnp.concatenate([grads[:depth], late[:depth]], axis=1),
+        small[10],
+        grad_in_proj,
         grad_conv_weight,
-        grad_conv_bias,
+        rows[taps],
         grad_state_proj,
         grad_step_proj,
-        grad_step_bias,
+        rows[taps + 1],
         grad_decay_log,
-        grad_skip_gain,
-        jnp.concatenate([late[depth:, :depth], late[depth:, depth:]], axis=0),
+        rows[taps + 2],
+        grad_out_proj.reshape(width, depth),
         small[8],
         small[:experts].T,
         grad_up[None],
         grad_down[None],
-        small[10, :experts].astype(jnp.int32),
-        small[10, 128 : 128 + experts].astype(jnp.int32),
+        small[9, :experts].astype(jnp.int32),
+        small[9, 128 : 128 + experts].astype(jnp.int32),
     )
 
 

time: 605 us -> 500 us (0.83)
  waiting for transfers between devices: 259 us -> 211 us
  other arithmetic: 70.7 us -> 25.3 us
  local copies, waits for them, and re-layouts: 52.6 us -> 20.2 us
  Pallas kernels: 129 us -> 152 us
    ppermute x66 -> x70, waiting for transfers between devices: 259 us -> 211 us  [swap_bits(): return lax.ppermute(block, AXES, [(i, i ^ bits) for i in range(self.total)])]
    pallas_call x24 -> x29, Pallas kernels: 129 us -> 152 us  [call(): pl.pallas_call(kernel, out_shape=outs, grid=grid or (), in_specs=in_specs...]
    concatenate x12 -> x9, other arithmetic: 19 us -> 1.1 us  [the longest x2 0.86 us: back_y(): return jnp.concatenate(rows, axis=0)]
    select_n x10 -> x8, other arithmetic: 14.5 us -> 2.08 us  [in_order(): jnp.where(turned, parts[i ^ bit], parts[i])]
    add x0 -> x6, other arithmetic: none -> 12 us  [the longest x1 4.76 us: third(): held['late'] = sum_first(grid, held['late_kept'] + held['late_got'])]
    dynamic_slice x10 -> x8, local copies, waits for them, and re-layouts: 12.2 us -> 1.43 us  [scatter_rows(): lax.dynamic_slice_in_dim(block, (place ^ s) * rows, rows, 0)]
    add x10 -> x8, other arithmetic: 13.3 us -> 3.22 us  [scatter_rows(): total = total + part]
    unnamed x147 -> x127, local copies, waits for them, and re-layouts: 21.5 us -> 11.8 us
  transfers between devices with their start and end apart: 68 -> 72, of which waited for: 48 -> 44; matrix products, arithmetic and copies ran while one was open for 8% -> 6% of each run, Pallas kernels for 17% -> 26%
where the time goes in v3:
time: 500 us; the launch traced here: 493 us
  waiting for transfers between devices  211 us (42%)
  Pallas kernels  152 us (30%)
  starting transfers between devices  80.9 us (16%)
  other arithmetic  25.3 us (5%)
  local copies, waits for them, and re-layouts  20.2 us (4%)
    ppermute x70, waiting for transfers between devices, swap_bits(): return lax.ppermute(block, AXES, [(i, i ^ bits) for i in range(self.total)])  211 us
    pallas_call x29, Pallas kernels, call(): pl.pallas_call(kernel, out_shape=outs, grid=grid or (), in_specs=in_specs...  152 us
    ppermute x70, starting transfers between devices, swap_bits(): return lax.ppermute(block, AXES, [(i, i ^ bits) for i in range(self.total)])  77 us
    unnamed x127, local copies, waits for them, and re-layouts  11.8 us
  transfers between devices with their start and end apart: 72, of which 44 were waited for; matrix products, arithmetic and copies ran while one was open for 6% of the time, Pallas kernels for 26%

profile of v3, /device:TPU:0, one launch (start us, length us, event | category | flops | bytes accessed | tf_op | source)
XLA Modules:
  0.0 492.9 jit_solution(18128337560681920565)
XLA Ops:
  12.5 7.8 %join.1.inner_ref.gate_z_ref = f32[144,3072]{1,0:T(8,128)} custom-call(f32[128,768]{1,0:T(8,128)S(1)} %copy-done.2, f32[16,768]{1,0:T(8,128)S(1)} %collective-permute-done.halo_ref, f32[1,768]{1,0:T(1,128)S(1)} %reshape.120.gain_ref, f32[768,3072]{1,0:T(8,128)} %weight_ref.3), custom_call_target="tpu_custom_call" | custom-call | flops 8800000000 | bytes 8000000 | tf_op jit(solution)/shard_map/join/pallas_call | solution.py:290
  21.6 8.2 %features.1 = (f32[128,1536]{1,0:T(8,128)S(1)}, f32[128,1536]{1,0:T(8,128)}, f32[128,1536]{1,0:T(8,128)}, f32[128,1536]{1,0:T(8,128)}, f32[128,1536]{1,0:T(8,128...) custom-call(f32[144,3072]{1,0:T(8,128)} %join.1.inner_ref.gate_z_ref, ...), custom_call_target="tpu_custom_call" | custom-call | flops 8800000000 | bytes 8000000 | tf_op jit(solution)/shard_map/features/pallas_call | solution.py:290
  40.4 3.8 collective-permute-done.5.got_ref
  45.1 4.4 collective-permute-done.6.got_ref
  49.6 9.1 %collective-permute-done.8.refs_2_.refs_6_ = f32[160,768]{1,0:T(8,128)} collective-permute-done((f32[160,768]{1,0:T(8,128)S(1)}, f32[160,768]{1,0:T(8,128)}, u32[]{:S(2)}, u32[]{:S(2)}) %collective-permute-start.8) | collective-permute-done | bytes 491552 | tf_op jit(solution)/shard_map/ppermute | solution.py:47
  60.3 3.7 collective-permute-done.9.got_ref
  68.4 5.1 %collective-permute-done.10.got_ref = f32[17,1536]{1,0:T(8,128)S(1)} collective-permute-done((f32[17,1536]{1,0:T(8,128)S(1)}, f32[17,1536]{1,0:T(8,128)S(1)}, u32[]{:S(2)}, u32[]{:S(2)}) %collective-permute-start.10) | collective-permute-done | bytes 104480 | tf_op jit(solution)/shard_map/ppermute | solution.py:47
  74.3 14.5 %scan.1 = (f32[128,1536]{1,0:T(8,128)}, f32[128,16,1536]{2,1,0:T(8,128)}, f32[128,768]{1,0:T(8,128)S(1)}, f32[168,768]{1,0:T(8,128)S(1)}, f32[128,8]{1,0:T(8,128)S(1)}, /*index=5*/f32[128,1]{1,0:T(8,128)S(1)}) custom-call(s32[1]{0:T(128)} %bitcast.1.me_ref, f32[128,1536]{1,0:T(8,128)} %get-tuple-element.218.masked_ref, ...), custom_call_target="tpu_custom_call" | custom-call | flops 15399999488 | bytes 14000000 | tf_op jit(solution)/shard_map/scan/pallas_call | solution.py:290
  91.5 6.4 %collective-permute-done.12 = f32[88,768]{1,0:T(8,128)S(1)} collective-permute-done((f32[88,768]{1,0:T(8,128)S(1)}, f32[88,768]{1,0:T(8,128)S(1)}, u32[]{:S(2)}, u32[]{:S(2)}) %collective-permute-start.12) | collective-permute-done | bytes 270368 | tf_op jit(solution)/shard_map/ppermute | solution.py:47
  98.0 6.7 %early.1 = (f32[2,160,384]{2,1,0:T(8,128)S(1)}, f32[2,160,384]{2,1,0:T(8,128)S(1)}, f32[2,160,384]{2,1,0:T(8,128)S(1)}, f32[2,160,384]{2,1,0:T(8,128)S(1)}) custom-call(f32[160,768]{1,0:T(8,128)} %copy-done.44, f32[160,768]{1,0:T(8,128)} %copy-done.60, f32[160,768]{1,0:T(8,128)} %collective-permute-done.8.refs_2_.refs_6_, f32[160,768]{1,0:T(8,128)} %copy-done.61, ...), custom_call_target="tpu_custom_call" | custom-call | flops 7699999744 | bytes 7000000 | tf_op jit(solution)/shard_map/early/pallas_call | solution.py:290
  104.9 3.5 collective-permute-start.15
  108.7 4.4 expert.4
  113.2 18.5 %collective-permute-done.15.refs_0_.refs_2_ = f32[168,768]{1,0:T(8,128)S(1)} collective-permute-done((f32[168,768]{1,0:T(8,128)S(1)}, f32[168,768]{1,0:T(8,128)S(1)}, u32[]{:S(2)}, u32[]{:S(2)}) %collective-permute-start.15) | collective-permute-done | bytes 516128 | tf_op jit(solution)/shard_map/ppermute | solution.py:47
  133.6 4.4 expert.6
  139.6 4.4 expert.5
  147.0 4.6 expert.7
  152.4 11.4 %collective-permute-done.18 = f32[168,768]{1,0:T(8,128)S(1)} collective-permute-done((f32[168,768]{1,0:T(8,128)S(1)}, f32[168,768]{1,0:T(8,128)S(1)}, u32[]{:S(2)}, u32[]{:S(2)}) %collective-permute-start.18) | collective-permute-done | bytes 516128 | tf_op jit(solution)/shard_map/ppermute | solution.py:47
  166.4 17.6 %expert_grads.1 = (f32[160,768]{1,0:T(8,128)S(1)}, f32[160,768]{1,0:T(8,128)S(1)}, f32[160,768]{1,0:T(8,128)S(1)}, f32[160,768]{1,0:T(8,128)S(1)}, f32[768,384]{...) custom-call(f32[168,768]{1,0:T(8,128)} %copy-done.43, f32[168,768]{1,0:T(8,128)} %copy-done.58, ...), custom_call_target="tpu_custom_call" | custom-call | flops 18699999232 | bytes 17000000 | tf_op jit(solution)/shard_map/expert_grads/pallas_call | solution.py:290
  190.8 6.8 %collective-permute-done.22 = f32[88,768]{1,0:T(8,128)S(1)} collective-permute-done((f32[88,768]{1,0:T(8,128)S(1)}, f32[88,768]{1,0:T(8,128)S(1)}, u32[]{:S(2)}, u32[]{:S(2)}) %collective-permute-start.22) | collective-permute-done | bytes 270368 | tf_op jit(solution)/shard_map/ppermute | solution.py:47
  198.4 4.9 collective-permute-done.23
  203.3 9.7 %mixer_back.1 = (f32[128,768]{1,0:T(8,128)S(1)}, f32[16,768]{1,0:T(8,128)S(1)}, f32[128,1536]{1,0:T(8,128)}, f32[128,1536]{1,0:T(8,128)}, f32[1,1536]{1,0:T(1,128)S(1)}, /*index=5*/f32[17,1536]{1,0:T(8,128)S(1)}) custom-call(s32[1]{0:T(128)} %bitcast.1.me_ref, f32[168,768]{1,0:T(8,128)} %pad_maximum_fusion.13.back_ref, ...), custom_call_target="tpu_custom_call" | custom-call | flops 10560000000 | bytes 9600000 | tf_op jit(solution)/shard_map/mixer_back/pallas_call | solution.py:290
  213.0 5.3 %late.2 = f32[768,1536]{1,0:T(8,128)} custom-call(s32[1]{0:T(128)} %bitcast.later_ref.which_ref.core_ref, f32[128,1536]{1,0:T(8,128)S(1)} %copy-done.11, f32[128,1536]{1,0:T(8,128)} %get-tuple-element.221.act_ref, f32[1,1536]{1,0:T(1,128)S(1)} %reshape.127.skip_ref, f32[144,3072]{1,0:T(8,128)} %join.1.inner_ref.gate_z_ref, ...), custom_call_target="tpu_custom_call" | custom-call | flops 6600000000 | bytes 6000000 | tf_op jit(solution)/shard_map/late/pallas_call | solution.py:290
  221.0 11.5 %collective-permute-done.24 = f32[160,768]{1,0:T(8,128)} collective-permute-done((f32[160,768]{1,0:T(8,128)S(1)}, f32[160,768]{1,0:T(8,128)}, u32[]{:S(2)}, u32[]{:S(2)}) %collective-permute-start.24) | collective-permute-done | bytes 491552 | tf_op jit(solution)/shard_map/ppermute | solution.py:47
  240.6 8.1 %late.3 = (f32[768,1536]{1,0:T(8,128)}, f32[128,768]{1,0:T(8,128)S(1)}) custom-call(s32[1]{0:T(128)S(6)} %sub.75.which_ref, f32[128,1536]{1,0:T(8,128)S(1)} %copy-done.12, f32[128,1536]{1,0:T(8,128)} %get-tuple-element.221.act_ref, f32[1,1536]{1,0:T(1,128)S(1)} %reshape.127.skip_ref, f32[144,3072]{1,0:T(8,128)} %join.1.inner_ref.gate_z_ref, ...), custom_call_target="tpu_custom_call" | custom-call | flops 6600000000 | bytes 6000000 | tf_op jit(solution)/shard_map/late/pallas_call | solution.py:290
  248.8 4.5 collective-permute-done.28
  255.4 4.7 collective-permute-done.29.got_ref
  261.0 4.8 add.247
  277.4 3.4 collective-permute-done.35.got_ref
  280.9 10.3 %scan_back.3 = (f32[128,1536]{1,0:T(8,128)S(1)}, f32[128,1536]{1,0:T(8,128)}, f32[16,1536]{1,0:T(8,128)S(1)}, f32[80,128]{1,0:T(8,128)S(1)}) custom-call(f32[128,1536]{1,0:T(8,128)} %get-tuple-element.218.masked_ref, f32[128,1536]{1,0:T(8,128)} %get-tuple-element.219.steps_ref, f32[128,1536]{1,0:T(8,128)} %get-tuple-element.220.drive_ref, ...), custom_call_target="tpu_custom_call" | custom-call | flops 11000000512 | bytes 10000000 | tf_op jit(solution)/shard_map/scan_back/pallas_call | solution.py:290
  291.1 5.2 %collective-permute-done.36 = f32[192,1536]{1,0:T(8,128)} collective-permute-done((f32[192,1536]{1,0:T(8,128)S(1)}, f32[192,1536]{1,0:T(8,128)}, u32[]{:S(2)}, u32[]{:S(2)}) %collective-permute-start.36) | collective-permute-done | bytes 1179680 | tf_op jit(solution)/shard_map/ppermute | solution.py:47
  297.8 4.2 collective-permute-done.37
  306.4 9.8 %scan_back.4 = (f32[128,1536]{1,0:T(8,128)S(1)}, f32[128,1536]{1,0:T(8,128)}, f32[16,1536]{1,0:T(8,128)S(1)}, f32[80,128]{1,0:T(8,128)S(1)}) custom-call(f32[128,1536]{1,0:T(8,128)} %get-tuple-element.218.masked_ref, f32[128,1536]{1,0:T(8,128)} %get-tuple-element.219.steps_ref, ...), custom_call_target="tpu_custom_call", output_to_operand_aliasing={{0}: (13, {}), {1}: (14, {}), {2}: (15, {})} | custom-call | flops 11000000512 | bytes 10000000 | tf_op jit(solution)/shard_map/scan_back/pallas_call | solution.py:290
  317.7 3.6 collective-permute-done.39
  322.2 9.7 %scan_back.5 = (f32[128,1536]{1,0:T(8,128)S(1)}, f32[128,1536]{1,0:T(8,128)}, f32[16,1536]{1,0:T(8,128)S(1)}, f32[80,128]{1,0:T(8,128)S(1)}) custom-call(f32[128,1536]{1,0:T(8,128)} %get-tuple-element.218.masked_ref, f32[128,1536]{1,0:T(8,128)} %get-tuple-element.219.steps_ref, ...), custom_call_target="tpu_custom_call", output_to_operand_aliasing={{0}: (13, {}), {1}: (14, {}), {2}: (15, {})} | custom-call | flops 11000000512 | bytes 10000000 | tf_op jit(solution)/shard_map/scan_back/pallas_call | solution.py:290
  335.1 11.1 %input_back.1 = (f32[480,1536]{1,0:T(8,128)}, f32[480,1536]{1,0:T(8,128)}, f32[128,768]{1,0:T(8,128)S(1)}, f32[16,768]{1,0:T(8,128)S(1)}) custom-call(s32[1]{0:T(128)} %bitcast.later_ref.which_ref.core_ref, f32[80,128]{1,0:T(8,128)S(1)} %get-tuple-element.328.proj_a_ref, f32[80,128]{1,0:T(8,128)S(1)} %get-tuple-element.340.proj_b_ref, ...), custom_call_target="tpu_custom_call" | custom-call | flops 12099999744 | bytes 11000000 | tf_op jit(solution)/shard_map/input_back/pallas_call | solution.py:290
  362.5 12.6 %collective-permute-done.48 = f32[120,1536]{1,0:T(8,128)S(1)} collective-permute-done((f32[120,1536]{1,0:T(8,128)S(1)}, f32[120,1536]{1,0:T(8,128)S(1)}, u32[]{:S(2)}, u32[]{:S(2)}) %collective-permute-start.48) | collective-permute-done | bytes 737312 | tf_op jit(solution)/shard_map/ppermute | solution.py:47
  381.2 6.2 %collective-permute-done.53 = f32[60,1536]{1,0:T(8,128)S(1)} collective-permute-done((f32[60,1536]{1,0:T(8,128)S(1)}, f32[60,1536]{1,0:T(8,128)S(1)}, u32[]{:S(2)}, u32[]{:S(2)}) %collective-permute-start.53) | collective-permute-done | bytes 368672 | tf_op jit(solution)/shard_map/ppermute | solution.py:47
  398.6 4.2 collective-permute-done.56
  402.8 3.2 collective-permute-done.58
  406.0 6.4 %collective-permute-done.57 = f32[120,384]{1,0:T(8,128)} collective-permute-done((f32[120,384]{1,0:T(8,128)S(1)}, f32[120,384]{1,0:T(8,128)}, u32[]{:S(2)}, u32[]{:S(2)}) %collective-permute-start.57) | collective-permute-done | bytes 184352 | tf_op jit(solution)/shard_map/ppermute | solution.py:47
  419.6 3.7 collective-permute-done.63
  423.3 6.7 %collective-permute-done.62 = f32[120,384]{1,0:T(8,128)S(1)} collective-permute-done((f32[120,384]{1,0:T(8,128)S(1)}, f32[120,384]{1,0:T(8,128)S(1)}, u32[]{:S(2)}, u32[]{:S(2)}) %collective-permute-start.62) | collective-permute-done | bytes 184352 | tf_op jit(solution)/shard_map/ppermute | solution.py:47
  430.2 9.5 %collective-permute-done.59 = f32[192,1536]{1,0:T(8,128)S(1)} collective-permute-done((f32[192,1536]{1,0:T(8,128)S(1)}, f32[192,1536]{1,0:T(8,128)S(1)}, u32[]{:S(2)}, u32[]{:S(2)}) %collective-permute-start.59) | collective-permute-done | bytes 1179680 | tf_op jit(solution)/shard_map/ppermute | solution.py:47
  440.0 4.2 collective-permute-done.60
  446.4 10.1 %collective-permute-done.65 = f32[60,1536]{1,0:T(8,128)S(1)} collective-permute-done((f32[60,1536]{1,0:T(8,128)S(1)}, f32[60,1536]{1,0:T(8,128)S(1)}, u32[]{:S(2)}, u32[]{:S(2)}) %collective-permute-start.65) | collective-permute-done | bytes 368672 | tf_op jit(solution)/shard_map/ppermute | solution.py:47
  459.4 7.8 %finish_late.1 = (f32[768,3072]{1,0:T(8,128)}, f32[2,768,768]{2,1,0:T(8,128)}) custom-call(s32[1]{0:T(128)} %bitcast.later_ref.which_ref.core_ref, f32[384,1536]{1,0:T(8,128)} %copy-done.29, f32[384,1536]{1,0:T(8,128)} %copy-done.30, f32[384,1536]{1,0:T(8,128)} %copy-done.53, f32[384,1536]{1,0:T(8,128)} %copy-done.54), custom_call_target="tpu_custom_call" | custom-call | flops 8800000000 | bytes 8000000 | tf_op jit(solution)/shard_map/finish_late/pallas_call | solution.py:290
  467.2 7.5 %collective-permute-done.68 = f32[120,1536]{1,0:T(8,128)S(1)} collective-permute-done((f32[120,1536]{1,0:T(8,128)S(1)}, f32[120,1536]{1,0:T(8,128)S(1)}, u32[]{:S(2)}, u32[]{:S(2)}) %collective-permute-start.68) | collective-permute-done | bytes 737312 | tf_op jit(solution)/shard_map/ppermute | solution.py:47
  482.5 5.9 %finish.1 = (f32[768,3072]{1,0:T(8,128)}, f32[1536,80]{1,0:T(8,128)S(1)}, f32[48,1536]{1,0:T(8,128)}, f32[1536,16]{1,0:T(8,128)S(1)}, f32[4,1536]{1,0:T(4,128)},...) custom-call(s32[1]{0:T(128)} %bitcast.later_ref.which_ref.core_ref, ...), custom_call_target="tpu_custom_call", output_to_operand_aliasing={{0}: (5, {})} | custom-call | flops 6600000000 | bytes 6000000 | tf_op jit(solution)/shard_map/finish/pallas_call | solution.py:290
  (370 shorter events, 146.3 us)
Async XLA Ops:
  3.8 28.6 %collective-permute-start.3 = (f32[384,768]{1,0:T(8,128)}, f32[384,768]{1,0:T(8,128)}, u32[]{:S(2)}, u32[]{:S(2)}) collective-permute-start(f32[384,768]{1,0:T(8,128)} %bitcast.37), channel_id=1, source_target_pairs={{0,4},{1,5},{2,6},{3,7},{4,0},{5,1},{6,2},{7,3},{8,12},{9,13},{10,... | collective-permute-start | bytes 3538952 | tf_op jit(solution)/shard_map/ppermute | solution.py:47
  33.3 25.3 %collective-permute-start.8 = (f32[160,768]{1,0:T(8,128)S(1)}, f32[160,768]{1,0:T(8,128)}, u32[]{:S(2)}, u32[]{:S(2)}) collective-permute-start(f32[160,768]{1,0:T(8,128)S(1)} %pad_maximum_fusion.14.refs_0_.refs_4_), channel_id=1, source_target_pairs={{0,16},{1,17},{2,18},{3,19},{4,20},{5,21},{6,22},{7,23},{8,24},{9,... | collective-permute-start | bytes 1474568 | tf_op jit(solution)/shard_map/ppermute | solution.py:47
  36.5 22.3 %collective-permute-start.7 = (f32[160,768]{1,0:T(8,128)S(1)}, f32[160,768]{1,0:T(8,128)S(1)}, u32[]{:S(2)}, u32[]{:S(2)}) collective-permute-start(f32[160,768]{1,0:T(8,128)S(1)} %pad_maximum_fusion.14.refs_0_.refs_4_), channel_id=1, source_target_pairs={{0,8},{1,9},{2,10},{3,11},{4,12},{5,13},{6,14},{7,15},{8,0},{9,1},... | collective-permute-start | bytes 1474568 | tf_op jit(solution)/shard_map/ppermute | solution.py:47
  66.8 41.8 %collective-permute-start.16 = (f32[768,384]{1,0:T(8,128)}, f32[768,384]{1,0:T(8,128)}, u32[]{:S(2)}, u32[]{:S(2)}) collective-permute-start(f32[768,384]{1,0:T(8,128)} %bitcast.11.refs_1_), channel_id=1, source_target_pairs={{0,4},{1,5},{2,6},{3,7},{4,0},{5,1},{6,2},{7,3},{8,12},{9,13},{10,... | collective-permute-start | bytes 3538952 | tf_op jit(solution)/shard_map/ppermute | solution.py:47
  73.6 15.3 %collective-permute-start.11 = (f32[160,768]{1,0:T(8,128)}, f32[160,768]{1,0:T(8,128)S(1)}, u32[]{:S(2)}, u32[]{:S(2)}) collective-permute-start(f32[160,768]{1,0:T(8,128)} %collective-permute-done.8.refs_2_.refs_6_), channel_id=1, source_target_pairs={{0,8},{1,9},{2,10},{3,11},{4,12},{5,13},{6,14},{7,15},{8,0},{9,1},... | collective-permute-start | bytes 1474568 | tf_op jit(solution)/shard_map/ppermute | solution.py:47
  104.9 26.8 %collective-permute-start.15 = (f32[168,768]{1,0:T(8,128)S(1)}, f32[168,768]{1,0:T(8,128)S(1)}, u32[]{:S(2)}, u32[]{:S(2)}) collective-permute-start(f32[168,768]{1,0:T(8,128)S(1)} %pad_maximum_fusion.12.refs_0_), channel_id=1, source_target_pairs={{0,16},{1,17},{2,18},{3,19},{4,20},{5,21},{6,22},{7,23},{8,24},{9,... | collective-permute-start | bytes 1548296 | tf_op jit(solution)/shard_map/ppermute | solution.py:47
  108.3 24.8 %collective-permute-start.14 = (f32[168,768]{1,0:T(8,128)S(1)}, f32[168,768]{1,0:T(8,128)S(1)}, u32[]{:S(2)}, u32[]{:S(2)}) collective-permute-start(f32[168,768]{1,0:T(8,128)S(1)} %pad_maximum_fusion.12.refs_0_), channel_id=1, source_target_pairs={{0,8},{1,9},{2,10},{3,11},{4,12},{5,13},{6,14},{7,15},{8,0},{9,1},... | collective-permute-start | bytes 1548296 | tf_op jit(solution)/shard_map/ppermute | solution.py:47
  133.2 13.0 %collective-permute-start.17 = (f32[168,768]{1,0:T(8,128)S(1)}, f32[168,768]{1,0:T(8,128)S(1)}, u32[]{:S(2)}, u32[]{:S(2)}) collective-permute-start(f32[168,768]{1,0:T(8,128)S(1)} %collective-permute-done.15.refs_0_.refs_2_), channel_id=1, source_target_pairs={{0,8},{1,9},{2,10},{3,11},{4,12},{5,13},{6,14},{7,15},{8,0},{9,1},... | collective-permute-start | bytes 1548296 | tf_op jit(solution)/shard_map/ppermute | solution.py:47
  151.6 12.2 %collective-permute-start.18 = (f32[168,768]{1,0:T(8,128)S(1)}, f32[168,768]{1,0:T(8,128)S(1)}, u32[]{:S(2)}, u32[]{:S(2)}) collective-permute-start(f32[168,768]{1,0:T(8,128)S(1)} %get-tuple-element.271), channel_id=1, source_target_pairs={{0,8},{1,9},{2,10},{3,11},{4,12},{5,13},{6,14},{7,15},{8,0},{9,1},... | collective-permute-start | bytes 1548296 | tf_op jit(solution)/shard_map/ppermute | solution.py:47
  163.9 23.2 %collective-permute-start.20 = (f32[168,768]{1,0:T(8,128)S(1)}, f32[168,768]{1,0:T(8,128)S(1)}, u32[]{:S(2)}, u32[]{:S(2)}) collective-permute-start(f32[168,768]{1,0:T(8,128)S(1)} %add.244), channel_id=1, source_target_pairs={{0,16},{1,17},{2,18},{3,19},{4,20},{5,21},{6,22},{7,23},{8,24},{9,... | collective-permute-start | bytes 1548296 | tf_op jit(solution)/shard_map/ppermute | solution.py:47
  165.0 22.1 %collective-permute-start.19 = (f32[168,768]{1,0:T(8,128)S(1)}, f32[168,768]{1,0:T(8,128)S(1)}, u32[]{:S(2)}, u32[]{:S(2)}) collective-permute-start(f32[168,768]{1,0:T(8,128)S(1)} %get-tuple-element.273), channel_id=1, source_target_pairs={{0,8},{1,9},{2,10},{3,11},{4,12},{5,13},{6,14},{7,15},{8,0},{9,1},... | collective-permute-start | bytes 1548296 | tf_op jit(solution)/shard_map/ppermute | solution.py:47
  187.4 15.9 %collective-permute-start.23 = (f32[384,384]{1,0:T(8,128)S(1)}, f32[384,384]{1,0:T(8,128)}, u32[]{:S(2)}, u32[]{:S(2)}) collective-permute-start(f32[384,384]{1,0:T(8,128)S(1)} %get-tuple-element.498), channel_id=1, source_target_pairs={{0,4},{1,5},{2,6},{3,7},{4,0},{5,1},{6,2},{7,3},{8,12},{9,13},{10,... | collective-permute-start | bytes 1769480 | tf_op jit(solution)/shard_map/ppermute | solution.py:47
  218.3 42.7 %collective-permute-start.30 = (f32[768,1536]{1,0:T(8,128)}, f32[768,1536]{1,0:T(8,128)}, u32[]{:S(2)}, u32[]{:S(2)}) collective-permute-start(f32[768,1536]{1,0:T(8,128)} %late.2), channel_id=1, source_target_pairs={{0,1},{1,0},{2,3},{3,2},{4,5},{5,4},{6,7},{7,6},{8,9},{9,8},{10,11... | collective-permute-start | bytes 14155784 | tf_op jit(solution)/shard_map/ppermute | solution.py:47
  218.3 15.8 %collective-permute-start.25 = (f32[384,384]{1,0:T(8,128)S(1)}, f32[384,384]{1,0:T(8,128)}, u32[]{:S(2)}, u32[]{:S(2)}) collective-permute-start(f32[384,384]{1,0:T(8,128)S(1)} %get-tuple-element.305), channel_id=1, source_target_pairs={{0,4},{1,5},{2,6},{3,7},{4,0},{5,1},{6,2},{7,3},{8,12},{9,13},{10,... | collective-permute-start | bytes 1769480 | tf_op jit(solution)/shard_map/ppermute | solution.py:47
  219.1 13.4 %collective-permute-start.24 = (f32[160,768]{1,0:T(8,128)S(1)}, f32[160,768]{1,0:T(8,128)}, u32[]{:S(2)}, u32[]{:S(2)}) collective-permute-start(f32[160,768]{1,0:T(8,128)S(1)} %get-tuple-element.303), channel_id=1, source_target_pairs={{0,8},{1,9},{2,10},{3,11},{4,12},{5,13},{6,14},{7,15},{8,0},{9,1},... | collective-permute-start | bytes 1474568 | tf_op jit(solution)/shard_map/ppermute | solution.py:47
  234.2 26.0 %collective-permute-start.31 = (f32[160,768]{1,0:T(8,128)S(1)}, f32[160,768]{1,0:T(8,128)S(1)}, u32[]{:S(2)}, u32[]{:S(2)}) collective-permute-start(f32[160,768]{1,0:T(8,128)S(1)} %get-tuple-element.319), channel_id=1, source_target_pairs={{0,8},{1,9},{2,10},{3,11},{4,12},{5,13},{6,14},{7,15},{8,0},{9,1},... | collective-permute-start | bytes 1474568 | tf_op jit(solution)/shard_map/ppermute | solution.py:47
  236.2 24.8 %collective-permute-start.32 = (f32[160,768]{1,0:T(8,128)S(1)}, f32[160,768]{1,0:T(8,128)S(1)}, u32[]{:S(2)}, u32[]{:S(2)}) collective-permute-start(f32[160,768]{1,0:T(8,128)S(1)} %add.246), channel_id=1, source_target_pairs={{0,16},{1,17},{2,18},{3,19},{4,20},{5,21},{6,22},{7,23},{8,24},{9,... | collective-permute-start | bytes 1474568 | tf_op jit(solution)/shard_map/ppermute | solution.py:47
  238.2 15.1 %collective-permute-start.28 = (f32[192,768]{1,0:T(8,128)S(1)}, f32[192,768]{1,0:T(8,128)S(1)}, u32[]{:S(2)}, u32[]{:S(2)}) collective-permute-start(f32[192,768]{1,0:T(8,128)S(1)} %copy-done.42), channel_id=1, source_target_pairs={{0,4},{1,5},{2,6},{3,7},{4,0},{5,1},{6,2},{7,3},{8,12},{9,13},{10,... | collective-permute-start | bytes 1769480 | tf_op jit(solution)/shard_map/ppermute | solution.py:47
  254.0 18.8 %collective-permute-start.34 = (f32[192,768]{1,0:T(8,128)S(1)}, f32[192,768]{1,0:T(8,128)S(1)}, u32[]{:S(2)}, u32[]{:S(2)}) collective-permute-start(f32[192,768]{1,0:T(8,128)S(1)} %copy-done.41), channel_id=1, source_target_pairs={{0,4},{1,5},{2,6},{3,7},{4,0},{5,1},{6,2},{7,3},{8,12},{9,13},{10,... | collective-permute-start | bytes 1769480 | tf_op jit(solution)/shard_map/ppermute | solution.py:47
  267.6 35.8 %collective-permute-start.38 = (f32[80,768]{1,0:T(8,128)S(1)}, f32[80,768]{1,0:T(8,128)S(1)}, u32[]{:S(2)}, u32[]{:S(2)}) collective-permute-start(f32[80,768]{1,0:T(8,128)S(1)} %slice.285), channel_id=1, source_target_pairs={{0,1},{1,0},{2,3},{3,2},{4,5},{5,4},{6,7},{7,6},{8,9},{9,8},{10,11... | collective-permute-start | bytes 737288 | tf_op jit(solution)/shard_map/ppermute | solution.py:47
  269.0 27.4 %collective-permute-start.36 = (f32[192,1536]{1,0:T(8,128)S(1)}, f32[192,1536]{1,0:T(8,128)}, u32[]{:S(2)}, u32[]{:S(2)}) collective-permute-start(f32[192,1536]{1,0:T(8,128)S(1)} %constant_dynamic-slice_fusion.12), channel_id=1, source_target_pairs={{0,4},{1,5},{2,6},{3,7},{4,0},{5,1},{6,2},{7,3},{8,12},{9,13},{10,... | collective-permute-start | bytes 3538952 | tf_op jit(solution)/shard_map/ppermute | solution.py:47
  275.6 26.4 %collective-permute-start.37 = (f32[192,1536]{1,0:T(8,128)}, f32[192,1536]{1,0:T(8,128)}, u32[]{:S(2)}, u32[]{:S(2)}) collective-permute-start(f32[192,1536]{1,0:T(8,128)} %constant_dynamic-slice_fusion.11), channel_id=1, source_target_pairs={{0,2},{1,3},{2,0},{3,1},{4,6},{5,7},{6,4},{7,5},{8,10},{9,11},{10,... | collective-permute-start | bytes 3538952 | tf_op jit(solution)/shard_map/ppermute | solution.py:47
  303.5 12.7 %collective-permute-start.42 = (f32[80,768]{1,0:T(8,128)S(1)}, f32[80,768]{1,0:T(8,128)S(1)}, u32[]{:S(2)}, u32[]{:S(2)}) collective-permute-start(f32[80,768]{1,0:T(8,128)S(1)} %pad_maximum_fusion.20), channel_id=1, source_target_pairs={{0,2},{1,3},{2,0},{3,1},{4,6},{5,7},{6,4},{7,5},{8,10},{9,11},{10,... | collective-permute-start | bytes 737288 | tf_op jit(solution)/shard_map/ppermute | solution.py:47
  305.3 12.3 %collective-permute-start.40 = (f32[96,1536]{1,0:T(8,128)S(1)}, f32[96,1536]{1,0:T(8,128)S(1)}, u32[]{:S(2)}, u32[]{:S(2)}) collective-permute-start(f32[96,1536]{1,0:T(8,128)S(1)} %constant_dynamic-slice_fusion.9), channel_id=1, source_target_pairs={{0,4},{1,5},{2,6},{3,7},{4,0},{5,1},{6,2},{7,3},{8,12},{9,13},{10,... | collective-permute-start | bytes 1769480 | tf_op jit(solution)/shard_map/ppermute | solution.py:47
  306.0 15.3 %collective-permute-start.39 = (f32[96,1536]{1,0:T(8,128)S(1)}, f32[96,1536]{1,0:T(8,128)S(1)}, u32[]{:S(2)}, u32[]{:S(2)}) collective-permute-start(f32[96,1536]{1,0:T(8,128)S(1)} %constant_dynamic-slice_fusion.10), channel_id=1, source_target_pairs={{0,2},{1,3},{2,0},{3,1},{4,6},{5,7},{6,4},{7,5},{8,10},{9,11},{10,... | collective-permute-start | bytes 1769480 | tf_op jit(solution)/shard_map/ppermute | solution.py:47
  321.6 10.3 %collective-permute-start.41 = (f32[192,384]{1,0:T(8,128)S(1)}, f32[192,384]{1,0:T(8,128)S(1)}, u32[]{:S(2)}, u32[]{:S(2)}) collective-permute-start(f32[192,384]{1,0:T(8,128)S(1)} %get-tuple-element.494), channel_id=1, source_target_pairs={{0,8},{1,9},{2,10},{3,11},{4,12},{5,13},{6,14},{7,15},{8,0},{9,1},... | collective-permute-start | bytes 884744 | tf_op jit(solution)/shard_map/ppermute | solution.py:47
  332.0 14.3 %collective-permute-start.44 = (f32[192,384]{1,0:T(8,128)S(1)}, f32[192,384]{1,0:T(8,128)S(1)}, u32[]{:S(2)}, u32[]{:S(2)}) collective-permute-start(f32[192,384]{1,0:T(8,128)S(1)} %dynamic-slice_add_fusion.8), channel_id=1, source_target_pairs={{0,16},{1,17},{2,18},{3,19},{4,20},{5,21},{6,22},{7,23},{8,24},{9,... | collective-permute-start | bytes 884744 | tf_op jit(solution)/shard_map/ppermute | solution.py:47
  334.1 12.1 %collective-permute-start.43 = (f32[192,384]{1,0:T(8,128)S(1)}, f32[192,384]{1,0:T(8,128)S(1)}, u32[]{:S(2)}, u32[]{:S(2)}) collective-permute-start(f32[192,384]{1,0:T(8,128)S(1)} %get-tuple-element.364), channel_id=1, source_target_pairs={{0,8},{1,9},{2,10},{3,11},{4,12},{5,13},{6,14},{7,15},{8,0},{9,1},... | collective-permute-start | bytes 884744 | tf_op jit(solution)/shard_map/ppermute | solution.py:47
  355.5 19.6 %collective-permute-start.48 = (f32[120,1536]{1,0:T(8,128)S(1)}, f32[120,1536]{1,0:T(8,128)S(1)}, u32[]{:S(2)}, u32[]{:S(2)}) collective-permute-start(f32[120,1536]{1,0:T(8,128)S(1)} %constant_dynamic-slice_fusion.6), channel_id=1, source_target_pairs={{0,4},{1,5},{2,6},{3,7},{4,0},{5,1},{6,2},{7,3},{8,12},{9,13},{10,... | collective-permute-start | bytes 2211848 | tf_op jit(solution)/shard_map/ppermute | solution.py:47
  359.7 17.1 %collective-permute-start.49 = (f32[120,1536]{1,0:T(8,128)S(1)}, f32[120,1536]{1,0:T(8,128)S(1)}, u32[]{:S(2)}, u32[]{:S(2)}) collective-permute-start(f32[120,1536]{1,0:T(8,128)S(1)} %constant_dynamic-slice_fusion.5), channel_id=1, source_target_pairs={{0,2},{1,3},{2,0},{3,1},{4,6},{5,7},{6,4},{7,5},{8,10},{9,11},{10,... | collective-permute-start | bytes 2211848 | tf_op jit(solution)/shard_map/ppermute | solution.py:47
  360.6 16.3 %collective-permute-start.46 = (f32[192,384]{1,0:T(8,128)S(1)}, f32[192,384]{1,0:T(8,128)}, u32[]{:S(2)}, u32[]{:S(2)}) collective-permute-start(f32[192,384]{1,0:T(8,128)S(1)} %add_add_fusion.2), channel_id=1, source_target_pairs={{0,16},{1,17},{2,18},{3,19},{4,20},{5,21},{6,22},{7,23},{8,24},{9,... | collective-permute-start | bytes 884744 | tf_op jit(solution)/shard_map/ppermute | solution.py:47
  361.9 15.1 %collective-permute-start.45 = (f32[192,384]{1,0:T(8,128)S(1)}, f32[192,384]{1,0:T(8,128)S(1)}, u32[]{:S(2)}, u32[]{:S(2)}) collective-permute-start(f32[192,384]{1,0:T(8,128)S(1)} %add_add_fusion.2), channel_id=1, source_target_pairs={{0,8},{1,9},{2,10},{3,11},{4,12},{5,13},{6,14},{7,15},{8,0},{9,1},... | collective-permute-start | bytes 884744 | tf_op jit(solution)/shard_map/ppermute | solution.py:47
  377.0 10.4 %collective-permute-start.53 = (f32[60,1536]{1,0:T(8,128)S(1)}, f32[60,1536]{1,0:T(8,128)S(1)}, u32[]{:S(2)}, u32[]{:S(2)}) collective-permute-start(f32[60,1536]{1,0:T(8,128)S(1)} %constant_dynamic-slice_fusion.3), channel_id=1, source_target_pairs={{0,4},{1,5},{2,6},{3,7},{4,0},{5,1},{6,2},{7,3},{8,12},{9,13},{10,... | collective-permute-start | bytes 1105928 | tf_op jit(solution)/shard_map/ppermute | solution.py:47
  378.3 11.1 %collective-permute-start.51 = (f32[192,384]{1,0:T(8,128)}, f32[192,384]{1,0:T(8,128)S(1)}, u32[]{:S(2)}, u32[]{:S(2)}) collective-permute-start(f32[192,384]{1,0:T(8,128)} %collective-permute-done.46), channel_id=1, source_target_pairs={{0,8},{1,9},{2,10},{3,11},{4,12},{5,13},{6,14},{7,15},{8,0},{9,1},... | collective-permute-start | bytes 884744 | tf_op jit(solution)/shard_map/ppermute | solution.py:47
  391.8 21.8 %collective-permute-start.55 = (f32[96,1536]{1,0:T(8,128)}, f32[96,1536]{1,0:T(8,128)S(1)}, u32[]{:S(2)}, u32[]{:S(2)}) collective-permute-start(f32[96,1536]{1,0:T(8,128)} %get-tuple-element.487), channel_id=1, source_target_pairs={{0,4},{1,5},{2,6},{3,7},{4,0},{5,1},{6,2},{7,3},{8,12},{9,13},{10,... | collective-permute-start | bytes 1769480 | tf_op jit(solution)/shard_map/ppermute | solution.py:47
  392.6 20.9 %collective-permute-start.54 = (f32[96,1536]{1,0:T(8,128)}, f32[96,1536]{1,0:T(8,128)S(1)}, u32[]{:S(2)}, u32[]{:S(2)}) collective-permute-start(f32[96,1536]{1,0:T(8,128)} %get-tuple-element.488), channel_id=1, source_target_pairs={{0,2},{1,3},{2,0},{3,1},{4,6},{5,7},{6,4},{7,5},{8,10},{9,11},{10,... | collective-permute-start | bytes 1769480 | tf_op jit(solution)/shard_map/ppermute | solution.py:47
  396.1 9.9 %collective-permute-start.58 = (f32[120,384]{1,0:T(8,128)S(1)}, f32[120,384]{1,0:T(8,128)}, u32[]{:S(2)}, u32[]{:S(2)}) collective-permute-start(f32[120,384]{1,0:T(8,128)S(1)} %get-tuple-element.512), channel_id=1, source_target_pairs={{0,24},{1,25},{2,26},{3,27},{4,28},{5,29},{6,30},{7,31},{8,16},{9,... | collective-permute-start | bytes 552968 | tf_op jit(solution)/shard_map/ppermute | solution.py:47
  397.3 15.1 %collective-permute-start.57 = (f32[120,384]{1,0:T(8,128)S(1)}, f32[120,384]{1,0:T(8,128)}, u32[]{:S(2)}, u32[]{:S(2)}) collective-permute-start(f32[120,384]{1,0:T(8,128)S(1)} %get-tuple-element.513), channel_id=1, source_target_pairs={{0,16},{1,17},{2,18},{3,19},{4,20},{5,21},{6,22},{7,23},{8,24},{9,... | collective-permute-start | bytes 552968 | tf_op jit(solution)/shard_map/ppermute | solution.py:47
  414.0 25.7 %collective-permute-start.59 = (f32[192,1536]{1,0:T(8,128)S(1)}, f32[192,1536]{1,0:T(8,128)S(1)}, u32[]{:S(2)}, u32[]{:S(2)}) collective-permute-start(f32[192,1536]{1,0:T(8,128)S(1)} %pad_maximum_fusion.6), channel_id=1, source_target_pairs={{0,4},{1,5},{2,6},{3,7},{4,0},{5,1},{6,2},{7,3},{8,12},{9,13},{10,... | collective-permute-start | bytes 3538952 | tf_op jit(solution)/shard_map/ppermute | solution.py:47
  414.9 15.1 %collective-permute-start.62 = (f32[120,384]{1,0:T(8,128)S(1)}, f32[120,384]{1,0:T(8,128)S(1)}, u32[]{:S(2)}, u32[]{:S(2)}) collective-permute-start(f32[120,384]{1,0:T(8,128)S(1)} %add_add_fusion.3), channel_id=1, source_target_pairs={{0,16},{1,17},{2,18},{3,19},{4,20},{5,21},{6,22},{7,23},{8,24},{9,... | collective-permute-start | bytes 552968 | tf_op jit(solution)/shard_map/ppermute | solution.py:47
  417.3 12.7 %collective-permute-start.61 = (f32[120,384]{1,0:T(8,128)S(1)}, f32[120,384]{1,0:T(8,128)S(1)}, u32[]{:S(2)}, u32[]{:S(2)}) collective-permute-start(f32[120,384]{1,0:T(8,128)S(1)} %add_add_fusion.3), channel_id=1, source_target_pairs={{0,24},{1,25},{2,26},{3,27},{4,28},{5,29},{6,30},{7,31},{8,16},{9,... | collective-permute-start | bytes 552968 | tf_op jit(solution)/shard_map/ppermute | solution.py:47
  419.3 25.0 %collective-permute-start.60 = (f32[192,1536]{1,0:T(8,128)S(1)}, f32[192,1536]{1,0:T(8,128)S(1)}, u32[]{:S(2)}, u32[]{:S(2)}) collective-permute-start(f32[192,1536]{1,0:T(8,128)S(1)} %pad_maximum_fusion.7), channel_id=1, source_target_pairs={{0,2},{1,3},{2,0},{3,1},{4,6},{5,7},{6,4},{7,5},{8,10},{9,11},{10,... | collective-permute-start | bytes 3538952 | tf_op jit(solution)/shard_map/ppermute | solution.py:47
  444.7 12.6 %collective-permute-start.66 = (f32[384,1536]{1,0:T(8,128)S(1)}, f32[384,1536]{1,0:T(8,128)S(1)}, u32[]{:S(2)}, u32[]{:S(2)}) collective-permute-start(f32[384,1536]{1,0:T(8,128)S(1)} %pad_maximum_fusion.first_ref), channel_id=1, source_target_pairs={{0,1},{1,0},{2,3},{3,2},{4,5},{5,4},{6,7},{7,6},{8,9},{9,8},{10,11... | collective-permute-start | bytes 7077896 | tf_op jit(solution)/shard_map/ppermute | solution.py:47
  444.7 12.5 %collective-permute-start.67 = (f32[384,1536]{1,0:T(8,128)S(1)}, f32[384,1536]{1,0:T(8,128)S(1)}, u32[]{:S(2)}, u32[]{:S(2)}) collective-permute-start(f32[384,1536]{1,0:T(8,128)S(1)} %pad_maximum_fusion.1.second_ref), channel_id=1, source_target_pairs={{0,1},{1,0},{2,3},{3,2},{4,5},{5,4},{6,7},{7,6},{8,9},{9,8},{10,11... | collective-permute-start | bytes 7077896 | tf_op jit(solution)/shard_map/ppermute | solution.py:47
  445.3 11.2 %collective-permute-start.65 = (f32[60,1536]{1,0:T(8,128)S(1)}, f32[60,1536]{1,0:T(8,128)S(1)}, u32[]{:S(2)}, u32[]{:S(2)}) collective-permute-start(f32[60,1536]{1,0:T(8,128)S(1)} %get-tuple-element.505), channel_id=1, source_target_pairs={{0,4},{1,5},{2,6},{3,7},{4,0},{5,1},{6,2},{7,3},{8,12},{9,13},{10,... | collective-permute-start | bytes 1105928 | tf_op jit(solution)/shard_map/ppermute | solution.py:47
  446.1 10.8 %collective-permute-start.64 = (f32[60,1536]{1,0:T(8,128)S(1)}, f32[60,1536]{1,0:T(8,128)S(1)}, u32[]{:S(2)}, u32[]{:S(2)}) collective-permute-start(f32[60,1536]{1,0:T(8,128)S(1)} %get-tuple-element.506), channel_id=1, source_target_pairs={{0,2},{1,3},{2,0},{3,1},{4,6},{5,7},{6,4},{7,5},{8,10},{9,11},{10,... | collective-permute-start | bytes 1105928 | tf_op jit(solution)/shard_map/ppermute | solution.py:47
  457.2 17.4 %collective-permute-start.68 = (f32[120,1536]{1,0:T(8,128)S(1)}, f32[120,1536]{1,0:T(8,128)S(1)}, u32[]{:S(2)}, u32[]{:S(2)}) collective-permute-start(f32[120,1536]{1,0:T(8,128)S(1)} %pad_maximum_fusion.10), channel_id=1, source_target_pairs={{0,4},{1,5},{2,6},{3,7},{4,0},{5,1},{6,2},{7,3},{8,12},{9,13},{10,... | collective-permute-start | bytes 2211848 | tf_op jit(solution)/shard_map/ppermute | solution.py:47
  458.6 17.0 %collective-permute-start.69 = (f32[120,1536]{1,0:T(8,128)S(1)}, f32[120,1536]{1,0:T(8,128)S(1)}, u32[]{:S(2)}, u32[]{:S(2)}) collective-permute-start(f32[120,1536]{1,0:T(8,128)S(1)} %pad_maximum_fusion.11), channel_id=1, source_target_pairs={{0,2},{1,3},{2,0},{3,1},{4,6},{5,7},{6,4},{7,5},{8,10},{9,11},{10,... | collective-permute-start | bytes 2211848 | tf_op jit(solution)/shard_map/ppermute | solution.py:47
  (86 other events, 512.1 us)

commit v4 on v3

--- a/solution.py
+++ b/solution.py
@@ -17,8 +17,8 @@
 NN, NT, TN = ((1,), (0,)), ((1,), (1,)), ((0,), (0,))
 VMEM_BYTES = 52 << 20
 MICROSECONDS = {
-    "route": 1, "join": 8, "features": 8, "join_states": 1, "scan": 14, "early": 7, "expert": 4.4,
-    "expert_grads": 17, "mixer_back": 9.6, "late": 6, "scan_back": 10, "input_back": 11, "finish_late": 8, "finish": 6,
+    "route": 1, "join": 8, "features": 250, "join_states": 1, "scan": 14, "early": 7, "expert": 4.4,
+    "expert_grads": 17, "mixer_back": 300, "late": 200, "scan_back": 10, "input_back": 11, "finish_late": 8, "finish": 6,
 }
 
 
@@ -71,17 +71,16 @@
     return parts
 
 
-def scatter_rows(grid, block, name):
+def rows_of(parts, first, rows):
+    return functools.reduce(jnp.add, [lax.dynamic_slice_in_dim(part, first, rows, 0) for part in parts])
+
+
+def scatter_rows(grid, parts, name, rows, start=0):
     count, place = grid.size[name], grid.at[name]
-    if count == 1:
-        return block
-    rows = block.shape[0] // count
-    piece = lambda s: lax.dynamic_slice_in_dim(block, (place ^ s) * rows, rows, 0)
+    rows = rows // count
+    piece = lambda s: rows_of(parts, start + (place ^ s) * rows, rows)
     got = [grid.swap(piece(s), name, s) for s in range(1, count)]
-    total = piece(0)
-    for part in got:
-        total = total + part
-    return total
+    return [piece(0)] + got
 
 
 def gather_rows(grid, block, name):
@@ -92,37 +91,37 @@
     return jnp.concatenate(in_order(parts, grid.at[name]), axis=0)
 
 
-def sum_first(grid, half):
-    rows = half.shape[0] // 2
-    return scatter_rows(grid, half[:rows], "inner"), scatter_rows(grid, half[rows:], "y")
+def sum_first(grid, parts):
+    rows = parts[0].shape[0] // 2
+    return scatter_rows(grid, parts, "inner", rows), scatter_rows(grid, parts, "y", rows, rows)
 
 
 def sum_second(grid, first, second):
-    return jnp.concatenate([scatter_rows(grid, first, "y"), scatter_rows(grid, second, "inner")], axis=0)
-
-
-def sum_outer(grid, both):
-    count, place = grid.size["outer"], grid.at["outer"]
-    columns = both.shape[1] // count
-    piece = lambda s: lax.dynamic_slice_in_dim(both, (place ^ s) * columns, columns, 1)
-    got = [grid.swap(piece(s), "outer", s) for s in range(1, count)]
-    total = piece(0)
-    for part in got:
-        total = total + part
-    return total
+    rows = first[0].shape[0]
+    first, second = scatter_rows(grid, first, "y", rows), scatter_rows(grid, second, "inner", rows)
+    return [jnp.concatenate(pair, axis=0) for pair in zip(first, second)]
+
+
+def cut_outer(grid, parts):
+    columns = parts[0].shape[1] // grid.outer
+    return [
+        functools.reduce(
+            jnp.add,
+            [lax.dynamic_slice_in_dim(p, (grid.at["outer"] ^ s) * columns, columns, 1) for p in parts],
+        )
+        for s in range(grid.outer)
+    ]
+
+
+def sum_outer(grid, parts):
+    own, *others = cut_outer(grid, parts)
+    return functools.reduce(jnp.add, [grid.swap(part, "outer", s) for s, part in enumerate(others, 1)], own)
 
 
 def spread_outer(grid, total):
     count = grid.size["outer"]
     parts = [total] + [grid.swap(total, "outer", s) for s in range(1, count)]
     return jnp.concatenate(in_order(parts, grid.at["outer"]), axis=1)
-
-
-def cut_outer(grid, both):
-    columns = both.shape[1] // 4
-    return [
-        lax.dynamic_slice_in_dim(both, (grid.at["outer"] ^ s) * columns, columns, 1) for s in range(4)
-    ]
 
 
 def join_outer(grid, own, near, far, last):
@@ -311,7 +310,7 @@
 
 
 def full(*dims):
-    return pl.BlockSpec(dims, lambda c: (0,) * len(dims))
+    return pl.BlockSpec(dims, lambda *_: (0,) * len(dims))
 
 
 def route_kernel(experts, cap, me_ref, ids_ref, grad_ref, sent_ref, table_ref, rank_ref, load_ref):
@@ -712,6 +711,7 @@
     grad_scan_ref,
     skip_ref,
     history_ref,
+    before_ref,
     start_ref,
     end_ref,
     rate_ref,
@@ -719,51 +719,75 @@
     step_proj_ref,
     *refs,
 ):
-    grad_act_ref, grad_pre_ref, grad_decay_ref, grad_proj_ref, in_lanes, out_lanes, grad_drive, grad_steps = refs[-8:]
+    (
+        grad_act_ref, grad_pre_ref, grad_decay_ref, grad_proj_ref,
+        in_lanes, out_lanes, grad_drive, grad_steps, at_in, at_out, carried_ref, decays_ref, sums_ref,
+    ) = refs[-13:]
     tokens, chunk = masked_ref.shape
-    over_lanes(in_lanes, proj_ref[rank_n : rank_n + states, :])
-    over_lanes(out_lanes, proj_ref[rank_n + states : rank_n + 2 * states, :])
+    block = history_ref.shape[0]
+    step, blocks = pl.program_id(0), pl.num_programs(0)
+    first = (blocks - 1 - step) * block
+
+    @pl.when(step == 0)
+    def _():
+        over_lanes(in_lanes, proj_ref[rank_n : rank_n + states, :])
+        over_lanes(out_lanes, proj_ref[rank_n + states : rank_n + 2 * states, :])
+        carried_ref[...] = end_ref[...]
+        decays_ref[...] = jnp.zeros_like(decays_ref)
+        sums_ref[...] = jnp.zeros_like(sums_ref)
 
     rate = rate_ref[...]
-    lane = iota((states, tokens), 1)
-
-    def one(t, before, carried):
-        state, decays, grad_in, grad_out = carried
+    entering_state = jnp.where(first == 0, start_ref[...], before_ref[7])
+
+    def narrow(value):
+        return functools.reduce(jnp.add, [value[:, c : c + 128] for c in range(0, chunk, 128)])
+
+    def one(local, before, carried):
+        state, decays = carried
+        t = first + local
         masked = masked_ref[pl.ds(t, 1), :]
         grad = grad_scan_ref[pl.ds(t, 1), :]
         decay = jnp.exp2(masked * rate)
         state = state + grad * widen(out_lanes[t], chunk)
-        at_out = jnp.sum(history_ref[t] * grad, axis=1, keepdims=True)
-        at_in = jnp.sum(state * drive_ref[pl.ds(t, 1), :], axis=1, keepdims=True)
-        grad_out = jnp.where(lane == t, at_out, grad_out)
-        grad_in = jnp.where(lane == t, at_in, grad_in)
+        at_out[local] = narrow(history_ref[local] * grad)
+        at_in[local] = narrow(state * drive_ref[pl.ds(t, 1), :])
         grad_drive[pl.ds(t, 1), :] = jnp.sum(state * widen(in_lanes[t], chunk), axis=0, keepdims=True)
         state = decay * state
         pulled = state * before
         grad_steps[pl.ds(t, 1), :] = jnp.sum(pulled * rate, axis=0, keepdims=True)
-        return state, decays + pulled * masked, grad_in, grad_out
-
-    def four(group, carried):
-        for i in range(4):
-            t = tokens - 1 - (group * 4 + i)
-            carried = one(t, history_ref[t - 1], carried)
+        return state, decays + pulled * masked
+
+    def eight(group, carried):
+        for i in range(8):
+            local = block - 1 - (group * 8 + i)
+            carried = one(local, history_ref[local - 1], carried)
         return carried
 
-    nothing = jnp.zeros((states, tokens), F32)
-    carried = lax.fori_loop(
-        0, tokens // 4 - 1, four, (end_ref[...], jnp.zeros((states, chunk), F32), nothing, nothing)
-    )
-    for t in (3, 2, 1):
-        carried = one(t, history_ref[t - 1], carried)
-    _, decays, grad_in, grad_out = one(0, start_ref[...], carried)
-    grad_decay_ref[...] = decays * (rate * (1.0 / LOG2E))
-    steps, act = steps_ref[...], act_ref[...]
-    grad_act_ref[...] = skip_ref[...] * grad_scan_ref[...] + grad_drive[...] * steps
-    grad_pre = (grad_steps[...] * (1.0 / LOG2E) + grad_drive[...] * act) * sigmoid(pre_ref[...])
-    grad_pre_ref[...] = grad_pre
-    grad_proj_ref[0:rank_n, :] = product(split(step_proj_ref[...]), split(grad_pre), NT)
-    grad_proj_ref[rank_n : rank_n + states, :] = grad_in
-    grad_proj_ref[rank_n + states : rank_n + 2 * states, :] = grad_out
+    carried = lax.fori_loop(0, block // 8 - 1, eight, (carried_ref[...], decays_ref[...]))
+    for local in range(7, 0, -1):
+        carried = one(local, history_ref[local - 1], carried)
+    carried_ref[...], decays_ref[...] = one(0, entering_state, carried)
+
+    ones = jnp.ones((128, 128), BF16)
+    lane = iota((states, 128), 1)
+    for i, held in enumerate((at_in, at_out)):
+        high, low = split(held[...].reshape(block * states, 128))
+        spread = (dot(high, ones, NN) + dot(low, ones, NN)).reshape(block, states, 128)
+        total = sums_ref[i]
+        for local in range(block):
+            total = jnp.where(lane == first + local, spread[local], total)
+        sums_ref[i] = total
+
+    @pl.when(step == blocks - 1)
+    def _():
+        grad_decay_ref[...] = decays_ref[...] * (rate * (1.0 / LOG2E))
+        steps, act = steps_ref[...], act_ref[...]
+        grad_act_ref[...] = skip_ref[...] * grad_scan_ref[...] + grad_drive[...] * steps
+        grad_pre = (grad_steps[...] * (1.0 / LOG2E) + grad_drive[...] * act) * sigmoid(pre_ref[...])
+        grad_pre_ref[...] = grad_pre
+        grad_proj_ref[0:rank_n, :] = product(split(step_proj_ref[...]), split(grad_pre), NT)
+        grad_proj_ref[rank_n : rank_n + states, :] = sums_ref[0]
+        grad_proj_ref[rank_n + states : rank_n + 2 * states, :] = sums_ref[1]
 
 
 def input_back_kernel(
@@ -974,6 +998,8 @@
     chunk = 512
     chunks = width // chunk
     pieces, slices = grid.size["outer"], grid.size["inner"]
+    token_block = 64
+    blocks = tokens // token_block
     me = lax.axis_index("exp").astype(jnp.int32).reshape(1)
     ext = HALO + tokens
 
@@ -1003,7 +1029,7 @@
     ups = [up] + [grid.swap(up, "inner", s) for s in range(1, slices)]
     downs = [down] + [grid.swap(down, "inner", s) for s in range(1, slices)]
 
-    block = lambda c: (0, c)
+    block = lambda c, *_: (0, c)
     joined = call(
         join_kernel,
         shape(ext, 2 * width),
@@ -1015,6 +1041,9 @@
         name="join",
     )
     joined, *held_grads = tie(joined, *held_grads)
+    own_grads = send_core(grid, held_grads, None, cap, False)
+    joined, own_grads = tie(joined, own_grads)
+    near_grads, far_grads = grid.swap(own_grads, "outer", 1), grid.swap(own_grads, "outer", 2)
     conv, act, pre, steps, masked, drive, proj, pair = call(
         functools.partial(features_kernel, rank_n, states),
         [shape(tokens, width)] * 6 + [shape(rank_n + 2 * states, tokens), shape(states + 1, width)],
@@ -1034,25 +1063,22 @@
         scratch=[pltpu.VMEM((tokens, states, 128), F32)],
         name="features",
     )
-    own_grads = send_core(grid, held_grads, None, cap, False)
-    pair, own_grads, *downs = tie(pair, own_grads, *downs)
-    near_grads, far_grads = grid.swap(own_grads, "outer", 1), grid.swap(own_grads, "outer", 2)
+    pair, *downs = tie(pair, *downs)
     held = {}
 
     def third(total):
         total, held["near"], held["far"] = tie(total, near_grads, far_grads)
         return total
 
-    start = entering(grid, pair, rate, False, {3: third})
-    near_grads = held["near"]
-    start, far_grads = tie(start, held["far"])
+    start = entering(grid, pair, rate, False, {2: third})
+    start, near_grads, far_grads = tie(start, held["near"], held["far"])
     last_grads = grid.swap(far_grads, "outer", 1)
     tok = pl.BlockSpec((tokens, chunk), block)
-    gate_half = pl.BlockSpec((ext, chunk), lambda c: (0, chunks + c))
+    gate_half = pl.BlockSpec((ext, chunk), lambda c, *_: (0, chunks + c))
     one_row = pl.BlockSpec((1, chunk), block)
     state_rows = pl.BlockSpec((states, chunk), block)
     history_block = pl.BlockSpec((tokens, states, chunk), lambda c: (0, 0, c))
-    out_rows = pl.BlockSpec((chunk, depth), lambda c: (c, 0))
+    out_rows = pl.BlockSpec((chunk, depth), lambda c, *_: (c, 0))
     proj_full = full(rank_n + 2 * states, tokens)
     lanes = pltpu.VMEM((tokens, states, 128), F32)
     scan, history, resid, sent, probs, gate = call(
@@ -1158,7 +1184,7 @@
         scratch=[lanes] + [pltpu.VMEM((tokens, depth), BF16)] * 2,
         name="mixer_back",
     )
-    back_pair, through, downs_sent, *up_second = tie(back_pair, through, downs_sent, *up_second)
+    back_pair, downs_sent = tie(back_pair, downs_sent)
     core = grid.at["core"].astype(jnp.int32).reshape(1)
     wide = pl.BlockSpec((tokens, depth), block)
 
@@ -1184,27 +1210,23 @@
     (late_sent,) = late(core, ())
     late_kept, grad_gate_normed = late(1 - core, (in_proj,))
     late_got = grid.swap(late_sent, "core", 1)
-    near = grid.swap(results[1], "outer", 1)
-    far = grid.swap(results[2] + through, "outer", 2)
     down_first = inner_swaps(downs_sent, 0)
 
+    def first(total):
+        total, held["through"], held["downs"], *held["up_second"] = tie(total, through, downs_sent, *up_second)
+        return total
+
     def second(total):
-        total, held["second"], *held["down_first"] = tie(total, downs_sent, *down_first)
-        held["down_second"] = inner_swaps(held["second"], 1)
+        total, got, kept, held["normed"], *held["down_first"] = tie(
+            total, late_got, late_kept, grad_gate_normed, *down_first
+        )
+        held["late"] = sum_first(grid, [kept, got])
         return total
 
-    def third(total):
-        total, held["late_got"], held["late_kept"], held["normed"], held["near"], held["far"] = tie(
-            total, late_got, late_kept, grad_gate_normed, near, far
-        )
-        held["late"] = sum_first(grid, held["late_kept"] + held["late_got"])
-        return total
-
-    def fourth(total):
-        total, *held["down_second"] = tie(total, *held["down_second"])
-        return total
-
-    end = entering(grid, back_pair, rate, True, {2: second, 3: third, 4: fourth})
+    end = entering(grid, back_pair, rate, True, {1: first, 2: second})
+    up_second = held["up_second"]
+    end, near, far = tie(end, results[1], results[2] + held["through"])
+    near, far = grid.swap(near, "outer", 1), grid.swap(far, "outer", 2)
     grad_gate_normed = held["normed"]
     late_first, late_second = held["late"]
 
@@ -1212,11 +1234,6 @@
         for pair in zip(firsts, seconds):
             own = own + jnp.concatenate(pair, axis=0)
         return own
-
-    grad_up = with_others(up_grads[0], up_first, up_second)
-    grad_down = with_others(down_grads[0], held["down_first"], held["down_second"])
-    result = results[0] + held["near"] + held["far"]
-    result_got = back_core(grid, result, cap, False)
 
     def scan_back(c, before):
         at = lambda _: (0, c)
@@ -1229,32 +1246,42 @@
                 shape(rank_n + 2 * states, tokens),
             ],
             (
-                masked, steps, drive, act, pre, grad_scan, row(skip_gain), history, start, end, rate, proj,
+                masked, steps, drive, act, pre, grad_scan, row(skip_gain), history, history, start, end, rate, proj,
                 step_proj, *before,
             ),
-            grid=(1,),
+            grid=(blocks,),
             in_specs=[
                 tok, tok, tok, tok, tok, tok, one_row,
-                pl.BlockSpec((tokens, states, chunk), lambda _: (0, 0, c)), state_rows, state_rows, state_rows,
-                proj_full, pl.BlockSpec((rank_n, chunk), at),
+                pl.BlockSpec((token_block, states, chunk), lambda i: (blocks - 1 - i, 0, c)),
+                pl.BlockSpec(
+                    (8, states, chunk),
+                    lambda i: (jnp.maximum((blocks - 1 - i) * (token_block // 8) - 1, 0), 0, c),
+                ),
+                state_rows, state_rows, state_rows, proj_full, pl.BlockSpec((rank_n, chunk), at),
             ]
             + [pl.BlockSpec(memory_space=pl.ANY)] * len(before),
             out_specs=[tok, tok, state_rows, proj_full],
-            scratch=[lanes, lanes] + [pltpu.VMEM((tokens, chunk), F32)] * 2,
+            scratch=[lanes, lanes]
+            + [pltpu.VMEM((tokens, chunk), F32)] * 2
+            + [pltpu.VMEM((token_block, states, 128), F32)] * 2
+            + [pltpu.VMEM((states, chunk), F32)] * 2
+            + [pltpu.VMEM((2, states, 128), F32)],
             name="scan_back",
-            aliases={13 + i: i for i in range(len(before))},
+            aliases={14 + i: i for i in range(len(before))},
         )
 
     *filled, grad_proj_a = scan_back(0, ())
-    *filled, late_first, late_second, result_got = tie(*filled, late_first, late_second, result_got)
+    filled, late_first, late_second = tie(filled, late_first, late_second)
     late_both = sum_second(grid, late_first, late_second)
-    result = back_y(grid, result, result_got, cap, False)
     *filled, grad_proj_b = scan_back(1, filled)
-    *filled, late_both = tie(*filled, late_both)
+    filled, late_both, near, far, downs_sent = tie(filled, late_both, near, far, held["downs"])
+    down_second = inner_swaps(downs_sent, 1)
+    result = results[0] + near + far
+    result_got = back_core(grid, result, cap, False)
     late_cut = cut_outer(grid, late_both)
     late_through = grid.swap(late_cut[3], "outer", 1)
     grad_act, grad_pre, grad_decay, grad_proj_c = scan_back(2, filled)
-    grad_act, late_through, result = tie(grad_act, late_through, result)
+    grad_act, late_through, result_got, down_second = tie(grad_act, late_through, result_got, down_second)
     late_total = outer_reduce_rest(grid, late_cut, late_through)
     unit = 2 * grid.size["inner"] * grid.size["y"]
     half = -(-max(depth // 2 + 3 * states + rank_n, depth // 2 + rank_n + 40) // unit) * unit
@@ -1284,23 +1311,30 @@
     )
     kept, sent_half, late_total = tie(kept, sent_half, late_total)
     late_near, late_far = grid.swap(late_total, "outer", 1), grid.swap(late_total, "outer", 2)
+    sent_got = grid.swap(sent_half, "core", 1)
+    kept, sent_got = tie(kept, sent_got)
+    grads_first, grads_second = sum_first(grid, [kept, sent_got])
+    late_near, late_far, grads_first, grads_second, edge, result, result_got, up_parts, down_parts = tie(
+        late_near, late_far, grads_first, grads_second, edge, result, result_got,
+        [up_grads[0], up_first, up_second], [down_grads[0], held["down_first"], down_second],
+    )
     from_next = grid.along(edge, -1)
     input_grad = jnp.concatenate([input_grad[: tokens - HALO], input_grad[tokens - HALO :] + from_next], axis=0)
+    grad_up, grad_down = with_others(*up_parts), with_others(*down_parts)
+    late_last = grid.swap(late_far, "outer", 1)
+    grads = sum_second(grid, grads_first, grads_second)
+    late_last, grads, input_grad = tie(late_last, grads, input_grad)
+    result = back_y(grid, result, result_got, cap, False)
+    late_first, late_second = spread_second(grid, join_outer(grid, late_total, late_near, late_far, late_last))
+    grads = sum_outer(grid, grads)
+    late_first, late_second, grads, result, grad_up = tie(late_first, late_second, grads, result, grad_up)
     combined = jnp.dot(table.T, result.astype(F32), precision=lax.Precision.HIGHEST, preferred_element_type=F32)
     block_output = resid + gate * combined
-    grads_first, grads_second = sum_first(grid, kept + grid.swap(sent_half, "core", 1))
-    late_near, late_far, grads_first, grads_second, input_grad, block_output, grad_up, grad_down = tie(
-        late_near, late_far, grads_first, grads_second, input_grad, block_output, grad_up, grad_down
-    )
-    late_last = grid.swap(late_far, "outer", 1)
-    grads = sum_second(grid, grads_first, grads_second)
-    late_last, grads = tie(late_last, grads)
-    late_first, late_second = spread_second(grid, join_outer(grid, late_total, late_near, late_far, late_last))
-    grads = sum_outer(grid, grads)
-    late_first, late_second, grads = tie(late_first, late_second, grads)
     late_first, late_second = gather_rows(grid, late_first, "inner"), gather_rows(grid, late_second, "y")
     grads = spread_outer(grid, grads)
-    late_first, late_second, grads = tie(late_first, late_second, grads)
+    late_first, late_second, grads, block_output, grad_down = tie(
+        late_first, late_second, grads, block_output, grad_down
+    )
     late_other = [grid.swap(late_first, "core", 1), grid.swap(late_second, "core", 1)]
     grads_first, grads_second = spread_second(grid, grads)
     grads_first, grads_second, *late_other = tie(grads_first, grads_second, *late_other)

time: 500 us -> 474 us (0.948)
  waiting for transfers between devices: 211 us -> 185 us
  other arithmetic: 25.3 us -> 32.9 us
    ppermute x70, waiting for transfers between devices: 211 us -> 185 us  [swap_bits(): return lax.ppermute(block, AXES, [(i, i ^ bits) for i in range(self.total)])]
    add x13 -> x11, other arithmetic: 12.6 us -> 13.9 us  [the longest x6 11.8 us: rows_of(): functools.reduce(jnp.add, [lax.dynamic_slice_in_dim(part, first, rows, 0)...]
    unnamed x127 -> x135, local copies, waits for them, and re-layouts: 11.8 us -> 10.9 us
  transfers between devices with their start and end apart: 72 -> 72, of which waited for: 44 -> 41; matrix products, arithmetic and copies ran while one was open for 6% -> 7% of each run, Pallas kernels for 26% -> 30%
where the time goes in v4:
time: 474 us; the launch traced here: 468 us
  waiting for transfers between devices  185 us (39%)
  Pallas kernels  149 us (31%)
  starting transfers between devices  77.5 us (16%)
  other arithmetic  32.9 us (7%)
  local copies, waits for them, and re-layouts  19.8 us (4%)
    ppermute x70, waiting for transfers between devices, swap_bits(): return lax.ppermute(block, AXES, [(i, i ^ bits) for i in range(self.total)])  185 us
    pallas_call x29, Pallas kernels, call(): pl.pallas_call(kernel, out_shape=outs, grid=grid or (), in_specs=in_specs...  149 us
    ppermute x70, starting transfers between devices, swap_bits(): return lax.ppermute(block, AXES, [(i, i ^ bits) for i in range(self.total)])  73.6 us
    add x6, other arithmetic, rows_of(): functools.reduce(jnp.add, [lax.dynamic_slice_in_dim(part, first, rows, 0)...  11.8 us
    unnamed x135, local copies, waits for them, and re-layouts  10.9 us
  transfers between devices with their start and end apart: 72, of which 41 were waited for; matrix products, arithmetic and copies ran while one was open for 7% of the time, Pallas kernels for 30%

profile of v4, /device:TPU:0, one launch (start us, length us, event | category | flops | bytes accessed | tf_op | source)
XLA Modules:
  0.0 467.5 jit_solution(6625086638925419405)
XLA Ops:
  12.2 7.9 %join.1.inner_ref.gate_z_ref = f32[144,3072]{1,0:T(8,128)} custom-call(f32[128,768]{1,0:T(8,128)S(1)} %copy-done.8, f32[16,768]{1,0:T(8,128)S(1)} %collective-permute-done.halo_ref, f32[1,768]{1,0:T(1,128)S(1)} %reshape.120.gain_ref, f32[768,3072]{1,0:T(8,128)} %weight_ref.3), custom_call_target="tpu_custom_call" | custom-call | flops 8800000000 | bytes 8000000 | tf_op jit(solution)/shard_map/join/pallas_call | solution.py:289
  26.8 8.3 %features.1 = (f32[128,1536]{1,0:T(8,128)S(1)}, f32[128,1536]{1,0:T(8,128)}, f32[128,1536]{1,0:T(8,128)}, f32[128,1536]{1,0:T(8,128)}, f32[128,1536]{1,0:T(8,128...) custom-call(f32[144,3072]{1,0:T(8,128)} %join.1.inner_ref.gate_z_ref, ...), custom_call_target="tpu_custom_call" | custom-call | flops 275000000512 | bytes 250000000 | tf_op jit(solution)/shard_map/features/pallas_call | solution.py:289
  39.2 4.7 %collective-permute-done.5.got_ref = f32[17,1536]{1,0:T(8,128)S(1)} collective-permute-done((f32[17,1536]{1,0:T(8,128)S(1)}, f32[17,1536]{1,0:T(8,128)S(1)}, u32[]{:S(2)}, u32[]{:S(2)}) %collective-permute-start.5) | collective-permute-done | bytes 104480 | tf_op jit(solution)/shard_map/ppermute | solution.py:47
  44.0 4.7 %collective-permute-done.7.refs_2_.refs_6_ = f32[160,768]{1,0:T(8,128)} collective-permute-done((f32[160,768]{1,0:T(8,128)}, f32[160,768]{1,0:T(8,128)}, u32[]{:S(2)}, u32[]{:S(2)}) %collective-permute-start.7) | collective-permute-done | bytes 491552 | tf_op jit(solution)/shard_map/ppermute | solution.py:47
  49.3 4.7 collective-permute-done.8.got_ref
  55.7 3.5 collective-permute-done.9.got_ref
  62.4 4.7 collective-permute-done.10.got_ref
  67.3 14.2 %scan.1 = (f32[128,1536]{1,0:T(8,128)}, f32[128,16,1536]{2,1,0:T(8,128)}, f32[128,768]{1,0:T(8,128)S(1)}, f32[168,768]{1,0:T(8,128)S(1)}, f32[128,8]{1,0:T(8,128)S(1)}, /*index=5*/f32[128,1]{1,0:T(8,128)S(1)}) custom-call(s32[1]{0:T(128)} %bitcast.1.me_ref, f32[128,1536]{1,0:T(8,128)} %get-tuple-element.243.masked_ref, ...), custom_call_target="tpu_custom_call" | custom-call | flops 15399999488 | bytes 14000000 | tf_op jit(solution)/shard_map/scan/pallas_call | solution.py:289
  83.3 5.5 %collective-permute-done.12 = f32[88,768]{1,0:T(8,128)S(1)} collective-permute-done((f32[88,768]{1,0:T(8,128)S(1)}, f32[88,768]{1,0:T(8,128)S(1)}, u32[]{:S(2)}, u32[]{:S(2)}) %collective-permute-start.12) | collective-permute-done | bytes 270368 | tf_op jit(solution)/shard_map/ppermute | solution.py:47
  88.9 6.7 %early.1 = (f32[2,160,384]{2,1,0:T(8,128)S(1)}, f32[2,160,384]{2,1,0:T(8,128)S(1)}, f32[2,160,384]{2,1,0:T(8,128)S(1)}, f32[2,160,384]{2,1,0:T(8,128)S(1)}) custom-call(f32[160,768]{1,0:T(8,128)} %pad_maximum_fusion.16.refs_0_.refs_4_, f32[160,768]{1,0:T(8,128)} %collective-permute-done.6.refs_1_.refs_5_, f32[160,768]{1,0:T(8,128)} %collective-permute-done.7.refs_2_.refs_6_, ...), custom_call_target="tpu_custom_call" | custom-call | flops 7699999744 | bytes 7000000 | tf_op jit(solution)/shard_map/early/pallas_call | solution.py:289
  95.8 3.5 collective-permute-start.15
  99.6 4.4 expert.4
  104.0 18.8 %collective-permute-done.15.refs_0_.refs_2_ = f32[168,768]{1,0:T(8,128)S(1)} collective-permute-done((f32[168,768]{1,0:T(8,128)S(1)}, f32[168,768]{1,0:T(8,128)S(1)}, u32[]{:S(2)}, u32[]{:S(2)}) %collective-permute-start.15) | collective-permute-done | bytes 516128 | tf_op jit(solution)/shard_map/ppermute | solution.py:47
  124.5 4.4 expert.6
  130.6 4.4 expert.5
  137.9 4.8 %expert.7 = (f32[168,768]{1,0:T(8,128)S(1)}, f32[2,160,384]{2,1,0:T(8,128)S(1)}, f32[2,160,384]{2,1,0:T(8,128)S(1)}) custom-call(f32[168,768]{1,0:T(8,128)} %copy-done.64, f32[768,384]{1,0:T(8,128)} %bitcast.11.refs_1_, f32[768,384]{1,0:T(8,128)} %collective-permute-done.16.refs_2_, f32[2,160,384]{2,1,0:T(8,128)S(1)} %get-tuple-element.294.refs_3_), custom_call_target="tpu_custom_call" | custom-call | flops 4840000000 | bytes 4400000 | tf_op jit(solution)/shard_map/expert/pallas_call | solution.py:289
  143.6 11.3 %collective-permute-done.18 = f32[168,768]{1,0:T(8,128)S(1)} collective-permute-done((f32[168,768]{1,0:T(8,128)S(1)}, f32[168,768]{1,0:T(8,128)S(1)}, u32[]{:S(2)}, u32[]{:S(2)}) %collective-permute-start.18) | collective-permute-done | bytes 516128 | tf_op jit(solution)/shard_map/ppermute | solution.py:47
  157.5 17.3 %expert_grads.1 = (f32[160,768]{1,0:T(8,128)S(1)}, f32[160,768]{1,0:T(8,128)S(1)}, f32[160,768]{1,0:T(8,128)S(1)}, f32[160,768]{1,0:T(8,128)}, f32[768,384]{1,0:...) custom-call(f32[168,768]{1,0:T(8,128)} %copy-done.49, f32[168,768]{1,0:T(8,128)} %copy-done.63, ...), custom_call_target="tpu_custom_call" | custom-call | flops 18699999232 | bytes 17000000 | tf_op jit(solution)/shard_map/expert_grads/pallas_call | solution.py:289
  174.8 3.4 collective-permute-done.20
  185.7 5.9 %collective-permute-done.22 = f32[88,768]{1,0:T(8,128)} collective-permute-done((f32[88,768]{1,0:T(8,128)}, f32[88,768]{1,0:T(8,128)}, u32[]{:S(2)}, u32[]{:S(2)}) %collective-permute-start.22) | collective-permute-done | bytes 270368 | tf_op jit(solution)/shard_map/ppermute | solution.py:47
  198.4 9.6 %mixer_back.1 = (f32[128,768]{1,0:T(8,128)S(1)}, f32[16,768]{1,0:T(8,128)S(1)}, f32[128,1536]{1,0:T(8,128)}, f32[128,1536]{1,0:T(8,128)}, f32[1,1536]{1,0:T(1,128)S(1)}, /*index=5*/f32[17,1536]{1,0:T(8,128)}) custom-call(s32[1]{0:T(128)} %bitcast.1.me_ref, f32[168,768]{1,0:T(8,128)} %pad_maximum_fusion.15.back_ref, ...), custom_call_target="tpu_custom_call" | custom-call | flops 330000007168 | bytes 300000000 | tf_op jit(solution)/shard_map/mixer_back/pallas_call | solution.py:289
  208.6 5.2 %late.2 = f32[768,1536]{1,0:T(8,128)} custom-call(s32[1]{0:T(128)} %bitcast.later_ref.which_ref.core_ref, f32[128,1536]{1,0:T(8,128)S(1)} %copy-done.36, f32[128,1536]{1,0:T(8,128)} %get-tuple-element.246.act_ref, f32[1,1536]{1,0:T(1,128)S(1)} %reshape.127.skip_ref, f32[144,3072]{1,0:T(8,128)} %join.1.inner_ref.gate_z_ref, ...), custom_call_target="tpu_custom_call" | custom-call | flops 219999993856 | bytes 200000000 | tf_op jit(solution)/shard_map/late/pallas_call | solution.py:289
  217.4 8.1 %late.3 = (f32[768,1536]{1,0:T(8,128)}, f32[128,768]{1,0:T(8,128)S(1)}) custom-call(s32[1]{0:T(128)S(6)} %sub.76.which_ref, f32[128,1536]{1,0:T(8,128)S(1)} %copy-done.36, f32[128,1536]{1,0:T(8,128)} %get-tuple-element.246.act_ref, f32[1,1536]{1,0:T(1,128)S(1)} %reshape.127.skip_ref, f32[144,3072]{1,0:T(8,128)} %join.1.inner_ref.gate_z_ref, ...), custom_call_target="tpu_custom_call" | custom-call | flops 219999993856 | bytes 200000000 | tf_op jit(solution)/shard_map/late/pallas_call | solution.py:289
  227.3 5.2 %collective-permute-done.30.got_ref = f32[17,1536]{1,0:T(8,128)S(1)} collective-permute-done((f32[17,1536]{1,0:T(8,128)S(1)}, f32[17,1536]{1,0:T(8,128)S(1)}, u32[]{:S(2)}, u32[]{:S(2)}) %collective-permute-start.30) | collective-permute-done | bytes 104480 | tf_op jit(solution)/shard_map/ppermute | solution.py:47
  233.7 4.7 %dynamic-slice_add_fusion = (f32[192,1536]{1,0:T(8,128)S(1)}, f32[192,1536]{1,0:T(8,128)S(1)}, f32[192,1536]{1,0:T(8,128)S(1)}, f32[192,1536]{1,0:T(8,128)S(1)}) fusion(f32[768,1536]{1,0:T(8,128)} %collective-permute-done.28, s32[]{:T(128)S(6)} %select_n.396, f32[768,1536]{1,0:T(8,128)} %get-tuple-element.355, s32[]{:T(128)S(6)} %select_n.395, ...), kind=kLoop, calls=%fused_computation.13 | loop fusion | flops 1179648 | bytes 14155792 | tf_op jit(solution)/shard_map/add | solution.py:75
  243.1 5.5 %collective-permute-done.32.got_ref = f32[17,1536]{1,0:T(8,128)S(1)} collective-permute-done((f32[17,1536]{1,0:T(8,128)S(1)}, f32[17,1536]{1,0:T(8,128)S(1)}, u32[]{:S(2)}, u32[]{:S(2)}) %collective-permute-start.32) | collective-permute-done | bytes 104480 | tf_op jit(solution)/shard_map/ppermute | solution.py:47
  248.8 2.7 collective-permute-start.38
  251.5 8.5 %scan_back.3 = (f32[128,1536]{1,0:T(8,128)S(1)}, f32[128,1536]{1,0:T(8,128)}, f32[16,1536]{1,0:T(8,128)S(1)}, f32[80,128]{1,0:T(8,128)S(1)}) custom-call(f32[128,1536]{1,0:T(8,128)} %get-tuple-element.243.masked_ref, f32[128,1536]{1,0:T(8,128)} %get-tuple-element.244.steps_ref, f32[128,1536]{1,0:T(8,128)} %get-tuple-element.245.drive_ref, ...), custom_call_target="tpu_custom_call" | custom-call | flops 11000000512 | bytes 10000000 | tf_op jit(solution)/shard_map/scan_back/pallas_call | solution.py:289
  260.0 5.2 %collective-permute-done.34 = f32[192,1536]{1,0:T(8,128)S(1)} collective-permute-done((f32[192,1536]{1,0:T(8,128)S(1)}, f32[192,1536]{1,0:T(8,128)S(1)}, u32[]{:S(2)}, u32[]{:S(2)}) %collective-permute-start.34) | collective-permute-done | bytes 1179680 | tf_op jit(solution)/shard_map/ppermute | solution.py:47
  267.8 8.3 %scan_back.4 = (f32[128,1536]{1,0:T(8,128)S(1)}, f32[128,1536]{1,0:T(8,128)}, f32[16,1536]{1,0:T(8,128)S(1)}, f32[80,128]{1,0:T(8,128)S(1)}) custom-call(f32[128,1536]{1,0:T(8,128)} %get-tuple-element.243.masked_ref, f32[128,1536]{1,0:T(8,128)} %get-tuple-element.244.steps_ref, ...), custom_call_target="tpu_custom_call", output_to_operand_aliasing={{0}: (14, {}), {1}: (15, {}), {2}: (16, {})} | custom-call | flops 11000000512 | bytes 10000000 | tf_op jit(solution)/shard_map/scan_back/pallas_call | solution.py:289
  281.9 8.3 %scan_back.5 = (f32[128,1536]{1,0:T(8,128)S(1)}, f32[128,1536]{1,0:T(8,128)}, f32[16,1536]{1,0:T(8,128)S(1)}, f32[80,128]{1,0:T(8,128)S(1)}) custom-call(f32[128,1536]{1,0:T(8,128)} %get-tuple-element.243.masked_ref, f32[128,1536]{1,0:T(8,128)} %get-tuple-element.244.steps_ref, ...), custom_call_target="tpu_custom_call", output_to_operand_aliasing={{0}: (14, {}), {1}: (15, {}), {2}: (16, {})} | custom-call | flops 11000000512 | bytes 10000000 | tf_op jit(solution)/shard_map/scan_back/pallas_call | solution.py:289
  290.3 6.5 %collective-permute-done.41 = f32[192,768]{1,0:T(8,128)S(1)} collective-permute-done((f32[192,768]{1,0:T(8,128)S(1)}, f32[192,768]{1,0:T(8,128)S(1)}, u32[]{:S(2)}, u32[]{:S(2)}) %collective-permute-start.41) | collective-permute-done | bytes 589856 | tf_op jit(solution)/shard_map/ppermute | solution.py:47
  299.6 11.1 %input_back.1 = (f32[480,1536]{1,0:T(8,128)}, f32[480,1536]{1,0:T(8,128)}, f32[128,768]{1,0:T(8,128)S(1)}, f32[16,768]{1,0:T(8,128)S(1)}) custom-call(s32[1]{0:T(128)} %bitcast.later_ref.which_ref.core_ref, f32[80,128]{1,0:T(8,128)S(1)} %get-tuple-element.351.proj_a_ref, f32[80,128]{1,0:T(8,128)S(1)} %get-tuple-element.360.proj_b_ref, ...), custom_call_target="tpu_custom_call" | custom-call | flops 12099999744 | bytes 11000000 | tf_op jit(solution)/shard_map/input_back/pallas_call | solution.py:289
  313.3 5.7 %collective-permute-done.46 = f32[480,1536]{1,0:T(8,128)} collective-permute-done((f32[480,1536]{1,0:T(8,128)}, f32[480,1536]{1,0:T(8,128)}, u32[]{:S(2)}, u32[]{:S(2)}) %collective-permute-start.46) | collective-permute-done | bytes 2949152 | tf_op jit(solution)/shard_map/ppermute | solution.py:47
  319.1 4.3 dynamic-slice_add_fusion.4
  327.8 13.5 %collective-permute-done.45 = f32[192,384]{1,0:T(8,128)} collective-permute-done((f32[192,384]{1,0:T(8,128)}, f32[192,384]{1,0:T(8,128)}, u32[]{:S(2)}, u32[]{:S(2)}) %collective-permute-start.45) | collective-permute-done | bytes 294944 | tf_op jit(solution)/shard_map/ppermute | solution.py:47
  353.7 8.6 %collective-permute-done.50 = f32[60,1536]{1,0:T(8,128)S(1)} collective-permute-done((f32[60,1536]{1,0:T(8,128)S(1)}, f32[60,1536]{1,0:T(8,128)S(1)}, u32[]{:S(2)}, u32[]{:S(2)}) %collective-permute-start.50) | collective-permute-done | bytes 368672 | tf_op jit(solution)/shard_map/ppermute | solution.py:47
  372.1 2.9 collective-permute-done.57
  375.0 7.3 %collective-permute-done.56 = f32[120,384]{1,0:T(8,128)S(1)} collective-permute-done((f32[120,384]{1,0:T(8,128)S(1)}, f32[120,384]{1,0:T(8,128)S(1)}, u32[]{:S(2)}, u32[]{:S(2)}) %collective-permute-start.56) | collective-permute-done | bytes 184352 | tf_op jit(solution)/shard_map/ppermute | solution.py:47
  394.8 2.8 collective-permute-done.63
  397.5 6.3 %collective-permute-done.62 = f32[120,384]{1,0:T(8,128)S(1)} collective-permute-done((f32[120,384]{1,0:T(8,128)S(1)}, f32[120,384]{1,0:T(8,128)S(1)}, u32[]{:S(2)}, u32[]{:S(2)}) %collective-permute-start.62) | collective-permute-done | bytes 184352 | tf_op jit(solution)/shard_map/ppermute | solution.py:47
  404.0 7.7 %collective-permute-done.59 = f32[192,1536]{1,0:T(8,128)} collective-permute-done((f32[192,1536]{1,0:T(8,128)}, f32[192,1536]{1,0:T(8,128)}, u32[]{:S(2)}, u32[]{:S(2)}) %collective-permute-start.59) | collective-permute-done | bytes 1179680 | tf_op jit(solution)/shard_map/ppermute | solution.py:47
  413.7 4.4 collective-permute-done.60
  421.2 9.1 %collective-permute-done.65 = f32[60,1536]{1,0:T(8,128)S(1)} collective-permute-done((f32[60,1536]{1,0:T(8,128)S(1)}, f32[60,1536]{1,0:T(8,128)S(1)}, u32[]{:S(2)}, u32[]{:S(2)}) %collective-permute-start.65) | collective-permute-done | bytes 368672 | tf_op jit(solution)/shard_map/ppermute | solution.py:47
  433.7 7.8 %finish_late.1 = (f32[768,3072]{1,0:T(8,128)}, f32[2,768,768]{2,1,0:T(8,128)}) custom-call(s32[1]{0:T(128)} %bitcast.later_ref.which_ref.core_ref, f32[384,1536]{1,0:T(8,128)} %copy-done.37, f32[384,1536]{1,0:T(8,128)} %copy-done.38, f32[384,1536]{1,0:T(8,128)} %copy-done.58, f32[384,1536]{1,0:T(8,128)} %copy-done.59), custom_call_target="tpu_custom_call" | custom-call | flops 8800000000 | bytes 8000000 | tf_op jit(solution)/shard_map/finish_late/pallas_call | solution.py:289
  441.5 7.5 %collective-permute-done.68 = f32[120,1536]{1,0:T(8,128)S(1)} collective-permute-done((f32[120,1536]{1,0:T(8,128)S(1)}, f32[120,1536]{1,0:T(8,128)S(1)}, u32[]{:S(2)}, u32[]{:S(2)}) %collective-permute-start.68) | collective-permute-done | bytes 737312 | tf_op jit(solution)/shard_map/ppermute | solution.py:47
  450.8 2.8 collective-permute-done.70.got_first_ref
  456.8 5.9 %finish.1 = (f32[768,3072]{1,0:T(8,128)}, f32[1536,80]{1,0:T(8,128)S(1)}, f32[48,1536]{1,0:T(8,128)}, f32[1536,16]{1,0:T(8,128)S(1)}, f32[4,1536]{1,0:T(4,128)},...) custom-call(s32[1]{0:T(128)} %bitcast.later_ref.which_ref.core_ref, ...), custom_call_target="tpu_custom_call", output_to_operand_aliasing={{0}: (5, {})} | custom-call | flops 6600000000 | bytes 6000000 | tf_op jit(solution)/shard_map/finish/pallas_call | solution.py:289
  (366 shorter events, 136.5 us)
Async XLA Ops:
  3.8 32.2 %collective-permute-start.3 = (f32[384,768]{1,0:T(8,128)}, f32[384,768]{1,0:T(8,128)}, u32[]{:S(2)}, u32[]{:S(2)}) collective-permute-start(f32[384,768]{1,0:T(8,128)} %bitcast.37), channel_id=1, source_target_pairs={{0,4},{1,5},{2,6},{3,7},{4,0},{5,1},{6,2},{7,3},{8,12},{9,13},{10,... | collective-permute-start | bytes 3538952 | tf_op jit(solution)/shard_map/ppermute | solution.py:47
  23.3 25.4 %collective-permute-start.7 = (f32[160,768]{1,0:T(8,128)}, f32[160,768]{1,0:T(8,128)}, u32[]{:S(2)}, u32[]{:S(2)}) collective-permute-start(f32[160,768]{1,0:T(8,128)} %pad_maximum_fusion.16.refs_0_.refs_4_), channel_id=1, source_target_pairs={{0,16},{1,17},{2,18},{3,19},{4,20},{5,21},{6,22},{7,23},{8,24},{9,... | collective-permute-start | bytes 1474568 | tf_op jit(solution)/shard_map/ppermute | solution.py:47
  25.9 22.9 %collective-permute-start.6 = (f32[160,768]{1,0:T(8,128)}, f32[160,768]{1,0:T(8,128)}, u32[]{:S(2)}, u32[]{:S(2)}) collective-permute-start(f32[160,768]{1,0:T(8,128)} %pad_maximum_fusion.16.refs_0_.refs_4_), channel_id=1, source_target_pairs={{0,8},{1,9},{2,10},{3,11},{4,12},{5,13},{6,14},{7,15},{8,0},{9,1},... | collective-permute-start | bytes 1474568 | tf_op jit(solution)/shard_map/ppermute | solution.py:47
  60.9 38.7 %collective-permute-start.16 = (f32[768,384]{1,0:T(8,128)}, f32[768,384]{1,0:T(8,128)}, u32[]{:S(2)}, u32[]{:S(2)}) collective-permute-start(f32[768,384]{1,0:T(8,128)} %bitcast.11.refs_1_), channel_id=1, source_target_pairs={{0,4},{1,5},{2,6},{3,7},{4,0},{5,1},{6,2},{7,3},{8,12},{9,13},{10,... | collective-permute-start | bytes 3538952 | tf_op jit(solution)/shard_map/ppermute | solution.py:47
  67.2 14.3 %collective-permute-start.11 = (f32[160,768]{1,0:T(8,128)}, f32[160,768]{1,0:T(8,128)S(1)}, u32[]{:S(2)}, u32[]{:S(2)}) collective-permute-start(f32[160,768]{1,0:T(8,128)} %collective-permute-done.7.refs_2_.refs_6_), channel_id=1, source_target_pairs={{0,8},{1,9},{2,10},{3,11},{4,12},{5,13},{6,14},{7,15},{8,0},{9,1},... | collective-permute-start | bytes 1474568 | tf_op jit(solution)/shard_map/ppermute | solution.py:47
  95.8 27.0 %collective-permute-start.15 = (f32[168,768]{1,0:T(8,128)S(1)}, f32[168,768]{1,0:T(8,128)S(1)}, u32[]{:S(2)}, u32[]{:S(2)}) collective-permute-start(f32[168,768]{1,0:T(8,128)S(1)} %pad_maximum_fusion.14.refs_0_), channel_id=1, source_target_pairs={{0,16},{1,17},{2,18},{3,19},{4,20},{5,21},{6,22},{7,23},{8,24},{9,... | collective-permute-start | bytes 1548296 | tf_op jit(solution)/shard_map/ppermute | solution.py:47
  99.3 24.8 %collective-permute-start.14 = (f32[168,768]{1,0:T(8,128)S(1)}, f32[168,768]{1,0:T(8,128)S(1)}, u32[]{:S(2)}, u32[]{:S(2)}) collective-permute-start(f32[168,768]{1,0:T(8,128)S(1)} %pad_maximum_fusion.14.refs_0_), channel_id=1, source_target_pairs={{0,8},{1,9},{2,10},{3,11},{4,12},{5,13},{6,14},{7,15},{8,0},{9,1},... | collective-permute-start | bytes 1548296 | tf_op jit(solution)/shard_map/ppermute | solution.py:47
  124.1 13.0 %collective-permute-start.17 = (f32[168,768]{1,0:T(8,128)S(1)}, f32[168,768]{1,0:T(8,128)S(1)}, u32[]{:S(2)}, u32[]{:S(2)}) collective-permute-start(f32[168,768]{1,0:T(8,128)S(1)} %collective-permute-done.15.refs_0_.refs_2_), channel_id=1, source_target_pairs={{0,8},{1,9},{2,10},{3,11},{4,12},{5,13},{6,14},{7,15},{8,0},{9,1},... | collective-permute-start | bytes 1548296 | tf_op jit(solution)/shard_map/ppermute | solution.py:47
  142.8 12.2 %collective-permute-start.18 = (f32[168,768]{1,0:T(8,128)S(1)}, f32[168,768]{1,0:T(8,128)S(1)}, u32[]{:S(2)}, u32[]{:S(2)}) collective-permute-start(f32[168,768]{1,0:T(8,128)S(1)} %get-tuple-element.295), channel_id=1, source_target_pairs={{0,8},{1,9},{2,10},{3,11},{4,12},{5,13},{6,14},{7,15},{8,0},{9,1},... | collective-permute-start | bytes 1548296 | tf_op jit(solution)/shard_map/ppermute | solution.py:47
  155.0 23.2 %collective-permute-start.20 = (f32[168,768]{1,0:T(8,128)S(1)}, f32[168,768]{1,0:T(8,128)S(1)}, u32[]{:S(2)}, u32[]{:S(2)}) collective-permute-start(f32[168,768]{1,0:T(8,128)S(1)} %add.335), channel_id=1, source_target_pairs={{0,16},{1,17},{2,18},{3,19},{4,20},{5,21},{6,22},{7,23},{8,24},{9,... | collective-permute-start | bytes 1548296 | tf_op jit(solution)/shard_map/ppermute | solution.py:47
  156.2 22.1 %collective-permute-start.19 = (f32[168,768]{1,0:T(8,128)S(1)}, f32[168,768]{1,0:T(8,128)S(1)}, u32[]{:S(2)}, u32[]{:S(2)}) collective-permute-start(f32[168,768]{1,0:T(8,128)S(1)} %get-tuple-element.297), channel_id=1, source_target_pairs={{0,8},{1,9},{2,10},{3,11},{4,12},{5,13},{6,14},{7,15},{8,0},{9,1},... | collective-permute-start | bytes 1548296 | tf_op jit(solution)/shard_map/ppermute | solution.py:47
  179.6 15.9 %collective-permute-start.23 = (f32[384,384]{1,0:T(8,128)}, f32[384,384]{1,0:T(8,128)S(1)}, u32[]{:S(2)}, u32[]{:S(2)}) collective-permute-start(f32[384,384]{1,0:T(8,128)} %get-tuple-element.557), channel_id=1, source_target_pairs={{0,4},{1,5},{2,6},{3,7},{4,0},{5,1},{6,2},{7,3},{8,12},{9,13},{10,... | collective-permute-start | bytes 1769480 | tf_op jit(solution)/shard_map/ppermute | solution.py:47
  195.5 20.1 %collective-permute-start.25 = (f32[160,768]{1,0:T(8,128)}, f32[160,768]{1,0:T(8,128)}, u32[]{:S(2)}, u32[]{:S(2)}) collective-permute-start(f32[160,768]{1,0:T(8,128)} %get-tuple-element.330), channel_id=1, source_target_pairs={{0,8},{1,9},{2,10},{3,11},{4,12},{5,13},{6,14},{7,15},{8,0},{9,1},... | collective-permute-start | bytes 1474568 | tf_op jit(solution)/shard_map/ppermute | solution.py:47
  196.7 18.9 %collective-permute-start.26 = (f32[384,384]{1,0:T(8,128)}, f32[384,384]{1,0:T(8,128)}, u32[]{:S(2)}, u32[]{:S(2)}) collective-permute-start(f32[384,384]{1,0:T(8,128)} %get-tuple-element.333), channel_id=1, source_target_pairs={{0,4},{1,5},{2,6},{3,7},{4,0},{5,1},{6,2},{7,3},{8,12},{9,13},{10,... | collective-permute-start | bytes 1769480 | tf_op jit(solution)/shard_map/ppermute | solution.py:47
  208.1 18.6 %collective-permute-start.29 = (f32[192,768]{1,0:T(8,128)}, f32[192,768]{1,0:T(8,128)}, u32[]{:S(2)}, u32[]{:S(2)}) collective-permute-start(f32[192,768]{1,0:T(8,128)} %get-tuple-element.331), channel_id=1, source_target_pairs={{0,4},{1,5},{2,6},{3,7},{4,0},{5,1},{6,2},{7,3},{8,12},{9,13},{10,... | collective-permute-start | bytes 1769480 | tf_op jit(solution)/shard_map/ppermute | solution.py:47
  213.7 13.0 %collective-permute-start.28 = (f32[768,1536]{1,0:T(8,128)}, f32[768,1536]{1,0:T(8,128)}, u32[]{:S(2)}, u32[]{:S(2)}) collective-permute-start(f32[768,1536]{1,0:T(8,128)} %late.2), channel_id=1, source_target_pairs={{0,1},{1,0},{2,3},{3,2},{4,5},{5,4},{6,7},{7,6},{8,9},{9,8},{10,11... | collective-permute-start | bytes 14155784 | tf_op jit(solution)/shard_map/ppermute | solution.py:47
  238.4 26.8 %collective-permute-start.34 = (f32[192,1536]{1,0:T(8,128)S(1)}, f32[192,1536]{1,0:T(8,128)S(1)}, u32[]{:S(2)}, u32[]{:S(2)}) collective-permute-start(f32[192,1536]{1,0:T(8,128)S(1)} %get-tuple-element.513), channel_id=1, source_target_pairs={{0,2},{1,3},{2,0},{3,1},{4,6},{5,7},{6,4},{7,5},{8,10},{9,11},{10,... | collective-permute-start | bytes 3538952 | tf_op jit(solution)/shard_map/ppermute | solution.py:47
  238.7 26.5 %collective-permute-start.33 = (f32[192,1536]{1,0:T(8,128)S(1)}, f32[192,1536]{1,0:T(8,128)S(1)}, u32[]{:S(2)}, u32[]{:S(2)}) collective-permute-start(f32[192,1536]{1,0:T(8,128)S(1)} %get-tuple-element.515), channel_id=1, source_target_pairs={{0,4},{1,5},{2,6},{3,7},{4,0},{5,1},{6,2},{7,3},{8,12},{9,13},{10,... | collective-permute-start | bytes 3538952 | tf_op jit(solution)/shard_map/ppermute | solution.py:47
  248.7 31.3 %collective-permute-start.37 = (f32[160,768]{1,0:T(8,128)S(1)}, f32[160,768]{1,0:T(8,128)S(1)}, u32[]{:S(2)}, u32[]{:S(2)}) collective-permute-start(f32[160,768]{1,0:T(8,128)S(1)} %get-tuple-element.368), channel_id=1, source_target_pairs={{0,8},{1,9},{2,10},{3,11},{4,12},{5,13},{6,14},{7,15},{8,0},{9,1},... | collective-permute-start | bytes 1474568 | tf_op jit(solution)/shard_map/ppermute | solution.py:47
  248.8 31.3 %collective-permute-start.38 = (f32[160,768]{1,0:T(8,128)S(1)}, f32[160,768]{1,0:T(8,128)S(1)}, u32[]{:S(2)}, u32[]{:S(2)}) collective-permute-start(f32[160,768]{1,0:T(8,128)S(1)} %add.337), channel_id=1, source_target_pairs={{0,16},{1,17},{2,18},{3,19},{4,20},{5,21},{6,22},{7,23},{8,24},{9,... | collective-permute-start | bytes 1474568 | tf_op jit(solution)/shard_map/ppermute | solution.py:47
  265.4 13.2 %collective-permute-start.35 = (f32[96,1536]{1,0:T(8,128)S(1)}, f32[96,1536]{1,0:T(8,128)S(1)}, u32[]{:S(2)}, u32[]{:S(2)}) collective-permute-start(f32[96,1536]{1,0:T(8,128)S(1)} %get-tuple-element.527), channel_id=1, source_target_pairs={{0,2},{1,3},{2,0},{3,1},{4,6},{5,7},{6,4},{7,5},{8,10},{9,11},{10,... | collective-permute-start | bytes 1769480 | tf_op jit(solution)/shard_map/ppermute | solution.py:47
  267.2 12.7 %collective-permute-start.36 = (f32[96,1536]{1,0:T(8,128)S(1)}, f32[96,1536]{1,0:T(8,128)S(1)}, u32[]{:S(2)}, u32[]{:S(2)}) collective-permute-start(f32[96,1536]{1,0:T(8,128)S(1)} %get-tuple-element.529), channel_id=1, source_target_pairs={{0,4},{1,5},{2,6},{3,7},{4,0},{5,1},{6,2},{7,3},{8,12},{9,13},{10,... | collective-permute-start | bytes 1769480 | tf_op jit(solution)/shard_map/ppermute | solution.py:47
  281.4 15.4 %collective-permute-start.41 = (f32[192,768]{1,0:T(8,128)S(1)}, f32[192,768]{1,0:T(8,128)S(1)}, u32[]{:S(2)}, u32[]{:S(2)}) collective-permute-start(f32[192,768]{1,0:T(8,128)S(1)} %copy-done.48), channel_id=1, source_target_pairs={{0,4},{1,5},{2,6},{3,7},{4,0},{5,1},{6,2},{7,3},{8,12},{9,13},{10,... | collective-permute-start | bytes 1769480 | tf_op jit(solution)/shard_map/ppermute | solution.py:47
  296.9 15.6 %collective-permute-start.43 = (f32[192,384]{1,0:T(8,128)S(1)}, f32[192,384]{1,0:T(8,128)S(1)}, u32[]{:S(2)}, u32[]{:S(2)}) collective-permute-start(f32[192,384]{1,0:T(8,128)S(1)} %add_add_fusion.2), channel_id=1, source_target_pairs={{0,16},{1,17},{2,18},{3,19},{4,20},{5,21},{6,22},{7,23},{8,24},{9,... | collective-permute-start | bytes 884744 | tf_op jit(solution)/shard_map/ppermute | solution.py:47
  298.8 13.8 %collective-permute-start.42 = (f32[192,384]{1,0:T(8,128)S(1)}, f32[192,384]{1,0:T(8,128)S(1)}, u32[]{:S(2)}, u32[]{:S(2)}) collective-permute-start(f32[192,384]{1,0:T(8,128)S(1)} %get-tuple-element.393), channel_id=1, source_target_pairs={{0,8},{1,9},{2,10},{3,11},{4,12},{5,13},{6,14},{7,15},{8,0},{9,1},... | collective-permute-start | bytes 884744 | tf_op jit(solution)/shard_map/ppermute | solution.py:47
  323.4 18.8 %collective-permute-start.48 = (f32[120,1536]{1,0:T(8,128)}, f32[120,1536]{1,0:T(8,128)}, u32[]{:S(2)}, u32[]{:S(2)}) collective-permute-start(f32[120,1536]{1,0:T(8,128)} %get-tuple-element.517), channel_id=1, source_target_pairs={{0,2},{1,3},{2,0},{3,1},{4,6},{5,7},{6,4},{7,5},{8,10},{9,11},{10,... | collective-permute-start | bytes 2211848 | tf_op jit(solution)/shard_map/ppermute | solution.py:47
  323.9 18.6 %collective-permute-start.47 = (f32[120,1536]{1,0:T(8,128)}, f32[120,1536]{1,0:T(8,128)}, u32[]{:S(2)}, u32[]{:S(2)}) collective-permute-start(f32[120,1536]{1,0:T(8,128)} %get-tuple-element.519), channel_id=1, source_target_pairs={{0,4},{1,5},{2,6},{3,7},{4,0},{5,1},{6,2},{7,3},{8,12},{9,13},{10,... | collective-permute-start | bytes 2211848 | tf_op jit(solution)/shard_map/ppermute | solution.py:47
  325.3 16.0 %collective-permute-start.45 = (f32[192,384]{1,0:T(8,128)}, f32[192,384]{1,0:T(8,128)}, u32[]{:S(2)}, u32[]{:S(2)}) collective-permute-start(f32[192,384]{1,0:T(8,128)} %add_add_fusion.3), channel_id=1, source_target_pairs={{0,16},{1,17},{2,18},{3,19},{4,20},{5,21},{6,22},{7,23},{8,24},{9,... | collective-permute-start | bytes 884744 | tf_op jit(solution)/shard_map/ppermute | solution.py:47
  326.3 15.0 %collective-permute-start.44 = (f32[192,384]{1,0:T(8,128)}, f32[192,384]{1,0:T(8,128)}, u32[]{:S(2)}, u32[]{:S(2)}) collective-permute-start(f32[192,384]{1,0:T(8,128)} %add_add_fusion.3), channel_id=1, source_target_pairs={{0,8},{1,9},{2,10},{3,11},{4,12},{5,13},{6,14},{7,15},{8,0},{9,1},... | collective-permute-start | bytes 884744 | tf_op jit(solution)/shard_map/ppermute | solution.py:47
  342.5 10.4 %collective-permute-start.52 = (f32[16,768]{1,0:T(8,128)S(1)}, f32[16,768]{1,0:T(8,128)S(1)}, u32[]{:S(2)}, u32[]{:S(2)}) collective-permute-start(f32[16,768]{1,0:T(8,128)S(1)} %get-tuple-element.414), channel_id=1, source_target_pairs={{1,0},{2,1},{3,2},{4,3},{5,4},{6,5},{7,6},{8,7},{9,8},{10,9},{11,1... | collective-permute-start | bytes 147464 | tf_op jit(solution)/shard_map/ppermute | solution.py:51
  345.1 24.2 %collective-permute-start.58 = (f32[80,768]{1,0:T(8,128)S(1)}, f32[80,768]{1,0:T(8,128)S(1)}, u32[]{:S(2)}, u32[]{:S(2)}) collective-permute-start(f32[80,768]{1,0:T(8,128)S(1)} %pad_maximum_fusion.22), channel_id=1, source_target_pairs={{0,2},{1,3},{2,0},{3,1},{4,6},{5,7},{6,4},{7,5},{8,10},{9,11},{10,... | collective-permute-start | bytes 737288 | tf_op jit(solution)/shard_map/ppermute | solution.py:47
  347.2 15.2 %collective-permute-start.49 = (f32[192,384]{1,0:T(8,128)}, f32[192,384]{1,0:T(8,128)S(1)}, u32[]{:S(2)}, u32[]{:S(2)}) collective-permute-start(f32[192,384]{1,0:T(8,128)} %collective-permute-done.45), channel_id=1, source_target_pairs={{0,8},{1,9},{2,10},{3,11},{4,12},{5,13},{6,14},{7,15},{8,0},{9,1},... | collective-permute-start | bytes 884744 | tf_op jit(solution)/shard_map/ppermute | solution.py:47
  349.4 13.0 %collective-permute-start.50 = (f32[60,1536]{1,0:T(8,128)S(1)}, f32[60,1536]{1,0:T(8,128)S(1)}, u32[]{:S(2)}, u32[]{:S(2)}) collective-permute-start(f32[60,1536]{1,0:T(8,128)S(1)} %get-tuple-element.542), channel_id=1, source_target_pairs={{0,2},{1,3},{2,0},{3,1},{4,6},{5,7},{6,4},{7,5},{8,10},{9,11},{10,... | collective-permute-start | bytes 1105928 | tf_op jit(solution)/shard_map/ppermute | solution.py:47
  351.8 10.5 %collective-permute-start.51 = (f32[60,1536]{1,0:T(8,128)S(1)}, f32[60,1536]{1,0:T(8,128)S(1)}, u32[]{:S(2)}, u32[]{:S(2)}) collective-permute-start(f32[60,1536]{1,0:T(8,128)S(1)} %get-tuple-element.544), channel_id=1, source_target_pairs={{0,4},{1,5},{2,6},{3,7},{4,0},{5,1},{6,2},{7,3},{8,12},{9,13},{10,... | collective-permute-start | bytes 1105928 | tf_op jit(solution)/shard_map/ppermute | solution.py:47
  363.7 11.3 %collective-permute-start.57 = (f32[120,384]{1,0:T(8,128)S(1)}, f32[120,384]{1,0:T(8,128)S(1)}, u32[]{:S(2)}, u32[]{:S(2)}) collective-permute-start(f32[120,384]{1,0:T(8,128)S(1)} %get-tuple-element.540), channel_id=1, source_target_pairs={{0,24},{1,25},{2,26},{3,27},{4,28},{5,29},{6,30},{7,31},{8,16},{9,... | collective-permute-start | bytes 552968 | tf_op jit(solution)/shard_map/ppermute | solution.py:47
  365.4 16.9 %collective-permute-start.56 = (f32[120,384]{1,0:T(8,128)S(1)}, f32[120,384]{1,0:T(8,128)S(1)}, u32[]{:S(2)}, u32[]{:S(2)}) collective-permute-start(f32[120,384]{1,0:T(8,128)S(1)} %get-tuple-element.541), channel_id=1, source_target_pairs={{0,16},{1,17},{2,18},{3,19},{4,20},{5,21},{6,22},{7,23},{8,24},{9,... | collective-permute-start | bytes 552968 | tf_op jit(solution)/shard_map/ppermute | solution.py:47
  367.6 15.5 %collective-permute-start.54 = (f32[96,1536]{1,0:T(8,128)S(1)}, f32[96,1536]{1,0:T(8,128)S(1)}, u32[]{:S(2)}, u32[]{:S(2)}) collective-permute-start(f32[96,1536]{1,0:T(8,128)S(1)} %get-tuple-element.548), channel_id=1, source_target_pairs={{0,4},{1,5},{2,6},{3,7},{4,0},{5,1},{6,2},{7,3},{8,12},{9,13},{10,... | collective-permute-start | bytes 1769480 | tf_op jit(solution)/shard_map/ppermute | solution.py:47
  369.2 13.9 %collective-permute-start.53 = (f32[96,1536]{1,0:T(8,128)S(1)}, f32[96,1536]{1,0:T(8,128)S(1)}, u32[]{:S(2)}, u32[]{:S(2)}) collective-permute-start(f32[96,1536]{1,0:T(8,128)S(1)} %get-tuple-element.549), channel_id=1, source_target_pairs={{0,2},{1,3},{2,0},{3,1},{4,6},{5,7},{6,4},{7,5},{8,10},{9,11},{10,... | collective-permute-start | bytes 1769480 | tf_op jit(solution)/shard_map/ppermute | solution.py:47
  384.5 27.2 %collective-permute-start.59 = (f32[192,1536]{1,0:T(8,128)}, f32[192,1536]{1,0:T(8,128)}, u32[]{:S(2)}, u32[]{:S(2)}) collective-permute-start(f32[192,1536]{1,0:T(8,128)} %pad_maximum_fusion.7), channel_id=1, source_target_pairs={{0,4},{1,5},{2,6},{3,7},{4,0},{5,1},{6,2},{7,3},{8,12},{9,13},{10,... | collective-permute-start | bytes 3538952 | tf_op jit(solution)/shard_map/ppermute | solution.py:47
  389.3 14.6 %collective-permute-start.62 = (f32[120,384]{1,0:T(8,128)S(1)}, f32[120,384]{1,0:T(8,128)S(1)}, u32[]{:S(2)}, u32[]{:S(2)}) collective-permute-start(f32[120,384]{1,0:T(8,128)S(1)} %copy-done.44), channel_id=1, source_target_pairs={{0,16},{1,17},{2,18},{3,19},{4,20},{5,21},{6,22},{7,23},{8,24},{9,... | collective-permute-start | bytes 552968 | tf_op jit(solution)/shard_map/ppermute | solution.py:47
  390.7 13.2 %collective-permute-start.61 = (f32[120,384]{1,0:T(8,128)S(1)}, f32[120,384]{1,0:T(8,128)S(1)}, u32[]{:S(2)}, u32[]{:S(2)}) collective-permute-start(f32[120,384]{1,0:T(8,128)S(1)} %copy-done.44), channel_id=1, source_target_pairs={{0,24},{1,25},{2,26},{3,27},{4,28},{5,29},{6,30},{7,31},{8,16},{9,... | collective-permute-start | bytes 552968 | tf_op jit(solution)/shard_map/ppermute | solution.py:47
  392.5 25.5 %collective-permute-start.60 = (f32[192,1536]{1,0:T(8,128)S(1)}, f32[192,1536]{1,0:T(8,128)S(1)}, u32[]{:S(2)}, u32[]{:S(2)}) collective-permute-start(f32[192,1536]{1,0:T(8,128)S(1)} %pad_maximum_fusion.8), channel_id=1, source_target_pairs={{0,2},{1,3},{2,0},{3,1},{4,6},{5,7},{6,4},{7,5},{8,10},{9,11},{10,... | collective-permute-start | bytes 3538952 | tf_op jit(solution)/shard_map/ppermute | solution.py:47
  418.4 13.1 %collective-permute-start.66 = (f32[384,1536]{1,0:T(8,128)S(1)}, f32[384,1536]{1,0:T(8,128)S(1)}, u32[]{:S(2)}, u32[]{:S(2)}) collective-permute-start(f32[384,1536]{1,0:T(8,128)S(1)} %pad_maximum_fusion.first_ref), channel_id=1, source_target_pairs={{0,1},{1,0},{2,3},{3,2},{4,5},{5,4},{6,7},{7,6},{8,9},{9,8},{10,11... | collective-permute-start | bytes 7077896 | tf_op jit(solution)/shard_map/ppermute | solution.py:47
  418.5 13.0 %collective-permute-start.67 = (f32[384,1536]{1,0:T(8,128)S(1)}, f32[384,1536]{1,0:T(8,128)S(1)}, u32[]{:S(2)}, u32[]{:S(2)}) collective-permute-start(f32[384,1536]{1,0:T(8,128)S(1)} %pad_maximum_fusion.1.second_ref), channel_id=1, source_target_pairs={{0,1},{1,0},{2,3},{3,2},{4,5},{5,4},{6,7},{7,6},{8,9},{9,8},{10,11... | collective-permute-start | bytes 7077896 | tf_op jit(solution)/shard_map/ppermute | solution.py:47
  419.1 11.2 %collective-permute-start.65 = (f32[60,1536]{1,0:T(8,128)S(1)}, f32[60,1536]{1,0:T(8,128)S(1)}, u32[]{:S(2)}, u32[]{:S(2)}) collective-permute-start(f32[60,1536]{1,0:T(8,128)S(1)} %get-tuple-element.564), channel_id=1, source_target_pairs={{0,4},{1,5},{2,6},{3,7},{4,0},{5,1},{6,2},{7,3},{8,12},{9,13},{10,... | collective-permute-start | bytes 1105928 | tf_op jit(solution)/shard_map/ppermute | solution.py:47
  420.4 10.8 %collective-permute-start.64 = (f32[60,1536]{1,0:T(8,128)S(1)}, f32[60,1536]{1,0:T(8,128)S(1)}, u32[]{:S(2)}, u32[]{:S(2)}) collective-permute-start(f32[60,1536]{1,0:T(8,128)S(1)} %get-tuple-element.565), channel_id=1, source_target_pairs={{0,2},{1,3},{2,0},{3,1},{4,6},{5,7},{6,4},{7,5},{8,10},{9,11},{10,... | collective-permute-start | bytes 1105928 | tf_op jit(solution)/shard_map/ppermute | solution.py:47
  431.6 17.4 %collective-permute-start.68 = (f32[120,1536]{1,0:T(8,128)S(1)}, f32[120,1536]{1,0:T(8,128)S(1)}, u32[]{:S(2)}, u32[]{:S(2)}) collective-permute-start(f32[120,1536]{1,0:T(8,128)S(1)} %pad_maximum_fusion.12), channel_id=1, source_target_pairs={{0,4},{1,5},{2,6},{3,7},{4,0},{5,1},{6,2},{7,3},{8,12},{9,13},{10,... | collective-permute-start | bytes 2211848 | tf_op jit(solution)/shard_map/ppermute | solution.py:47
  432.4 17.0 %collective-permute-start.69 = (f32[120,1536]{1,0:T(8,128)S(1)}, f32[120,1536]{1,0:T(8,128)S(1)}, u32[]{:S(2)}, u32[]{:S(2)}) collective-permute-start(f32[120,1536]{1,0:T(8,128)S(1)} %pad_maximum_fusion.13), channel_id=1, source_target_pairs={{0,2},{1,3},{2,0},{3,1},{4,6},{5,7},{6,4},{7,5},{8,10},{9,11},{10,... | collective-permute-start | bytes 2211848 | tf_op jit(solution)/shard_map/ppermute | solution.py:47
  (90 other events, 806.3 us)

commit v5 on v4

--- a/solution.py
+++ b/solution.py
@@ -17,8 +17,8 @@
 NN, NT, TN = ((1,), (0,)), ((1,), (1,)), ((0,), (0,))
 VMEM_BYTES = 52 << 20
 MICROSECONDS = {
-    "route": 1, "join": 8, "features": 250, "join_states": 1, "scan": 14, "early": 7, "expert": 4.4,
-    "expert_grads": 17, "mixer_back": 300, "late": 200, "scan_back": 10, "input_back": 11, "finish_late": 8, "finish": 6,
+    "route": 1, "join": 8, "features": 250, "join_states": 1, "scan": 200, "early": 200, "expert": 60,
+    "expert_grads": 300, "mixer_back": 300, "late": 200, "scan_back": 10, "input_back": 11, "finish_late": 8, "finish": 6,
 }
 
 
@@ -186,53 +186,36 @@
     return jnp.pad(block, ((0, rows - block.shape[0]), (0, 0)))
 
 
-def send_y(grid, block, cap, tail):
-    width, slots = 2 * cap, grid.exp * cap
-    held, tails = [block[:width]], [block[slots:]]
-    for s in range(1, grid.size["y"]):
-        part = block[s * width : (s + 1) * width]
-        got = grid.swap(jnp.concatenate([part, block[slots:]], axis=0) if tail else part, "y", s)
-        held.append(got[:width])
-        tails.append(got[width:])
-    return held, tails
-
-
-def send_core(grid, held, tails, cap, tail):
+def core_first(grid, block, cap, tail):
+    ny, width = grid.size["y"], 2 * cap
+    slots = ny * width
+    send = [block[s * width + cap : (s + 1) * width] for s in range(ny)] + ([block[slots:]] if tail else [])
+    got = grid.swap(jnp.concatenate(send, axis=0), "core", 1)
+    parts = []
+    for s in range(ny):
+        rows = [block[s * width : s * width + cap], got[s * cap : (s + 1) * cap]]
+        if tail:
+            ends = [block[slots + 2 * s : slots + 2 * s + 1], got[ny * cap + 2 * s + 1 : ny * cap + 2 * s + 2]]
+            rows.append(pad_rows(jnp.concatenate(ends, axis=0), 8))
+        parts.append(jnp.concatenate(rows, axis=0))
+    return parts
+
+
+def swap_y(grid, parts):
+    return [parts[0]] + [grid.swap(part, "y", s) for s, part in enumerate(parts[1:], 1)]
+
+
+def core_last(grid, parts, cap, tail):
     ny = grid.size["y"]
-    mine, others = [h[:cap] for h in held], [h[cap:] for h in held]
+    send = [p[cap : 2 * cap] for p in parts]
     if tail:
-        others.append(pad_rows(jnp.concatenate([t[2 * s + 1 : 2 * s + 2] for s, t in enumerate(tails)], axis=0), 8))
-    got = grid.swap(jnp.concatenate(others, axis=0), "core", 1)
-    out = mine + [got[: ny * cap]]
-    if tail:
-        ends = [t[2 * s : 2 * s + 1] for s, t in enumerate(tails)] + [got[ny * cap : ny * cap + ny]]
-        out.append(pad_rows(jnp.concatenate(ends, axis=0), 8))
-    return jnp.concatenate(out, axis=0)
-
-
-def back_core(grid, block, cap, tail):
-    ny = grid.size["y"]
-    half, slots = ny * cap, 2 * ny * cap
-    send = block[half:slots]
-    if tail:
-        send = jnp.concatenate([send, pad_rows(block[slots + ny : slots + 2 * ny], 8)], axis=0)
-    return grid.swap(send, "core", 1)
-
-
-def back_y(grid, block, got, cap, tail):
-    ny = grid.size["y"]
-    half, slots = ny * cap, 2 * ny * cap
+        send.append(pad_rows(jnp.concatenate([p[2 * cap + 1 : 2 * cap + 2] for p in parts], axis=0), 8))
+    got = grid.swap(jnp.concatenate(send, axis=0), "core", 1)
     rows, ends = [], []
-    for s in range(ny):
-        pair = [block[s * cap : (s + 1) * cap], got[s * cap : (s + 1) * cap]]
-        both = [block[slots + s : slots + s + 1], got[half + s : half + s + 1]] if tail else []
-        if s:
-            if tail:
-                pair.append(pad_rows(jnp.concatenate(both, axis=0), 8))
-            back = grid.swap(jnp.concatenate(pair, axis=0), "y", s)
-            pair, both = [back[: 2 * cap]], [back[2 * cap : 2 * cap + 2]]
-        rows += pair
-        ends += both
+    for s, p in enumerate(parts):
+        rows += [p[:cap], got[s * cap : (s + 1) * cap]]
+        if tail:
+            ends += [p[2 * cap : 2 * cap + 1], got[ny * cap + s : ny * cap + s + 1]]
     if tail:
         rows.append(pad_rows(jnp.concatenate(ends, axis=0), 8))
     return jnp.concatenate(rows, axis=0)
@@ -511,14 +494,15 @@
     return 0.5 * value * (1.0 + tanh), slope
 
 
-def expert_kernel(slices, experts, cap, *refs):
-    tokens_ref, ups, pulled_ref = refs[0], refs[1 : slices + 1], refs[slices + 1]
-    back_ref, hidden_ref, grad_ref = refs[slices + 2 :]
-    slots = experts * cap
-    block, within = slot_tables(slots, cap, experts)
+def expert_kernel(parts, slices, cap, *refs):
+    tokens, ups, pulled_ref = refs[:parts], refs[parts : parts + slices], refs[parts + slices]
+    backs, hidden_ref, grad_ref = refs[parts + slices + 1 : -2], refs[-2], refs[-1]
+    width = 2 * cap
+    slots, depth = parts * width, tokens[0].shape[1]
+    block, within = slot_tables(width, cap, 2)
     within = within.astype(BF16)
-    rows = split(tokens_ref[0:slots, :])
-    back = jnp.zeros((slots, tokens_ref.shape[1]), F32)
+    rows = split(jnp.concatenate([t[0:width, :] for t in tokens], axis=0))
+    back = jnp.zeros((slots, depth), F32)
     to_gate = jnp.zeros((slots, 1), F32)
     for i in range(slices):
         up = split(ups[i][...])
@@ -529,29 +513,36 @@
         grad_ref[i] = grad
         to_gate += jnp.sum(hidden * pull, axis=1, keepdims=True)
         back += product(split(grad), up, NT)
-    back_ref[0:slots, :] = back
-    back_ref[slots:, :] = jnp.zeros((8, tokens_ref.shape[1]), F32)
-    high, low = split(block * to_gate)
-    rest = (block * to_gate - high.astype(F32) - low.astype(F32)).astype(BF16)
-    back_ref[slots:, 0:128] = dot(high, within, TN) + (dot(low, within, TN) + dot(rest, within, TN))
-
-
-def expert_grads_kernel(pieces, slices, experts, cap, *refs):
-    tokens, grads, hiddens, pulls = (refs[i * pieces : (i + 1) * pieces] for i in range(4))
-    downs, outs = refs[4 * pieces : 4 * pieces + slices], refs[4 * pieces + slices :]
+    for p in range(parts):
+        part = slice(p * width, (p + 1) * width)
+        backs[p][0:width, :] = back[part]
+        backs[p][width:, :] = jnp.zeros((8, depth), F32)
+        mine = block * to_gate[part]
+        high, low = split(mine)
+        rest = (mine - high.astype(F32) - low.astype(F32)).astype(BF16)
+        backs[p][width:, 0:128] = dot(high, within, TN) + (dot(low, within, TN) + dot(rest, within, TN))
+
+
+def expert_grads_kernel(pieces, parts, slices, cap, *refs):
+    tokens, refs = refs[: pieces * parts], refs[pieces * parts :]
+    grads, hiddens, pulls = (refs[i * pieces : (i + 1) * pieces] for i in range(3))
+    downs, outs = refs[3 * pieces : 3 * pieces + slices], refs[3 * pieces + slices :]
     results, up_outs, down_outs = outs[:pieces], outs[pieces : pieces + slices], outs[pieces + slices :]
-    slots = experts * cap
+    width = 2 * cap
     downs = [split(d[...]) for d in downs]
-    block, within = slot_tables(slots, cap, experts)
+    block, within = slot_tables(width, cap, 2)
     within = within.astype(BF16)
     for p in range(pieces):
-        ends = tokens[p][slots:, 0:128]
-        high, low = split(ends)
-        rest = (ends - high.astype(F32) - low.astype(F32)).astype(BF16)
-        spread = dot(within, high, NT) + (dot(within, low, NT) + dot(within, rest, NT))
-        gate = jnp.sum(spread * block, axis=1, keepdims=True)
-        rows = split(tokens[p][0:slots, :] * gate)
-        gated = split(grads[p][...] * gate)
+        rows, gates = [], []
+        for token in tokens[p * parts : (p + 1) * parts]:
+            ends = token[width:, 0:128]
+            high, low = split(ends)
+            rest = (ends - high.astype(F32) - low.astype(F32)).astype(BF16)
+            spread = dot(within, high, NT) + (dot(within, low, NT) + dot(within, rest, NT))
+            gates.append(jnp.sum(spread * block, axis=1, keepdims=True))
+            rows.append(token[0:width, :] * gates[-1])
+        rows = split(jnp.concatenate(rows, axis=0))
+        gated = split(grads[p][...] * jnp.concatenate(gates, axis=0))
         total = None
         for i in range(slices):
             hidden = split(hiddens[p][i])
@@ -1024,9 +1015,9 @@
         name="route",
     )
     halo, sent_grads = tie(halo, sent_grads)
-    held_grads, _ = send_y(grid, sent_grads, cap, False)
+    held_grads = core_first(grid, sent_grads, cap, False)
     up, down = expert_up[0], expert_down[0]
-    ups = [up] + [grid.swap(up, "inner", s) for s in range(1, slices)]
+    up_rows = depth // 2
     downs = [down] + [grid.swap(down, "inner", s) for s in range(1, slices)]
 
     block = lambda c, *_: (0, c)
@@ -1040,8 +1031,8 @@
         scratch=[pltpu.VMEM((ext, depth), BF16)] * 2,
         name="join",
     )
-    joined, *held_grads = tie(joined, *held_grads)
-    own_grads = send_core(grid, held_grads, None, cap, False)
+    joined, *held_grads = tie(joined, *swap_y(grid, held_grads))
+    own_grads = jnp.concatenate(held_grads, axis=0)
     joined, own_grads = tie(joined, own_grads)
     near_grads, far_grads = grid.swap(own_grads, "outer", 1), grid.swap(own_grads, "outer", 2)
     conv, act, pre, steps, masked, drive, proj, pair = call(
@@ -1072,6 +1063,7 @@
 
     start = entering(grid, pair, rate, False, {2: third})
     start, near_grads, far_grads = tie(start, held["near"], held["far"])
+    up_top = [grid.swap(up[:up_rows], "inner", s) for s in range(1, slices)]
     last_grads = grid.swap(far_grads, "outer", 1)
     tok = pl.BlockSpec((tokens, chunk), block)
     gate_half = pl.BlockSpec((ext, chunk), lambda c, *_: (0, chunks + c))
@@ -1108,7 +1100,9 @@
         name="scan",
     )
 
-    sent, last_grads = tie(sent, last_grads)
+    sent, last_grads, up_top, up_bottom = tie(sent, last_grads, up_top, up[up_rows:])
+    up_bottom = [grid.swap(up_bottom, "inner", s) for s in range(1, slices)]
+    own_tokens, last_grads = tie(core_first(grid, sent, cap, True), last_grads)
     grad_pieces = [own_grads, near_grads, far_grads, last_grads]
     pulled = call(
         functools.partial(early_kernel, pieces, slices),
@@ -1116,35 +1110,51 @@
         (*grad_pieces, *downs),
         name="early",
     )
-    own_tokens = send_core(grid, *send_y(grid, sent, cap, True), cap, True)
-    own_tokens, *pulled = tie(own_tokens, *pulled)
-    near_tokens, far_tokens = grid.swap(own_tokens, "outer", 1), grid.swap(own_tokens, "outer", 2)
+    parts = grid.size["y"]
+    outer_swap = lambda blocks, mask: [grid.swap(block, "outer", mask) for block in blocks]
+    near_first, far_first = outer_swap(own_tokens[:1], 1), outer_swap(own_tokens[:1], 2)
+    own_tokens, pulled, up_bottom = tie(swap_y(grid, own_tokens), pulled, up_bottom)
+    ups = [up] + [jnp.concatenate(pair, axis=0) for pair in zip(up_top, up_bottom)]
+    near_second, far_second = outer_swap(own_tokens[1:], 1), outer_swap(own_tokens[1:], 2)
 
     def expert(rows, pulled_rows):
-        return call(
-            functools.partial(expert_kernel, slices, experts, cap),
-            [shape(slots + 8, depth)] + [shape(slices, slots, hidden)] * 2,
-            (rows, *ups, pulled_rows),
+        *outs, hidden_rows, pull_rows = call(
+            functools.partial(expert_kernel, parts, slices, cap),
+            [shape(2 * cap + 8, depth)] * parts + [shape(slices, slots, hidden)] * 2,
+            (*rows, *ups, pulled_rows),
             name="expert",
         )
+        return outs, hidden_rows, pull_rows
 
     own_outs = expert(own_tokens, pulled[0])
-    near_tokens, far_tokens, *own_outs = tie(near_tokens, far_tokens, *own_outs)
-    last_tokens = grid.swap(far_tokens, "outer", 1)
+    near_first, far_first, own_outs = tie(near_first, far_first, own_outs)
+    last_first = outer_swap(far_first, 1)
+    near_second, far_second = tie(near_second, far_second)
+    last_second = outer_swap(far_second, 1)
+    near_tokens, far_tokens = near_first + near_second, far_first + far_second
     near_outs, far_outs = expert(near_tokens, pulled[1]), expert(far_tokens, pulled[2])
-    last_tokens, near_outs, far_outs = tie(last_tokens, near_outs, far_outs)
+    last_first, last_second, near_outs, far_outs = tie(last_first, last_second, near_outs, far_outs)
+    last_tokens = last_first + last_second
     last_outs = expert(last_tokens, pulled[3])
     token_pieces = [own_tokens, near_tokens, far_tokens, last_tokens]
     backs, hiddens, pulls = zip(own_outs, near_outs, far_outs, last_outs)
-    back_through = grid.swap(backs[3], "outer", 1)
+    back_through = outer_swap(backs[3][1:], 1)
+    back_through, last_zero = tie(back_through, backs[3][0])
+    zero_through = grid.swap(last_zero, "outer", 1)
+    back_parts = [
+        outer_reduce_rest(grid, [b[part] for b in backs], back_through[part - 1]) for part in range(1, parts)
+    ]
     outs = call(
-        functools.partial(expert_grads_kernel, pieces, slices, experts, cap),
+        functools.partial(expert_grads_kernel, pieces, parts, slices, cap),
         [shape(slots, depth)] * pieces + [shape(depth, hidden)] * slices + [shape(hidden, depth)] * slices,
-        (*token_pieces, *grad_pieces, *hiddens, *pulls, *downs),
+        (*sum(token_pieces, []), *grad_pieces, *hiddens, *pulls, *downs),
         name="expert_grads",
     )
-    back, *outs = tie(outer_reduce_rest(grid, backs, back_through), *outs)
-    back = back_y(grid, back, back_core(grid, back, cap, True), cap, True)
+    back_parts, zero_through, zero, outs = tie(back_parts, zero_through, [b[0] for b in backs], outs)
+    first_part = outer_reduce_rest(grid, zero, zero_through)
+    back_parts = swap_y(grid, [None] + back_parts)[1:]
+    first_part, back_parts = tie(first_part, back_parts)
+    back = core_last(grid, [first_part] + back_parts, cap, True)
     results, up_grads, down_grads = outs[:pieces], outs[pieces : pieces + slices], outs[pieces + slices :]
     halves = lambda array: [array[: array.shape[0] // 2], array[array.shape[0] // 2 :]]
     ups_sent, downs_sent = ([halves(g) for g in grads[1:]] for grads in (up_grads, down_grads))
@@ -1153,7 +1163,7 @@
         return [grid.swap(pair[half], "inner", s) for s, pair in enumerate(sent, 1)]
 
     up_first = inner_swaps(ups_sent, 0)
-    back, last_result, ups_sent, *up_first = tie(back, results[3], ups_sent, *up_first)
+    back, last_result, ups_sent = tie(back, results[3], ups_sent)
     through = grid.swap(last_result, "outer", 1)
     up_second = inner_swaps(ups_sent, 1)
 
@@ -1184,7 +1194,7 @@
         scratch=[lanes] + [pltpu.VMEM((tokens, depth), BF16)] * 2,
         name="mixer_back",
     )
-    back_pair, downs_sent = tie(back_pair, downs_sent)
+    back_pair, downs_sent, *up_first = tie(back_pair, downs_sent, *up_first)
     core = grid.at["core"].astype(jnp.int32).reshape(1)
     wide = pl.BlockSpec((tokens, depth), block)
 
@@ -1277,11 +1287,11 @@
     filled, late_both, near, far, downs_sent = tie(filled, late_both, near, far, held["downs"])
     down_second = inner_swaps(downs_sent, 1)
     result = results[0] + near + far
-    result_got = back_core(grid, result, cap, False)
+    result_parts = swap_y(grid, [result[p * 2 * cap : (p + 1) * 2 * cap] for p in range(parts)])
     late_cut = cut_outer(grid, late_both)
     late_through = grid.swap(late_cut[3], "outer", 1)
     grad_act, grad_pre, grad_decay, grad_proj_c = scan_back(2, filled)
-    grad_act, late_through, result_got, down_second = tie(grad_act, late_through, result_got, down_second)
+    grad_act, late_through, result_parts, down_second = tie(grad_act, late_through, result_parts, down_second)
     late_total = outer_reduce_rest(grid, late_cut, late_through)
     unit = 2 * grid.size["inner"] * grid.size["y"]
     half = -(-max(depth // 2 + 3 * states + rank_n, depth // 2 + rank_n + 40) // unit) * unit
@@ -1314,20 +1324,22 @@
     sent_got = grid.swap(sent_half, "core", 1)
     kept, sent_got = tie(kept, sent_got)
     grads_first, grads_second = sum_first(grid, [kept, sent_got])
-    late_near, late_far, grads_first, grads_second, edge, result, result_got, up_parts, down_parts = tie(
-        late_near, late_far, grads_first, grads_second, edge, result, result_got,
+    late_near, late_far, grads_first, grads_second = tie(late_near, late_far, grads_first, grads_second)
+    late_last = grid.swap(late_far, "outer", 1)
+    grads = sum_second(grid, grads_first, grads_second)
+    late_last, grads, edge, result_parts, up_parts, down_parts = tie(
+        late_last, grads, edge, result_parts,
         [up_grads[0], up_first, up_second], [down_grads[0], held["down_first"], down_second],
     )
     from_next = grid.along(edge, -1)
     input_grad = jnp.concatenate([input_grad[: tokens - HALO], input_grad[tokens - HALO :] + from_next], axis=0)
     grad_up, grad_down = with_others(*up_parts), with_others(*down_parts)
-    late_last = grid.swap(late_far, "outer", 1)
-    grads = sum_second(grid, grads_first, grads_second)
-    late_last, grads, input_grad = tie(late_last, grads, input_grad)
-    result = back_y(grid, result, result_got, cap, False)
+    result = core_last(grid, result_parts, cap, False)
     late_first, late_second = spread_second(grid, join_outer(grid, late_total, late_near, late_far, late_last))
     grads = sum_outer(grid, grads)
-    late_first, late_second, grads, result, grad_up = tie(late_first, late_second, grads, result, grad_up)
+    late_first, late_second, grads, result, grad_up, input_grad = tie(
+        late_first, late_second, grads, result, grad_up, input_grad
+    )
     combined = jnp.dot(table.T, result.astype(F32), precision=lax.Precision.HIGHEST, preferred_element_type=F32)
     block_output = resid + gate * combined
     late_first, late_second = gather_rows(grid, late_first, "inner"), gather_rows(grid, late_second, "y")

time: 474 us -> 462 us (0.975)
  waiting for transfers between devices: 185 us -> 159 us
  starting transfers between devices: 77.5 us -> 85.3 us
    ppermute x70 -> x77, waiting for transfers between devices: 185 us -> 159 us  [swap_bits(): return lax.ppermute(block, AXES, [(i, i ^ bits) for i in range(self.total)])]
    ppermute x70 -> x77, starting transfers between devices: 73.6 us -> 81.4 us  [swap_bits(): return lax.ppermute(block, AXES, [(i, i ^ bits) for i in range(self.total)])]
    unnamed x135 -> x177, local copies, waits for them, and re-layouts: 10.9 us -> 15.4 us
  transfers between devices with their start and end apart: 72 -> 79, of which waited for: 41 -> 40; matrix products, arithmetic and copies ran while one was open for 7% -> 7% of each run, Pallas kernels for 30% -> 31%
where the time goes in v5:
time: 462 us; the launch traced here: 455 us
  waiting for transfers between devices  159 us (34%)
  Pallas kernels  151 us (33%)
  starting transfers between devices  85.3 us (18%)
  other arithmetic  33.1 us (7%)
  local copies, waits for them, and re-layouts  22.6 us (5%)
    ppermute x77, waiting for transfers between devices, swap_bits(): return lax.ppermute(block, AXES, [(i, i ^ bits) for i in range(self.total)])  159 us
    pallas_call x29, Pallas kernels, call(): pl.pallas_call(kernel, out_shape=outs, grid=grid or (), in_specs=in_specs...  151 us
    ppermute x77, starting transfers between devices, swap_bits(): return lax.ppermute(block, AXES, [(i, i ^ bits) for i in range(self.total)])  81.4 us
    unnamed x177, local copies, waits for them, and re-layouts  15.4 us
    add x6, other arithmetic, rows_of(): functools.reduce(jnp.add, [lax.dynamic_slice_in_dim(part, first, rows, 0)...  12.3 us
  transfers between devices with their start and end apart: 79, of which 40 were waited for; matrix products, arithmetic and copies ran while one was open for 7% of the time, Pallas kernels for 31%

profile of v5, /device:TPU:0, one launch (start us, length us, event | category | flops | bytes accessed | tf_op | source)
XLA Modules:
  0.0 455.1 jit_solution(4557548401742997906)
XLA Ops:
  14.9 7.8 %join.1.inner_ref.gate_z_ref = f32[144,3072]{1,0:T(8,128)} custom-call(f32[128,768]{1,0:T(8,128)S(1)} %copy-done.22, f32[16,768]{1,0:T(8,128)S(1)} %collective-permute-done.halo_ref, f32[1,768]{1,0:T(1,128)S(1)} %reshape.122.gain_ref, f32[768,3072]{1,0:T(8,128)} %weight_ref.3), custom_call_target="tpu_custom_call" | custom-call | flops 8800000000 | bytes 8000000 | tf_op jit(solution)/shard_map/join/pallas_call | solution.py:272
  26.9 8.3 %features.1 = (f32[128,1536]{1,0:T(8,128)S(1)}, f32[128,1536]{1,0:T(8,128)}, f32[128,1536]{1,0:T(8,128)}, f32[128,1536]{1,0:T(8,128)}, f32[128,1536]{1,0:T(8,128...) custom-call(f32[144,3072]{1,0:T(8,128)} %join.1.inner_ref.gate_z_ref, ...), custom_call_target="tpu_custom_call" | custom-call | flops 275000000512 | bytes 250000000 | tf_op jit(solution)/shard_map/features/pallas_call | solution.py:272
  39.7 4.4 collective-permute-done.5.got_ref
  44.1 4.6 %collective-permute-done.7.refs_2_.refs_10_ = f32[160,768]{1,0:T(8,128)} collective-permute-done((f32[160,768]{1,0:T(8,128)}, f32[160,768]{1,0:T(8,128)}, u32[]{:S(2)}, u32[]{:S(2)}) %collective-permute-start.7) | collective-permute-done | bytes 491552 | tf_op jit(solution)/shard_map/ppermute | solution.py:47
  49.4 4.7 %collective-permute-done.8.got_ref = f32[17,1536]{1,0:T(8,128)S(1)} collective-permute-done((f32[17,1536]{1,0:T(8,128)S(1)}, f32[17,1536]{1,0:T(8,128)S(1)}, u32[]{:S(2)}, u32[]{:S(2)}) %collective-permute-start.8) | collective-permute-done | bytes 104480 | tf_op jit(solution)/shard_map/ppermute | solution.py:47
  55.6 3.7 collective-permute-done.9.got_ref
  63.6 3.6 collective-permute-done.10.got_ref
  68.2 14.2 %scan.1 = (f32[128,1536]{1,0:T(8,128)}, f32[128,16,1536]{2,1,0:T(8,128)}, f32[128,768]{1,0:T(8,128)S(1)}, f32[168,768]{1,0:T(8,128)S(1)}, f32[128,8]{1,0:T(8,128)S(1)}, /*index=5*/f32[128,1]{1,0:T(8,128)S(1)}) custom-call(s32[1]{0:T(128)} %bitcast.1.me_ref, f32[128,1536]{1,0:T(8,128)} %get-tuple-element.271.masked_ref, ...), custom_call_target="tpu_custom_call" | custom-call | flops 219999993856 | bytes 200000000 | tf_op jit(solution)/shard_map/scan/pallas_call | solution.py:272
  86.4 3.3 collective-permute-start.15
  91.1 6.8 %early.1 = (f32[2,160,384]{2,1,0:T(8,128)S(1)}, f32[2,160,384]{2,1,0:T(8,128)S(1)}, f32[2,160,384]{2,1,0:T(8,128)S(1)}, f32[2,160,384]{2,1,0:T(8,128)S(1)}) custom-call(f32[160,768]{1,0:T(8,128)} %pad_maximum_fusion.14.refs_0_.refs_8_, f32[160,768]{1,0:T(8,128)} %collective-permute-done.6.refs_1_.refs_9_, ...), custom_call_target="tpu_custom_call" | custom-call | flops 219999993856 | bytes 200000000 | tf_op jit(solution)/shard_map/early/pallas_call | solution.py:272
  104.0 4.6 %expert.4 = (f32[88,768]{1,0:T(8,128)S(1)}, f32[88,768]{1,0:T(8,128)S(1)}, f32[2,160,384]{2,1,0:T(8,128)S(1)}, f32[2,160,384]{2,1,0:T(8,128)}) custom-call(f32[88,768]{1,0:T(8,128)} %get-tuple-element.309.refs_0_, f32[88,768]{1,0:T(8,128)} %collective-permute-done.16.refs_1_, f32[768,384]{1,0:T(8,128)} %bitcast.39, f32[768,384]{1,0:T(8,128)} %copy-done.71, ...), custom_call_target="tpu_custom_call" | custom-call | flops 65999998976 | bytes 60000000 | tf_op jit(solution)/shard_map/expert/pallas_call | solution.py:272
  110.6 3.7 collective-permute-done.20.refs_1_.refs_5_
  116.5 4.5 expert.6
  121.0 5.4 %expert.5 = (f32[88,768]{1,0:T(8,128)S(1)}, f32[88,768]{1,0:T(8,128)}, f32[2,160,384]{2,1,0:T(8,128)S(1)}, f32[2,160,384]{2,1,0:T(8,128)}) custom-call(f32[88,768]{1,0:T(8,128)} %collective-permute-done.14.refs_0_.refs_2_, f32[88,768]{1,0:T(8,128)S(1)} %collective-permute-done.19.refs_1_.refs_3_, f32[768,384]{1,0:T(8,128)} %bitcast.41, ...), custom_call_target="tpu_custom_call" | custom-call | flops 65999998976 | bytes 60000000 | tf_op jit(solution)/shard_map/expert/pallas_call | solution.py:272
  127.2 5.6 %expert.7 = (f32[88,768]{1,0:T(8,128)}, f32[88,768]{1,0:T(8,128)S(1)}, f32[2,160,384]{2,1,0:T(8,128)S(1)}, f32[2,160,384]{2,1,0:T(8,128)}) custom-call(f32[88,768]{1,0:T(8,128)S(1)} %collective-permute-done.18.refs_0_.refs_6_, f32[88,768]{1,0:T(8,128)S(1)} %collective-permute-done.21.refs_1_.refs_7_, f32[768,384]{1,0:T(8,128)} %bitcast.42, ...), custom_call_target="tpu_custom_call" | custom-call | flops 65999998976 | bytes 60000000 | tf_op jit(solution)/shard_map/expert/pallas_call | solution.py:272
  134.4 5.7 %collective-permute-done.22 = f32[88,768]{1,0:T(8,128)S(1)} collective-permute-done((f32[88,768]{1,0:T(8,128)S(1)}, f32[88,768]{1,0:T(8,128)S(1)}, u32[]{:S(2)}, u32[]{:S(2)}) %collective-permute-start.22) | collective-permute-done | bytes 270368 | tf_op jit(solution)/shard_map/ppermute | solution.py:47
  144.4 17.5 %expert_grads.1 = (f32[160,768]{1,0:T(8,128)}, f32[160,768]{1,0:T(8,128)}, f32[160,768]{1,0:T(8,128)}, f32[160,768]{1,0:T(8,128)}, f32[768,384]{1,0:T(8,128)}, /...) custom-call(f32[88,768]{1,0:T(8,128)} %get-tuple-element.309.refs_0_, ...), custom_call_target="tpu_custom_call" | custom-call | flops 330000007168 | bytes 300000000 | tf_op jit(solution)/shard_map/expert_grads/pallas_call | solution.py:272
  168.1 8.8 %collective-permute-done.27 = f32[88,768]{1,0:T(8,128)S(1)} collective-permute-done((f32[88,768]{1,0:T(8,128)S(1)}, f32[88,768]{1,0:T(8,128)S(1)}, u32[]{:S(2)}, u32[]{:S(2)}) %collective-permute-start.27) | collective-permute-done | bytes 270368 | tf_op jit(solution)/shard_map/ppermute | solution.py:47
  182.0 9.6 %mixer_back.1 = (f32[128,768]{1,0:T(8,128)S(1)}, f32[16,768]{1,0:T(8,128)S(1)}, f32[128,1536]{1,0:T(8,128)}, f32[128,1536]{1,0:T(8,128)}, f32[1,1536]{1,0:T(1,128)S(1)}, /*index=5*/f32[17,1536]{1,0:T(8,128)}) custom-call(s32[1]{0:T(128)} %bitcast.1.me_ref, f32[168,768]{1,0:T(8,128)} %copy-done.74, bf16[160,128]{1,0:T(8,128)(2,1)S(1)} %copy-done.16, ...), custom_call_target="tpu_custom_call" | custom-call | flops 330000007168 | bytes 300000000 | tf_op jit(solution)/shard_map/mixer_back/pallas_call | solution.py:272
  191.6 3.3 collective-permute-done.30
  195.0 5.2 %late.2 = f32[768,1536]{1,0:T(8,128)} custom-call(s32[1]{0:T(128)} %bitcast.later_ref.which_ref.core_ref, f32[128,1536]{1,0:T(8,128)S(1)} %copy-done.56, f32[128,1536]{1,0:T(8,128)} %get-tuple-element.274.act_ref, f32[1,1536]{1,0:T(1,128)S(1)} %copy-done.21, f32[144,3072]{1,0:T(8,128)} %join.1.inner_ref.gate_z_ref, ...), custom_call_target="tpu_custom_call" | custom-call | flops 219999993856 | bytes 200000000 | tf_op jit(solution)/shard_map/late/pallas_call | solution.py:272
  202.9 4.6 %collective-permute-done.33 = f32[384,384]{1,0:T(8,128)} collective-permute-done((f32[384,384]{1,0:T(8,128)}, f32[384,384]{1,0:T(8,128)}, u32[]{:S(2)}, u32[]{:S(2)}) %collective-permute-start.33) | collective-permute-done | bytes 589856 | tf_op jit(solution)/shard_map/ppermute | solution.py:47
  208.3 8.1 %late.3 = (f32[768,1536]{1,0:T(8,128)}, f32[128,768]{1,0:T(8,128)S(1)}) custom-call(s32[1]{0:T(128)S(6)} %sub.76.which_ref, f32[128,1536]{1,0:T(8,128)S(1)} %copy-done.56, f32[128,1536]{1,0:T(8,128)} %get-tuple-element.274.act_ref, f32[1,1536]{1,0:T(1,128)S(1)} %copy-done.21, f32[144,3072]{1,0:T(8,128)} %join.1.inner_ref.gate_z_ref, ...), custom_call_target="tpu_custom_call" | custom-call | flops 219999993856 | bytes 200000000 | tf_op jit(solution)/shard_map/late/pallas_call | solution.py:272
  220.4 4.9 %collective-permute-done.37.got_ref = f32[17,1536]{1,0:T(8,128)S(1)} collective-permute-done((f32[17,1536]{1,0:T(8,128)S(1)}, f32[17,1536]{1,0:T(8,128)S(1)}, u32[]{:S(2)}, u32[]{:S(2)}) %collective-permute-start.37) | collective-permute-done | bytes 104480 | tf_op jit(solution)/shard_map/ppermute | solution.py:47
  225.4 4.7 %dynamic-slice_add_fusion = (f32[192,1536]{1,0:T(8,128)S(1)}, f32[192,1536]{1,0:T(8,128)S(1)}, f32[192,1536]{1,0:T(8,128)S(1)}, f32[192,1536]{1,0:T(8,128)S(1)}) fusion(f32[768,1536]{1,0:T(8,128)} %collective-permute-done.35, s32[]{:T(128)S(6)} %select_n.396, f32[768,1536]{1,0:T(8,128)} %get-tuple-element.410, s32[]{:T(128)S(6)} %select_n.395, ...), kind=kLoop, calls=%fused_computation.13 | loop fusion | flops 1179648 | bytes 14155792 | tf_op jit(solution)/shard_map/add | solution.py:75
  232.9 3.3 collective-permute-start.39
  237.4 4.0 collective-permute-done.39.got_ref
  241.5 3.0 collective-permute-start.45
  244.6 8.5 %scan_back.3 = (f32[128,1536]{1,0:T(8,128)S(1)}, f32[128,1536]{1,0:T(8,128)}, f32[16,1536]{1,0:T(8,128)S(1)}, f32[80,128]{1,0:T(8,128)S(1)}) custom-call(f32[128,1536]{1,0:T(8,128)} %get-tuple-element.271.masked_ref, f32[128,1536]{1,0:T(8,128)} %get-tuple-element.272.steps_ref, f32[128,1536]{1,0:T(8,128)} %get-tuple-element.273.drive_ref, ...), custom_call_target="tpu_custom_call" | custom-call | flops 11000000512 | bytes 10000000 | tf_op jit(solution)/shard_map/scan_back/pallas_call | solution.py:272
  253.0 3.8 collective-permute-done.41
  260.0 8.2 %scan_back.4 = (f32[128,1536]{1,0:T(8,128)S(1)}, f32[128,1536]{1,0:T(8,128)}, f32[16,1536]{1,0:T(8,128)S(1)}, f32[80,128]{1,0:T(8,128)S(1)}) custom-call(f32[128,1536]{1,0:T(8,128)} %get-tuple-element.271.masked_ref, f32[128,1536]{1,0:T(8,128)} %get-tuple-element.272.steps_ref, ...), custom_call_target="tpu_custom_call", output_to_operand_aliasing={{0}: (14, {}), {1}: (15, {}), {2}: (16, {})} | custom-call | flops 11000000512 | bytes 10000000 | tf_op jit(solution)/shard_map/scan_back/pallas_call | solution.py:272
  268.4 2.9 collective-permute-done.42
  276.2 8.3 %scan_back.5 = (f32[128,1536]{1,0:T(8,128)S(1)}, f32[128,1536]{1,0:T(8,128)}, f32[16,1536]{1,0:T(8,128)S(1)}, f32[80,128]{1,0:T(8,128)S(1)}) custom-call(f32[128,1536]{1,0:T(8,128)} %get-tuple-element.271.masked_ref, f32[128,1536]{1,0:T(8,128)} %get-tuple-element.272.steps_ref, ...), custom_call_target="tpu_custom_call", output_to_operand_aliasing={{0}: (14, {}), {1}: (15, {}), {2}: (16, {})} | custom-call | flops 11000000512 | bytes 10000000 | tf_op jit(solution)/shard_map/scan_back/pallas_call | solution.py:272
  289.8 11.1 %input_back.1 = (f32[480,1536]{1,0:T(8,128)}, f32[480,1536]{1,0:T(8,128)}, f32[128,768]{1,0:T(8,128)S(1)}, f32[16,768]{1,0:T(8,128)S(1)}) custom-call(s32[1]{0:T(128)} %bitcast.later_ref.which_ref.core_ref, f32[80,128]{1,0:T(8,128)S(1)} %get-tuple-element.406.proj_a_ref, f32[80,128]{1,0:T(8,128)S(1)} %get-tuple-element.415.proj_b_ref, ...), custom_call_target="tpu_custom_call" | custom-call | flops 12099999744 | bytes 11000000 | tf_op jit(solution)/shard_map/input_back/pallas_call | solution.py:272
  301.1 5.7 %collective-permute-done.53 = f32[480,1536]{1,0:T(8,128)} collective-permute-done((f32[480,1536]{1,0:T(8,128)}, f32[480,1536]{1,0:T(8,128)}, u32[]{:S(2)}, u32[]{:S(2)}) %collective-permute-start.53) | collective-permute-done | bytes 2949152 | tf_op jit(solution)/shard_map/ppermute | solution.py:47
  306.8 4.3 dynamic-slice_add_fusion.4
  314.4 14.0 %collective-permute-done.52 = f32[192,384]{1,0:T(8,128)} collective-permute-done((f32[192,384]{1,0:T(8,128)S(1)}, f32[192,384]{1,0:T(8,128)}, u32[]{:S(2)}, u32[]{:S(2)}) %collective-permute-start.52) | collective-permute-done | bytes 294944 | tf_op jit(solution)/shard_map/ppermute | solution.py:47
  336.1 7.3 %collective-permute-done.57 = f32[60,1536]{1,0:T(8,128)S(1)} collective-permute-done((f32[60,1536]{1,0:T(8,128)}, f32[60,1536]{1,0:T(8,128)S(1)}, u32[]{:S(2)}, u32[]{:S(2)}) %collective-permute-start.57) | collective-permute-done | bytes 368672 | tf_op jit(solution)/shard_map/ppermute | solution.py:47
  359.3 8.2 %collective-permute-done.62 = f32[120,384]{1,0:T(8,128)S(1)} collective-permute-done((f32[120,384]{1,0:T(8,128)S(1)}, f32[120,384]{1,0:T(8,128)S(1)}, u32[]{:S(2)}, u32[]{:S(2)}) %collective-permute-start.62) | collective-permute-done | bytes 184352 | tf_op jit(solution)/shard_map/ppermute | solution.py:47
  367.7 3.2 collective-permute-done.60
  374.0 2.8 maximum_add_fusion.1
  383.5 9.5 %collective-permute-done.69 = f32[120,384]{1,0:T(8,128)S(1)} collective-permute-done((f32[120,384]{1,0:T(8,128)S(1)}, f32[120,384]{1,0:T(8,128)S(1)}, u32[]{:S(2)}, u32[]{:S(2)}) %collective-permute-start.69) | collective-permute-done | bytes 184352 | tf_op jit(solution)/shard_map/ppermute | solution.py:47
  393.2 5.6 %collective-permute-done.66 = f32[192,1536]{1,0:T(8,128)} collective-permute-done((f32[192,1536]{1,0:T(8,128)S(1)}, f32[192,1536]{1,0:T(8,128)}, u32[]{:S(2)}, u32[]{:S(2)}) %collective-permute-start.66) | collective-permute-done | bytes 1179680 | tf_op jit(solution)/shard_map/ppermute | solution.py:47
  400.4 5.6 %collective-permute-done.67 = f32[192,1536]{1,0:T(8,128)S(1)} collective-permute-done((f32[192,1536]{1,0:T(8,128)S(1)}, f32[192,1536]{1,0:T(8,128)S(1)}, u32[]{:S(2)}, u32[]{:S(2)}) %collective-permute-start.67) | collective-permute-done | bytes 1179680 | tf_op jit(solution)/shard_map/ppermute | solution.py:47
  409.1 9.1 %collective-permute-done.72 = f32[60,1536]{1,0:T(8,128)S(1)} collective-permute-done((f32[60,1536]{1,0:T(8,128)S(1)}, f32[60,1536]{1,0:T(8,128)S(1)}, u32[]{:S(2)}, u32[]{:S(2)}) %collective-permute-start.72) | collective-permute-done | bytes 368672 | tf_op jit(solution)/shard_map/ppermute | solution.py:47
  421.5 7.8 %finish_late.1 = (f32[768,3072]{1,0:T(8,128)}, f32[2,768,768]{2,1,0:T(8,128)}) custom-call(s32[1]{0:T(128)} %bitcast.later_ref.which_ref.core_ref, f32[384,1536]{1,0:T(8,128)} %copy-done.57, f32[384,1536]{1,0:T(8,128)} %copy-done.58, f32[384,1536]{1,0:T(8,128)} %copy-done.81, f32[384,1536]{1,0:T(8,128)} %copy-done.82), custom_call_target="tpu_custom_call" | custom-call | flops 8800000000 | bytes 8000000 | tf_op jit(solution)/shard_map/finish_late/pallas_call | solution.py:272
  429.3 7.2 %collective-permute-done.75 = f32[120,1536]{1,0:T(8,128)S(1)} collective-permute-done((f32[120,1536]{1,0:T(8,128)S(1)}, f32[120,1536]{1,0:T(8,128)S(1)}, u32[]{:S(2)}, u32[]{:S(2)}) %collective-permute-start.75) | collective-permute-done | bytes 737312 | tf_op jit(solution)/shard_map/ppermute | solution.py:47
  444.5 5.9 %finish.1 = (f32[768,3072]{1,0:T(8,128)}, f32[1536,80]{1,0:T(8,128)S(1)}, f32[48,1536]{1,0:T(8,128)}, f32[1536,16]{1,0:T(8,128)S(1)}, f32[4,1536]{1,0:T(4,128)},...) custom-call(s32[1]{0:T(128)} %bitcast.later_ref.which_ref.core_ref, ...), custom_call_target="tpu_custom_call", output_to_operand_aliasing={{0}: (5, {})} | custom-call | flops 6600000000 | bytes 6000000 | tf_op jit(solution)/shard_map/finish/pallas_call | solution.py:272
  (422 shorter events, 145.2 us)
Async XLA Ops:
  3.8 32.3 %collective-permute-start.3 = (f32[384,768]{1,0:T(8,128)}, f32[384,768]{1,0:T(8,128)}, u32[]{:S(2)}, u32[]{:S(2)}) collective-permute-start(f32[384,768]{1,0:T(8,128)} %bitcast.45), channel_id=1, source_target_pairs={{0,4},{1,5},{2,6},{3,7},{4,0},{5,1},{6,2},{7,3},{8,12},{9,13},{10,... | collective-permute-start | bytes 3538952 | tf_op jit(solution)/shard_map/ppermute | solution.py:47
  23.6 25.1 %collective-permute-start.7 = (f32[160,768]{1,0:T(8,128)}, f32[160,768]{1,0:T(8,128)}, u32[]{:S(2)}, u32[]{:S(2)}) collective-permute-start(f32[160,768]{1,0:T(8,128)} %pad_maximum_fusion.14.refs_0_.refs_8_), channel_id=1, source_target_pairs={{0,16},{1,17},{2,18},{3,19},{4,20},{5,21},{6,22},{7,23},{8,24},{9,... | collective-permute-start | bytes 1474568 | tf_op jit(solution)/shard_map/ppermute | solution.py:47
  26.2 22.7 %collective-permute-start.6 = (f32[160,768]{1,0:T(8,128)}, f32[160,768]{1,0:T(8,128)}, u32[]{:S(2)}, u32[]{:S(2)}) collective-permute-start(f32[160,768]{1,0:T(8,128)} %pad_maximum_fusion.14.refs_0_.refs_8_), channel_id=1, source_target_pairs={{0,8},{1,9},{2,10},{3,11},{4,12},{5,13},{6,14},{7,15},{8,0},{9,1},... | collective-permute-start | bytes 1474568 | tf_op jit(solution)/shard_map/ppermute | solution.py:47
  61.9 20.6 %collective-permute-start.12 = (f32[384,384]{1,0:T(8,128)}, f32[384,384]{1,0:T(8,128)}, u32[]{:S(2)}, u32[]{:S(2)}) collective-permute-start(f32[384,384]{1,0:T(8,128)} %get-tuple-element.615), channel_id=1, source_target_pairs={{0,4},{1,5},{2,6},{3,7},{4,0},{5,1},{6,2},{7,3},{8,12},{9,13},{10,... | collective-permute-start | bytes 1769480 | tf_op jit(solution)/shard_map/ppermute | solution.py:47
  67.2 15.2 %collective-permute-start.11 = (f32[160,768]{1,0:T(8,128)}, f32[160,768]{1,0:T(8,128)}, u32[]{:S(2)}, u32[]{:S(2)}) collective-permute-start(f32[160,768]{1,0:T(8,128)} %collective-permute-done.7.refs_2_.refs_10_), channel_id=1, source_target_pairs={{0,8},{1,9},{2,10},{3,11},{4,12},{5,13},{6,14},{7,15},{8,0},{9,1},... | collective-permute-start | bytes 1474568 | tf_op jit(solution)/shard_map/ppermute | solution.py:47
  82.6 16.9 %collective-permute-start.17 = (f32[384,384]{1,0:T(8,128)}, f32[384,384]{1,0:T(8,128)}, u32[]{:S(2)}, u32[]{:S(2)}) collective-permute-start(f32[384,384]{1,0:T(8,128)} %get-tuple-element.308), channel_id=1, source_target_pairs={{0,4},{1,5},{2,6},{3,7},{4,0},{5,1},{6,2},{7,3},{8,12},{9,13},{10,... | collective-permute-start | bytes 1769480 | tf_op jit(solution)/shard_map/ppermute | solution.py:47
  86.4 23.0 %collective-permute-start.15 = (f32[88,768]{1,0:T(8,128)}, f32[88,768]{1,0:T(8,128)}, u32[]{:S(2)}, u32[]{:S(2)}) collective-permute-start(f32[88,768]{1,0:T(8,128)} %get-tuple-element.309.refs_0_), channel_id=1, source_target_pairs={{0,16},{1,17},{2,18},{3,19},{4,20},{5,21},{6,22},{7,23},{8,24},{9,... | collective-permute-start | bytes 811016 | tf_op jit(solution)/shard_map/ppermute | solution.py:47
  89.7 19.7 %collective-permute-start.14 = (f32[88,768]{1,0:T(8,128)}, f32[88,768]{1,0:T(8,128)}, u32[]{:S(2)}, u32[]{:S(2)}) collective-permute-start(f32[88,768]{1,0:T(8,128)} %get-tuple-element.309.refs_0_), channel_id=1, source_target_pairs={{0,8},{1,9},{2,10},{3,11},{4,12},{5,13},{6,14},{7,15},{8,0},{9,1},... | collective-permute-start | bytes 811016 | tf_op jit(solution)/shard_map/ppermute | solution.py:47
  99.5 14.8 %collective-permute-start.20 = (f32[88,768]{1,0:T(8,128)}, f32[88,768]{1,0:T(8,128)S(1)}, u32[]{:S(2)}, u32[]{:S(2)}) collective-permute-start(f32[88,768]{1,0:T(8,128)} %collective-permute-done.16.refs_1_), channel_id=1, source_target_pairs={{0,16},{1,17},{2,18},{3,19},{4,20},{5,21},{6,22},{7,23},{8,24},{9,... | collective-permute-start | bytes 811016 | tf_op jit(solution)/shard_map/ppermute | solution.py:47
  101.1 15.0 %collective-permute-start.19 = (f32[88,768]{1,0:T(8,128)}, f32[88,768]{1,0:T(8,128)S(1)}, u32[]{:S(2)}, u32[]{:S(2)}) collective-permute-start(f32[88,768]{1,0:T(8,128)} %collective-permute-done.16.refs_1_), channel_id=1, source_target_pairs={{0,8},{1,9},{2,10},{3,11},{4,12},{5,13},{6,14},{7,15},{8,0},{9,1},... | collective-permute-start | bytes 811016 | tf_op jit(solution)/shard_map/ppermute | solution.py:47
  109.4 17.7 %collective-permute-start.18 = (f32[88,768]{1,0:T(8,128)}, f32[88,768]{1,0:T(8,128)S(1)}, u32[]{:S(2)}, u32[]{:S(2)}) collective-permute-start(f32[88,768]{1,0:T(8,128)} %collective-permute-done.15.refs_0_.refs_4_), channel_id=1, source_target_pairs={{0,8},{1,9},{2,10},{3,11},{4,12},{5,13},{6,14},{7,15},{8,0},{9,1},... | collective-permute-start | bytes 811016 | tf_op jit(solution)/shard_map/ppermute | solution.py:47
  140.8 21.1 %collective-permute-start.24 = (f32[88,768]{1,0:T(8,128)}, f32[88,768]{1,0:T(8,128)}, u32[]{:S(2)}, u32[]{:S(2)}) collective-permute-start(f32[88,768]{1,0:T(8,128)} %add.342), channel_id=1, source_target_pairs={{0,16},{1,17},{2,18},{3,19},{4,20},{5,21},{6,22},{7,23},{8,24},{9,... | collective-permute-start | bytes 811016 | tf_op jit(solution)/shard_map/ppermute | solution.py:47
  142.4 19.5 %collective-permute-start.23 = (f32[88,768]{1,0:T(8,128)}, f32[88,768]{1,0:T(8,128)}, u32[]{:S(2)}, u32[]{:S(2)}) collective-permute-start(f32[88,768]{1,0:T(8,128)} %get-tuple-element.340), channel_id=1, source_target_pairs={{0,8},{1,9},{2,10},{3,11},{4,12},{5,13},{6,14},{7,15},{8,0},{9,1},... | collective-permute-start | bytes 811016 | tf_op jit(solution)/shard_map/ppermute | solution.py:47
  143.9 19.1 %collective-permute-start.25 = (f32[88,768]{1,0:T(8,128)}, f32[88,768]{1,0:T(8,128)}, u32[]{:S(2)}, u32[]{:S(2)}) collective-permute-start(f32[88,768]{1,0:T(8,128)} %get-tuple-element.343), channel_id=1, source_target_pairs={{0,8},{1,9},{2,10},{3,11},{4,12},{5,13},{6,14},{7,15},{8,0},{9,1},... | collective-permute-start | bytes 811016 | tf_op jit(solution)/shard_map/ppermute | solution.py:47
  164.2 12.7 %collective-permute-start.27 = (f32[88,768]{1,0:T(8,128)S(1)}, f32[88,768]{1,0:T(8,128)S(1)}, u32[]{:S(2)}, u32[]{:S(2)}) collective-permute-start(f32[88,768]{1,0:T(8,128)S(1)} %add.345), channel_id=1, source_target_pairs={{0,16},{1,17},{2,18},{3,19},{4,20},{5,21},{6,22},{7,23},{8,24},{9,... | collective-permute-start | bytes 811016 | tf_op jit(solution)/shard_map/ppermute | solution.py:47
  165.6 11.3 %collective-permute-start.26 = (f32[88,768]{1,0:T(8,128)S(1)}, f32[88,768]{1,0:T(8,128)S(1)}, u32[]{:S(2)}, u32[]{:S(2)}) collective-permute-start(f32[88,768]{1,0:T(8,128)S(1)} %get-tuple-element.366), channel_id=1, source_target_pairs={{0,8},{1,9},{2,10},{3,11},{4,12},{5,13},{6,14},{7,15},{8,0},{9,1},... | collective-permute-start | bytes 811016 | tf_op jit(solution)/shard_map/ppermute | solution.py:47
  178.4 16.5 %collective-permute-start.30 = (f32[384,384]{1,0:T(8,128)}, f32[384,384]{1,0:T(8,128)}, u32[]{:S(2)}, u32[]{:S(2)}) collective-permute-start(f32[384,384]{1,0:T(8,128)} %get-tuple-element.613), channel_id=1, source_target_pairs={{0,4},{1,5},{2,6},{3,7},{4,0},{5,1},{6,2},{7,3},{8,12},{9,13},{10,... | collective-permute-start | bytes 1769480 | tf_op jit(solution)/shard_map/ppermute | solution.py:47
  180.2 22.7 %collective-permute-start.32 = (f32[160,768]{1,0:T(8,128)}, f32[160,768]{1,0:T(8,128)}, u32[]{:S(2)}, u32[]{:S(2)}) collective-permute-start(f32[160,768]{1,0:T(8,128)} %get-tuple-element.385), channel_id=1, source_target_pairs={{0,8},{1,9},{2,10},{3,11},{4,12},{5,13},{6,14},{7,15},{8,0},{9,1},... | collective-permute-start | bytes 1474568 | tf_op jit(solution)/shard_map/ppermute | solution.py:47
  181.1 26.5 %collective-permute-start.33 = (f32[384,384]{1,0:T(8,128)}, f32[384,384]{1,0:T(8,128)}, u32[]{:S(2)}, u32[]{:S(2)}) collective-permute-start(f32[384,384]{1,0:T(8,128)} %get-tuple-element.388), channel_id=1, source_target_pairs={{0,4},{1,5},{2,6},{3,7},{4,0},{5,1},{6,2},{7,3},{8,12},{9,13},{10,... | collective-permute-start | bytes 1769480 | tf_op jit(solution)/shard_map/ppermute | solution.py:47
  200.1 19.7 %collective-permute-start.35 = (f32[768,1536]{1,0:T(8,128)}, f32[768,1536]{1,0:T(8,128)}, u32[]{:S(2)}, u32[]{:S(2)}) collective-permute-start(f32[768,1536]{1,0:T(8,128)} %late.2), channel_id=1, source_target_pairs={{0,1},{1,0},{2,3},{3,2},{4,5},{5,4},{6,7},{7,6},{8,9},{9,8},{10,11... | collective-permute-start | bytes 14155784 | tf_op jit(solution)/shard_map/ppermute | solution.py:47
  200.7 19.1 %collective-permute-start.36 = (f32[192,768]{1,0:T(8,128)}, f32[192,768]{1,0:T(8,128)}, u32[]{:S(2)}, u32[]{:S(2)}) collective-permute-start(f32[192,768]{1,0:T(8,128)} %get-tuple-element.386), channel_id=1, source_target_pairs={{0,4},{1,5},{2,6},{3,7},{4,0},{5,1},{6,2},{7,3},{8,12},{9,13},{10,... | collective-permute-start | bytes 1769480 | tf_op jit(solution)/shard_map/ppermute | solution.py:47
  230.1 26.7 %collective-permute-start.41 = (f32[192,1536]{1,0:T(8,128)S(1)}, f32[192,1536]{1,0:T(8,128)S(1)}, u32[]{:S(2)}, u32[]{:S(2)}) collective-permute-start(f32[192,1536]{1,0:T(8,128)S(1)} %get-tuple-element.569), channel_id=1, source_target_pairs={{0,2},{1,3},{2,0},{3,1},{4,6},{5,7},{6,4},{7,5},{8,10},{9,11},{10,... | collective-permute-start | bytes 3538952 | tf_op jit(solution)/shard_map/ppermute | solution.py:47
  231.3 26.6 %collective-permute-start.40 = (f32[192,1536]{1,0:T(8,128)S(1)}, f32[192,1536]{1,0:T(8,128)S(1)}, u32[]{:S(2)}, u32[]{:S(2)}) collective-permute-start(f32[192,1536]{1,0:T(8,128)S(1)} %get-tuple-element.571), channel_id=1, source_target_pairs={{0,4},{1,5},{2,6},{3,7},{4,0},{5,1},{6,2},{7,3},{8,12},{9,13},{10,... | collective-permute-start | bytes 3538952 | tf_op jit(solution)/shard_map/ppermute | solution.py:47
  241.5 30.4 %collective-permute-start.44 = (f32[160,768]{1,0:T(8,128)}, f32[160,768]{1,0:T(8,128)S(1)}, u32[]{:S(2)}, u32[]{:S(2)}) collective-permute-start(f32[160,768]{1,0:T(8,128)} %get-tuple-element.423), channel_id=1, source_target_pairs={{0,8},{1,9},{2,10},{3,11},{4,12},{5,13},{6,14},{7,15},{8,0},{9,1},... | collective-permute-start | bytes 1474568 | tf_op jit(solution)/shard_map/ppermute | solution.py:47
  241.5 30.3 %collective-permute-start.45 = (f32[160,768]{1,0:T(8,128)S(1)}, f32[160,768]{1,0:T(8,128)S(1)}, u32[]{:S(2)}, u32[]{:S(2)}) collective-permute-start(f32[160,768]{1,0:T(8,128)S(1)} %add.347), channel_id=1, source_target_pairs={{0,16},{1,17},{2,18},{3,19},{4,20},{5,21},{6,22},{7,23},{8,24},{9,... | collective-permute-start | bytes 1474568 | tf_op jit(solution)/shard_map/ppermute | solution.py:47
  258.1 13.1 %collective-permute-start.42 = (f32[96,1536]{1,0:T(8,128)S(1)}, f32[96,1536]{1,0:T(8,128)S(1)}, u32[]{:S(2)}, u32[]{:S(2)}) collective-permute-start(f32[96,1536]{1,0:T(8,128)S(1)} %get-tuple-element.583), channel_id=1, source_target_pairs={{0,2},{1,3},{2,0},{3,1},{4,6},{5,7},{6,4},{7,5},{8,10},{9,11},{10,... | collective-permute-start | bytes 1769480 | tf_op jit(solution)/shard_map/ppermute | solution.py:47
  259.0 12.8 %collective-permute-start.43 = (f32[96,1536]{1,0:T(8,128)S(1)}, f32[96,1536]{1,0:T(8,128)S(1)}, u32[]{:S(2)}, u32[]{:S(2)}) collective-permute-start(f32[96,1536]{1,0:T(8,128)S(1)} %get-tuple-element.585), channel_id=1, source_target_pairs={{0,4},{1,5},{2,6},{3,7},{4,0},{5,1},{6,2},{7,3},{8,12},{9,13},{10,... | collective-permute-start | bytes 1769480 | tf_op jit(solution)/shard_map/ppermute | solution.py:47
  272.0 12.5 %collective-permute-start.47 = (f32[80,768]{1,0:T(8,128)S(1)}, f32[80,768]{1,0:T(8,128)S(1)}, u32[]{:S(2)}, u32[]{:S(2)}) collective-permute-start(f32[80,768]{1,0:T(8,128)S(1)} %get-tuple-element.633), channel_id=1, source_target_pairs={{0,2},{1,3},{2,0},{3,1},{4,6},{5,7},{6,4},{7,5},{8,10},{9,11},{10,... | collective-permute-start | bytes 737288 | tf_op jit(solution)/shard_map/ppermute | solution.py:47
  286.4 14.5 %collective-permute-start.50 = (f32[192,384]{1,0:T(8,128)S(1)}, f32[192,384]{1,0:T(8,128)S(1)}, u32[]{:S(2)}, u32[]{:S(2)}) collective-permute-start(f32[192,384]{1,0:T(8,128)S(1)} %add_add_fusion.1), channel_id=1, source_target_pairs={{0,16},{1,17},{2,18},{3,19},{4,20},{5,21},{6,22},{7,23},{8,24},{9,... | collective-permute-start | bytes 884744 | tf_op jit(solution)/shard_map/ppermute | solution.py:47
  288.1 12.7 %collective-permute-start.49 = (f32[192,384]{1,0:T(8,128)S(1)}, f32[192,384]{1,0:T(8,128)S(1)}, u32[]{:S(2)}, u32[]{:S(2)}) collective-permute-start(f32[192,384]{1,0:T(8,128)S(1)} %get-tuple-element.448), channel_id=1, source_target_pairs={{0,8},{1,9},{2,10},{3,11},{4,12},{5,13},{6,14},{7,15},{8,0},{9,1},... | collective-permute-start | bytes 884744 | tf_op jit(solution)/shard_map/ppermute | solution.py:47
  311.1 18.7 %collective-permute-start.55 = (f32[120,1536]{1,0:T(8,128)}, f32[120,1536]{1,0:T(8,128)S(1)}, u32[]{:S(2)}, u32[]{:S(2)}) collective-permute-start(f32[120,1536]{1,0:T(8,128)} %get-tuple-element.573), channel_id=1, source_target_pairs={{0,2},{1,3},{2,0},{3,1},{4,6},{5,7},{6,4},{7,5},{8,10},{9,11},{10,... | collective-permute-start | bytes 2211848 | tf_op jit(solution)/shard_map/ppermute | solution.py:47
  311.8 18.6 %collective-permute-start.54 = (f32[120,1536]{1,0:T(8,128)}, f32[120,1536]{1,0:T(8,128)}, u32[]{:S(2)}, u32[]{:S(2)}) collective-permute-start(f32[120,1536]{1,0:T(8,128)} %get-tuple-element.575), channel_id=1, source_target_pairs={{0,4},{1,5},{2,6},{3,7},{4,0},{5,1},{6,2},{7,3},{8,12},{9,13},{10,... | collective-permute-start | bytes 2211848 | tf_op jit(solution)/shard_map/ppermute | solution.py:47
  312.8 15.7 %collective-permute-start.52 = (f32[192,384]{1,0:T(8,128)S(1)}, f32[192,384]{1,0:T(8,128)}, u32[]{:S(2)}, u32[]{:S(2)}) collective-permute-start(f32[192,384]{1,0:T(8,128)S(1)} %add_add_fusion.2), channel_id=1, source_target_pairs={{0,16},{1,17},{2,18},{3,19},{4,20},{5,21},{6,22},{7,23},{8,24},{9,... | collective-permute-start | bytes 884744 | tf_op jit(solution)/shard_map/ppermute | solution.py:47
  313.1 15.4 %collective-permute-start.51 = (f32[192,384]{1,0:T(8,128)S(1)}, f32[192,384]{1,0:T(8,128)}, u32[]{:S(2)}, u32[]{:S(2)}) collective-permute-start(f32[192,384]{1,0:T(8,128)S(1)} %add_add_fusion.2), channel_id=1, source_target_pairs={{0,8},{1,9},{2,10},{3,11},{4,12},{5,13},{6,14},{7,15},{8,0},{9,1},... | collective-permute-start | bytes 884744 | tf_op jit(solution)/shard_map/ppermute | solution.py:47
  344.9 11.5 %collective-permute-start.65 = (f32[16,768]{1,0:T(8,128)S(1)}, f32[16,768]{1,0:T(8,128)S(1)}, u32[]{:S(2)}, u32[]{:S(2)}) collective-permute-start(f32[16,768]{1,0:T(8,128)S(1)} %get-tuple-element.479), channel_id=1, source_target_pairs={{1,0},{2,1},{3,2},{4,3},{5,4},{6,5},{7,6},{8,7},{9,8},{10,9},{11,1... | collective-permute-start | bytes 147464 | tf_op jit(solution)/shard_map/ppermute | solution.py:51
  346.5 21.1 %collective-permute-start.64 = (f32[80,768]{1,0:T(8,128)S(1)}, f32[80,768]{1,0:T(8,128)S(1)}, u32[]{:S(2)}, u32[]{:S(2)}) collective-permute-start(f32[80,768]{1,0:T(8,128)S(1)} %pad_maximum_fusion.24), channel_id=1, source_target_pairs={{0,1},{1,0},{2,3},{3,2},{4,5},{5,4},{6,7},{7,6},{8,9},{9,8},{10,11... | collective-permute-start | bytes 737288 | tf_op jit(solution)/shard_map/ppermute | solution.py:47
  349.7 17.8 %collective-permute-start.62 = (f32[120,384]{1,0:T(8,128)S(1)}, f32[120,384]{1,0:T(8,128)S(1)}, u32[]{:S(2)}, u32[]{:S(2)}) collective-permute-start(f32[120,384]{1,0:T(8,128)S(1)} %get-tuple-element.597), channel_id=1, source_target_pairs={{0,16},{1,17},{2,18},{3,19},{4,20},{5,21},{6,22},{7,23},{8,24},{9,... | collective-permute-start | bytes 552968 | tf_op jit(solution)/shard_map/ppermute | solution.py:47
  356.4 14.4 %collective-permute-start.60 = (f32[96,1536]{1,0:T(8,128)S(1)}, f32[96,1536]{1,0:T(8,128)S(1)}, u32[]{:S(2)}, u32[]{:S(2)}) collective-permute-start(f32[96,1536]{1,0:T(8,128)S(1)} %get-tuple-element.604), channel_id=1, source_target_pairs={{0,4},{1,5},{2,6},{3,7},{4,0},{5,1},{6,2},{7,3},{8,12},{9,13},{10,... | collective-permute-start | bytes 1769480 | tf_op jit(solution)/shard_map/ppermute | solution.py:47
  358.2 14.1 %collective-permute-start.59 = (f32[96,1536]{1,0:T(8,128)S(1)}, f32[96,1536]{1,0:T(8,128)S(1)}, u32[]{:S(2)}, u32[]{:S(2)}) collective-permute-start(f32[96,1536]{1,0:T(8,128)S(1)} %get-tuple-element.605), channel_id=1, source_target_pairs={{0,2},{1,3},{2,0},{3,1},{4,6},{5,7},{6,4},{7,5},{8,10},{9,11},{10,... | collective-permute-start | bytes 1769480 | tf_op jit(solution)/shard_map/ppermute | solution.py:47
  372.7 26.0 %collective-permute-start.66 = (f32[192,1536]{1,0:T(8,128)S(1)}, f32[192,1536]{1,0:T(8,128)}, u32[]{:S(2)}, u32[]{:S(2)}) collective-permute-start(f32[192,1536]{1,0:T(8,128)S(1)} %pad_maximum_fusion.7), channel_id=1, source_target_pairs={{0,4},{1,5},{2,6},{3,7},{4,0},{5,1},{6,2},{7,3},{8,12},{9,13},{10,... | collective-permute-start | bytes 3538952 | tf_op jit(solution)/shard_map/ppermute | solution.py:47
  378.4 14.6 %collective-permute-start.69 = (f32[120,384]{1,0:T(8,128)S(1)}, f32[120,384]{1,0:T(8,128)S(1)}, u32[]{:S(2)}, u32[]{:S(2)}) collective-permute-start(f32[120,384]{1,0:T(8,128)S(1)} %add_add_fusion.5), channel_id=1, source_target_pairs={{0,16},{1,17},{2,18},{3,19},{4,20},{5,21},{6,22},{7,23},{8,24},{9,... | collective-permute-start | bytes 552968 | tf_op jit(solution)/shard_map/ppermute | solution.py:47
  378.7 14.3 %collective-permute-start.68 = (f32[120,384]{1,0:T(8,128)S(1)}, f32[120,384]{1,0:T(8,128)S(1)}, u32[]{:S(2)}, u32[]{:S(2)}) collective-permute-start(f32[120,384]{1,0:T(8,128)S(1)} %add_add_fusion.5), channel_id=1, source_target_pairs={{0,24},{1,25},{2,26},{3,27},{4,28},{5,29},{6,30},{7,31},{8,16},{9,... | collective-permute-start | bytes 552968 | tf_op jit(solution)/shard_map/ppermute | solution.py:47
  381.2 24.9 %collective-permute-start.67 = (f32[192,1536]{1,0:T(8,128)S(1)}, f32[192,1536]{1,0:T(8,128)S(1)}, u32[]{:S(2)}, u32[]{:S(2)}) collective-permute-start(f32[192,1536]{1,0:T(8,128)S(1)} %pad_maximum_fusion.8), channel_id=1, source_target_pairs={{0,2},{1,3},{2,0},{3,1},{4,6},{5,7},{6,4},{7,5},{8,10},{9,11},{10,... | collective-permute-start | bytes 3538952 | tf_op jit(solution)/shard_map/ppermute | solution.py:47
  406.4 12.7 %collective-permute-start.73 = (f32[384,1536]{1,0:T(8,128)S(1)}, f32[384,1536]{1,0:T(8,128)S(1)}, u32[]{:S(2)}, u32[]{:S(2)}) collective-permute-start(f32[384,1536]{1,0:T(8,128)S(1)} %pad_maximum_fusion.first_ref), channel_id=1, source_target_pairs={{0,1},{1,0},{2,3},{3,2},{4,5},{5,4},{6,7},{7,6},{8,9},{9,8},{10,11... | collective-permute-start | bytes 7077896 | tf_op jit(solution)/shard_map/ppermute | solution.py:47
  406.5 12.7 %collective-permute-start.74 = (f32[384,1536]{1,0:T(8,128)S(1)}, f32[384,1536]{1,0:T(8,128)S(1)}, u32[]{:S(2)}, u32[]{:S(2)}) collective-permute-start(f32[384,1536]{1,0:T(8,128)S(1)} %pad_maximum_fusion.1.second_ref), channel_id=1, source_target_pairs={{0,1},{1,0},{2,3},{3,2},{4,5},{5,4},{6,7},{7,6},{8,9},{9,8},{10,11... | collective-permute-start | bytes 7077896 | tf_op jit(solution)/shard_map/ppermute | solution.py:47
  407.0 11.2 %collective-permute-start.72 = (f32[60,1536]{1,0:T(8,128)S(1)}, f32[60,1536]{1,0:T(8,128)S(1)}, u32[]{:S(2)}, u32[]{:S(2)}) collective-permute-start(f32[60,1536]{1,0:T(8,128)S(1)} %get-tuple-element.622), channel_id=1, source_target_pairs={{0,4},{1,5},{2,6},{3,7},{4,0},{5,1},{6,2},{7,3},{8,12},{9,13},{10,... | collective-permute-start | bytes 1105928 | tf_op jit(solution)/shard_map/ppermute | solution.py:47
  419.1 17.4 %collective-permute-start.75 = (f32[120,1536]{1,0:T(8,128)S(1)}, f32[120,1536]{1,0:T(8,128)S(1)}, u32[]{:S(2)}, u32[]{:S(2)}) collective-permute-start(f32[120,1536]{1,0:T(8,128)S(1)} %pad_maximum_fusion.12), channel_id=1, source_target_pairs={{0,4},{1,5},{2,6},{3,7},{4,0},{5,1},{6,2},{7,3},{8,12},{9,13},{10,... | collective-permute-start | bytes 2211848 | tf_op jit(solution)/shard_map/ppermute | solution.py:47
  420.4 17.0 %collective-permute-start.76 = (f32[120,1536]{1,0:T(8,128)S(1)}, f32[120,1536]{1,0:T(8,128)S(1)}, u32[]{:S(2)}, u32[]{:S(2)}) collective-permute-start(f32[120,1536]{1,0:T(8,128)S(1)} %pad_maximum_fusion.13), channel_id=1, source_target_pairs={{0,2},{1,3},{2,0},{3,1},{4,6},{5,7},{6,4},{7,5},{8,10},{9,11},{10,... | collective-permute-start | bytes 2211848 | tf_op jit(solution)/shard_map/ppermute | solution.py:47
  (116 other events, 925.1 us)

commit v6 on v5

--- a/solution.py
+++ b/solution.py
@@ -1333,23 +1333,22 @@
     )
     from_next = grid.along(edge, -1)
     input_grad = jnp.concatenate([input_grad[: tokens - HALO], input_grad[tokens - HALO :] + from_next], axis=0)
-    grad_up, grad_down = with_others(*up_parts), with_others(*down_parts)
+    grad_up = with_others(*up_parts)
     result = core_last(grid, result_parts, cap, False)
     late_first, late_second = spread_second(grid, join_outer(grid, late_total, late_near, late_far, late_last))
     grads = sum_outer(grid, grads)
-    late_first, late_second, grads, result, grad_up, input_grad = tie(
-        late_first, late_second, grads, result, grad_up, input_grad
-    )
+    late_first, late_second, grads, grad_up = tie(late_first, late_second, grads, grad_up)
+    late_first, late_second = gather_rows(grid, late_first, "inner"), gather_rows(grid, late_second, "y")
+    grads = spread_outer(grid, grads)
+    late_first, late_second, grads, result, input_grad = tie(late_first, late_second, grads, result, input_grad)
     combined = jnp.dot(table.T, result.astype(F32), precision=lax.Precision.HIGHEST, preferred_element_type=F32)
     block_output = resid + gate * combined
-    late_first, late_second = gather_rows(grid, late_first, "inner"), gather_rows(grid, late_second, "y")
-    grads = spread_outer(grid, grads)
-    late_first, late_second, grads, block_output, grad_down = tie(
-        late_first, late_second, grads, block_output, grad_down
-    )
     late_other = [grid.swap(late_first, "core", 1), grid.swap(late_second, "core", 1)]
     grads_first, grads_second = spread_second(grid, grads)
-    grads_first, grads_second, *late_other = tie(grads_first, grads_second, *late_other)
+    grads_first, grads_second, down_parts, block_output, *late_other = tie(
+        grads_first, grads_second, down_parts, block_output, *late_other
+    )
+    grad_down = with_others(*down_parts)
     grads_first, grads_second = gather_rows(grid, grads_first, "inner"), gather_rows(grid, grads_second, "y")
     quarter = pl.BlockSpec((half // 2, chunk), block)
     late_rows = full(depth // 2, width)
@@ -1365,7 +1364,7 @@
         ],
         name="finish_late",
     )
-    grads_first, grads_second, grad_in_proj = tie(grads_first, grads_second, grad_in_proj)
+    grads_first, grads_second, grad_in_proj, grad_down = tie(grads_first, grads_second, grad_in_proj, grad_down)
     grads_other = [grid.swap(grads_first, "core", 1), grid.swap(grads_second, "core", 1)]
     tall = lambda columns: pl.BlockSpec((chunk, columns), lambda c: (c, 0))
     (

time: 462 us -> 456 us (0.987)
  waiting for transfers between devices: 159 us -> 150 us
    ppermute x77, waiting for transfers between devices: 159 us -> 150 us  [swap_bits(): return lax.ppermute(block, AXES, [(i, i ^ bits) for i in range(self.total)])]
    unnamed x177 -> x175, local copies, waits for them, and re-layouts: 15.4 us -> 15.2 us
  transfers between devices with their start and end apart: 79 -> 79, of which waited for: 40 -> 40; matrix products, arithmetic and copies ran while one was open for 7% -> 8% of each run, Pallas kernels for 31% -> 31%
where the time goes in v6:
time: 456 us; the launch traced here: 449 us
  Pallas kernels  151 us (33%)
  waiting for transfers between devices  150 us (33%)
  starting transfers between devices  84.5 us (19%)
  other arithmetic  37.1 us (8%)
  local copies, waits for them, and re-layouts  22.4 us (5%)
    pallas_call x29, Pallas kernels, call(): pl.pallas_call(kernel, out_shape=outs, grid=grid or (), in_specs=in_specs...  151 us
    ppermute x77, waiting for transfers between devices, swap_bits(): return lax.ppermute(block, AXES, [(i, i ^ bits) for i in range(self.total)])  150 us
    ppermute x77, starting transfers between devices, swap_bits(): return lax.ppermute(block, AXES, [(i, i ^ bits) for i in range(self.total)])  80.9 us
    unnamed x175, local copies, waits for them, and re-layouts  15.2 us
    add x6, other arithmetic, rows_of(): functools.reduce(jnp.add, [lax.dynamic_slice_in_dim(part, first, rows, 0)...  13.4 us
  transfers between devices with their start and end apart: 79, of which 40 were waited for; matrix products, arithmetic and copies ran while one was open for 8% of the time, Pallas kernels for 31%

profile of v6, /device:TPU:0, one launch (start us, length us, event | category | flops | bytes accessed | tf_op | source)
XLA Modules:
  0.0 449.0 jit_solution(14734448280994340586)
XLA Ops:
  14.9 7.8 %join.1.inner_ref.gate_z_ref = f32[144,3072]{1,0:T(8,128)} custom-call(f32[128,768]{1,0:T(8,128)S(1)} %copy-done.22, f32[16,768]{1,0:T(8,128)S(1)} %collective-permute-done.halo_ref, f32[1,768]{1,0:T(1,128)S(1)} %reshape.122.gain_ref, f32[768,3072]{1,0:T(8,128)} %weight_ref.3), custom_call_target="tpu_custom_call" | custom-call | flops 8800000000 | bytes 8000000 | tf_op jit(solution)/shard_map/join/pallas_call | solution.py:272
  26.9 8.4 %features.1 = (f32[128,1536]{1,0:T(8,128)S(1)}, f32[128,1536]{1,0:T(8,128)}, f32[128,1536]{1,0:T(8,128)}, f32[128,1536]{1,0:T(8,128)}, f32[128,1536]{1,0:T(8,128...) custom-call(f32[144,3072]{1,0:T(8,128)} %join.1.inner_ref.gate_z_ref, ...), custom_call_target="tpu_custom_call" | custom-call | flops 275000000512 | bytes 250000000 | tf_op jit(solution)/shard_map/features/pallas_call | solution.py:272
  39.7 4.4 collective-permute-done.5.got_ref
  44.1 4.6 %collective-permute-done.7.refs_2_.refs_10_ = f32[160,768]{1,0:T(8,128)} collective-permute-done((f32[160,768]{1,0:T(8,128)}, f32[160,768]{1,0:T(8,128)}, u32[]{:S(2)}, u32[]{:S(2)}) %collective-permute-start.7) | collective-permute-done | bytes 491552 | tf_op jit(solution)/shard_map/ppermute | solution.py:47
  49.4 4.7 %collective-permute-done.8.got_ref = f32[17,1536]{1,0:T(8,128)S(1)} collective-permute-done((f32[17,1536]{1,0:T(8,128)S(1)}, f32[17,1536]{1,0:T(8,128)S(1)}, u32[]{:S(2)}, u32[]{:S(2)}) %collective-permute-start.8) | collective-permute-done | bytes 104480 | tf_op jit(solution)/shard_map/ppermute | solution.py:47
  55.6 3.7 collective-permute-done.9.got_ref
  63.6 3.6 collective-permute-done.10.got_ref
  68.3 14.1 %scan.1 = (f32[128,1536]{1,0:T(8,128)}, f32[128,16,1536]{2,1,0:T(8,128)}, f32[128,768]{1,0:T(8,128)S(1)}, f32[168,768]{1,0:T(8,128)S(1)}, f32[128,8]{1,0:T(8,128)S(1)}, /*index=5*/f32[128,1]{1,0:T(8,128)S(1)}) custom-call(s32[1]{0:T(128)} %bitcast.1.me_ref, f32[128,1536]{1,0:T(8,128)} %get-tuple-element.274.masked_ref, ...), custom_call_target="tpu_custom_call" | custom-call | flops 219999993856 | bytes 200000000 | tf_op jit(solution)/shard_map/scan/pallas_call | solution.py:272
  86.4 3.2 collective-permute-start.15
  91.1 6.8 %early.1 = (f32[2,160,384]{2,1,0:T(8,128)S(1)}, f32[2,160,384]{2,1,0:T(8,128)S(1)}, f32[2,160,384]{2,1,0:T(8,128)S(1)}, f32[2,160,384]{2,1,0:T(8,128)S(1)}) custom-call(f32[160,768]{1,0:T(8,128)} %pad_maximum_fusion.14.refs_0_.refs_8_, f32[160,768]{1,0:T(8,128)} %collective-permute-done.6.refs_1_.refs_9_, ...), custom_call_target="tpu_custom_call" | custom-call | flops 219999993856 | bytes 200000000 | tf_op jit(solution)/shard_map/early/pallas_call | solution.py:272
  104.0 4.6 %expert.4 = (f32[88,768]{1,0:T(8,128)S(1)}, f32[88,768]{1,0:T(8,128)S(1)}, f32[2,160,384]{2,1,0:T(8,128)S(1)}, f32[2,160,384]{2,1,0:T(8,128)}) custom-call(f32[88,768]{1,0:T(8,128)} %get-tuple-element.312.refs_0_, f32[88,768]{1,0:T(8,128)} %collective-permute-done.16.refs_1_, f32[768,384]{1,0:T(8,128)} %bitcast.39, f32[768,384]{1,0:T(8,128)} %copy-done.68, ...), custom_call_target="tpu_custom_call" | custom-call | flops 65999998976 | bytes 60000000 | tf_op jit(solution)/shard_map/expert/pallas_call | solution.py:272
  110.5 3.7 collective-permute-done.20.refs_1_.refs_5_
  116.4 4.5 %expert.6 = (f32[88,768]{1,0:T(8,128)S(1)}, f32[88,768]{1,0:T(8,128)S(1)}, f32[2,160,384]{2,1,0:T(8,128)S(1)}, f32[2,160,384]{2,1,0:T(8,128)}) custom-call(f32[88,768]{1,0:T(8,128)} %collective-permute-done.15.refs_0_.refs_4_, f32[88,768]{1,0:T(8,128)S(1)} %collective-permute-done.20.refs_1_.refs_5_, f32[768,384]{1,0:T(8,128)} %bitcast.40, ...), custom_call_target="tpu_custom_call" | custom-call | flops 65999998976 | bytes 60000000 | tf_op jit(solution)/shard_map/expert/pallas_call | solution.py:272
  120.9 5.4 %expert.5 = (f32[88,768]{1,0:T(8,128)S(1)}, f32[88,768]{1,0:T(8,128)}, f32[2,160,384]{2,1,0:T(8,128)S(1)}, f32[2,160,384]{2,1,0:T(8,128)}) custom-call(f32[88,768]{1,0:T(8,128)} %collective-permute-done.14.refs_0_.refs_2_, f32[88,768]{1,0:T(8,128)S(1)} %collective-permute-done.19.refs_1_.refs_3_, f32[768,384]{1,0:T(8,128)} %bitcast.41, ...), custom_call_target="tpu_custom_call" | custom-call | flops 65999998976 | bytes 60000000 | tf_op jit(solution)/shard_map/expert/pallas_call | solution.py:272
  127.1 5.6 %expert.7 = (f32[88,768]{1,0:T(8,128)}, f32[88,768]{1,0:T(8,128)S(1)}, f32[2,160,384]{2,1,0:T(8,128)S(1)}, f32[2,160,384]{2,1,0:T(8,128)}) custom-call(f32[88,768]{1,0:T(8,128)S(1)} %collective-permute-done.18.refs_0_.refs_6_, f32[88,768]{1,0:T(8,128)S(1)} %collective-permute-done.21.refs_1_.refs_7_, f32[768,384]{1,0:T(8,128)} %bitcast.42, ...), custom_call_target="tpu_custom_call" | custom-call | flops 65999998976 | bytes 60000000 | tf_op jit(solution)/shard_map/expert/pallas_call | solution.py:272
  134.2 5.8 %collective-permute-done.22 = f32[88,768]{1,0:T(8,128)S(1)} collective-permute-done((f32[88,768]{1,0:T(8,128)S(1)}, f32[88,768]{1,0:T(8,128)S(1)}, u32[]{:S(2)}, u32[]{:S(2)}) %collective-permute-start.22) | collective-permute-done | bytes 270368 | tf_op jit(solution)/shard_map/ppermute | solution.py:47
  144.4 17.5 %expert_grads.1 = (f32[160,768]{1,0:T(8,128)}, f32[160,768]{1,0:T(8,128)}, f32[160,768]{1,0:T(8,128)}, f32[160,768]{1,0:T(8,128)}, f32[768,384]{1,0:T(8,128)}, /...) custom-call(f32[88,768]{1,0:T(8,128)} %get-tuple-element.312.refs_0_, ...), custom_call_target="tpu_custom_call" | custom-call | flops 330000007168 | bytes 300000000 | tf_op jit(solution)/shard_map/expert_grads/pallas_call | solution.py:272
  168.0 8.8 %collective-permute-done.27 = f32[88,768]{1,0:T(8,128)S(1)} collective-permute-done((f32[88,768]{1,0:T(8,128)S(1)}, f32[88,768]{1,0:T(8,128)S(1)}, u32[]{:S(2)}, u32[]{:S(2)}) %collective-permute-start.27) | collective-permute-done | bytes 270368 | tf_op jit(solution)/shard_map/ppermute | solution.py:47
  182.0 9.6 %mixer_back.1 = (f32[128,768]{1,0:T(8,128)S(1)}, f32[16,768]{1,0:T(8,128)S(1)}, f32[128,1536]{1,0:T(8,128)}, f32[128,1536]{1,0:T(8,128)}, f32[1,1536]{1,0:T(1,128)S(1)}, /*index=5*/f32[17,1536]{1,0:T(8,128)}) custom-call(s32[1]{0:T(128)} %bitcast.1.me_ref, f32[168,768]{1,0:T(8,128)} %copy-done.74, bf16[160,128]{1,0:T(8,128)(2,1)S(1)} %copy-done.16, ...), custom_call_target="tpu_custom_call" | custom-call | flops 330000007168 | bytes 300000000 | tf_op jit(solution)/shard_map/mixer_back/pallas_call | solution.py:272
  191.6 3.3 collective-permute-done.30
  194.9 5.2 %late.2 = f32[768,1536]{1,0:T(8,128)} custom-call(s32[1]{0:T(128)} %bitcast.later_ref.which_ref.core_ref, f32[128,1536]{1,0:T(8,128)S(1)} %copy-done.56, f32[128,1536]{1,0:T(8,128)} %get-tuple-element.277.act_ref, f32[1,1536]{1,0:T(1,128)S(1)} %copy-done.21, f32[144,3072]{1,0:T(8,128)} %join.1.inner_ref.gate_z_ref, ...), custom_call_target="tpu_custom_call" | custom-call | flops 219999993856 | bytes 200000000 | tf_op jit(solution)/shard_map/late/pallas_call | solution.py:272
  202.9 4.6 %collective-permute-done.33 = f32[384,384]{1,0:T(8,128)} collective-permute-done((f32[384,384]{1,0:T(8,128)}, f32[384,384]{1,0:T(8,128)}, u32[]{:S(2)}, u32[]{:S(2)}) %collective-permute-start.33) | collective-permute-done | bytes 589856 | tf_op jit(solution)/shard_map/ppermute | solution.py:47
  208.3 8.1 %late.3 = (f32[768,1536]{1,0:T(8,128)}, f32[128,768]{1,0:T(8,128)S(1)}) custom-call(s32[1]{0:T(128)S(6)} %sub.76.which_ref, f32[128,1536]{1,0:T(8,128)S(1)} %copy-done.56, f32[128,1536]{1,0:T(8,128)} %get-tuple-element.277.act_ref, f32[1,1536]{1,0:T(1,128)S(1)} %copy-done.21, f32[144,3072]{1,0:T(8,128)} %join.1.inner_ref.gate_z_ref, ...), custom_call_target="tpu_custom_call" | custom-call | flops 219999993856 | bytes 200000000 | tf_op jit(solution)/shard_map/late/pallas_call | solution.py:272
  220.4 4.9 %collective-permute-done.37.got_ref = f32[17,1536]{1,0:T(8,128)S(1)} collective-permute-done((f32[17,1536]{1,0:T(8,128)S(1)}, f32[17,1536]{1,0:T(8,128)S(1)}, u32[]{:S(2)}, u32[]{:S(2)}) %collective-permute-start.37) | collective-permute-done | bytes 104480 | tf_op jit(solution)/shard_map/ppermute | solution.py:47
  225.4 4.7 %dynamic-slice_add_fusion = (f32[192,1536]{1,0:T(8,128)S(1)}, f32[192,1536]{1,0:T(8,128)S(1)}, f32[192,1536]{1,0:T(8,128)S(1)}, f32[192,1536]{1,0:T(8,128)S(1)}) fusion(f32[768,1536]{1,0:T(8,128)} %collective-permute-done.35, s32[]{:T(128)S(6)} %select_n.397, f32[768,1536]{1,0:T(8,128)} %get-tuple-element.413, s32[]{:T(128)S(6)} %select_n.396, ...), kind=kLoop, calls=%fused_computation.13 | loop fusion | flops 1179648 | bytes 14155792 | tf_op jit(solution)/shard_map/add | solution.py:75
  232.8 3.3 collective-permute-start.39
  237.3 4.0 collective-permute-done.39.got_ref
  242.4 3.0 collective-permute-start.45
  245.4 8.5 %scan_back.3 = (f32[128,1536]{1,0:T(8,128)S(1)}, f32[128,1536]{1,0:T(8,128)}, f32[16,1536]{1,0:T(8,128)S(1)}, f32[80,128]{1,0:T(8,128)S(1)}) custom-call(f32[128,1536]{1,0:T(8,128)} %get-tuple-element.274.masked_ref, f32[128,1536]{1,0:T(8,128)} %get-tuple-element.275.steps_ref, f32[128,1536]{1,0:T(8,128)} %get-tuple-element.276.drive_ref, ...), custom_call_target="tpu_custom_call" | custom-call | flops 11000000512 | bytes 10000000 | tf_op jit(solution)/shard_map/scan_back/pallas_call | solution.py:272
  253.9 2.9 collective-permute-done.41
  260.0 8.2 %scan_back.4 = (f32[128,1536]{1,0:T(8,128)S(1)}, f32[128,1536]{1,0:T(8,128)}, f32[16,1536]{1,0:T(8,128)S(1)}, f32[80,128]{1,0:T(8,128)S(1)}) custom-call(f32[128,1536]{1,0:T(8,128)} %get-tuple-element.274.masked_ref, f32[128,1536]{1,0:T(8,128)} %get-tuple-element.275.steps_ref, ...), custom_call_target="tpu_custom_call", output_to_operand_aliasing={{0}: (14, {}), {1}: (15, {}), {2}: (16, {})} | custom-call | flops 11000000512 | bytes 10000000 | tf_op jit(solution)/shard_map/scan_back/pallas_call | solution.py:272
  268.3 2.8 collective-permute-done.42
  276.1 8.2 %scan_back.5 = (f32[128,1536]{1,0:T(8,128)S(1)}, f32[128,1536]{1,0:T(8,128)}, f32[16,1536]{1,0:T(8,128)S(1)}, f32[80,128]{1,0:T(8,128)S(1)}) custom-call(f32[128,1536]{1,0:T(8,128)} %get-tuple-element.274.masked_ref, f32[128,1536]{1,0:T(8,128)} %get-tuple-element.275.steps_ref, ...), custom_call_target="tpu_custom_call", output_to_operand_aliasing={{0}: (14, {}), {1}: (15, {}), {2}: (16, {})} | custom-call | flops 11000000512 | bytes 10000000 | tf_op jit(solution)/shard_map/scan_back/pallas_call | solution.py:272
  289.6 11.3 %input_back.1 = (f32[480,1536]{1,0:T(8,128)}, f32[480,1536]{1,0:T(8,128)}, f32[128,768]{1,0:T(8,128)S(1)}, f32[16,768]{1,0:T(8,128)S(1)}) custom-call(s32[1]{0:T(128)} %bitcast.later_ref.which_ref.core_ref, f32[80,128]{1,0:T(8,128)S(1)} %get-tuple-element.409.proj_a_ref, f32[80,128]{1,0:T(8,128)S(1)} %get-tuple-element.418.proj_b_ref, ...), custom_call_target="tpu_custom_call" | custom-call | flops 12099999744 | bytes 11000000 | tf_op jit(solution)/shard_map/input_back/pallas_call | solution.py:272
  301.1 5.7 %collective-permute-done.53 = f32[480,1536]{1,0:T(8,128)} collective-permute-done((f32[480,1536]{1,0:T(8,128)}, f32[480,1536]{1,0:T(8,128)}, u32[]{:S(2)}, u32[]{:S(2)}) %collective-permute-start.53) | collective-permute-done | bytes 2949152 | tf_op jit(solution)/shard_map/ppermute | solution.py:47
  306.8 4.3 dynamic-slice_add_fusion.4
  314.5 13.9 %collective-permute-done.52 = f32[192,384]{1,0:T(8,128)S(1)} collective-permute-done((f32[192,384]{1,0:T(8,128)S(1)}, f32[192,384]{1,0:T(8,128)S(1)}, u32[]{:S(2)}, u32[]{:S(2)}) %collective-permute-start.52) | collective-permute-done | bytes 294944 | tf_op jit(solution)/shard_map/ppermute | solution.py:47
  337.2 5.6 %collective-permute-done.57 = f32[60,1536]{1,0:T(8,128)} collective-permute-done((f32[60,1536]{1,0:T(8,128)}, f32[60,1536]{1,0:T(8,128)}, u32[]{:S(2)}, u32[]{:S(2)}) %collective-permute-start.57) | collective-permute-done | bytes 368672 | tf_op jit(solution)/shard_map/ppermute | solution.py:47
  342.8 2.9 collective-permute-done.58
  358.7 5.7 %collective-permute-done.62 = f32[120,384]{1,0:T(8,128)S(1)} collective-permute-done((f32[120,384]{1,0:T(8,128)S(1)}, f32[120,384]{1,0:T(8,128)S(1)}, u32[]{:S(2)}, u32[]{:S(2)}) %collective-permute-start.62) | collective-permute-done | bytes 184352 | tf_op jit(solution)/shard_map/ppermute | solution.py:47
  374.7 9.1 %collective-permute-done.67 = f32[120,384]{1,0:T(8,128)S(1)} collective-permute-done((f32[120,384]{1,0:T(8,128)S(1)}, f32[120,384]{1,0:T(8,128)S(1)}, u32[]{:S(2)}, u32[]{:S(2)}) %collective-permute-start.67) | collective-permute-done | bytes 184352 | tf_op jit(solution)/shard_map/ppermute | solution.py:47
  384.0 7.3 %collective-permute-done.64 = f32[192,1536]{1,0:T(8,128)S(1)} collective-permute-done((f32[192,1536]{1,0:T(8,128)S(1)}, f32[192,1536]{1,0:T(8,128)S(1)}, u32[]{:S(2)}, u32[]{:S(2)}) %collective-permute-start.64) | collective-permute-done | bytes 1179680 | tf_op jit(solution)/shard_map/ppermute | solution.py:47
  393.1 4.3 collective-permute-done.65
  402.6 8.2 %collective-permute-done.72 = f32[60,1536]{1,0:T(8,128)S(1)} collective-permute-done((f32[60,1536]{1,0:T(8,128)S(1)}, f32[60,1536]{1,0:T(8,128)S(1)}, u32[]{:S(2)}, u32[]{:S(2)}) %collective-permute-start.72) | collective-permute-done | bytes 368672 | tf_op jit(solution)/shard_map/ppermute | solution.py:47
  417.2 7.8 %finish_late.1 = (f32[768,3072]{1,0:T(8,128)}, f32[2,768,768]{2,1,0:T(8,128)}) custom-call(s32[1]{0:T(128)} %bitcast.later_ref.which_ref.core_ref, f32[384,1536]{1,0:T(8,128)} %pad_maximum_fusion.first_ref, f32[384,1536]{1,0:T(8,128)} %pad_maximum_fusion.1.second_ref, f32[384,1536]{1,0:T(8,128)} %collective-permute-done.73.got_first_ref, ...), custom_call_target="tpu_custom_call" | custom-call | flops 8800000000 | bytes 8000000 | tf_op jit(solution)/shard_map/finish_late/pallas_call | solution.py:272
  425.0 5.5 %collective-permute-done.75 = f32[120,1536]{1,0:T(8,128)S(1)} collective-permute-done((f32[120,1536]{1,0:T(8,128)S(1)}, f32[120,1536]{1,0:T(8,128)S(1)}, u32[]{:S(2)}, u32[]{:S(2)}) %collective-permute-start.75) | collective-permute-done | bytes 737312 | tf_op jit(solution)/shard_map/ppermute | solution.py:47
  432.3 2.8 collective-permute-done.77.got_first_ref
  438.3 5.9 %finish.1 = (f32[768,3072]{1,0:T(8,128)}, f32[1536,80]{1,0:T(8,128)S(1)}, f32[48,1536]{1,0:T(8,128)}, f32[1536,16]{1,0:T(8,128)S(1)}, f32[4,1536]{1,0:T(4,128)},...) custom-call(s32[1]{0:T(128)} %bitcast.later_ref.which_ref.core_ref, ...), custom_call_target="tpu_custom_call", output_to_operand_aliasing={{0}: (5, {})} | custom-call | flops 6600000000 | bytes 6000000 | tf_op jit(solution)/shard_map/finish/pallas_call | solution.py:272
  (420 shorter events, 147.2 us)
Async XLA Ops:
  3.8 32.3 %collective-permute-start.3 = (f32[384,768]{1,0:T(8,128)}, f32[384,768]{1,0:T(8,128)}, u32[]{:S(2)}, u32[]{:S(2)}) collective-permute-start(f32[384,768]{1,0:T(8,128)} %bitcast.45), channel_id=1, source_target_pairs={{0,4},{1,5},{2,6},{3,7},{4,0},{5,1},{6,2},{7,3},{8,12},{9,13},{10,... | collective-permute-start | bytes 3538952 | tf_op jit(solution)/shard_map/ppermute | solution.py:47
  23.7 25.1 %collective-permute-start.7 = (f32[160,768]{1,0:T(8,128)}, f32[160,768]{1,0:T(8,128)}, u32[]{:S(2)}, u32[]{:S(2)}) collective-permute-start(f32[160,768]{1,0:T(8,128)} %pad_maximum_fusion.14.refs_0_.refs_8_), channel_id=1, source_target_pairs={{0,16},{1,17},{2,18},{3,19},{4,20},{5,21},{6,22},{7,23},{8,24},{9,... | collective-permute-start | bytes 1474568 | tf_op jit(solution)/shard_map/ppermute | solution.py:47
  26.3 22.7 %collective-permute-start.6 = (f32[160,768]{1,0:T(8,128)}, f32[160,768]{1,0:T(8,128)}, u32[]{:S(2)}, u32[]{:S(2)}) collective-permute-start(f32[160,768]{1,0:T(8,128)} %pad_maximum_fusion.14.refs_0_.refs_8_), channel_id=1, source_target_pairs={{0,8},{1,9},{2,10},{3,11},{4,12},{5,13},{6,14},{7,15},{8,0},{9,1},... | collective-permute-start | bytes 1474568 | tf_op jit(solution)/shard_map/ppermute | solution.py:47
  61.9 20.5 %collective-permute-start.12 = (f32[384,384]{1,0:T(8,128)}, f32[384,384]{1,0:T(8,128)}, u32[]{:S(2)}, u32[]{:S(2)}) collective-permute-start(f32[384,384]{1,0:T(8,128)} %get-tuple-element.621), channel_id=1, source_target_pairs={{0,4},{1,5},{2,6},{3,7},{4,0},{5,1},{6,2},{7,3},{8,12},{9,13},{10,... | collective-permute-start | bytes 1769480 | tf_op jit(solution)/shard_map/ppermute | solution.py:47
  67.2 15.1 %collective-permute-start.11 = (f32[160,768]{1,0:T(8,128)}, f32[160,768]{1,0:T(8,128)}, u32[]{:S(2)}, u32[]{:S(2)}) collective-permute-start(f32[160,768]{1,0:T(8,128)} %collective-permute-done.7.refs_2_.refs_10_), channel_id=1, source_target_pairs={{0,8},{1,9},{2,10},{3,11},{4,12},{5,13},{6,14},{7,15},{8,0},{9,1},... | collective-permute-start | bytes 1474568 | tf_op jit(solution)/shard_map/ppermute | solution.py:47
  82.5 16.9 %collective-permute-start.17 = (f32[384,384]{1,0:T(8,128)}, f32[384,384]{1,0:T(8,128)}, u32[]{:S(2)}, u32[]{:S(2)}) collective-permute-start(f32[384,384]{1,0:T(8,128)} %get-tuple-element.311), channel_id=1, source_target_pairs={{0,4},{1,5},{2,6},{3,7},{4,0},{5,1},{6,2},{7,3},{8,12},{9,13},{10,... | collective-permute-start | bytes 1769480 | tf_op jit(solution)/shard_map/ppermute | solution.py:47
  86.4 23.0 %collective-permute-start.15 = (f32[88,768]{1,0:T(8,128)}, f32[88,768]{1,0:T(8,128)}, u32[]{:S(2)}, u32[]{:S(2)}) collective-permute-start(f32[88,768]{1,0:T(8,128)} %get-tuple-element.312.refs_0_), channel_id=1, source_target_pairs={{0,16},{1,17},{2,18},{3,19},{4,20},{5,21},{6,22},{7,23},{8,24},{9,... | collective-permute-start | bytes 811016 | tf_op jit(solution)/shard_map/ppermute | solution.py:47
  89.6 19.7 %collective-permute-start.14 = (f32[88,768]{1,0:T(8,128)}, f32[88,768]{1,0:T(8,128)}, u32[]{:S(2)}, u32[]{:S(2)}) collective-permute-start(f32[88,768]{1,0:T(8,128)} %get-tuple-element.312.refs_0_), channel_id=1, source_target_pairs={{0,8},{1,9},{2,10},{3,11},{4,12},{5,13},{6,14},{7,15},{8,0},{9,1},... | collective-permute-start | bytes 811016 | tf_op jit(solution)/shard_map/ppermute | solution.py:47
  99.5 14.8 %collective-permute-start.20 = (f32[88,768]{1,0:T(8,128)}, f32[88,768]{1,0:T(8,128)S(1)}, u32[]{:S(2)}, u32[]{:S(2)}) collective-permute-start(f32[88,768]{1,0:T(8,128)} %collective-permute-done.16.refs_1_), channel_id=1, source_target_pairs={{0,16},{1,17},{2,18},{3,19},{4,20},{5,21},{6,22},{7,23},{8,24},{9,... | collective-permute-start | bytes 811016 | tf_op jit(solution)/shard_map/ppermute | solution.py:47
  101.0 14.9 %collective-permute-start.19 = (f32[88,768]{1,0:T(8,128)}, f32[88,768]{1,0:T(8,128)S(1)}, u32[]{:S(2)}, u32[]{:S(2)}) collective-permute-start(f32[88,768]{1,0:T(8,128)} %collective-permute-done.16.refs_1_), channel_id=1, source_target_pairs={{0,8},{1,9},{2,10},{3,11},{4,12},{5,13},{6,14},{7,15},{8,0},{9,1},... | collective-permute-start | bytes 811016 | tf_op jit(solution)/shard_map/ppermute | solution.py:47
  109.4 17.7 %collective-permute-start.18 = (f32[88,768]{1,0:T(8,128)}, f32[88,768]{1,0:T(8,128)S(1)}, u32[]{:S(2)}, u32[]{:S(2)}) collective-permute-start(f32[88,768]{1,0:T(8,128)} %collective-permute-done.15.refs_0_.refs_4_), channel_id=1, source_target_pairs={{0,8},{1,9},{2,10},{3,11},{4,12},{5,13},{6,14},{7,15},{8,0},{9,1},... | collective-permute-start | bytes 811016 | tf_op jit(solution)/shard_map/ppermute | solution.py:47
  115.9 11.2 %collective-permute-start.21 = (f32[88,768]{1,0:T(8,128)S(1)}, f32[88,768]{1,0:T(8,128)S(1)}, u32[]{:S(2)}, u32[]{:S(2)}) collective-permute-start(f32[88,768]{1,0:T(8,128)S(1)} %collective-permute-done.20.refs_1_.refs_5_), channel_id=1, source_target_pairs={{0,8},{1,9},{2,10},{3,11},{4,12},{5,13},{6,14},{7,15},{8,0},{9,1},... | collective-permute-start | bytes 811016 | tf_op jit(solution)/shard_map/ppermute | solution.py:47
  140.7 21.1 %collective-permute-start.24 = (f32[88,768]{1,0:T(8,128)}, f32[88,768]{1,0:T(8,128)}, u32[]{:S(2)}, u32[]{:S(2)}) collective-permute-start(f32[88,768]{1,0:T(8,128)} %add.342), channel_id=1, source_target_pairs={{0,16},{1,17},{2,18},{3,19},{4,20},{5,21},{6,22},{7,23},{8,24},{9,... | collective-permute-start | bytes 811016 | tf_op jit(solution)/shard_map/ppermute | solution.py:47
  142.3 19.5 %collective-permute-start.23 = (f32[88,768]{1,0:T(8,128)}, f32[88,768]{1,0:T(8,128)}, u32[]{:S(2)}, u32[]{:S(2)}) collective-permute-start(f32[88,768]{1,0:T(8,128)} %get-tuple-element.343), channel_id=1, source_target_pairs={{0,8},{1,9},{2,10},{3,11},{4,12},{5,13},{6,14},{7,15},{8,0},{9,1},... | collective-permute-start | bytes 811016 | tf_op jit(solution)/shard_map/ppermute | solution.py:47
  143.9 19.1 %collective-permute-start.25 = (f32[88,768]{1,0:T(8,128)}, f32[88,768]{1,0:T(8,128)}, u32[]{:S(2)}, u32[]{:S(2)}) collective-permute-start(f32[88,768]{1,0:T(8,128)} %get-tuple-element.346), channel_id=1, source_target_pairs={{0,8},{1,9},{2,10},{3,11},{4,12},{5,13},{6,14},{7,15},{8,0},{9,1},... | collective-permute-start | bytes 811016 | tf_op jit(solution)/shard_map/ppermute | solution.py:47
  164.2 12.7 %collective-permute-start.27 = (f32[88,768]{1,0:T(8,128)S(1)}, f32[88,768]{1,0:T(8,128)S(1)}, u32[]{:S(2)}, u32[]{:S(2)}) collective-permute-start(f32[88,768]{1,0:T(8,128)S(1)} %add.345), channel_id=1, source_target_pairs={{0,16},{1,17},{2,18},{3,19},{4,20},{5,21},{6,22},{7,23},{8,24},{9,... | collective-permute-start | bytes 811016 | tf_op jit(solution)/shard_map/ppermute | solution.py:47
  165.5 11.4 %collective-permute-start.26 = (f32[88,768]{1,0:T(8,128)S(1)}, f32[88,768]{1,0:T(8,128)S(1)}, u32[]{:S(2)}, u32[]{:S(2)}) collective-permute-start(f32[88,768]{1,0:T(8,128)S(1)} %get-tuple-element.369), channel_id=1, source_target_pairs={{0,8},{1,9},{2,10},{3,11},{4,12},{5,13},{6,14},{7,15},{8,0},{9,1},... | collective-permute-start | bytes 811016 | tf_op jit(solution)/shard_map/ppermute | solution.py:47
  178.4 16.5 %collective-permute-start.30 = (f32[384,384]{1,0:T(8,128)}, f32[384,384]{1,0:T(8,128)}, u32[]{:S(2)}, u32[]{:S(2)}) collective-permute-start(f32[384,384]{1,0:T(8,128)} %get-tuple-element.619), channel_id=1, source_target_pairs={{0,4},{1,5},{2,6},{3,7},{4,0},{5,1},{6,2},{7,3},{8,12},{9,13},{10,... | collective-permute-start | bytes 1769480 | tf_op jit(solution)/shard_map/ppermute | solution.py:47
  180.2 22.7 %collective-permute-start.32 = (f32[160,768]{1,0:T(8,128)}, f32[160,768]{1,0:T(8,128)}, u32[]{:S(2)}, u32[]{:S(2)}) collective-permute-start(f32[160,768]{1,0:T(8,128)} %get-tuple-element.388), channel_id=1, source_target_pairs={{0,8},{1,9},{2,10},{3,11},{4,12},{5,13},{6,14},{7,15},{8,0},{9,1},... | collective-permute-start | bytes 1474568 | tf_op jit(solution)/shard_map/ppermute | solution.py:47
  181.0 26.6 %collective-permute-start.33 = (f32[384,384]{1,0:T(8,128)}, f32[384,384]{1,0:T(8,128)}, u32[]{:S(2)}, u32[]{:S(2)}) collective-permute-start(f32[384,384]{1,0:T(8,128)} %get-tuple-element.391), channel_id=1, source_target_pairs={{0,4},{1,5},{2,6},{3,7},{4,0},{5,1},{6,2},{7,3},{8,12},{9,13},{10,... | collective-permute-start | bytes 1769480 | tf_op jit(solution)/shard_map/ppermute | solution.py:47
  200.1 19.7 %collective-permute-start.35 = (f32[768,1536]{1,0:T(8,128)}, f32[768,1536]{1,0:T(8,128)}, u32[]{:S(2)}, u32[]{:S(2)}) collective-permute-start(f32[768,1536]{1,0:T(8,128)} %late.2), channel_id=1, source_target_pairs={{0,1},{1,0},{2,3},{3,2},{4,5},{5,4},{6,7},{7,6},{8,9},{9,8},{10,11... | collective-permute-start | bytes 14155784 | tf_op jit(solution)/shard_map/ppermute | solution.py:47
  200.6 19.1 %collective-permute-start.36 = (f32[192,768]{1,0:T(8,128)}, f32[192,768]{1,0:T(8,128)}, u32[]{:S(2)}, u32[]{:S(2)}) collective-permute-start(f32[192,768]{1,0:T(8,128)} %get-tuple-element.389), channel_id=1, source_target_pairs={{0,4},{1,5},{2,6},{3,7},{4,0},{5,1},{6,2},{7,3},{8,12},{9,13},{10,... | collective-permute-start | bytes 1769480 | tf_op jit(solution)/shard_map/ppermute | solution.py:47
  230.1 26.8 %collective-permute-start.41 = (f32[192,1536]{1,0:T(8,128)S(1)}, f32[192,1536]{1,0:T(8,128)S(1)}, u32[]{:S(2)}, u32[]{:S(2)}) collective-permute-start(f32[192,1536]{1,0:T(8,128)S(1)} %get-tuple-element.575), channel_id=1, source_target_pairs={{0,2},{1,3},{2,0},{3,1},{4,6},{5,7},{6,4},{7,5},{8,10},{9,11},{10,... | collective-permute-start | bytes 3538952 | tf_op jit(solution)/shard_map/ppermute | solution.py:47
  231.3 26.6 %collective-permute-start.40 = (f32[192,1536]{1,0:T(8,128)S(1)}, f32[192,1536]{1,0:T(8,128)S(1)}, u32[]{:S(2)}, u32[]{:S(2)}) collective-permute-start(f32[192,1536]{1,0:T(8,128)S(1)} %get-tuple-element.577), channel_id=1, source_target_pairs={{0,4},{1,5},{2,6},{3,7},{4,0},{5,1},{6,2},{7,3},{8,12},{9,13},{10,... | collective-permute-start | bytes 3538952 | tf_op jit(solution)/shard_map/ppermute | solution.py:47
  242.4 29.3 %collective-permute-start.44 = (f32[160,768]{1,0:T(8,128)S(1)}, f32[160,768]{1,0:T(8,128)S(1)}, u32[]{:S(2)}, u32[]{:S(2)}) collective-permute-start(f32[160,768]{1,0:T(8,128)S(1)} %copy-done.83), channel_id=1, source_target_pairs={{0,8},{1,9},{2,10},{3,11},{4,12},{5,13},{6,14},{7,15},{8,0},{9,1},... | collective-permute-start | bytes 1474568 | tf_op jit(solution)/shard_map/ppermute | solution.py:47
  242.4 29.3 %collective-permute-start.45 = (f32[160,768]{1,0:T(8,128)S(1)}, f32[160,768]{1,0:T(8,128)S(1)}, u32[]{:S(2)}, u32[]{:S(2)}) collective-permute-start(f32[160,768]{1,0:T(8,128)S(1)} %add.347), channel_id=1, source_target_pairs={{0,16},{1,17},{2,18},{3,19},{4,20},{5,21},{6,22},{7,23},{8,24},{9,... | collective-permute-start | bytes 1474568 | tf_op jit(solution)/shard_map/ppermute | solution.py:47
  258.0 13.1 %collective-permute-start.42 = (f32[96,1536]{1,0:T(8,128)S(1)}, f32[96,1536]{1,0:T(8,128)S(1)}, u32[]{:S(2)}, u32[]{:S(2)}) collective-permute-start(f32[96,1536]{1,0:T(8,128)S(1)} %get-tuple-element.589), channel_id=1, source_target_pairs={{0,2},{1,3},{2,0},{3,1},{4,6},{5,7},{6,4},{7,5},{8,10},{9,11},{10,... | collective-permute-start | bytes 1769480 | tf_op jit(solution)/shard_map/ppermute | solution.py:47
  258.9 12.6 %collective-permute-start.43 = (f32[96,1536]{1,0:T(8,128)S(1)}, f32[96,1536]{1,0:T(8,128)S(1)}, u32[]{:S(2)}, u32[]{:S(2)}) collective-permute-start(f32[96,1536]{1,0:T(8,128)S(1)} %get-tuple-element.591), channel_id=1, source_target_pairs={{0,4},{1,5},{2,6},{3,7},{4,0},{5,1},{6,2},{7,3},{8,12},{9,13},{10,... | collective-permute-start | bytes 1769480 | tf_op jit(solution)/shard_map/ppermute | solution.py:47
  271.8 12.6 %collective-permute-start.47 = (f32[80,768]{1,0:T(8,128)S(1)}, f32[80,768]{1,0:T(8,128)S(1)}, u32[]{:S(2)}, u32[]{:S(2)}) collective-permute-start(f32[80,768]{1,0:T(8,128)S(1)} %get-tuple-element.639), channel_id=1, source_target_pairs={{0,2},{1,3},{2,0},{3,1},{4,6},{5,7},{6,4},{7,5},{8,10},{9,11},{10,... | collective-permute-start | bytes 737288 | tf_op jit(solution)/shard_map/ppermute | solution.py:47
  286.1 14.8 %collective-permute-start.50 = (f32[192,384]{1,0:T(8,128)S(1)}, f32[192,384]{1,0:T(8,128)S(1)}, u32[]{:S(2)}, u32[]{:S(2)}) collective-permute-start(f32[192,384]{1,0:T(8,128)S(1)} %add_add_fusion.1), channel_id=1, source_target_pairs={{0,16},{1,17},{2,18},{3,19},{4,20},{5,21},{6,22},{7,23},{8,24},{9,... | collective-permute-start | bytes 884744 | tf_op jit(solution)/shard_map/ppermute | solution.py:47
  287.9 13.0 %collective-permute-start.49 = (f32[192,384]{1,0:T(8,128)S(1)}, f32[192,384]{1,0:T(8,128)S(1)}, u32[]{:S(2)}, u32[]{:S(2)}) collective-permute-start(f32[192,384]{1,0:T(8,128)S(1)} %get-tuple-element.451), channel_id=1, source_target_pairs={{0,8},{1,9},{2,10},{3,11},{4,12},{5,13},{6,14},{7,15},{8,0},{9,1},... | collective-permute-start | bytes 884744 | tf_op jit(solution)/shard_map/ppermute | solution.py:47
  311.1 18.8 %collective-permute-start.55 = (f32[120,1536]{1,0:T(8,128)}, f32[120,1536]{1,0:T(8,128)}, u32[]{:S(2)}, u32[]{:S(2)}) collective-permute-start(f32[120,1536]{1,0:T(8,128)} %get-tuple-element.579), channel_id=1, source_target_pairs={{0,2},{1,3},{2,0},{3,1},{4,6},{5,7},{6,4},{7,5},{8,10},{9,11},{10,... | collective-permute-start | bytes 2211848 | tf_op jit(solution)/shard_map/ppermute | solution.py:47
  311.9 18.6 %collective-permute-start.54 = (f32[120,1536]{1,0:T(8,128)}, f32[120,1536]{1,0:T(8,128)}, u32[]{:S(2)}, u32[]{:S(2)}) collective-permute-start(f32[120,1536]{1,0:T(8,128)} %get-tuple-element.581), channel_id=1, source_target_pairs={{0,4},{1,5},{2,6},{3,7},{4,0},{5,1},{6,2},{7,3},{8,12},{9,13},{10,... | collective-permute-start | bytes 2211848 | tf_op jit(solution)/shard_map/ppermute | solution.py:47
  312.9 15.6 %collective-permute-start.52 = (f32[192,384]{1,0:T(8,128)S(1)}, f32[192,384]{1,0:T(8,128)S(1)}, u32[]{:S(2)}, u32[]{:S(2)}) collective-permute-start(f32[192,384]{1,0:T(8,128)S(1)} %add_add_fusion.2), channel_id=1, source_target_pairs={{0,16},{1,17},{2,18},{3,19},{4,20},{5,21},{6,22},{7,23},{8,24},{9,... | collective-permute-start | bytes 884744 | tf_op jit(solution)/shard_map/ppermute | solution.py:47
  313.2 15.2 %collective-permute-start.51 = (f32[192,384]{1,0:T(8,128)S(1)}, f32[192,384]{1,0:T(8,128)}, u32[]{:S(2)}, u32[]{:S(2)}) collective-permute-start(f32[192,384]{1,0:T(8,128)S(1)} %add_add_fusion.2), channel_id=1, source_target_pairs={{0,8},{1,9},{2,10},{3,11},{4,12},{5,13},{6,14},{7,15},{8,0},{9,1},... | collective-permute-start | bytes 884744 | tf_op jit(solution)/shard_map/ppermute | solution.py:47
  348.8 15.6 %collective-permute-start.62 = (f32[120,384]{1,0:T(8,128)S(1)}, f32[120,384]{1,0:T(8,128)S(1)}, u32[]{:S(2)}, u32[]{:S(2)}) collective-permute-start(f32[120,384]{1,0:T(8,128)S(1)} %get-tuple-element.603), channel_id=1, source_target_pairs={{0,16},{1,17},{2,18},{3,19},{4,20},{5,21},{6,22},{7,23},{8,24},{9,... | collective-permute-start | bytes 552968 | tf_op jit(solution)/shard_map/ppermute | solution.py:47
  351.9 12.6 %collective-permute-start.60 = (f32[96,1536]{1,0:T(8,128)S(1)}, f32[96,1536]{1,0:T(8,128)S(1)}, u32[]{:S(2)}, u32[]{:S(2)}) collective-permute-start(f32[96,1536]{1,0:T(8,128)S(1)} %get-tuple-element.610), channel_id=1, source_target_pairs={{0,4},{1,5},{2,6},{3,7},{4,0},{5,1},{6,2},{7,3},{8,12},{9,13},{10,... | collective-permute-start | bytes 1769480 | tf_op jit(solution)/shard_map/ppermute | solution.py:47
  352.8 11.9 %collective-permute-start.59 = (f32[96,1536]{1,0:T(8,128)S(1)}, f32[96,1536]{1,0:T(8,128)S(1)}, u32[]{:S(2)}, u32[]{:S(2)}) collective-permute-start(f32[96,1536]{1,0:T(8,128)S(1)} %get-tuple-element.611), channel_id=1, source_target_pairs={{0,2},{1,3},{2,0},{3,1},{4,6},{5,7},{6,4},{7,5},{8,10},{9,11},{10,... | collective-permute-start | bytes 1769480 | tf_op jit(solution)/shard_map/ppermute | solution.py:47
  357.5 14.0 %collective-permute-start.69 = (f32[80,768]{1,0:T(8,128)S(1)}, f32[80,768]{1,0:T(8,128)S(1)}, u32[]{:S(2)}, u32[]{:S(2)}) collective-permute-start(f32[80,768]{1,0:T(8,128)S(1)} %pad_maximum_fusion.24), channel_id=1, source_target_pairs={{0,1},{1,0},{2,3},{3,2},{4,5},{5,4},{6,7},{7,6},{8,9},{9,8},{10,11... | collective-permute-start | bytes 737288 | tf_op jit(solution)/shard_map/ppermute | solution.py:47
  365.0 26.2 %collective-permute-start.64 = (f32[192,1536]{1,0:T(8,128)S(1)}, f32[192,1536]{1,0:T(8,128)S(1)}, u32[]{:S(2)}, u32[]{:S(2)}) collective-permute-start(f32[192,1536]{1,0:T(8,128)S(1)} %pad_maximum_fusion.7), channel_id=1, source_target_pairs={{0,4},{1,5},{2,6},{3,7},{4,0},{5,1},{6,2},{7,3},{8,12},{9,13},{10,... | collective-permute-start | bytes 3538952 | tf_op jit(solution)/shard_map/ppermute | solution.py:47
  368.3 15.5 %collective-permute-start.67 = (f32[120,384]{1,0:T(8,128)S(1)}, f32[120,384]{1,0:T(8,128)S(1)}, u32[]{:S(2)}, u32[]{:S(2)}) collective-permute-start(f32[120,384]{1,0:T(8,128)S(1)} %add_add_fusion.5), channel_id=1, source_target_pairs={{0,16},{1,17},{2,18},{3,19},{4,20},{5,21},{6,22},{7,23},{8,24},{9,... | collective-permute-start | bytes 552968 | tf_op jit(solution)/shard_map/ppermute | solution.py:47
  368.8 15.0 %collective-permute-start.66 = (f32[120,384]{1,0:T(8,128)S(1)}, f32[120,384]{1,0:T(8,128)S(1)}, u32[]{:S(2)}, u32[]{:S(2)}) collective-permute-start(f32[120,384]{1,0:T(8,128)S(1)} %add_add_fusion.5), channel_id=1, source_target_pairs={{0,24},{1,25},{2,26},{3,27},{4,28},{5,29},{6,30},{7,31},{8,16},{9,... | collective-permute-start | bytes 552968 | tf_op jit(solution)/shard_map/ppermute | solution.py:47
  371.5 25.8 %collective-permute-start.65 = (f32[192,1536]{1,0:T(8,128)S(1)}, f32[192,1536]{1,0:T(8,128)S(1)}, u32[]{:S(2)}, u32[]{:S(2)}) collective-permute-start(f32[192,1536]{1,0:T(8,128)S(1)} %pad_maximum_fusion.8), channel_id=1, source_target_pairs={{0,2},{1,3},{2,0},{3,1},{4,6},{5,7},{6,4},{7,5},{8,10},{9,11},{10,... | collective-permute-start | bytes 3538952 | tf_op jit(solution)/shard_map/ppermute | solution.py:47
  399.1 14.0 %collective-permute-start.73 = (f32[384,1536]{1,0:T(8,128)}, f32[384,1536]{1,0:T(8,128)}, u32[]{:S(2)}, u32[]{:S(2)}) collective-permute-start(f32[384,1536]{1,0:T(8,128)} %pad_maximum_fusion.first_ref), channel_id=1, source_target_pairs={{0,1},{1,0},{2,3},{3,2},{4,5},{5,4},{6,7},{7,6},{8,9},{9,8},{10,11... | collective-permute-start | bytes 7077896 | tf_op jit(solution)/shard_map/ppermute | solution.py:47
  399.1 14.0 %collective-permute-start.74 = (f32[384,1536]{1,0:T(8,128)}, f32[384,1536]{1,0:T(8,128)}, u32[]{:S(2)}, u32[]{:S(2)}) collective-permute-start(f32[384,1536]{1,0:T(8,128)} %pad_maximum_fusion.1.second_ref), channel_id=1, source_target_pairs={{0,1},{1,0},{2,3},{3,2},{4,5},{5,4},{6,7},{7,6},{8,9},{9,8},{10,11... | collective-permute-start | bytes 7077896 | tf_op jit(solution)/shard_map/ppermute | solution.py:47
  399.7 11.1 %collective-permute-start.72 = (f32[60,1536]{1,0:T(8,128)S(1)}, f32[60,1536]{1,0:T(8,128)S(1)}, u32[]{:S(2)}, u32[]{:S(2)}) collective-permute-start(f32[60,1536]{1,0:T(8,128)S(1)} %get-tuple-element.628), channel_id=1, source_target_pairs={{0,4},{1,5},{2,6},{3,7},{4,0},{5,1},{6,2},{7,3},{8,12},{9,13},{10,... | collective-permute-start | bytes 1105928 | tf_op jit(solution)/shard_map/ppermute | solution.py:47
  413.1 17.3 %collective-permute-start.75 = (f32[120,1536]{1,0:T(8,128)S(1)}, f32[120,1536]{1,0:T(8,128)S(1)}, u32[]{:S(2)}, u32[]{:S(2)}) collective-permute-start(f32[120,1536]{1,0:T(8,128)S(1)} %pad_maximum_fusion.12), channel_id=1, source_target_pairs={{0,4},{1,5},{2,6},{3,7},{4,0},{5,1},{6,2},{7,3},{8,12},{9,13},{10,... | collective-permute-start | bytes 2211848 | tf_op jit(solution)/shard_map/ppermute | solution.py:47
  414.0 16.9 %collective-permute-start.76 = (f32[120,1536]{1,0:T(8,128)S(1)}, f32[120,1536]{1,0:T(8,128)S(1)}, u32[]{:S(2)}, u32[]{:S(2)}) collective-permute-start(f32[120,1536]{1,0:T(8,128)S(1)} %pad_maximum_fusion.13), channel_id=1, source_target_pairs={{0,2},{1,3},{2,0},{3,1},{4,6},{5,7},{6,4},{7,5},{8,10},{9,11},{10,... | collective-permute-start | bytes 2211848 | tf_op jit(solution)/shard_map/ppermute | solution.py:47
  (115 other events, 893.3 us)

commit v7 on v6

--- a/solution.py
+++ b/solution.py
@@ -78,9 +78,10 @@
 def scatter_rows(grid, parts, name, rows, start=0):
     count, place = grid.size[name], grid.at[name]
     rows = rows // count
-    piece = lambda s: rows_of(parts, start + (place ^ s) * rows, rows)
-    got = [grid.swap(piece(s), name, s) for s in range(1, count)]
-    return [piece(0)] + got
+    sent = [rows_of(parts, start + (place ^ s) * rows, rows) for s in range(1, count)]
+    got = [grid.swap(block, name, s) for s, block in enumerate(sent, 1)]
+    parts, _ = tie(list(parts), sent)
+    return [rows_of(parts, start + place * rows, rows)] + got
 
 
 def gather_rows(grid, block, name):

time: 456 us -> 448 us (0.982)
  waiting for transfers between devices: 150 us -> 139 us
    ppermute x77, waiting for transfers between devices: 150 us -> 139 us  [swap_bits(): return lax.ppermute(block, AXES, [(i, i ^ bits) for i in range(self.total)])]
    add x6 -> x14, other arithmetic: 13.4 us -> 18.8 us  [rows_of(): functools.reduce(jnp.add, [lax.dynamic_slice_in_dim(part, first, rows, 0)...]
    unnamed x175 -> x171, local copies, waits for them, and re-layouts: 15.2 us -> 15.2 us
  transfers between devices with their start and end apart: 79 -> 79, of which waited for: 40 -> 38; matrix products, arithmetic and copies ran while one was open for 8% -> 9% of each run, Pallas kernels for 31% -> 31%
where the time goes in v7:
time: 448 us; the launch traced here: 441 us
  Pallas kernels  150 us (33%)
  waiting for transfers between devices  139 us (31%)
  starting transfers between devices  84.2 us (19%)
  other arithmetic  40.6 us (9%)
  local copies, waits for them, and re-layouts  23.7 us (5%)
    pallas_call x29, Pallas kernels, call(): pl.pallas_call(kernel, out_shape=outs, grid=grid or (), in_specs=in_specs...  150 us
    ppermute x77, waiting for transfers between devices, swap_bits(): return lax.ppermute(block, AXES, [(i, i ^ bits) for i in range(self.total)])  139 us
    ppermute x77, starting transfers between devices, swap_bits(): return lax.ppermute(block, AXES, [(i, i ^ bits) for i in range(self.total)])  80.6 us
    add x14, other arithmetic, rows_of(): functools.reduce(jnp.add, [lax.dynamic_slice_in_dim(part, first, rows, 0)...  18.8 us
    unnamed x171, local copies, waits for them, and re-layouts  15.2 us
  transfers between devices with their start and end apart: 79, of which 38 were waited for; matrix products, arithmetic and copies ran while one was open for 9% of the time, Pallas kernels for 31%

profile of v7, /device:TPU:0, one launch (start us, length us, event | category | flops | bytes accessed | tf_op | source)
XLA Modules:
  0.0 441.1 jit_solution(8652374811928213498)
XLA Ops:
  3.8 2.6 collective-permute-start.3
  14.9 7.9 %join.1.inner_ref.gate_z_ref = f32[144,3072]{1,0:T(8,128)} custom-call(f32[128,768]{1,0:T(8,128)S(1)} %copy-done.21, f32[16,768]{1,0:T(8,128)S(1)} %collective-permute-done.halo_ref, f32[1,768]{1,0:T(1,128)S(1)} %reshape.122.gain_ref, f32[768,3072]{1,0:T(8,128)} %weight_ref.3), custom_call_target="tpu_custom_call" | custom-call | flops 8800000000 | bytes 8000000 | tf_op jit(solution)/shard_map/join/pallas_call | solution.py:273
  23.7 2.6 collective-permute-start.7
  26.9 8.3 %features.1 = (f32[128,1536]{1,0:T(8,128)S(1)}, f32[128,1536]{1,0:T(8,128)}, f32[128,1536]{1,0:T(8,128)}, f32[128,1536]{1,0:T(8,128)}, f32[128,1536]{1,0:T(8,128...) custom-call(f32[144,3072]{1,0:T(8,128)} %join.1.inner_ref.gate_z_ref, ...), custom_call_target="tpu_custom_call" | custom-call | flops 275000000512 | bytes 250000000 | tf_op jit(solution)/shard_map/features/pallas_call | solution.py:273
  39.7 4.4 %collective-permute-done.5.got_ref = f32[17,1536]{1,0:T(8,128)S(1)} collective-permute-done((f32[17,1536]{1,0:T(8,128)S(1)}, f32[17,1536]{1,0:T(8,128)S(1)}, u32[]{:S(2)}, u32[]{:S(2)}) %collective-permute-start.5) | collective-permute-done | bytes 104480 | tf_op jit(solution)/shard_map/ppermute | solution.py:47
  44.2 4.6 %collective-permute-done.7.refs_2_.refs_10_ = f32[160,768]{1,0:T(8,128)} collective-permute-done((f32[160,768]{1,0:T(8,128)}, f32[160,768]{1,0:T(8,128)}, u32[]{:S(2)}, u32[]{:S(2)}) %collective-permute-start.7) | collective-permute-done | bytes 491552 | tf_op jit(solution)/shard_map/ppermute | solution.py:47
  49.4 4.7 %collective-permute-done.8.got_ref = f32[17,1536]{1,0:T(8,128)S(1)} collective-permute-done((f32[17,1536]{1,0:T(8,128)S(1)}, f32[17,1536]{1,0:T(8,128)S(1)}, u32[]{:S(2)}, u32[]{:S(2)}) %collective-permute-start.8) | collective-permute-done | bytes 104480 | tf_op jit(solution)/shard_map/ppermute | solution.py:47
  55.6 3.7 collective-permute-done.9.got_ref
  63.6 3.6 collective-permute-done.10.got_ref
  68.3 14.0 %scan.1 = (f32[128,1536]{1,0:T(8,128)}, f32[128,16,1536]{2,1,0:T(8,128)}, f32[128,768]{1,0:T(8,128)S(1)}, f32[168,768]{1,0:T(8,128)S(1)}, f32[128,8]{1,0:T(8,128)S(1)}, /*index=5*/f32[128,1]{1,0:T(8,128)S(1)}) custom-call(s32[1]{0:T(128)} %bitcast.1.me_ref, f32[128,1536]{1,0:T(8,128)} %get-tuple-element.290.masked_ref, ...), custom_call_target="tpu_custom_call" | custom-call | flops 219999993856 | bytes 200000000 | tf_op jit(solution)/shard_map/scan/pallas_call | solution.py:273
  86.4 3.2 collective-permute-start.15
  91.1 6.8 %early.1 = (f32[2,160,384]{2,1,0:T(8,128)S(1)}, f32[2,160,384]{2,1,0:T(8,128)S(1)}, f32[2,160,384]{2,1,0:T(8,128)S(1)}, f32[2,160,384]{2,1,0:T(8,128)S(1)}) custom-call(f32[160,768]{1,0:T(8,128)} %pad_maximum_fusion.14.refs_0_.refs_8_, f32[160,768]{1,0:T(8,128)} %collective-permute-done.6.refs_1_.refs_9_, ...), custom_call_target="tpu_custom_call" | custom-call | flops 219999993856 | bytes 200000000 | tf_op jit(solution)/shard_map/early/pallas_call | solution.py:273
  104.0 4.6 %expert.4 = (f32[88,768]{1,0:T(8,128)S(1)}, f32[88,768]{1,0:T(8,128)S(1)}, f32[2,160,384]{2,1,0:T(8,128)S(1)}, f32[2,160,384]{2,1,0:T(8,128)}) custom-call(f32[88,768]{1,0:T(8,128)} %get-tuple-element.328.refs_0_, f32[88,768]{1,0:T(8,128)} %collective-permute-done.16.refs_1_, f32[768,384]{1,0:T(8,128)} %bitcast.39, f32[768,384]{1,0:T(8,128)} %copy-done.68, ...), custom_call_target="tpu_custom_call" | custom-call | flops 65999998976 | bytes 60000000 | tf_op jit(solution)/shard_map/expert/pallas_call | solution.py:273
  110.6 3.6 collective-permute-done.20.refs_1_.refs_5_
  116.4 4.5 %expert.6 = (f32[88,768]{1,0:T(8,128)S(1)}, f32[88,768]{1,0:T(8,128)S(1)}, f32[2,160,384]{2,1,0:T(8,128)S(1)}, f32[2,160,384]{2,1,0:T(8,128)}) custom-call(f32[88,768]{1,0:T(8,128)} %collective-permute-done.15.refs_0_.refs_4_, f32[88,768]{1,0:T(8,128)S(1)} %collective-permute-done.20.refs_1_.refs_5_, f32[768,384]{1,0:T(8,128)} %bitcast.40, ...), custom_call_target="tpu_custom_call" | custom-call | flops 65999998976 | bytes 60000000 | tf_op jit(solution)/shard_map/expert/pallas_call | solution.py:273
  120.9 5.4 %expert.5 = (f32[88,768]{1,0:T(8,128)S(1)}, f32[88,768]{1,0:T(8,128)}, f32[2,160,384]{2,1,0:T(8,128)S(1)}, f32[2,160,384]{2,1,0:T(8,128)}) custom-call(f32[88,768]{1,0:T(8,128)} %collective-permute-done.14.refs_0_.refs_2_, f32[88,768]{1,0:T(8,128)S(1)} %collective-permute-done.19.refs_1_.refs_3_, f32[768,384]{1,0:T(8,128)} %bitcast.41, ...), custom_call_target="tpu_custom_call" | custom-call | flops 65999998976 | bytes 60000000 | tf_op jit(solution)/shard_map/expert/pallas_call | solution.py:273
  127.1 5.6 %expert.7 = (f32[88,768]{1,0:T(8,128)}, f32[88,768]{1,0:T(8,128)S(1)}, f32[2,160,384]{2,1,0:T(8,128)S(1)}, f32[2,160,384]{2,1,0:T(8,128)}) custom-call(f32[88,768]{1,0:T(8,128)S(1)} %collective-permute-done.18.refs_0_.refs_6_, f32[88,768]{1,0:T(8,128)S(1)} %collective-permute-done.21.refs_1_.refs_7_, f32[768,384]{1,0:T(8,128)} %bitcast.42, ...), custom_call_target="tpu_custom_call" | custom-call | flops 65999998976 | bytes 60000000 | tf_op jit(solution)/shard_map/expert/pallas_call | solution.py:273
  134.2 5.9 %collective-permute-done.22 = f32[88,768]{1,0:T(8,128)S(1)} collective-permute-done((f32[88,768]{1,0:T(8,128)S(1)}, f32[88,768]{1,0:T(8,128)S(1)}, u32[]{:S(2)}, u32[]{:S(2)}) %collective-permute-start.22) | collective-permute-done | bytes 270368 | tf_op jit(solution)/shard_map/ppermute | solution.py:47
  144.4 17.5 %expert_grads.1 = (f32[160,768]{1,0:T(8,128)}, f32[160,768]{1,0:T(8,128)}, f32[160,768]{1,0:T(8,128)}, f32[160,768]{1,0:T(8,128)}, f32[768,384]{1,0:T(8,128)}, /...) custom-call(f32[88,768]{1,0:T(8,128)} %get-tuple-element.328.refs_0_, ...), custom_call_target="tpu_custom_call" | custom-call | flops 330000007168 | bytes 300000000 | tf_op jit(solution)/shard_map/expert_grads/pallas_call | solution.py:273
  168.6 8.3 %collective-permute-done.27 = f32[88,768]{1,0:T(8,128)S(1)} collective-permute-done((f32[88,768]{1,0:T(8,128)S(1)}, f32[88,768]{1,0:T(8,128)S(1)}, u32[]{:S(2)}, u32[]{:S(2)}) %collective-permute-start.27) | collective-permute-done | bytes 270368 | tf_op jit(solution)/shard_map/ppermute | solution.py:47
  181.9 9.6 %mixer_back.1 = (f32[128,768]{1,0:T(8,128)S(1)}, f32[16,768]{1,0:T(8,128)S(1)}, f32[128,1536]{1,0:T(8,128)}, f32[128,1536]{1,0:T(8,128)}, f32[1,1536]{1,0:T(1,128)S(1)}, /*index=5*/f32[17,1536]{1,0:T(8,128)}) custom-call(s32[1]{0:T(128)} %bitcast.1.me_ref, f32[168,768]{1,0:T(8,128)} %copy-done.71, bf16[160,128]{1,0:T(8,128)(2,1)S(1)} %copy-done.15, ...), custom_call_target="tpu_custom_call" | custom-call | flops 330000007168 | bytes 300000000 | tf_op jit(solution)/shard_map/mixer_back/pallas_call | solution.py:273
  191.6 5.2 %late.2 = f32[768,1536]{1,0:T(8,128)} custom-call(s32[1]{0:T(128)} %bitcast.later_ref.which_ref.core_ref, f32[128,1536]{1,0:T(8,128)S(1)} %copy-done.50, f32[128,1536]{1,0:T(8,128)} %get-tuple-element.293.act_ref, f32[1,1536]{1,0:T(1,128)S(1)} %copy-done.20, f32[144,3072]{1,0:T(8,128)} %join.1.inner_ref.gate_z_ref, ...), custom_call_target="tpu_custom_call" | custom-call | flops 219999993856 | bytes 200000000 | tf_op jit(solution)/shard_map/late/pallas_call | solution.py:273
  198.5 8.2 %late.3 = (f32[768,1536]{1,0:T(8,128)}, f32[128,768]{1,0:T(8,128)S(1)}) custom-call(s32[1]{0:T(128)S(6)} %sub.76.which_ref, f32[128,1536]{1,0:T(8,128)S(1)} %copy-done.50, f32[128,1536]{1,0:T(8,128)} %get-tuple-element.293.act_ref, f32[1,1536]{1,0:T(1,128)S(1)} %copy-done.20, f32[144,3072]{1,0:T(8,128)} %join.1.inner_ref.gate_z_ref, ...), custom_call_target="tpu_custom_call" | custom-call | flops 219999993856 | bytes 200000000 | tf_op jit(solution)/shard_map/late/pallas_call | solution.py:273
  210.6 2.7 collective-permute-done.34.got_ref
  213.4 6.3 %collective-permute-done.36 = f32[192,768]{1,0:T(8,128)} collective-permute-done((f32[192,768]{1,0:T(8,128)}, f32[192,768]{1,0:T(8,128)}, u32[]{:S(2)}, u32[]{:S(2)}) %collective-permute-start.36) | collective-permute-done | bytes 589856 | tf_op jit(solution)/shard_map/ppermute | solution.py:47
  220.3 3.3 dynamic-slice_add_fusion.1
  227.8 3.5 collective-permute-done.38.got_ref
  234.5 5.0 %collective-permute-done.39.got_ref = f32[17,1536]{1,0:T(8,128)S(1)} collective-permute-done((f32[17,1536]{1,0:T(8,128)S(1)}, f32[17,1536]{1,0:T(8,128)S(1)}, u32[]{:S(2)}, u32[]{:S(2)}) %collective-permute-start.39) | collective-permute-done | bytes 104480 | tf_op jit(solution)/shard_map/ppermute | solution.py:47
  240.5 3.1 collective-permute-start.45
  243.7 8.5 %scan_back.3 = (f32[128,1536]{1,0:T(8,128)S(1)}, f32[128,1536]{1,0:T(8,128)}, f32[16,1536]{1,0:T(8,128)S(1)}, f32[80,128]{1,0:T(8,128)S(1)}) custom-call(f32[128,1536]{1,0:T(8,128)} %get-tuple-element.290.masked_ref, f32[128,1536]{1,0:T(8,128)} %get-tuple-element.291.steps_ref, f32[128,1536]{1,0:T(8,128)} %get-tuple-element.292.drive_ref, ...), custom_call_target="tpu_custom_call" | custom-call | flops 11000000512 | bytes 10000000 | tf_op jit(solution)/shard_map/scan_back/pallas_call | solution.py:273
  256.4 8.3 %scan_back.4 = (f32[128,1536]{1,0:T(8,128)S(1)}, f32[128,1536]{1,0:T(8,128)}, f32[16,1536]{1,0:T(8,128)S(1)}, f32[80,128]{1,0:T(8,128)S(1)}) custom-call(f32[128,1536]{1,0:T(8,128)} %get-tuple-element.290.masked_ref, f32[128,1536]{1,0:T(8,128)} %get-tuple-element.291.steps_ref, ...), custom_call_target="tpu_custom_call", output_to_operand_aliasing={{0}: (14, {}), {1}: (15, {}), {2}: (16, {})} | custom-call | flops 11000000512 | bytes 10000000 | tf_op jit(solution)/shard_map/scan_back/pallas_call | solution.py:273
  271.7 8.3 %scan_back.5 = (f32[128,1536]{1,0:T(8,128)S(1)}, f32[128,1536]{1,0:T(8,128)}, f32[16,1536]{1,0:T(8,128)S(1)}, f32[80,128]{1,0:T(8,128)S(1)}) custom-call(f32[128,1536]{1,0:T(8,128)} %get-tuple-element.290.masked_ref, f32[128,1536]{1,0:T(8,128)} %get-tuple-element.291.steps_ref, ...), custom_call_target="tpu_custom_call", output_to_operand_aliasing={{0}: (14, {}), {1}: (15, {}), {2}: (16, {})} | custom-call | flops 11000000512 | bytes 10000000 | tf_op jit(solution)/shard_map/scan_back/pallas_call | solution.py:273
  282.3 2.8 collective-permute-start.50
  285.6 11.4 %input_back.1 = (f32[480,1536]{1,0:T(8,128)}, f32[480,1536]{1,0:T(8,128)}, f32[128,768]{1,0:T(8,128)S(1)}, f32[16,768]{1,0:T(8,128)S(1)}) custom-call(s32[1]{0:T(128)} %bitcast.later_ref.which_ref.core_ref, f32[80,128]{1,0:T(8,128)S(1)} %get-tuple-element.425.proj_a_ref, f32[80,128]{1,0:T(8,128)S(1)} %get-tuple-element.438.proj_b_ref, ...), custom_call_target="tpu_custom_call" | custom-call | flops 12099999744 | bytes 11000000 | tf_op jit(solution)/shard_map/input_back/pallas_call | solution.py:273
  297.8 5.7 %collective-permute-done.53 = f32[480,1536]{1,0:T(8,128)} collective-permute-done((f32[480,1536]{1,0:T(8,128)}, f32[480,1536]{1,0:T(8,128)}, u32[]{:S(2)}, u32[]{:S(2)}) %collective-permute-start.53) | collective-permute-done | bytes 2949152 | tf_op jit(solution)/shard_map/ppermute | solution.py:47
  303.6 3.2 dynamic-slice_add_fusion.5
  313.8 11.7 %collective-permute-done.52 = f32[192,384]{1,0:T(8,128)S(1)} collective-permute-done((f32[192,384]{1,0:T(8,128)}, f32[192,384]{1,0:T(8,128)S(1)}, u32[]{:S(2)}, u32[]{:S(2)}) %collective-permute-start.52) | collective-permute-done | bytes 294944 | tf_op jit(solution)/shard_map/ppermute | solution.py:47
  335.2 2.8 collective-permute-done.58
  345.8 2.5 maximum_add_fusion
  352.1 5.7 %collective-permute-done.62 = f32[120,384]{1,0:T(8,128)S(1)} collective-permute-done((f32[120,384]{1,0:T(8,128)S(1)}, f32[120,384]{1,0:T(8,128)S(1)}, u32[]{:S(2)}, u32[]{:S(2)}) %collective-permute-start.62) | collective-permute-done | bytes 184352 | tf_op jit(solution)/shard_map/ppermute | solution.py:47
  367.1 10.0 %collective-permute-done.67 = f32[120,384]{1,0:T(8,128)S(1)} collective-permute-done((f32[120,384]{1,0:T(8,128)S(1)}, f32[120,384]{1,0:T(8,128)S(1)}, u32[]{:S(2)}, u32[]{:S(2)}) %collective-permute-start.67) | collective-permute-done | bytes 184352 | tf_op jit(solution)/shard_map/ppermute | solution.py:47
  377.2 6.5 %collective-permute-done.64 = f32[192,1536]{1,0:T(8,128)S(1)} collective-permute-done((f32[192,1536]{1,0:T(8,128)S(1)}, f32[192,1536]{1,0:T(8,128)S(1)}, u32[]{:S(2)}, u32[]{:S(2)}) %collective-permute-start.64) | collective-permute-done | bytes 1179680 | tf_op jit(solution)/shard_map/ppermute | solution.py:47
  385.5 5.1 %collective-permute-done.65 = f32[192,1536]{1,0:T(8,128)S(1)} collective-permute-done((f32[192,1536]{1,0:T(8,128)S(1)}, f32[192,1536]{1,0:T(8,128)S(1)}, u32[]{:S(2)}, u32[]{:S(2)}) %collective-permute-start.65) | collective-permute-done | bytes 1179680 | tf_op jit(solution)/shard_map/ppermute | solution.py:47
  396.0 8.0 %collective-permute-done.72 = f32[60,1536]{1,0:T(8,128)S(1)} collective-permute-done((f32[60,1536]{1,0:T(8,128)S(1)}, f32[60,1536]{1,0:T(8,128)S(1)}, u32[]{:S(2)}, u32[]{:S(2)}) %collective-permute-start.72) | collective-permute-done | bytes 368672 | tf_op jit(solution)/shard_map/ppermute | solution.py:47
  409.4 7.8 %finish_late.1 = (f32[768,3072]{1,0:T(8,128)}, f32[2,768,768]{2,1,0:T(8,128)}) custom-call(s32[1]{0:T(128)} %bitcast.later_ref.which_ref.core_ref, f32[384,1536]{1,0:T(8,128)} %pad_maximum_fusion.first_ref, f32[384,1536]{1,0:T(8,128)} %pad_maximum_fusion.1.second_ref, f32[384,1536]{1,0:T(8,128)} %collective-permute-done.73.got_first_ref, ...), custom_call_target="tpu_custom_call" | custom-call | flops 8800000000 | bytes 8000000 | tf_op jit(solution)/shard_map/finish_late/pallas_call | solution.py:273
  417.1 5.4 %collective-permute-done.75 = f32[120,1536]{1,0:T(8,128)S(1)} collective-permute-done((f32[120,1536]{1,0:T(8,128)S(1)}, f32[120,1536]{1,0:T(8,128)S(1)}, u32[]{:S(2)}, u32[]{:S(2)}) %collective-permute-start.75) | collective-permute-done | bytes 737312 | tf_op jit(solution)/shard_map/ppermute | solution.py:47
  424.3 2.8 collective-permute-done.77.got_first_ref
  430.4 5.9 %finish.1 = (f32[768,3072]{1,0:T(8,128)}, f32[1536,80]{1,0:T(8,128)S(1)}, f32[48,1536]{1,0:T(8,128)}, f32[1536,16]{1,0:T(8,128)S(1)}, f32[4,1536]{1,0:T(4,128)},...) custom-call(s32[1]{0:T(128)} %bitcast.later_ref.which_ref.core_ref, ...), custom_call_target="tpu_custom_call", output_to_operand_aliasing={{0}: (5, {})} | custom-call | flops 6600000000 | bytes 6000000 | tf_op jit(solution)/shard_map/finish/pallas_call | solution.py:273
  (424 shorter events, 147.4 us)
Async XLA Ops:
  3.8 32.4 %collective-permute-start.3 = (f32[384,768]{1,0:T(8,128)}, f32[384,768]{1,0:T(8,128)}, u32[]{:S(2)}, u32[]{:S(2)}) collective-permute-start(f32[384,768]{1,0:T(8,128)} %bitcast.45), channel_id=1, source_target_pairs={{0,4},{1,5},{2,6},{3,7},{4,0},{5,1},{6,2},{7,3},{8,12},{9,13},{10,... | collective-permute-start | bytes 3538952 | tf_op jit(solution)/shard_map/ppermute | solution.py:47
  23.7 25.1 %collective-permute-start.7 = (f32[160,768]{1,0:T(8,128)}, f32[160,768]{1,0:T(8,128)}, u32[]{:S(2)}, u32[]{:S(2)}) collective-permute-start(f32[160,768]{1,0:T(8,128)} %pad_maximum_fusion.14.refs_0_.refs_8_), channel_id=1, source_target_pairs={{0,16},{1,17},{2,18},{3,19},{4,20},{5,21},{6,22},{7,23},{8,24},{9,... | collective-permute-start | bytes 1474568 | tf_op jit(solution)/shard_map/ppermute | solution.py:47
  26.3 22.7 %collective-permute-start.6 = (f32[160,768]{1,0:T(8,128)}, f32[160,768]{1,0:T(8,128)}, u32[]{:S(2)}, u32[]{:S(2)}) collective-permute-start(f32[160,768]{1,0:T(8,128)} %pad_maximum_fusion.14.refs_0_.refs_8_), channel_id=1, source_target_pairs={{0,8},{1,9},{2,10},{3,11},{4,12},{5,13},{6,14},{7,15},{8,0},{9,1},... | collective-permute-start | bytes 1474568 | tf_op jit(solution)/shard_map/ppermute | solution.py:47
  61.9 20.5 %collective-permute-start.12 = (f32[384,384]{1,0:T(8,128)}, f32[384,384]{1,0:T(8,128)}, u32[]{:S(2)}, u32[]{:S(2)}) collective-permute-start(f32[384,384]{1,0:T(8,128)} %get-tuple-element.641), channel_id=1, source_target_pairs={{0,4},{1,5},{2,6},{3,7},{4,0},{5,1},{6,2},{7,3},{8,12},{9,13},{10,... | collective-permute-start | bytes 1769480 | tf_op jit(solution)/shard_map/ppermute | solution.py:47
  67.3 15.1 %collective-permute-start.11 = (f32[160,768]{1,0:T(8,128)}, f32[160,768]{1,0:T(8,128)}, u32[]{:S(2)}, u32[]{:S(2)}) collective-permute-start(f32[160,768]{1,0:T(8,128)} %collective-permute-done.7.refs_2_.refs_10_), channel_id=1, source_target_pairs={{0,8},{1,9},{2,10},{3,11},{4,12},{5,13},{6,14},{7,15},{8,0},{9,1},... | collective-permute-start | bytes 1474568 | tf_op jit(solution)/shard_map/ppermute | solution.py:47
  82.5 16.9 %collective-permute-start.17 = (f32[384,384]{1,0:T(8,128)}, f32[384,384]{1,0:T(8,128)}, u32[]{:S(2)}, u32[]{:S(2)}) collective-permute-start(f32[384,384]{1,0:T(8,128)} %get-tuple-element.327), channel_id=1, source_target_pairs={{0,4},{1,5},{2,6},{3,7},{4,0},{5,1},{6,2},{7,3},{8,12},{9,13},{10,... | collective-permute-start | bytes 1769480 | tf_op jit(solution)/shard_map/ppermute | solution.py:47
  86.4 23.0 %collective-permute-start.15 = (f32[88,768]{1,0:T(8,128)}, f32[88,768]{1,0:T(8,128)}, u32[]{:S(2)}, u32[]{:S(2)}) collective-permute-start(f32[88,768]{1,0:T(8,128)} %get-tuple-element.328.refs_0_), channel_id=1, source_target_pairs={{0,16},{1,17},{2,18},{3,19},{4,20},{5,21},{6,22},{7,23},{8,24},{9,... | collective-permute-start | bytes 811016 | tf_op jit(solution)/shard_map/ppermute | solution.py:47
  89.6 19.8 %collective-permute-start.14 = (f32[88,768]{1,0:T(8,128)}, f32[88,768]{1,0:T(8,128)}, u32[]{:S(2)}, u32[]{:S(2)}) collective-permute-start(f32[88,768]{1,0:T(8,128)} %get-tuple-element.328.refs_0_), channel_id=1, source_target_pairs={{0,8},{1,9},{2,10},{3,11},{4,12},{5,13},{6,14},{7,15},{8,0},{9,1},... | collective-permute-start | bytes 811016 | tf_op jit(solution)/shard_map/ppermute | solution.py:47
  99.4 14.8 %collective-permute-start.20 = (f32[88,768]{1,0:T(8,128)}, f32[88,768]{1,0:T(8,128)S(1)}, u32[]{:S(2)}, u32[]{:S(2)}) collective-permute-start(f32[88,768]{1,0:T(8,128)} %collective-permute-done.16.refs_1_), channel_id=1, source_target_pairs={{0,16},{1,17},{2,18},{3,19},{4,20},{5,21},{6,22},{7,23},{8,24},{9,... | collective-permute-start | bytes 811016 | tf_op jit(solution)/shard_map/ppermute | solution.py:47
  101.0 14.8 %collective-permute-start.19 = (f32[88,768]{1,0:T(8,128)}, f32[88,768]{1,0:T(8,128)S(1)}, u32[]{:S(2)}, u32[]{:S(2)}) collective-permute-start(f32[88,768]{1,0:T(8,128)} %collective-permute-done.16.refs_1_), channel_id=1, source_target_pairs={{0,8},{1,9},{2,10},{3,11},{4,12},{5,13},{6,14},{7,15},{8,0},{9,1},... | collective-permute-start | bytes 811016 | tf_op jit(solution)/shard_map/ppermute | solution.py:47
  109.4 17.7 %collective-permute-start.18 = (f32[88,768]{1,0:T(8,128)}, f32[88,768]{1,0:T(8,128)S(1)}, u32[]{:S(2)}, u32[]{:S(2)}) collective-permute-start(f32[88,768]{1,0:T(8,128)} %collective-permute-done.15.refs_0_.refs_4_), channel_id=1, source_target_pairs={{0,8},{1,9},{2,10},{3,11},{4,12},{5,13},{6,14},{7,15},{8,0},{9,1},... | collective-permute-start | bytes 811016 | tf_op jit(solution)/shard_map/ppermute | solution.py:47
  115.9 11.2 %collective-permute-start.21 = (f32[88,768]{1,0:T(8,128)S(1)}, f32[88,768]{1,0:T(8,128)S(1)}, u32[]{:S(2)}, u32[]{:S(2)}) collective-permute-start(f32[88,768]{1,0:T(8,128)S(1)} %collective-permute-done.20.refs_1_.refs_5_), channel_id=1, source_target_pairs={{0,8},{1,9},{2,10},{3,11},{4,12},{5,13},{6,14},{7,15},{8,0},{9,1},... | collective-permute-start | bytes 811016 | tf_op jit(solution)/shard_map/ppermute | solution.py:47
  140.8 21.1 %collective-permute-start.24 = (f32[88,768]{1,0:T(8,128)}, f32[88,768]{1,0:T(8,128)}, u32[]{:S(2)}, u32[]{:S(2)}) collective-permute-start(f32[88,768]{1,0:T(8,128)} %add.342), channel_id=1, source_target_pairs={{0,16},{1,17},{2,18},{3,19},{4,20},{5,21},{6,22},{7,23},{8,24},{9,... | collective-permute-start | bytes 811016 | tf_op jit(solution)/shard_map/ppermute | solution.py:47
  142.4 19.5 %collective-permute-start.23 = (f32[88,768]{1,0:T(8,128)}, f32[88,768]{1,0:T(8,128)}, u32[]{:S(2)}, u32[]{:S(2)}) collective-permute-start(f32[88,768]{1,0:T(8,128)} %get-tuple-element.359), channel_id=1, source_target_pairs={{0,8},{1,9},{2,10},{3,11},{4,12},{5,13},{6,14},{7,15},{8,0},{9,1},... | collective-permute-start | bytes 811016 | tf_op jit(solution)/shard_map/ppermute | solution.py:47
  143.9 19.3 %collective-permute-start.25 = (f32[88,768]{1,0:T(8,128)}, f32[88,768]{1,0:T(8,128)}, u32[]{:S(2)}, u32[]{:S(2)}) collective-permute-start(f32[88,768]{1,0:T(8,128)} %get-tuple-element.362), channel_id=1, source_target_pairs={{0,8},{1,9},{2,10},{3,11},{4,12},{5,13},{6,14},{7,15},{8,0},{9,1},... | collective-permute-start | bytes 811016 | tf_op jit(solution)/shard_map/ppermute | solution.py:47
  164.2 12.8 %collective-permute-start.27 = (f32[88,768]{1,0:T(8,128)S(1)}, f32[88,768]{1,0:T(8,128)S(1)}, u32[]{:S(2)}, u32[]{:S(2)}) collective-permute-start(f32[88,768]{1,0:T(8,128)S(1)} %add.345), channel_id=1, source_target_pairs={{0,16},{1,17},{2,18},{3,19},{4,20},{5,21},{6,22},{7,23},{8,24},{9,... | collective-permute-start | bytes 811016 | tf_op jit(solution)/shard_map/ppermute | solution.py:47
  165.6 11.4 %collective-permute-start.26 = (f32[88,768]{1,0:T(8,128)S(1)}, f32[88,768]{1,0:T(8,128)S(1)}, u32[]{:S(2)}, u32[]{:S(2)}) collective-permute-start(f32[88,768]{1,0:T(8,128)S(1)} %get-tuple-element.385), channel_id=1, source_target_pairs={{0,8},{1,9},{2,10},{3,11},{4,12},{5,13},{6,14},{7,15},{8,0},{9,1},... | collective-permute-start | bytes 811016 | tf_op jit(solution)/shard_map/ppermute | solution.py:47
  178.4 18.4 %collective-permute-start.30 = (f32[384,384]{1,0:T(8,128)}, f32[384,384]{1,0:T(8,128)}, u32[]{:S(2)}, u32[]{:S(2)}) collective-permute-start(f32[384,384]{1,0:T(8,128)} %get-tuple-element.639), channel_id=1, source_target_pairs={{0,4},{1,5},{2,6},{3,7},{4,0},{5,1},{6,2},{7,3},{8,12},{9,13},{10,... | collective-permute-start | bytes 1769480 | tf_op jit(solution)/shard_map/ppermute | solution.py:47
  180.1 27.7 %collective-permute-start.32 = (f32[160,768]{1,0:T(8,128)}, f32[160,768]{1,0:T(8,128)}, u32[]{:S(2)}, u32[]{:S(2)}) collective-permute-start(f32[160,768]{1,0:T(8,128)} %get-tuple-element.404), channel_id=1, source_target_pairs={{0,8},{1,9},{2,10},{3,11},{4,12},{5,13},{6,14},{7,15},{8,0},{9,1},... | collective-permute-start | bytes 1474568 | tf_op jit(solution)/shard_map/ppermute | solution.py:47
  180.9 26.9 %collective-permute-start.33 = (f32[384,384]{1,0:T(8,128)}, f32[384,384]{1,0:T(8,128)}, u32[]{:S(2)}, u32[]{:S(2)}) collective-permute-start(f32[384,384]{1,0:T(8,128)} %get-tuple-element.407), channel_id=1, source_target_pairs={{0,4},{1,5},{2,6},{3,7},{4,0},{5,1},{6,2},{7,3},{8,12},{9,13},{10,... | collective-permute-start | bytes 1769480 | tf_op jit(solution)/shard_map/ppermute | solution.py:47
  196.8 23.0 %collective-permute-start.35 = (f32[768,1536]{1,0:T(8,128)}, f32[768,1536]{1,0:T(8,128)}, u32[]{:S(2)}, u32[]{:S(2)}) collective-permute-start(f32[768,1536]{1,0:T(8,128)} %late.2), channel_id=1, source_target_pairs={{0,1},{1,0},{2,3},{3,2},{4,5},{5,4},{6,7},{7,6},{8,9},{9,8},{10,11... | collective-permute-start | bytes 14155784 | tf_op jit(solution)/shard_map/ppermute | solution.py:47
  197.3 22.4 %collective-permute-start.36 = (f32[192,768]{1,0:T(8,128)}, f32[192,768]{1,0:T(8,128)}, u32[]{:S(2)}, u32[]{:S(2)}) collective-permute-start(f32[192,768]{1,0:T(8,128)} %get-tuple-element.405), channel_id=1, source_target_pairs={{0,4},{1,5},{2,6},{3,7},{4,0},{5,1},{6,2},{7,3},{8,12},{9,13},{10,... | collective-permute-start | bytes 1769480 | tf_op jit(solution)/shard_map/ppermute | solution.py:47
  223.6 28.9 %collective-permute-start.40 = (f32[192,1536]{1,0:T(8,128)}, f32[192,1536]{1,0:T(8,128)S(1)}, u32[]{:S(2)}, u32[]{:S(2)}) collective-permute-start(f32[192,1536]{1,0:T(8,128)} %get-tuple-element.608), channel_id=1, source_target_pairs={{0,4},{1,5},{2,6},{3,7},{4,0},{5,1},{6,2},{7,3},{8,12},{9,13},{10,... | collective-permute-start | bytes 3538952 | tf_op jit(solution)/shard_map/ppermute | solution.py:47
  225.1 27.3 %collective-permute-start.41 = (f32[192,1536]{1,0:T(8,128)}, f32[192,1536]{1,0:T(8,128)}, u32[]{:S(2)}, u32[]{:S(2)}) collective-permute-start(f32[192,1536]{1,0:T(8,128)} %get-tuple-element.607), channel_id=1, source_target_pairs={{0,2},{1,3},{2,0},{3,1},{4,6},{5,7},{6,4},{7,5},{8,10},{9,11},{10,... | collective-permute-start | bytes 3538952 | tf_op jit(solution)/shard_map/ppermute | solution.py:47
  240.5 27.8 %collective-permute-start.44 = (f32[160,768]{1,0:T(8,128)S(1)}, f32[160,768]{1,0:T(8,128)S(1)}, u32[]{:S(2)}, u32[]{:S(2)}) collective-permute-start(f32[160,768]{1,0:T(8,128)S(1)} %copy-done.81), channel_id=1, source_target_pairs={{0,8},{1,9},{2,10},{3,11},{4,12},{5,13},{6,14},{7,15},{8,0},{9,1},... | collective-permute-start | bytes 1474568 | tf_op jit(solution)/shard_map/ppermute | solution.py:47
  240.5 27.8 %collective-permute-start.45 = (f32[160,768]{1,0:T(8,128)S(1)}, f32[160,768]{1,0:T(8,128)S(1)}, u32[]{:S(2)}, u32[]{:S(2)}) collective-permute-start(f32[160,768]{1,0:T(8,128)S(1)} %add.347), channel_id=1, source_target_pairs={{0,16},{1,17},{2,18},{3,19},{4,20},{5,21},{6,22},{7,23},{8,24},{9,... | collective-permute-start | bytes 1474568 | tf_op jit(solution)/shard_map/ppermute | solution.py:47
  252.6 15.6 %collective-permute-start.42 = (f32[96,1536]{1,0:T(8,128)S(1)}, f32[96,1536]{1,0:T(8,128)S(1)}, u32[]{:S(2)}, u32[]{:S(2)}) collective-permute-start(f32[96,1536]{1,0:T(8,128)S(1)} %dynamic-slice_add_fusion.11), channel_id=1, source_target_pairs={{0,2},{1,3},{2,0},{3,1},{4,6},{5,7},{6,4},{7,5},{8,10},{9,11},{10,... | collective-permute-start | bytes 1769480 | tf_op jit(solution)/shard_map/ppermute | solution.py:47
  254.8 13.4 %collective-permute-start.43 = (f32[96,1536]{1,0:T(8,128)S(1)}, f32[96,1536]{1,0:T(8,128)S(1)}, u32[]{:S(2)}, u32[]{:S(2)}) collective-permute-start(f32[96,1536]{1,0:T(8,128)S(1)} %dynamic-slice_add_fusion.9), channel_id=1, source_target_pairs={{0,4},{1,5},{2,6},{3,7},{4,0},{5,1},{6,2},{7,3},{8,12},{9,13},{10,... | collective-permute-start | bytes 1769480 | tf_op jit(solution)/shard_map/ppermute | solution.py:47
  270.2 12.0 %collective-permute-start.48 = (f32[192,768]{1,0:T(8,128)S(1)}, f32[192,768]{1,0:T(8,128)S(1)}, u32[]{:S(2)}, u32[]{:S(2)}) collective-permute-start(f32[192,768]{1,0:T(8,128)S(1)} %copy-done.64), channel_id=1, source_target_pairs={{0,4},{1,5},{2,6},{3,7},{4,0},{5,1},{6,2},{7,3},{8,12},{9,13},{10,... | collective-permute-start | bytes 1769480 | tf_op jit(solution)/shard_map/ppermute | solution.py:47
  282.3 14.7 %collective-permute-start.50 = (f32[192,384]{1,0:T(8,128)S(1)}, f32[192,384]{1,0:T(8,128)S(1)}, u32[]{:S(2)}, u32[]{:S(2)}) collective-permute-start(f32[192,384]{1,0:T(8,128)S(1)} %add_add_fusion.1), channel_id=1, source_target_pairs={{0,16},{1,17},{2,18},{3,19},{4,20},{5,21},{6,22},{7,23},{8,24},{9,... | collective-permute-start | bytes 884744 | tf_op jit(solution)/shard_map/ppermute | solution.py:47
  285.0 12.0 %collective-permute-start.49 = (f32[192,384]{1,0:T(8,128)S(1)}, f32[192,384]{1,0:T(8,128)S(1)}, u32[]{:S(2)}, u32[]{:S(2)}) collective-permute-start(f32[192,384]{1,0:T(8,128)S(1)} %get-tuple-element.475), channel_id=1, source_target_pairs={{0,8},{1,9},{2,10},{3,11},{4,12},{5,13},{6,14},{7,15},{8,0},{9,1},... | collective-permute-start | bytes 884744 | tf_op jit(solution)/shard_map/ppermute | solution.py:47
  306.8 18.8 %collective-permute-start.55 = (f32[120,1536]{1,0:T(8,128)}, f32[120,1536]{1,0:T(8,128)}, u32[]{:S(2)}, u32[]{:S(2)}) collective-permute-start(f32[120,1536]{1,0:T(8,128)} %get-tuple-element.609), channel_id=1, source_target_pairs={{0,2},{1,3},{2,0},{3,1},{4,6},{5,7},{6,4},{7,5},{8,10},{9,11},{10,... | collective-permute-start | bytes 2211848 | tf_op jit(solution)/shard_map/ppermute | solution.py:47
  308.3 18.6 %collective-permute-start.54 = (f32[120,1536]{1,0:T(8,128)}, f32[120,1536]{1,0:T(8,128)}, u32[]{:S(2)}, u32[]{:S(2)}) collective-permute-start(f32[120,1536]{1,0:T(8,128)} %get-tuple-element.610), channel_id=1, source_target_pairs={{0,4},{1,5},{2,6},{3,7},{4,0},{5,1},{6,2},{7,3},{8,12},{9,13},{10,... | collective-permute-start | bytes 2211848 | tf_op jit(solution)/shard_map/ppermute | solution.py:47
  309.5 16.0 %collective-permute-start.52 = (f32[192,384]{1,0:T(8,128)}, f32[192,384]{1,0:T(8,128)S(1)}, u32[]{:S(2)}, u32[]{:S(2)}) collective-permute-start(f32[192,384]{1,0:T(8,128)} %add_add_fusion.2), channel_id=1, source_target_pairs={{0,16},{1,17},{2,18},{3,19},{4,20},{5,21},{6,22},{7,23},{8,24},{9,... | collective-permute-start | bytes 884744 | tf_op jit(solution)/shard_map/ppermute | solution.py:47
  310.8 14.7 %collective-permute-start.51 = (f32[192,384]{1,0:T(8,128)}, f32[192,384]{1,0:T(8,128)S(1)}, u32[]{:S(2)}, u32[]{:S(2)}) collective-permute-start(f32[192,384]{1,0:T(8,128)} %add_add_fusion.2), channel_id=1, source_target_pairs={{0,8},{1,9},{2,10},{3,11},{4,12},{5,13},{6,14},{7,15},{8,0},{9,1},... | collective-permute-start | bytes 884744 | tf_op jit(solution)/shard_map/ppermute | solution.py:47
  343.2 14.7 %collective-permute-start.62 = (f32[120,384]{1,0:T(8,128)S(1)}, f32[120,384]{1,0:T(8,128)S(1)}, u32[]{:S(2)}, u32[]{:S(2)}) collective-permute-start(f32[120,384]{1,0:T(8,128)S(1)} %get-tuple-element.627), channel_id=1, source_target_pairs={{0,16},{1,17},{2,18},{3,19},{4,20},{5,21},{6,22},{7,23},{8,24},{9,... | collective-permute-start | bytes 552968 | tf_op jit(solution)/shard_map/ppermute | solution.py:47
  344.3 13.6 %collective-permute-start.60 = (f32[96,1536]{1,0:T(8,128)S(1)}, f32[96,1536]{1,0:T(8,128)S(1)}, u32[]{:S(2)}, u32[]{:S(2)}) collective-permute-start(f32[96,1536]{1,0:T(8,128)S(1)} %get-tuple-element.630), channel_id=1, source_target_pairs={{0,4},{1,5},{2,6},{3,7},{4,0},{5,1},{6,2},{7,3},{8,12},{9,13},{10,... | collective-permute-start | bytes 1769480 | tf_op jit(solution)/shard_map/ppermute | solution.py:47
  345.2 12.7 %collective-permute-start.59 = (f32[96,1536]{1,0:T(8,128)S(1)}, f32[96,1536]{1,0:T(8,128)S(1)}, u32[]{:S(2)}, u32[]{:S(2)}) collective-permute-start(f32[96,1536]{1,0:T(8,128)S(1)} %get-tuple-element.631), channel_id=1, source_target_pairs={{0,2},{1,3},{2,0},{3,1},{4,6},{5,7},{6,4},{7,5},{8,10},{9,11},{10,... | collective-permute-start | bytes 1769480 | tf_op jit(solution)/shard_map/ppermute | solution.py:47
  351.9 12.5 %collective-permute-start.69 = (f32[80,768]{1,0:T(8,128)S(1)}, f32[80,768]{1,0:T(8,128)S(1)}, u32[]{:S(2)}, u32[]{:S(2)}) collective-permute-start(f32[80,768]{1,0:T(8,128)S(1)} %pad_maximum_fusion.24), channel_id=1, source_target_pairs={{0,1},{1,0},{2,3},{3,2},{4,5},{5,4},{6,7},{7,6},{8,9},{9,8},{10,11... | collective-permute-start | bytes 737288 | tf_op jit(solution)/shard_map/ppermute | solution.py:47
  358.3 25.4 %collective-permute-start.64 = (f32[192,1536]{1,0:T(8,128)S(1)}, f32[192,1536]{1,0:T(8,128)S(1)}, u32[]{:S(2)}, u32[]{:S(2)}) collective-permute-start(f32[192,1536]{1,0:T(8,128)S(1)} %pad_maximum_fusion.7), channel_id=1, source_target_pairs={{0,4},{1,5},{2,6},{3,7},{4,0},{5,1},{6,2},{7,3},{8,12},{9,13},{10,... | collective-permute-start | bytes 3538952 | tf_op jit(solution)/shard_map/ppermute | solution.py:47
  362.0 15.1 %collective-permute-start.67 = (f32[120,384]{1,0:T(8,128)S(1)}, f32[120,384]{1,0:T(8,128)S(1)}, u32[]{:S(2)}, u32[]{:S(2)}) collective-permute-start(f32[120,384]{1,0:T(8,128)S(1)} %add_add_fusion.5), channel_id=1, source_target_pairs={{0,16},{1,17},{2,18},{3,19},{4,20},{5,21},{6,22},{7,23},{8,24},{9,... | collective-permute-start | bytes 552968 | tf_op jit(solution)/shard_map/ppermute | solution.py:47
  362.8 14.3 %collective-permute-start.66 = (f32[120,384]{1,0:T(8,128)S(1)}, f32[120,384]{1,0:T(8,128)S(1)}, u32[]{:S(2)}, u32[]{:S(2)}) collective-permute-start(f32[120,384]{1,0:T(8,128)S(1)} %add_add_fusion.5), channel_id=1, source_target_pairs={{0,24},{1,25},{2,26},{3,27},{4,28},{5,29},{6,30},{7,31},{8,16},{9,... | collective-permute-start | bytes 552968 | tf_op jit(solution)/shard_map/ppermute | solution.py:47
  364.5 26.1 %collective-permute-start.65 = (f32[192,1536]{1,0:T(8,128)S(1)}, f32[192,1536]{1,0:T(8,128)S(1)}, u32[]{:S(2)}, u32[]{:S(2)}) collective-permute-start(f32[192,1536]{1,0:T(8,128)S(1)} %pad_maximum_fusion.8), channel_id=1, source_target_pairs={{0,2},{1,3},{2,0},{3,1},{4,6},{5,7},{6,4},{7,5},{8,10},{9,11},{10,... | collective-permute-start | bytes 3538952 | tf_op jit(solution)/shard_map/ppermute | solution.py:47
  392.3 12.9 %collective-permute-start.73 = (f32[384,1536]{1,0:T(8,128)}, f32[384,1536]{1,0:T(8,128)}, u32[]{:S(2)}, u32[]{:S(2)}) collective-permute-start(f32[384,1536]{1,0:T(8,128)} %pad_maximum_fusion.first_ref), channel_id=1, source_target_pairs={{0,1},{1,0},{2,3},{3,2},{4,5},{5,4},{6,7},{7,6},{8,9},{9,8},{10,11... | collective-permute-start | bytes 7077896 | tf_op jit(solution)/shard_map/ppermute | solution.py:47
  392.3 12.9 %collective-permute-start.74 = (f32[384,1536]{1,0:T(8,128)}, f32[384,1536]{1,0:T(8,128)}, u32[]{:S(2)}, u32[]{:S(2)}) collective-permute-start(f32[384,1536]{1,0:T(8,128)} %pad_maximum_fusion.1.second_ref), channel_id=1, source_target_pairs={{0,1},{1,0},{2,3},{3,2},{4,5},{5,4},{6,7},{7,6},{8,9},{9,8},{10,11... | collective-permute-start | bytes 7077896 | tf_op jit(solution)/shard_map/ppermute | solution.py:47
  392.9 11.1 %collective-permute-start.72 = (f32[60,1536]{1,0:T(8,128)S(1)}, f32[60,1536]{1,0:T(8,128)S(1)}, u32[]{:S(2)}, u32[]{:S(2)}) collective-permute-start(f32[60,1536]{1,0:T(8,128)S(1)} %get-tuple-element.648), channel_id=1, source_target_pairs={{0,4},{1,5},{2,6},{3,7},{4,0},{5,1},{6,2},{7,3},{8,12},{9,13},{10,... | collective-permute-start | bytes 1105928 | tf_op jit(solution)/shard_map/ppermute | solution.py:47
  405.2 17.3 %collective-permute-start.75 = (f32[120,1536]{1,0:T(8,128)S(1)}, f32[120,1536]{1,0:T(8,128)S(1)}, u32[]{:S(2)}, u32[]{:S(2)}) collective-permute-start(f32[120,1536]{1,0:T(8,128)S(1)} %pad_maximum_fusion.12), channel_id=1, source_target_pairs={{0,4},{1,5},{2,6},{3,7},{4,0},{5,1},{6,2},{7,3},{8,12},{9,13},{10,... | collective-permute-start | bytes 2211848 | tf_op jit(solution)/shard_map/ppermute | solution.py:47
  406.2 16.9 %collective-permute-start.76 = (f32[120,1536]{1,0:T(8,128)S(1)}, f32[120,1536]{1,0:T(8,128)S(1)}, u32[]{:S(2)}, u32[]{:S(2)}) collective-permute-start(f32[120,1536]{1,0:T(8,128)S(1)} %pad_maximum_fusion.13), channel_id=1, source_target_pairs={{0,2},{1,3},{2,0},{3,1},{4,6},{5,7},{6,4},{7,5},{8,10},{9,11},{10,... | collective-permute-start | bytes 2211848 | tf_op jit(solution)/shard_map/ppermute | solution.py:47
  (113 other events, 799.8 us)

commit v8 on v7

--- a/solution.py
+++ b/solution.py
@@ -105,13 +105,14 @@
 
 def cut_outer(grid, parts):
     columns = parts[0].shape[1] // grid.outer
-    return [
-        functools.reduce(
-            jnp.add,
-            [lax.dynamic_slice_in_dim(p, (grid.at["outer"] ^ s) * columns, columns, 1) for p in parts],
-        )
-        for s in range(grid.outer)
-    ]
+
+    def block(parts, s):
+        cut = [lax.dynamic_slice_in_dim(p, (grid.at["outer"] ^ s) * columns, columns, 1) for p in parts]
+        return functools.reduce(jnp.add, cut)
+
+    others = [block(parts, s) for s in range(1, grid.outer)]
+    parts, _ = tie(list(parts), others)
+    return [block(parts, 0)] + others
 
 
 def sum_outer(grid, parts):
@@ -938,8 +939,8 @@
         in_ref[0:quarter, :] = one[...]
         in_ref[quarter:half, :] = two[0:rest, :]
         at = rest + 2 * states + rank_n
-        state_proj_ref[...] = two[rest:at, :].T
-        decay_ref[...] = two[at : at + states, :].T
+        state_proj_ref[...] = two[rest:at, :]
+        decay_ref[...] = two[at : at + states, :]
 
     def second_half(one, two):
         in_ref[half : half + quarter, :] = one[...]
@@ -1367,21 +1368,20 @@
     )
     grads_first, grads_second, grad_in_proj, grad_down = tie(grads_first, grads_second, grad_in_proj, grad_down)
     grads_other = [grid.swap(grads_first, "core", 1), grid.swap(grads_second, "core", 1)]
-    tall = lambda columns: pl.BlockSpec((chunk, columns), lambda c: (c, 0))
     (
         grad_in_proj, grad_state_proj, grad_step_proj, grad_decay_log, grad_conv_weight, rows, small,
     ) = call(
         functools.partial(finish_kernel, rank_n, states, taps),
         [
-            shape(depth, 2 * width), shape(width, rank_n + 2 * states), shape(rank_n, width),
-            shape(width, states), shape(taps, width), shape(8, width), shape(32, chunk),
+            shape(depth, 2 * width), shape(rank_n + 2 * states, width), shape(rank_n, width),
+            shape(states, width), shape(taps, width), shape(8, width), shape(32, chunk),
         ],
         (core, grads_first, grads_second, *grads_other, grad_in_proj),
         grid=(chunks,),
         in_specs=[SMEM] + [quarter] * 4 + [pl.BlockSpec(memory_space=pl.ANY)],
         out_specs=[
-            pl.BlockSpec((depth, chunk), block), tall(rank_n + 2 * states), pl.BlockSpec((rank_n, chunk), block),
-            tall(states), pl.BlockSpec((taps, chunk), block), pl.BlockSpec((8, chunk), block), full(32, chunk),
+            pl.BlockSpec((depth, chunk), block), pl.BlockSpec((rank_n + 2 * states, chunk), block), pl.BlockSpec((rank_n, chunk), block),
+            state_rows, pl.BlockSpec((taps, chunk), block), pl.BlockSpec((8, chunk), block), full(32, chunk),
         ],
         name="finish",
         aliases={5: 0},
@@ -1394,10 +1394,10 @@
         grad_in_proj,
         grad_conv_weight,
         rows[taps],
-        grad_state_proj,
+        grad_state_proj.T,
         grad_step_proj,
         rows[taps + 1],
-        grad_decay_log,
+        grad_decay_log.T,
         rows[taps + 2],
         grad_out_proj.reshape(width, depth),
         small[8],

time: 448 us -> 446 us (level)
    unnamed x171 -> x167, local copies, waits for them, and re-layouts: 15.2 us -> 12.7 us
  transfers between devices with their start and end apart: 79 -> 79, of which waited for: 38 -> 37; matrix products, arithmetic and copies ran while one was open for 9% -> 9% of each run, Pallas kernels for 31% -> 32%
where the time goes in v8:
time: 446 us; the launch traced here: 438 us
  Pallas kernels  150 us (34%)
  waiting for transfers between devices  139 us (31%)
  starting transfers between devices  84.3 us (19%)
  other arithmetic  40.6 us (9%)
  local copies, waits for them, and re-layouts  21.3 us (5%)
    pallas_call x29, Pallas kernels, call(): pl.pallas_call(kernel, out_shape=outs, grid=grid or (), in_specs=in_specs...  150 us
    ppermute x77, waiting for transfers between devices, swap_bits(): return lax.ppermute(block, AXES, [(i, i ^ bits) for i in range(self.total)])  139 us
    ppermute x77, starting transfers between devices, swap_bits(): return lax.ppermute(block, AXES, [(i, i ^ bits) for i in range(self.total)])  80.7 us
    add x14, other arithmetic, rows_of(): functools.reduce(jnp.add, [lax.dynamic_slice_in_dim(part, first, rows, 0)...  18.8 us
    unnamed x167, local copies, waits for them, and re-layouts  12.7 us
  transfers between devices with their start and end apart: 79, of which 37 were waited for; matrix products, arithmetic and copies ran while one was open for 9% of the time, Pallas kernels for 32%

profile of v8, /device:TPU:0, one launch (start us, length us, event | category | flops | bytes accessed | tf_op | source)
XLA Modules:
  0.0 438.3 jit_solution(2445838177659919508)
XLA Ops:
  1.5 2.3 collective-permute-start
  3.8 2.6 collective-permute-start.3
  14.9 7.9 %join.1.inner_ref.gate_z_ref = f32[144,3072]{1,0:T(8,128)} custom-call(f32[128,768]{1,0:T(8,128)S(1)} %copy-done.21, f32[16,768]{1,0:T(8,128)S(1)} %collective-permute-done.halo_ref, f32[1,768]{1,0:T(1,128)S(1)} %reshape.122.gain_ref, f32[768,3072]{1,0:T(8,128)} %weight_ref.3), custom_call_target="tpu_custom_call" | custom-call | flops 8800000000 | bytes 8000000 | tf_op jit(solution)/shard_map/join/pallas_call | solution.py:274
  23.7 2.6 collective-permute-start.7
  26.9 8.3 %features.1 = (f32[128,1536]{1,0:T(8,128)S(1)}, f32[128,1536]{1,0:T(8,128)}, f32[128,1536]{1,0:T(8,128)}, f32[128,1536]{1,0:T(8,128)}, f32[128,1536]{1,0:T(8,128...) custom-call(f32[144,3072]{1,0:T(8,128)} %join.1.inner_ref.gate_z_ref, ...), custom_call_target="tpu_custom_call" | custom-call | flops 275000000512 | bytes 250000000 | tf_op jit(solution)/shard_map/features/pallas_call | solution.py:274
  39.7 4.4 %collective-permute-done.5.got_ref = f32[17,1536]{1,0:T(8,128)S(1)} collective-permute-done((f32[17,1536]{1,0:T(8,128)S(1)}, f32[17,1536]{1,0:T(8,128)S(1)}, u32[]{:S(2)}, u32[]{:S(2)}) %collective-permute-start.5) | collective-permute-done | bytes 104480 | tf_op jit(solution)/shard_map/ppermute | solution.py:47
  44.2 4.6 %collective-permute-done.7.refs_2_.refs_10_ = f32[160,768]{1,0:T(8,128)} collective-permute-done((f32[160,768]{1,0:T(8,128)}, f32[160,768]{1,0:T(8,128)}, u32[]{:S(2)}, u32[]{:S(2)}) %collective-permute-start.7) | collective-permute-done | bytes 491552 | tf_op jit(solution)/shard_map/ppermute | solution.py:47
  49.4 4.7 %collective-permute-done.8.got_ref = f32[17,1536]{1,0:T(8,128)S(1)} collective-permute-done((f32[17,1536]{1,0:T(8,128)S(1)}, f32[17,1536]{1,0:T(8,128)S(1)}, u32[]{:S(2)}, u32[]{:S(2)}) %collective-permute-start.8) | collective-permute-done | bytes 104480 | tf_op jit(solution)/shard_map/ppermute | solution.py:47
  55.6 3.7 collective-permute-done.9.got_ref
  63.6 3.6 collective-permute-done.10.got_ref
  68.3 14.2 %scan.1 = (f32[128,1536]{1,0:T(8,128)}, f32[128,16,1536]{2,1,0:T(8,128)}, f32[128,768]{1,0:T(8,128)S(1)}, f32[168,768]{1,0:T(8,128)S(1)}, f32[128,8]{1,0:T(8,128)S(1)}, /*index=5*/f32[128,1]{1,0:T(8,128)S(1)}) custom-call(s32[1]{0:T(128)} %bitcast.1.me_ref, f32[128,1536]{1,0:T(8,128)} %get-tuple-element.294.masked_ref, ...), custom_call_target="tpu_custom_call" | custom-call | flops 219999993856 | bytes 200000000 | tf_op jit(solution)/shard_map/scan/pallas_call | solution.py:274
  86.5 3.3 collective-permute-start.15
  91.2 6.8 %early.1 = (f32[2,160,384]{2,1,0:T(8,128)S(1)}, f32[2,160,384]{2,1,0:T(8,128)S(1)}, f32[2,160,384]{2,1,0:T(8,128)S(1)}, f32[2,160,384]{2,1,0:T(8,128)S(1)}) custom-call(f32[160,768]{1,0:T(8,128)} %pad_maximum_fusion.14.refs_0_.refs_8_, f32[160,768]{1,0:T(8,128)} %collective-permute-done.6.refs_1_.refs_9_, ...), custom_call_target="tpu_custom_call" | custom-call | flops 219999993856 | bytes 200000000 | tf_op jit(solution)/shard_map/early/pallas_call | solution.py:274
  104.1 4.6 %expert.4 = (f32[88,768]{1,0:T(8,128)S(1)}, f32[88,768]{1,0:T(8,128)S(1)}, f32[2,160,384]{2,1,0:T(8,128)S(1)}, f32[2,160,384]{2,1,0:T(8,128)}) custom-call(f32[88,768]{1,0:T(8,128)} %get-tuple-element.332.refs_0_, f32[88,768]{1,0:T(8,128)} %collective-permute-done.16.refs_1_, f32[768,384]{1,0:T(8,128)} %bitcast.41, f32[768,384]{1,0:T(8,128)} %copy-done.67, ...), custom_call_target="tpu_custom_call" | custom-call | flops 65999998976 | bytes 60000000 | tf_op jit(solution)/shard_map/expert/pallas_call | solution.py:274
  110.8 3.6 collective-permute-done.20.refs_1_.refs_5_
  116.6 4.5 %expert.6 = (f32[88,768]{1,0:T(8,128)S(1)}, f32[88,768]{1,0:T(8,128)S(1)}, f32[2,160,384]{2,1,0:T(8,128)S(1)}, f32[2,160,384]{2,1,0:T(8,128)}) custom-call(f32[88,768]{1,0:T(8,128)} %collective-permute-done.15.refs_0_.refs_4_, f32[88,768]{1,0:T(8,128)S(1)} %collective-permute-done.20.refs_1_.refs_5_, f32[768,384]{1,0:T(8,128)} %bitcast.42, ...), custom_call_target="tpu_custom_call" | custom-call | flops 65999998976 | bytes 60000000 | tf_op jit(solution)/shard_map/expert/pallas_call | solution.py:274
  121.1 5.4 %expert.5 = (f32[88,768]{1,0:T(8,128)S(1)}, f32[88,768]{1,0:T(8,128)}, f32[2,160,384]{2,1,0:T(8,128)S(1)}, f32[2,160,384]{2,1,0:T(8,128)}) custom-call(f32[88,768]{1,0:T(8,128)} %collective-permute-done.14.refs_0_.refs_2_, f32[88,768]{1,0:T(8,128)S(1)} %collective-permute-done.19.refs_1_.refs_3_, f32[768,384]{1,0:T(8,128)} %bitcast.43, ...), custom_call_target="tpu_custom_call" | custom-call | flops 65999998976 | bytes 60000000 | tf_op jit(solution)/shard_map/expert/pallas_call | solution.py:274
  127.3 5.6 %expert.7 = (f32[88,768]{1,0:T(8,128)}, f32[88,768]{1,0:T(8,128)S(1)}, f32[2,160,384]{2,1,0:T(8,128)S(1)}, f32[2,160,384]{2,1,0:T(8,128)}) custom-call(f32[88,768]{1,0:T(8,128)S(1)} %collective-permute-done.18.refs_0_.refs_6_, f32[88,768]{1,0:T(8,128)S(1)} %collective-permute-done.21.refs_1_.refs_7_, f32[768,384]{1,0:T(8,128)} %bitcast.44, ...), custom_call_target="tpu_custom_call" | custom-call | flops 65999998976 | bytes 60000000 | tf_op jit(solution)/shard_map/expert/pallas_call | solution.py:274
  134.4 5.8 %collective-permute-done.22 = f32[88,768]{1,0:T(8,128)S(1)} collective-permute-done((f32[88,768]{1,0:T(8,128)S(1)}, f32[88,768]{1,0:T(8,128)S(1)}, u32[]{:S(2)}, u32[]{:S(2)}) %collective-permute-start.22) | collective-permute-done | bytes 270368 | tf_op jit(solution)/shard_map/ppermute | solution.py:47
  144.5 17.5 %expert_grads.1 = (f32[160,768]{1,0:T(8,128)}, f32[160,768]{1,0:T(8,128)}, f32[160,768]{1,0:T(8,128)}, f32[160,768]{1,0:T(8,128)}, f32[768,384]{1,0:T(8,128)}, /...) custom-call(f32[88,768]{1,0:T(8,128)} %get-tuple-element.332.refs_0_, ...), custom_call_target="tpu_custom_call" | custom-call | flops 330000007168 | bytes 300000000 | tf_op jit(solution)/shard_map/expert_grads/pallas_call | solution.py:274
  168.8 8.2 %collective-permute-done.27 = f32[88,768]{1,0:T(8,128)S(1)} collective-permute-done((f32[88,768]{1,0:T(8,128)S(1)}, f32[88,768]{1,0:T(8,128)S(1)}, u32[]{:S(2)}, u32[]{:S(2)}) %collective-permute-start.27) | collective-permute-done | bytes 270368 | tf_op jit(solution)/shard_map/ppermute | solution.py:47
  182.0 9.6 %mixer_back.1 = (f32[128,768]{1,0:T(8,128)S(1)}, f32[16,768]{1,0:T(8,128)S(1)}, f32[128,1536]{1,0:T(8,128)}, f32[128,1536]{1,0:T(8,128)}, f32[1,1536]{1,0:T(1,128)S(1)}, /*index=5*/f32[17,1536]{1,0:T(8,128)}) custom-call(s32[1]{0:T(128)} %bitcast.1.me_ref, f32[168,768]{1,0:T(8,128)} %copy-done.70, bf16[160,128]{1,0:T(8,128)(2,1)S(1)} %copy-done.15, ...), custom_call_target="tpu_custom_call" | custom-call | flops 330000007168 | bytes 300000000 | tf_op jit(solution)/shard_map/mixer_back/pallas_call | solution.py:274
  191.7 5.2 %late.2 = f32[768,1536]{1,0:T(8,128)} custom-call(s32[1]{0:T(128)} %bitcast.later_ref.which_ref.core_ref, f32[128,1536]{1,0:T(8,128)S(1)} %copy-done.50, f32[128,1536]{1,0:T(8,128)} %get-tuple-element.297.act_ref, f32[1,1536]{1,0:T(1,128)S(1)} %copy-done.20, f32[144,3072]{1,0:T(8,128)} %join.1.inner_ref.gate_z_ref, ...), custom_call_target="tpu_custom_call" | custom-call | flops 219999993856 | bytes 200000000 | tf_op jit(solution)/shard_map/late/pallas_call | solution.py:274
  198.6 8.2 %late.3 = (f32[768,1536]{1,0:T(8,128)}, f32[128,768]{1,0:T(8,128)S(1)}) custom-call(s32[1]{0:T(128)S(6)} %sub.76.which_ref, f32[128,1536]{1,0:T(8,128)S(1)} %copy-done.50, f32[128,1536]{1,0:T(8,128)} %get-tuple-element.297.act_ref, f32[1,1536]{1,0:T(1,128)S(1)} %copy-done.20, f32[144,3072]{1,0:T(8,128)} %join.1.inner_ref.gate_z_ref, ...), custom_call_target="tpu_custom_call" | custom-call | flops 219999993856 | bytes 200000000 | tf_op jit(solution)/shard_map/late/pallas_call | solution.py:274
  210.8 2.7 collective-permute-done.34.got_ref
  213.6 6.3 %collective-permute-done.36 = f32[192,768]{1,0:T(8,128)} collective-permute-done((f32[192,768]{1,0:T(8,128)}, f32[192,768]{1,0:T(8,128)}, u32[]{:S(2)}, u32[]{:S(2)}) %collective-permute-start.36) | collective-permute-done | bytes 589856 | tf_op jit(solution)/shard_map/ppermute | solution.py:47
  220.4 3.3 dynamic-slice_add_fusion.1
  227.9 3.5 collective-permute-done.38.got_ref
  234.7 5.0 %collective-permute-done.39.got_ref = f32[17,1536]{1,0:T(8,128)S(1)} collective-permute-done((f32[17,1536]{1,0:T(8,128)S(1)}, f32[17,1536]{1,0:T(8,128)S(1)}, u32[]{:S(2)}, u32[]{:S(2)}) %collective-permute-start.39) | collective-permute-done | bytes 104480 | tf_op jit(solution)/shard_map/ppermute | solution.py:47
  240.7 3.2 collective-permute-start.45
  243.9 8.6 %scan_back.3 = (f32[128,1536]{1,0:T(8,128)S(1)}, f32[128,1536]{1,0:T(8,128)}, f32[16,1536]{1,0:T(8,128)S(1)}, f32[80,128]{1,0:T(8,128)S(1)}) custom-call(f32[128,1536]{1,0:T(8,128)} %get-tuple-element.294.masked_ref, f32[128,1536]{1,0:T(8,128)} %get-tuple-element.295.steps_ref, f32[128,1536]{1,0:T(8,128)} %get-tuple-element.296.drive_ref, ...), custom_call_target="tpu_custom_call" | custom-call | flops 11000000512 | bytes 10000000 | tf_op jit(solution)/shard_map/scan_back/pallas_call | solution.py:274
  256.6 8.3 %scan_back.4 = (f32[128,1536]{1,0:T(8,128)S(1)}, f32[128,1536]{1,0:T(8,128)}, f32[16,1536]{1,0:T(8,128)S(1)}, f32[80,128]{1,0:T(8,128)S(1)}) custom-call(f32[128,1536]{1,0:T(8,128)} %get-tuple-element.294.masked_ref, f32[128,1536]{1,0:T(8,128)} %get-tuple-element.295.steps_ref, ...), custom_call_target="tpu_custom_call", output_to_operand_aliasing={{0}: (14, {}), {1}: (15, {}), {2}: (16, {})} | custom-call | flops 11000000512 | bytes 10000000 | tf_op jit(solution)/shard_map/scan_back/pallas_call | solution.py:274
  271.9 8.3 %scan_back.5 = (f32[128,1536]{1,0:T(8,128)S(1)}, f32[128,1536]{1,0:T(8,128)}, f32[16,1536]{1,0:T(8,128)S(1)}, f32[80,128]{1,0:T(8,128)S(1)}) custom-call(f32[128,1536]{1,0:T(8,128)} %get-tuple-element.294.masked_ref, f32[128,1536]{1,0:T(8,128)} %get-tuple-element.295.steps_ref, ...), custom_call_target="tpu_custom_call", output_to_operand_aliasing={{0}: (14, {}), {1}: (15, {}), {2}: (16, {})} | custom-call | flops 11000000512 | bytes 10000000 | tf_op jit(solution)/shard_map/scan_back/pallas_call | solution.py:274
  285.7 11.3 %input_back.1 = (f32[480,1536]{1,0:T(8,128)}, f32[480,1536]{1,0:T(8,128)}, f32[128,768]{1,0:T(8,128)S(1)}, f32[16,768]{1,0:T(8,128)S(1)}) custom-call(s32[1]{0:T(128)} %bitcast.later_ref.which_ref.core_ref, f32[80,128]{1,0:T(8,128)S(1)} %get-tuple-element.429.proj_a_ref, f32[80,128]{1,0:T(8,128)S(1)} %get-tuple-element.442.proj_b_ref, ...), custom_call_target="tpu_custom_call" | custom-call | flops 12099999744 | bytes 11000000 | tf_op jit(solution)/shard_map/input_back/pallas_call | solution.py:274
  297.9 5.7 %collective-permute-done.53 = f32[480,1536]{1,0:T(8,128)} collective-permute-done((f32[480,1536]{1,0:T(8,128)}, f32[480,1536]{1,0:T(8,128)}, u32[]{:S(2)}, u32[]{:S(2)}) %collective-permute-start.53) | collective-permute-done | bytes 2949152 | tf_op jit(solution)/shard_map/ppermute | solution.py:47
  303.6 3.2 dynamic-slice_add_fusion.5
  314.0 11.7 %collective-permute-done.52 = f32[192,384]{1,0:T(8,128)S(1)} collective-permute-done((f32[192,384]{1,0:T(8,128)}, f32[192,384]{1,0:T(8,128)S(1)}, u32[]{:S(2)}, u32[]{:S(2)}) %collective-permute-start.52) | collective-permute-done | bytes 294944 | tf_op jit(solution)/shard_map/ppermute | solution.py:47
  335.3 2.9 collective-permute-done.58
  346.0 2.5 maximum_add_fusion
  352.3 5.7 %collective-permute-done.62 = f32[120,384]{1,0:T(8,128)S(1)} collective-permute-done((f32[120,384]{1,0:T(8,128)S(1)}, f32[120,384]{1,0:T(8,128)S(1)}, u32[]{:S(2)}, u32[]{:S(2)}) %collective-permute-start.62) | collective-permute-done | bytes 184352 | tf_op jit(solution)/shard_map/ppermute | solution.py:47
  367.4 9.9 %collective-permute-done.67 = f32[120,384]{1,0:T(8,128)S(1)} collective-permute-done((f32[120,384]{1,0:T(8,128)S(1)}, f32[120,384]{1,0:T(8,128)S(1)}, u32[]{:S(2)}, u32[]{:S(2)}) %collective-permute-start.67) | collective-permute-done | bytes 184352 | tf_op jit(solution)/shard_map/ppermute | solution.py:47
  377.5 6.3 %collective-permute-done.64 = f32[192,1536]{1,0:T(8,128)S(1)} collective-permute-done((f32[192,1536]{1,0:T(8,128)S(1)}, f32[192,1536]{1,0:T(8,128)S(1)}, u32[]{:S(2)}, u32[]{:S(2)}) %collective-permute-start.64) | collective-permute-done | bytes 1179680 | tf_op jit(solution)/shard_map/ppermute | solution.py:47
  385.6 5.1 %collective-permute-done.65 = f32[192,1536]{1,0:T(8,128)S(1)} collective-permute-done((f32[192,1536]{1,0:T(8,128)S(1)}, f32[192,1536]{1,0:T(8,128)S(1)}, u32[]{:S(2)}, u32[]{:S(2)}) %collective-permute-start.65) | collective-permute-done | bytes 1179680 | tf_op jit(solution)/shard_map/ppermute | solution.py:47
  396.2 8.0 %collective-permute-done.72 = f32[60,1536]{1,0:T(8,128)S(1)} collective-permute-done((f32[60,1536]{1,0:T(8,128)S(1)}, f32[60,1536]{1,0:T(8,128)S(1)}, u32[]{:S(2)}, u32[]{:S(2)}) %collective-permute-start.72) | collective-permute-done | bytes 368672 | tf_op jit(solution)/shard_map/ppermute | solution.py:47
  409.5 7.8 %finish_late.1 = (f32[768,3072]{1,0:T(8,128)}, f32[2,768,768]{2,1,0:T(8,128)}) custom-call(s32[1]{0:T(128)} %bitcast.later_ref.which_ref.core_ref, f32[384,1536]{1,0:T(8,128)} %pad_maximum_fusion.first_ref, f32[384,1536]{1,0:T(8,128)} %pad_maximum_fusion.1.second_ref, f32[384,1536]{1,0:T(8,128)} %collective-permute-done.73.got_first_ref, ...), custom_call_target="tpu_custom_call" | custom-call | flops 8800000000 | bytes 8000000 | tf_op jit(solution)/shard_map/finish_late/pallas_call | solution.py:274
  417.2 5.4 %collective-permute-done.75 = f32[120,1536]{1,0:T(8,128)S(1)} collective-permute-done((f32[120,1536]{1,0:T(8,128)S(1)}, f32[120,1536]{1,0:T(8,128)S(1)}, u32[]{:S(2)}, u32[]{:S(2)}) %collective-permute-start.75) | collective-permute-done | bytes 737312 | tf_op jit(solution)/shard_map/ppermute | solution.py:47
  424.1 2.8 collective-permute-done.77.got_first_ref
  430.0 5.5 %finish.1 = (f32[768,3072]{1,0:T(8,128)}, f32[80,1536]{1,0:T(8,128)}, f32[48,1536]{1,0:T(8,128)}, f32[16,1536]{1,0:T(8,128)}, f32[4,1536]{1,0:T(4,128)}, /*index=5*/f32[8,1536]{1,0:T(8,128)S(1)}, f32[32,512]{1,0:T(8,128)S(1)}) custom-call(s32[1]{0:T(128)} %bitcast.later_ref.which_ref.core_ref, ...), custom_call_target="tpu_custom_call", output_to_operand_aliasing={{0}: (5, {})} | custom-call | flops 6600000000 | bytes 6000000 | tf_op jit(solution)/shard_map/finish/pallas_call | solution.py:274
  (420 shorter events, 145.5 us)
Async XLA Ops:
  3.8 32.4 %collective-permute-start.3 = (f32[384,768]{1,0:T(8,128)}, f32[384,768]{1,0:T(8,128)}, u32[]{:S(2)}, u32[]{:S(2)}) collective-permute-start(f32[384,768]{1,0:T(8,128)} %bitcast.47), channel_id=1, source_target_pairs={{0,4},{1,5},{2,6},{3,7},{4,0},{5,1},{6,2},{7,3},{8,12},{9,13},{10,... | collective-permute-start | bytes 3538952 | tf_op jit(solution)/shard_map/ppermute | solution.py:47
  23.7 25.1 %collective-permute-start.7 = (f32[160,768]{1,0:T(8,128)}, f32[160,768]{1,0:T(8,128)}, u32[]{:S(2)}, u32[]{:S(2)}) collective-permute-start(f32[160,768]{1,0:T(8,128)} %pad_maximum_fusion.14.refs_0_.refs_8_), channel_id=1, source_target_pairs={{0,16},{1,17},{2,18},{3,19},{4,20},{5,21},{6,22},{7,23},{8,24},{9,... | collective-permute-start | bytes 1474568 | tf_op jit(solution)/shard_map/ppermute | solution.py:47
  26.3 22.7 %collective-permute-start.6 = (f32[160,768]{1,0:T(8,128)}, f32[160,768]{1,0:T(8,128)}, u32[]{:S(2)}, u32[]{:S(2)}) collective-permute-start(f32[160,768]{1,0:T(8,128)} %pad_maximum_fusion.14.refs_0_.refs_8_), channel_id=1, source_target_pairs={{0,8},{1,9},{2,10},{3,11},{4,12},{5,13},{6,14},{7,15},{8,0},{9,1},... | collective-permute-start | bytes 1474568 | tf_op jit(solution)/shard_map/ppermute | solution.py:47
  61.9 20.6 %collective-permute-start.12 = (f32[384,384]{1,0:T(8,128)}, f32[384,384]{1,0:T(8,128)}, u32[]{:S(2)}, u32[]{:S(2)}) collective-permute-start(f32[384,384]{1,0:T(8,128)} %get-tuple-element.597), channel_id=1, source_target_pairs={{0,4},{1,5},{2,6},{3,7},{4,0},{5,1},{6,2},{7,3},{8,12},{9,13},{10,... | collective-permute-start | bytes 1769480 | tf_op jit(solution)/shard_map/ppermute | solution.py:47
  67.3 15.3 %collective-permute-start.11 = (f32[160,768]{1,0:T(8,128)}, f32[160,768]{1,0:T(8,128)}, u32[]{:S(2)}, u32[]{:S(2)}) collective-permute-start(f32[160,768]{1,0:T(8,128)} %collective-permute-done.7.refs_2_.refs_10_), channel_id=1, source_target_pairs={{0,8},{1,9},{2,10},{3,11},{4,12},{5,13},{6,14},{7,15},{8,0},{9,1},... | collective-permute-start | bytes 1474568 | tf_op jit(solution)/shard_map/ppermute | solution.py:47
  82.7 16.9 %collective-permute-start.17 = (f32[384,384]{1,0:T(8,128)}, f32[384,384]{1,0:T(8,128)}, u32[]{:S(2)}, u32[]{:S(2)}) collective-permute-start(f32[384,384]{1,0:T(8,128)} %get-tuple-element.331), channel_id=1, source_target_pairs={{0,4},{1,5},{2,6},{3,7},{4,0},{5,1},{6,2},{7,3},{8,12},{9,13},{10,... | collective-permute-start | bytes 1769480 | tf_op jit(solution)/shard_map/ppermute | solution.py:47
  86.5 23.0 %collective-permute-start.15 = (f32[88,768]{1,0:T(8,128)}, f32[88,768]{1,0:T(8,128)}, u32[]{:S(2)}, u32[]{:S(2)}) collective-permute-start(f32[88,768]{1,0:T(8,128)} %get-tuple-element.332.refs_0_), channel_id=1, source_target_pairs={{0,16},{1,17},{2,18},{3,19},{4,20},{5,21},{6,22},{7,23},{8,24},{9,... | collective-permute-start | bytes 811016 | tf_op jit(solution)/shard_map/ppermute | solution.py:47
  89.8 19.8 %collective-permute-start.14 = (f32[88,768]{1,0:T(8,128)}, f32[88,768]{1,0:T(8,128)}, u32[]{:S(2)}, u32[]{:S(2)}) collective-permute-start(f32[88,768]{1,0:T(8,128)} %get-tuple-element.332.refs_0_), channel_id=1, source_target_pairs={{0,8},{1,9},{2,10},{3,11},{4,12},{5,13},{6,14},{7,15},{8,0},{9,1},... | collective-permute-start | bytes 811016 | tf_op jit(solution)/shard_map/ppermute | solution.py:47
  99.6 14.8 %collective-permute-start.20 = (f32[88,768]{1,0:T(8,128)}, f32[88,768]{1,0:T(8,128)S(1)}, u32[]{:S(2)}, u32[]{:S(2)}) collective-permute-start(f32[88,768]{1,0:T(8,128)} %collective-permute-done.16.refs_1_), channel_id=1, source_target_pairs={{0,16},{1,17},{2,18},{3,19},{4,20},{5,21},{6,22},{7,23},{8,24},{9,... | collective-permute-start | bytes 811016 | tf_op jit(solution)/shard_map/ppermute | solution.py:47
  101.2 14.9 %collective-permute-start.19 = (f32[88,768]{1,0:T(8,128)}, f32[88,768]{1,0:T(8,128)S(1)}, u32[]{:S(2)}, u32[]{:S(2)}) collective-permute-start(f32[88,768]{1,0:T(8,128)} %collective-permute-done.16.refs_1_), channel_id=1, source_target_pairs={{0,8},{1,9},{2,10},{3,11},{4,12},{5,13},{6,14},{7,15},{8,0},{9,1},... | collective-permute-start | bytes 811016 | tf_op jit(solution)/shard_map/ppermute | solution.py:47
  109.6 17.7 %collective-permute-start.18 = (f32[88,768]{1,0:T(8,128)}, f32[88,768]{1,0:T(8,128)S(1)}, u32[]{:S(2)}, u32[]{:S(2)}) collective-permute-start(f32[88,768]{1,0:T(8,128)} %collective-permute-done.15.refs_0_.refs_4_), channel_id=1, source_target_pairs={{0,8},{1,9},{2,10},{3,11},{4,12},{5,13},{6,14},{7,15},{8,0},{9,1},... | collective-permute-start | bytes 811016 | tf_op jit(solution)/shard_map/ppermute | solution.py:47
  116.1 11.2 %collective-permute-start.21 = (f32[88,768]{1,0:T(8,128)S(1)}, f32[88,768]{1,0:T(8,128)S(1)}, u32[]{:S(2)}, u32[]{:S(2)}) collective-permute-start(f32[88,768]{1,0:T(8,128)S(1)} %collective-permute-done.20.refs_1_.refs_5_), channel_id=1, source_target_pairs={{0,8},{1,9},{2,10},{3,11},{4,12},{5,13},{6,14},{7,15},{8,0},{9,1},... | collective-permute-start | bytes 811016 | tf_op jit(solution)/shard_map/ppermute | solution.py:47
  140.9 21.1 %collective-permute-start.24 = (f32[88,768]{1,0:T(8,128)}, f32[88,768]{1,0:T(8,128)}, u32[]{:S(2)}, u32[]{:S(2)}) collective-permute-start(f32[88,768]{1,0:T(8,128)} %add.342), channel_id=1, source_target_pairs={{0,16},{1,17},{2,18},{3,19},{4,20},{5,21},{6,22},{7,23},{8,24},{9,... | collective-permute-start | bytes 811016 | tf_op jit(solution)/shard_map/ppermute | solution.py:47
  142.5 19.6 %collective-permute-start.23 = (f32[88,768]{1,0:T(8,128)}, f32[88,768]{1,0:T(8,128)}, u32[]{:S(2)}, u32[]{:S(2)}) collective-permute-start(f32[88,768]{1,0:T(8,128)} %get-tuple-element.363), channel_id=1, source_target_pairs={{0,8},{1,9},{2,10},{3,11},{4,12},{5,13},{6,14},{7,15},{8,0},{9,1},... | collective-permute-start | bytes 811016 | tf_op jit(solution)/shard_map/ppermute | solution.py:47
  144.0 19.3 %collective-permute-start.25 = (f32[88,768]{1,0:T(8,128)}, f32[88,768]{1,0:T(8,128)}, u32[]{:S(2)}, u32[]{:S(2)}) collective-permute-start(f32[88,768]{1,0:T(8,128)} %get-tuple-element.366), channel_id=1, source_target_pairs={{0,8},{1,9},{2,10},{3,11},{4,12},{5,13},{6,14},{7,15},{8,0},{9,1},... | collective-permute-start | bytes 811016 | tf_op jit(solution)/shard_map/ppermute | solution.py:47
  164.3 12.7 %collective-permute-start.27 = (f32[88,768]{1,0:T(8,128)S(1)}, f32[88,768]{1,0:T(8,128)S(1)}, u32[]{:S(2)}, u32[]{:S(2)}) collective-permute-start(f32[88,768]{1,0:T(8,128)S(1)} %add.345), channel_id=1, source_target_pairs={{0,16},{1,17},{2,18},{3,19},{4,20},{5,21},{6,22},{7,23},{8,24},{9,... | collective-permute-start | bytes 811016 | tf_op jit(solution)/shard_map/ppermute | solution.py:47
  165.7 11.3 %collective-permute-start.26 = (f32[88,768]{1,0:T(8,128)S(1)}, f32[88,768]{1,0:T(8,128)S(1)}, u32[]{:S(2)}, u32[]{:S(2)}) collective-permute-start(f32[88,768]{1,0:T(8,128)S(1)} %get-tuple-element.389), channel_id=1, source_target_pairs={{0,8},{1,9},{2,10},{3,11},{4,12},{5,13},{6,14},{7,15},{8,0},{9,1},... | collective-permute-start | bytes 811016 | tf_op jit(solution)/shard_map/ppermute | solution.py:47
  178.5 18.4 %collective-permute-start.30 = (f32[384,384]{1,0:T(8,128)}, f32[384,384]{1,0:T(8,128)}, u32[]{:S(2)}, u32[]{:S(2)}) collective-permute-start(f32[384,384]{1,0:T(8,128)} %get-tuple-element.595), channel_id=1, source_target_pairs={{0,4},{1,5},{2,6},{3,7},{4,0},{5,1},{6,2},{7,3},{8,12},{9,13},{10,... | collective-permute-start | bytes 1769480 | tf_op jit(solution)/shard_map/ppermute | solution.py:47
  180.3 27.6 %collective-permute-start.32 = (f32[160,768]{1,0:T(8,128)}, f32[160,768]{1,0:T(8,128)}, u32[]{:S(2)}, u32[]{:S(2)}) collective-permute-start(f32[160,768]{1,0:T(8,128)} %get-tuple-element.408), channel_id=1, source_target_pairs={{0,8},{1,9},{2,10},{3,11},{4,12},{5,13},{6,14},{7,15},{8,0},{9,1},... | collective-permute-start | bytes 1474568 | tf_op jit(solution)/shard_map/ppermute | solution.py:47
  181.1 26.9 %collective-permute-start.33 = (f32[384,384]{1,0:T(8,128)}, f32[384,384]{1,0:T(8,128)}, u32[]{:S(2)}, u32[]{:S(2)}) collective-permute-start(f32[384,384]{1,0:T(8,128)} %get-tuple-element.411), channel_id=1, source_target_pairs={{0,4},{1,5},{2,6},{3,7},{4,0},{5,1},{6,2},{7,3},{8,12},{9,13},{10,... | collective-permute-start | bytes 1769480 | tf_op jit(solution)/shard_map/ppermute | solution.py:47
  196.9 22.9 %collective-permute-start.35 = (f32[768,1536]{1,0:T(8,128)}, f32[768,1536]{1,0:T(8,128)}, u32[]{:S(2)}, u32[]{:S(2)}) collective-permute-start(f32[768,1536]{1,0:T(8,128)} %late.2), channel_id=1, source_target_pairs={{0,1},{1,0},{2,3},{3,2},{4,5},{5,4},{6,7},{7,6},{8,9},{9,8},{10,11... | collective-permute-start | bytes 14155784 | tf_op jit(solution)/shard_map/ppermute | solution.py:47
  197.4 22.4 %collective-permute-start.36 = (f32[192,768]{1,0:T(8,128)}, f32[192,768]{1,0:T(8,128)}, u32[]{:S(2)}, u32[]{:S(2)}) collective-permute-start(f32[192,768]{1,0:T(8,128)} %get-tuple-element.409), channel_id=1, source_target_pairs={{0,4},{1,5},{2,6},{3,7},{4,0},{5,1},{6,2},{7,3},{8,12},{9,13},{10,... | collective-permute-start | bytes 1769480 | tf_op jit(solution)/shard_map/ppermute | solution.py:47
  223.8 28.8 %collective-permute-start.40 = (f32[192,1536]{1,0:T(8,128)}, f32[192,1536]{1,0:T(8,128)S(1)}, u32[]{:S(2)}, u32[]{:S(2)}) collective-permute-start(f32[192,1536]{1,0:T(8,128)} %get-tuple-element.564), channel_id=1, source_target_pairs={{0,4},{1,5},{2,6},{3,7},{4,0},{5,1},{6,2},{7,3},{8,12},{9,13},{10,... | collective-permute-start | bytes 3538952 | tf_op jit(solution)/shard_map/ppermute | solution.py:47
  225.2 27.3 %collective-permute-start.41 = (f32[192,1536]{1,0:T(8,128)}, f32[192,1536]{1,0:T(8,128)}, u32[]{:S(2)}, u32[]{:S(2)}) collective-permute-start(f32[192,1536]{1,0:T(8,128)} %get-tuple-element.563), channel_id=1, source_target_pairs={{0,2},{1,3},{2,0},{3,1},{4,6},{5,7},{6,4},{7,5},{8,10},{9,11},{10,... | collective-permute-start | bytes 3538952 | tf_op jit(solution)/shard_map/ppermute | solution.py:47
  240.7 27.8 %collective-permute-start.44 = (f32[160,768]{1,0:T(8,128)S(1)}, f32[160,768]{1,0:T(8,128)S(1)}, u32[]{:S(2)}, u32[]{:S(2)}) collective-permute-start(f32[160,768]{1,0:T(8,128)S(1)} %copy-done.80), channel_id=1, source_target_pairs={{0,8},{1,9},{2,10},{3,11},{4,12},{5,13},{6,14},{7,15},{8,0},{9,1},... | collective-permute-start | bytes 1474568 | tf_op jit(solution)/shard_map/ppermute | solution.py:47
  240.7 27.8 %collective-permute-start.45 = (f32[160,768]{1,0:T(8,128)S(1)}, f32[160,768]{1,0:T(8,128)S(1)}, u32[]{:S(2)}, u32[]{:S(2)}) collective-permute-start(f32[160,768]{1,0:T(8,128)S(1)} %add.347), channel_id=1, source_target_pairs={{0,16},{1,17},{2,18},{3,19},{4,20},{5,21},{6,22},{7,23},{8,24},{9,... | collective-permute-start | bytes 1474568 | tf_op jit(solution)/shard_map/ppermute | solution.py:47
  252.7 15.8 %collective-permute-start.42 = (f32[96,1536]{1,0:T(8,128)S(1)}, f32[96,1536]{1,0:T(8,128)S(1)}, u32[]{:S(2)}, u32[]{:S(2)}) collective-permute-start(f32[96,1536]{1,0:T(8,128)S(1)} %dynamic-slice_add_fusion.11), channel_id=1, source_target_pairs={{0,2},{1,3},{2,0},{3,1},{4,6},{5,7},{6,4},{7,5},{8,10},{9,11},{10,... | collective-permute-start | bytes 1769480 | tf_op jit(solution)/shard_map/ppermute | solution.py:47
  255.0 13.4 %collective-permute-start.43 = (f32[96,1536]{1,0:T(8,128)S(1)}, f32[96,1536]{1,0:T(8,128)S(1)}, u32[]{:S(2)}, u32[]{:S(2)}) collective-permute-start(f32[96,1536]{1,0:T(8,128)S(1)} %dynamic-slice_add_fusion.9), channel_id=1, source_target_pairs={{0,4},{1,5},{2,6},{3,7},{4,0},{5,1},{6,2},{7,3},{8,12},{9,13},{10,... | collective-permute-start | bytes 1769480 | tf_op jit(solution)/shard_map/ppermute | solution.py:47
  270.5 11.9 %collective-permute-start.48 = (f32[192,768]{1,0:T(8,128)S(1)}, f32[192,768]{1,0:T(8,128)S(1)}, u32[]{:S(2)}, u32[]{:S(2)}) collective-permute-start(f32[192,768]{1,0:T(8,128)S(1)} %copy-done.63), channel_id=1, source_target_pairs={{0,4},{1,5},{2,6},{3,7},{4,0},{5,1},{6,2},{7,3},{8,12},{9,13},{10,... | collective-permute-start | bytes 1769480 | tf_op jit(solution)/shard_map/ppermute | solution.py:47
  282.5 14.6 %collective-permute-start.49 = (f32[192,384]{1,0:T(8,128)S(1)}, f32[192,384]{1,0:T(8,128)S(1)}, u32[]{:S(2)}, u32[]{:S(2)}) collective-permute-start(f32[192,384]{1,0:T(8,128)S(1)} %get-tuple-element.481), channel_id=1, source_target_pairs={{0,8},{1,9},{2,10},{3,11},{4,12},{5,13},{6,14},{7,15},{8,0},{9,1},... | collective-permute-start | bytes 884744 | tf_op jit(solution)/shard_map/ppermute | solution.py:47
  284.1 13.0 %collective-permute-start.50 = (f32[192,384]{1,0:T(8,128)S(1)}, f32[192,384]{1,0:T(8,128)S(1)}, u32[]{:S(2)}, u32[]{:S(2)}) collective-permute-start(f32[192,384]{1,0:T(8,128)S(1)} %fusion.3), channel_id=1, source_target_pairs={{0,16},{1,17},{2,18},{3,19},{4,20},{5,21},{6,22},{7,23},{8,24},{9,... | collective-permute-start | bytes 884744 | tf_op jit(solution)/shard_map/ppermute | solution.py:47
  306.8 18.8 %collective-permute-start.55 = (f32[120,1536]{1,0:T(8,128)}, f32[120,1536]{1,0:T(8,128)}, u32[]{:S(2)}, u32[]{:S(2)}) collective-permute-start(f32[120,1536]{1,0:T(8,128)} %get-tuple-element.565), channel_id=1, source_target_pairs={{0,2},{1,3},{2,0},{3,1},{4,6},{5,7},{6,4},{7,5},{8,10},{9,11},{10,... | collective-permute-start | bytes 2211848 | tf_op jit(solution)/shard_map/ppermute | solution.py:47
  308.5 18.6 %collective-permute-start.54 = (f32[120,1536]{1,0:T(8,128)}, f32[120,1536]{1,0:T(8,128)}, u32[]{:S(2)}, u32[]{:S(2)}) collective-permute-start(f32[120,1536]{1,0:T(8,128)} %get-tuple-element.566), channel_id=1, source_target_pairs={{0,4},{1,5},{2,6},{3,7},{4,0},{5,1},{6,2},{7,3},{8,12},{9,13},{10,... | collective-permute-start | bytes 2211848 | tf_op jit(solution)/shard_map/ppermute | solution.py:47
  309.7 16.0 %collective-permute-start.52 = (f32[192,384]{1,0:T(8,128)}, f32[192,384]{1,0:T(8,128)S(1)}, u32[]{:S(2)}, u32[]{:S(2)}) collective-permute-start(f32[192,384]{1,0:T(8,128)} %add_add_fusion.1), channel_id=1, source_target_pairs={{0,16},{1,17},{2,18},{3,19},{4,20},{5,21},{6,22},{7,23},{8,24},{9,... | collective-permute-start | bytes 884744 | tf_op jit(solution)/shard_map/ppermute | solution.py:47
  310.9 14.7 %collective-permute-start.51 = (f32[192,384]{1,0:T(8,128)}, f32[192,384]{1,0:T(8,128)S(1)}, u32[]{:S(2)}, u32[]{:S(2)}) collective-permute-start(f32[192,384]{1,0:T(8,128)} %add_add_fusion.1), channel_id=1, source_target_pairs={{0,8},{1,9},{2,10},{3,11},{4,12},{5,13},{6,14},{7,15},{8,0},{9,1},... | collective-permute-start | bytes 884744 | tf_op jit(solution)/shard_map/ppermute | solution.py:47
  343.3 14.7 %collective-permute-start.62 = (f32[120,384]{1,0:T(8,128)S(1)}, f32[120,384]{1,0:T(8,128)S(1)}, u32[]{:S(2)}, u32[]{:S(2)}) collective-permute-start(f32[120,384]{1,0:T(8,128)S(1)} %get-tuple-element.583), channel_id=1, source_target_pairs={{0,16},{1,17},{2,18},{3,19},{4,20},{5,21},{6,22},{7,23},{8,24},{9,... | collective-permute-start | bytes 552968 | tf_op jit(solution)/shard_map/ppermute | solution.py:47
  344.4 13.6 %collective-permute-start.60 = (f32[96,1536]{1,0:T(8,128)S(1)}, f32[96,1536]{1,0:T(8,128)S(1)}, u32[]{:S(2)}, u32[]{:S(2)}) collective-permute-start(f32[96,1536]{1,0:T(8,128)S(1)} %get-tuple-element.586), channel_id=1, source_target_pairs={{0,4},{1,5},{2,6},{3,7},{4,0},{5,1},{6,2},{7,3},{8,12},{9,13},{10,... | collective-permute-start | bytes 1769480 | tf_op jit(solution)/shard_map/ppermute | solution.py:47
  345.4 12.7 %collective-permute-start.59 = (f32[96,1536]{1,0:T(8,128)S(1)}, f32[96,1536]{1,0:T(8,128)S(1)}, u32[]{:S(2)}, u32[]{:S(2)}) collective-permute-start(f32[96,1536]{1,0:T(8,128)S(1)} %get-tuple-element.587), channel_id=1, source_target_pairs={{0,2},{1,3},{2,0},{3,1},{4,6},{5,7},{6,4},{7,5},{8,10},{9,11},{10,... | collective-permute-start | bytes 1769480 | tf_op jit(solution)/shard_map/ppermute | solution.py:47
  352.0 12.6 %collective-permute-start.69 = (f32[80,768]{1,0:T(8,128)S(1)}, f32[80,768]{1,0:T(8,128)S(1)}, u32[]{:S(2)}, u32[]{:S(2)}) collective-permute-start(f32[80,768]{1,0:T(8,128)S(1)} %pad_maximum_fusion.24), channel_id=1, source_target_pairs={{0,1},{1,0},{2,3},{3,2},{4,5},{5,4},{6,7},{7,6},{8,9},{9,8},{10,11... | collective-permute-start | bytes 737288 | tf_op jit(solution)/shard_map/ppermute | solution.py:47
  358.4 25.3 %collective-permute-start.64 = (f32[192,1536]{1,0:T(8,128)S(1)}, f32[192,1536]{1,0:T(8,128)S(1)}, u32[]{:S(2)}, u32[]{:S(2)}) collective-permute-start(f32[192,1536]{1,0:T(8,128)S(1)} %pad_maximum_fusion.7), channel_id=1, source_target_pairs={{0,4},{1,5},{2,6},{3,7},{4,0},{5,1},{6,2},{7,3},{8,12},{9,13},{10,... | collective-permute-start | bytes 3538952 | tf_op jit(solution)/shard_map/ppermute | solution.py:47
  362.1 15.2 %collective-permute-start.67 = (f32[120,384]{1,0:T(8,128)S(1)}, f32[120,384]{1,0:T(8,128)S(1)}, u32[]{:S(2)}, u32[]{:S(2)}) collective-permute-start(f32[120,384]{1,0:T(8,128)S(1)} %add_add_fusion.4), channel_id=1, source_target_pairs={{0,16},{1,17},{2,18},{3,19},{4,20},{5,21},{6,22},{7,23},{8,24},{9,... | collective-permute-start | bytes 552968 | tf_op jit(solution)/shard_map/ppermute | solution.py:47
  363.0 14.4 %collective-permute-start.66 = (f32[120,384]{1,0:T(8,128)S(1)}, f32[120,384]{1,0:T(8,128)S(1)}, u32[]{:S(2)}, u32[]{:S(2)}) collective-permute-start(f32[120,384]{1,0:T(8,128)S(1)} %add_add_fusion.4), channel_id=1, source_target_pairs={{0,24},{1,25},{2,26},{3,27},{4,28},{5,29},{6,30},{7,31},{8,16},{9,... | collective-permute-start | bytes 552968 | tf_op jit(solution)/shard_map/ppermute | solution.py:47
  364.6 26.1 %collective-permute-start.65 = (f32[192,1536]{1,0:T(8,128)S(1)}, f32[192,1536]{1,0:T(8,128)S(1)}, u32[]{:S(2)}, u32[]{:S(2)}) collective-permute-start(f32[192,1536]{1,0:T(8,128)S(1)} %pad_maximum_fusion.8), channel_id=1, source_target_pairs={{0,2},{1,3},{2,0},{3,1},{4,6},{5,7},{6,4},{7,5},{8,10},{9,11},{10,... | collective-permute-start | bytes 3538952 | tf_op jit(solution)/shard_map/ppermute | solution.py:47
  392.5 12.9 %collective-permute-start.73 = (f32[384,1536]{1,0:T(8,128)}, f32[384,1536]{1,0:T(8,128)}, u32[]{:S(2)}, u32[]{:S(2)}) collective-permute-start(f32[384,1536]{1,0:T(8,128)} %pad_maximum_fusion.first_ref), channel_id=1, source_target_pairs={{0,1},{1,0},{2,3},{3,2},{4,5},{5,4},{6,7},{7,6},{8,9},{9,8},{10,11... | collective-permute-start | bytes 7077896 | tf_op jit(solution)/shard_map/ppermute | solution.py:47
  392.5 12.9 %collective-permute-start.74 = (f32[384,1536]{1,0:T(8,128)}, f32[384,1536]{1,0:T(8,128)}, u32[]{:S(2)}, u32[]{:S(2)}) collective-permute-start(f32[384,1536]{1,0:T(8,128)} %pad_maximum_fusion.1.second_ref), channel_id=1, source_target_pairs={{0,1},{1,0},{2,3},{3,2},{4,5},{5,4},{6,7},{7,6},{8,9},{9,8},{10,11... | collective-permute-start | bytes 7077896 | tf_op jit(solution)/shard_map/ppermute | solution.py:47
  393.1 11.1 %collective-permute-start.72 = (f32[60,1536]{1,0:T(8,128)S(1)}, f32[60,1536]{1,0:T(8,128)S(1)}, u32[]{:S(2)}, u32[]{:S(2)}) collective-permute-start(f32[60,1536]{1,0:T(8,128)S(1)} %get-tuple-element.604), channel_id=1, source_target_pairs={{0,4},{1,5},{2,6},{3,7},{4,0},{5,1},{6,2},{7,3},{8,12},{9,13},{10,... | collective-permute-start | bytes 1105928 | tf_op jit(solution)/shard_map/ppermute | solution.py:47
  405.4 17.3 %collective-permute-start.75 = (f32[120,1536]{1,0:T(8,128)S(1)}, f32[120,1536]{1,0:T(8,128)S(1)}, u32[]{:S(2)}, u32[]{:S(2)}) collective-permute-start(f32[120,1536]{1,0:T(8,128)S(1)} %pad_maximum_fusion.12), channel_id=1, source_target_pairs={{0,4},{1,5},{2,6},{3,7},{4,0},{5,1},{6,2},{7,3},{8,12},{9,13},{10,... | collective-permute-start | bytes 2211848 | tf_op jit(solution)/shard_map/ppermute | solution.py:47
  406.3 16.9 %collective-permute-start.76 = (f32[120,1536]{1,0:T(8,128)S(1)}, f32[120,1536]{1,0:T(8,128)S(1)}, u32[]{:S(2)}, u32[]{:S(2)}) collective-permute-start(f32[120,1536]{1,0:T(8,128)S(1)} %pad_maximum_fusion.13), channel_id=1, source_target_pairs={{0,2},{1,3},{2,0},{3,1},{4,6},{5,7},{6,4},{7,5},{8,10},{9,11},{10,... | collective-permute-start | bytes 2211848 | tf_op jit(solution)/shard_map/ppermute | solution.py:47
  (112 other events, 798.4 us)
